TPU v7x, 128 devices: a whole 4x4x4 slice. The times are simulated.
128 devices in a mesh: member: 4 (over y_lo, core), region: 32 (over z, y_hi, x).
Axes of the slice: x: 4, y: 4 (y_hi: 2, y_lo: 2; y = y_hi * 2 + y_lo), z: 4, core: 2. Of those that a mesh axis runs over, the one named last changes fastest.
Arguments:
- latent: bfloat16 [8, 4096, 1024], P('member', 'region'), may hold values from -6 to 6
- w_node: bfloat16 [1024, 1024], replicated, may hold values from -0.1875 to 0.1875
- bias: float32 [1024], replicated, may hold values from -3 to 3
- w_out: bfloat16 [100, 1024], replicated, may hold values from -0.1875 to 0.1875
- edge_src: int32 [65536, 3], P('region'), may hold values from 0 to 383
- edge_weight: float32 [65536, 3], P('region'), may hold values from 0.2 to 0.6
- target: float32 [100, 65536], P(None, 'region'), may hold values from -6 to 6
- area: float32 [65536], P('region'), may hold values from 0.3 to 30
Outputs:
- grad_node: float32 [1024, 1024], P('region')
- grad_out: float32 [100, 1024], replicated
- grad_bias: float32 [1024], replicated
- loss: float32 [32], P('region')
Inputs may be any that keep to these rules, and one draw needn't show every extreme that they name: `edge_src`: an index into the latent nodes of the previous region, then the grid point's own region, then the next region, 128 each; regions form a loop.
All inputs are finite; a program needn't handle non-finite values.
Results may differ from a plain program's by a relative error of at most 0.007.
Values may be sent and summed in bfloat16 or wider, within the bound.
No kernel may reach another device: no remote copies, remote signals or barrier semaphores. Data moves between devices by JAX's collectives and lax.ppermute only.
A program may use at most 128 MiB of HBM per device.

v0:
```python
import jax
import jax.numpy as jnp
from jax import lax
from jax.experimental import pallas as pl
from jax.experimental.pallas import tpu as pltpu
from jax.sharding import Mesh
from jax.sharding import PartitionSpec as P

REGION = ("z", "yhi", "x")
MEMBER = ("ylo", "core")
CHIPS = ("ylo", "z", "yhi", "x")
EVERY = ("ylo", "core", "z", "yhi", "x")

SMOOTH_SQ = 0.01
C0 = 0.7978845608028654
C1 = 0.044715
WIDE = 256
PAD = 128
bf16 = jnp.bfloat16
f32 = jnp.float32
f16 = jnp.float16


def dot(a, b, ca=1, cb=0):
    return lax.dot_general(a, b, (((ca,), (cb,)), ((), ())), preferred_element_type=f32)


def params(semantics, mib=48):
    return pltpu.CompilerParams(dimension_semantics=semantics, vmem_limit_bytes=mib << 20)


def prep_kernel(src, weight, at_hi, at_lo, a_hi, a_lo):
    nodes, wide = at_hi.shape
    place = lax.broadcasted_iota(jnp.int32, (nodes, wide), 0)
    total = jnp.zeros((nodes, wide), f32)
    for k in range(src.shape[0]):
        total = total + jnp.where(src[k : k + 1, :] == place, weight[k : k + 1, :], 0.0)
    high = total.astype(bf16)
    low = total - high.astype(f32)
    at_hi[...] = high
    at_lo[...] = low.astype(bf16)
    a_hi[...] = total.T.astype(bf16)
    a_lo[...] = low.T.astype(bf16)


def prep(src, weight, nodes):
    fan, points = src.shape
    row = pl.BlockSpec((fan, WIDE), lambda i: (0, i))
    wide = pl.BlockSpec((nodes, WIDE), lambda i: (0, i))
    tall = pl.BlockSpec((WIDE, nodes), lambda i: (i, 0))
    return pl.pallas_call(
        prep_kernel,
        grid=(points // WIDE,),
        in_specs=[row, row],
        out_specs=[wide, wide, tall, tall],
        out_shape=[jax.ShapeDtypeStruct((nodes, points), bf16)] * 2
        + [jax.ShapeDtypeStruct((points, nodes), bf16)] * 2,
        compiler_params=params(("arbitrary",)),
        name="prep",
    )(src, weight)


def forward_kernel(low, own, high, w_node, at_hi, at_lo, bias, w_out, target, hid, slope, err):
    step = pl.program_id(0)
    parts = [dot(block[...], w_node[...]).T.astype(bf16) for block in (low, own, high)]
    proj = jnp.concatenate(parts, axis=1)
    shift = bias[...]
    for g in range(at_hi.shape[1] // WIDE):
        at = slice(g * WIDE, (g + 1) * WIDE)
        x = dot(proj, at_hi[:, at]) + dot(proj, at_lo[:, at]) + shift
        sq = x * x
        u = 0.5 + 0.5 * jnp.tanh(x * (C0 + (C0 * C1) * sq))
        h = x * u
        hb = h.astype(bf16)
        hid[:, at] = hb
        slope[:, at] = (u + h * (1.0 - u) * (2.0 * C0 + (6.0 * C0 * C1) * sq)).astype(bf16)
        part = dot(w_out[...], hb)

        @pl.when(step == 0)
        def _():
            err[:, at] = part - target[:, at]

        @pl.when(step > 0)
        def _():
            err[:, at] += part


def forward(low, own, high, w_node, at_hi, at_lo, bias, w_out, target):
    width = w_node.shape[1]
    nodes, points = at_hi.shape
    variables = target.shape[0]

    def whole(a):
        return pl.BlockSpec(a.shape, lambda i: (0,) * a.ndim)

    rows = pl.BlockSpec((WIDE, points), lambda i: (i, 0))
    field = pl.BlockSpec((variables, points), lambda i: (0, 0))
    return pl.pallas_call(
        forward_kernel,
        grid=(width // WIDE,),
        in_specs=[
            whole(low),
            whole(own),
            whole(high),
            pl.BlockSpec((w_node.shape[0], WIDE), lambda i: (0, i)),
            whole(at_hi),
            whole(at_lo),
            pl.BlockSpec((WIDE, 1), lambda i: (i, 0)),
            pl.BlockSpec((variables, WIDE), lambda i: (0, i)),
            whole(target),
        ],
        out_specs=[rows, rows, field],
        out_shape=[
            jax.ShapeDtypeStruct((width, points), bf16),
            jax.ShapeDtypeStruct((width, points), bf16),
            jax.ShapeDtypeStruct((variables, points), f32),
        ],
        compiler_params=params(("arbitrary",)),
        name="forward",
    )(low, own, high, w_node, at_hi, at_lo, bias, w_out, target)


def crps_kernel(count, scale, own_0, own_1, *rest):
    others, (area, d_0, d_1, loss) = rest[:-4], rest[-4:]
    variables, wide = own_0.shape

    @pl.when(pl.program_id(0) == 0)
    def _():
        loss[...] = jnp.zeros_like(loss)

    def apart(d):
        q = d * d + SMOOTH_SQ
        r = lax.rsqrt(q)
        return q * r, d * r

    for c in range(wide // PAD):
        at = slice(c * PAD, (c + 1) * PAD)
        a, b = own_0[:, at], own_1[:, at]
        own_a, slope_a = apart(a)
        own_b, slope_b = apart(b)
        dist, t = apart(a - b)
        dist = 2.0 * dist
        sum_a, sum_b = t, -t
        for other in others:
            o = other[:, at]
            s, t = apart(a - o)
            dist = dist + s
            sum_a = sum_a + t
            s, t = apart(b - o)
            dist = dist + s
            sum_b = sum_b + t
        where = area[:, at]
        pairs = count * (count - 1)
        crps = (own_a + own_b) * (1.0 / count) - dist * (0.5 / pairs)
        loss[...] += jnp.sum(crps, axis=0, keepdims=True) * where * (1.0 / scale)
        fold = where * (1.0 / variables)
        for ref, s, t in ((d_0, slope_a, sum_a), (d_1, slope_b, sum_b)):
            ref[:variables, at] = ((s * (1.0 / count) - t * (1.0 / pairs)) * fold).astype(bf16)
            ref[variables:, at] = jnp.zeros((PAD - variables, PAD), bf16)


def crps(own, others, area, count):
    variables, points = own[0].shape
    wide = 512
    field = pl.BlockSpec((variables, wide), lambda i: (0, i))
    padded = pl.BlockSpec((PAD, wide), lambda i: (0, i))
    return pl.pallas_call(
        lambda *refs: crps_kernel(count, variables * points, *refs),
        grid=(points // wide,),
        in_specs=[field] * (2 + len(others)) + [pl.BlockSpec((1, wide), lambda i: (0, i))],
        out_specs=[padded, padded, pl.BlockSpec((1, PAD), lambda i: (0, 0))],
        out_shape=[jax.ShapeDtypeStruct((PAD, points), bf16)] * 2
        + [jax.ShapeDtypeStruct((1, PAD), f32)],
        compiler_params=params(("arbitrary",)),
        name="crps",
    )(*own, *others, area)


def backward_kernel(variables, d_0, d_1, w_out_t, s_0, s_1, h_0, h_1, a_hi, a_lo, c_0, c_1, heads, dpre):
    column = lax.broadcasted_iota(jnp.int32, heads.shape, 1)
    total = jnp.zeros(heads.shape, f32)
    for d, slope, hid, out in ((d_0, s_0, h_0, c_0), (d_1, s_1, h_1, c_1)):
        summed = jnp.zeros((WIDE, PAD), f32)
        for g in range(d.shape[1] // WIDE):
            at = slice(g * WIDE, (g + 1) * WIDE)
            part = (dot(w_out_t[...], d[:, at]) * slope[:, at].astype(f32)).astype(bf16)
            dpre[:, at] = part
            wide = part.astype(f32)
            summed = summed + wide[:, :PAD] + wide[:, PAD:]
        out[...] = (dot(dpre[...], a_hi[...]) + dot(dpre[...], a_lo[...])).astype(bf16)
        total = total + dot(hid[...], d[...], 1, 1)
        total = total + jnp.where(column == variables, jnp.sum(summed, axis=1, keepdims=True), 0.0)
    heads[...] = total


def backward(variables, dpred, w_out_t, slope, hid, a_hi, a_lo):
    width, points = hid[0].shape
    nodes = a_hi.shape[1]

    def whole(a):
        return pl.BlockSpec(a.shape, lambda i: (0,) * a.ndim)

    rows = pl.BlockSpec((WIDE, points), lambda i: (i, 0))
    contrib = pl.BlockSpec((WIDE, nodes), lambda i: (i, 0))
    narrow = pl.BlockSpec((WIDE, PAD), lambda i: (i, 0))
    return pl.pallas_call(
        lambda *refs: backward_kernel(variables, *refs),
        grid=(width // WIDE,),
        in_specs=[whole(dpred[0]), whole(dpred[1]), narrow, rows, rows, rows, rows, whole(a_hi), whole(a_lo)],
        out_specs=[contrib, contrib, narrow],
        out_shape=[jax.ShapeDtypeStruct((width, nodes), bf16)] * 2
        + [jax.ShapeDtypeStruct((width, PAD), f32)],
        scratch_shapes=[pltpu.VMEM((WIDE, points), bf16)],
        compiler_params=params(("arbitrary",)),
        name="backward",
    )(*dpred, w_out_t, *slope, *hid, a_hi, a_lo)


def outer_kernel(lat_own, lat_other, c_own, c_other, out):
    total = None
    for lat, c in ((lat_own, c_own), (lat_other, c_other)):
        for m in range(lat.shape[0]):
            part = dot(lat[m], c[m], 1, 1)
            total = part if total is None else total + part
    out[...] = total.astype(bf16)


def outer(lat_own, lat_other, c_own, c_other):
    members, inputs, nodes = lat_own.shape
    halves, quarter = c_own.shape[1], c_own.shape[2]
    lat = pl.BlockSpec((members, WIDE, nodes), lambda y, i: (0, i, 0))
    col = pl.BlockSpec((members, None, quarter, nodes), lambda y, i: (0, y, 0, 0))
    return pl.pallas_call(
        outer_kernel,
        grid=(halves, inputs // WIDE),
        in_specs=[lat, lat, col, col],
        out_specs=pl.BlockSpec((None, WIDE, quarter), lambda y, i: (y, i, 0)),
        out_shape=jax.ShapeDtypeStruct((halves, inputs, quarter), bf16),
        compiler_params=params(("arbitrary", "arbitrary")),
        name="outer",
    )(lat_own, lat_other, c_own, c_other)


def local(latent, w_node, bias, w_out, edge_src, edge_weight, target, area):
    members, nodes, width = latent.shape
    points = edge_src.shape[0]
    variables = target.shape[0]
    regions = lax.axis_size(REGION)
    count = members * lax.axis_size(MEMBER)
    ahead = [(i, (i + 1) % regions) for i in range(regions)]
    behind = [(t, s) for s, t in ahead]
    swap = [(0, 1), (1, 0)]

    low = [lax.ppermute(latent[m], REGION, ahead) for m in range(members)]
    high = [lax.ppermute(latent[m], REGION, behind) for m in range(members)]
    at_hi, at_lo, a_hi, a_lo = prep(edge_src.T, edge_weight.T, 3 * nodes)
    w_out_t = jnp.pad(w_out, ((0, PAD - variables), (0, 0))).T
    bias_col = bias[:, None]

    hid, slope, err, near, far, beside = [], [], [], [], [], []
    for m in range(members):
        h, s, e = forward(
            low[m], latent[m], high[m], w_node, at_hi, at_lo, bias_col, w_out, target
        )
        hid.append(h)
        slope.append(s)
        err.append(e)
        sent = (e * 0.125).astype(f16)
        over = lax.ppermute(sent, "ylo", swap)
        near.append(lax.ppermute(sent, "core", swap))
        far.append(over)
        beside.append(lax.ppermute(over, "core", swap))

    lat_t = jnp.stack(
        [jnp.concatenate([low[m], latent[m], high[m]], axis=0).T for m in range(members)]
    )
    lat_t_other = lax.ppermute(lat_t, "core", swap)

    d_0, d_1, loss = crps(err, [o.astype(f32) * 8.0 for o in near + far + beside], area[None, :], count)
    c_0, c_1, heads = backward(variables, (d_0, d_1), w_out_t, slope, hid, a_hi, a_lo)

    where = lax.axis_index(REGION)
    row = lax.broadcasted_iota(jnp.int32, heads.shape, 0)
    column = lax.broadcasted_iota(jnp.int32, heads.shape, 1)
    heads = jnp.where((row == where) & (column == variables + 1), jnp.sum(loss), heads)
    every = lax.axis_size(EVERY)
    pieces = lax.all_to_all(
        heads.reshape(every, width // every, PAD), EVERY, split_axis=0, concat_axis=0, tiled=True
    )
    mine = pieces.sum(axis=0)
    table = lax.all_to_all(
        jnp.broadcast_to(mine, pieces.shape), EVERY, split_axis=0, concat_axis=0, tiled=True
    ).reshape(width, PAD)
    grad_out = table[:, :variables].T
    grad_bias = table[:, variables]
    loss_here = lax.dynamic_slice(table, (where, variables + 1), (1, 1)).reshape(1)

    core = lax.axis_index("core")
    quarters = jnp.stack([c_0, c_1]).reshape(members, 2, 2, width // 4, 3 * nodes)
    kept = lax.dynamic_index_in_dim(quarters, core, 2, keepdims=False)
    given = lax.dynamic_index_in_dim(quarters, 1 - core, 2, keepdims=False)
    taken = lax.ppermute(given, "core", swap)
    part = outer(lat_t, lat_t_other, kept, taken)
    chips = lax.axis_size(CHIPS)
    shares = lax.all_to_all(
        part.reshape(chips, width // regions, width // 4), CHIPS, split_axis=0, concat_axis=0, tiled=True
    )
    own = shares.astype(f32).sum(axis=0)
    grad_node = lax.all_gather(own, MEMBER, axis=1, tiled=True)
    return grad_node, grad_out, grad_bias, loss_here


def solution(mesh):
    finer = Mesh(mesh.devices.reshape(2, 2, 4, 2, 4), EVERY)
    in_specs = (
        P(MEMBER, REGION, None),
        P(),
        P(),
        P(),
        P(REGION, None),
        P(REGION, None),
        P(None, REGION),
        P(REGION),
    )
    out_specs = (P(REGION, None), P(), P(), P(REGION))
    return jax.shard_map(local, mesh=finer, in_specs=in_specs, out_specs=out_specs, check_vma=False)
```

profile of v0, /device:TPU:1, one launch (start us, length us, event | category | flops | bytes accessed | tf_op | source)
XLA Modules:
  0.0 210.4 jit_solution(16304249564482774460)
XLA Ops:
  0.7 2.0 slice_bitcast_fusion.1
  2.9 2.1 collective-permute-start.2
  5.0 7.5 %collective-permute-start.3 = (bf16[128,1024]{0,1:T(8,128)(2,1)S(1)}, bf16[128,1024]{0,1:T(8,128)(2,1)}, u32[]{:S(2)}, u32[]{:S(2)}) collective-permute-start(bf16[128,1024]{0,1:T(8,128)(2,1)S(1)} %bitcast.43), channel_id=1, source_target_pairs={{1,0},{2,1},{3,2},{4,3},{5,4},{6,5},{7,6},{8,7},{9,8},{10,9},{11,1... | collective-permute-start | bytes 786440 | tf_op jit(solution)/shard_map/ppermute | solution.py:255
  12.4 0.8 copy.52
  13.3 7.2 %collective-permute-start.1 = (bf16[128,1024]{0,1:T(8,128)(2,1)}, bf16[128,1024]{0,1:T(8,128)(2,1)}, u32[]{:S(2)}, u32[]{:S(2)}) collective-permute-start(bf16[128,1024]{0,1:T(8,128)(2,1)} %bitcast), channel_id=1, source_target_pairs={{1,0},{2,1},{3,2},{4,3},{5,4},{6,5},{7,6},{8,7},{9,8},{10,9},{11,1... | collective-permute-start | bytes 786440 | tf_op jit(solution)/shard_map/ppermute | solution.py:255
  20.5 0.2 copy.42.bias
  20.9 4.3 %prep.1 = (bf16[384,2048]{1,0:T(8,128)(2,1)S(1)}, bf16[384,2048]{1,0:T(8,128)(2,1)S(1)}, bf16[2048,384]{1,0:T(8,128)(2,1)S(1)}, bf16[2048,384]{1,0:T(8,128)(2,1)}) custom-call(s32[3,2048]{1,0:T(4,128)S(1)} %bitcast.39, f32[3,2048]{1,0:T(4,128)S(1)} %bitcast.40), custom_call_target="tpu_custom_call" | custom-call | tf_op jit(solution)/shard_map/prep/pallas_call | solution.py:51
  25.2 1.1 copy-done
  26.3 1.2 copy-done.4
  27.6 0.9 copy.43.low
  28.4 1.8 copy.45.high
  30.2 1.2 copy-done.1
  31.4 0.9 copy-done.8
  32.3 0.9 copy-done.9
  33.3 0.9 copy-done.11
  34.2 25.2 %forward.3 = (bf16[1024,2048]{1,0:T(8,128)(2,1)}, bf16[1024,2048]{1,0:T(8,128)(2,1)}, f32[100,2048]{1,0:T(8,128)S(1)}) custom-call(bf16[128,1024]{1,0:T(8,128)(2,1)S(1)} %copy-done.8, bf16[128,1024]{1,0:T(8,128)(2,1)S(1)} %copy-done.11, bf16[128,1024]{1,0:T(8,128)(2,1)S(1)} %copy-done.9, bf16[1024,1024]{1,0:T(8,128)(2,1)} %w_node.3, ...), custom_call_target="tpu_custom_call" | custom-call | tf_op jit(solution)/shard_map/forward/pallas_call | solution.py:98
  59.5 0.8 multiply_convert_fusion
  60.3 0.4 collective-permute-start.8
  60.7 1.8 collective-permute-start.6
  62.5 1.8 copy.39.low
  64.3 1.8 copy.41.high
  66.1 1.2 copy-done.2
  67.2 0.9 copy-done.6
  68.2 0.9 copy-done.7
  69.2 0.9 copy-done.10
  70.1 25.1 %forward.2 = (bf16[1024,2048]{1,0:T(8,128)(2,1)}, bf16[1024,2048]{1,0:T(8,128)(2,1)}, f32[100,2048]{1,0:T(8,128)S(1)}) custom-call(bf16[128,1024]{1,0:T(8,128)(2,1)S(1)} %copy-done.6, bf16[128,1024]{1,0:T(8,128)(2,1)S(1)} %copy-done.10, bf16[128,1024]{1,0:T(8,128)(2,1)S(1)} %copy-done.7, bf16[1024,1024]{1,0:T(8,128)(2,1)} %w_node.3, ...), custom_call_target="tpu_custom_call" | custom-call | tf_op jit(solution)/shard_map/forward/pallas_call | solution.py:98
  95.3 1.1 collective-permute-start.7
  96.5 0.3 collective-permute-start.5
  96.8 1.2 maximum_bitcast_fusion
  98.0 1.1 maximum_bitcast_fusion.1
  99.3 0.3 collective-permute-start.4
  99.6 0.3 collective-permute-start.10
  99.9 1.1 convert_multiply_fusion.2.refs_5_
  101.0 5.8 %collective-permute-done.7 = f16[100,2048]{1,0:T(8,128)(2,1)S(1)} collective-permute-done((f16[100,2048]{1,0:T(8,128)(2,1)S(1)}, f16[100,2048]{1,0:T(8,128)(2,1)S(1)}, u32[]{:S(2)}, u32[]{:S(2)}) %collective-permute-start.7) | collective-permute-done | bytes 409632 | tf_op jit(solution)/shard_map/ppermute | solution.py:269
  106.8 0.9 collective-permute-start.9
  107.7 1.1 convert_multiply_fusion.4.refs_3_
  109.0 1.0 convert_multiply_fusion.refs_7_
  110.0 1.0 convert_multiply_fusion.1.refs_6_
  111.0 6.2 %crps.1 = (bf16[128,2048]{1,0:T(8,128)(2,1)S(1)}, bf16[128,2048]{1,0:T(8,128)(2,1)S(1)}, f32[1,128]{1,0:T(1,128)S(1)}) custom-call(f32[100,2048]{1,0:T(8,128)S(1)} %get-tuple-element.22.refs_0_, f32[100,2048]{1,0:T(8,128)S(1)} %get-tuple-element.23.refs_1_, f32[100,2048]{1,0:T(8,128)S(1)} %convert_multiply_fusion.5.refs_2_, ...), custom_call_target="tpu_custom_call" | custom-call | tf_op jit(solution)/shard_map/crps/pallas_call | solution.py:167
  117.2 0.8 copy-done.13
  118.0 0.8 copy-done.15
  118.8 0.6 reduce_sum.28
  119.4 1.4 copy-done.5
  120.8 1.0 copy-done.14
  121.9 1.0 copy-done.16
  122.9 17.1 %backward.1 = (bf16[1024,384]{1,0:T(8,128)(2,1)S(1)}, bf16[1024,384]{1,0:T(8,128)(2,1)S(1)}, f32[1024,128]{1,0:T(8,128)S(1)}) custom-call(bf16[128,2048]{1,0:T(8,128)(2,1)S(1)} %copy-done.14, bf16[128,2048]{1,0:T(8,128)(2,1)S(1)} %copy-done.16, bf16[1024,128]{1,0:T(8,128)(2,1)S(1)} %pad_bitcast_fusion.refs_2_, bf16[1024,2048]{1,0:T(8,128)(2,1)} %get-tuple-element.26.refs_3_, ...), custom_call_target="tpu_custom_call" | custom-call | tf_op jit(solution)/shard_map/backward/pallas_call | solution.py:206
  140.0 1.7 select_bitcast_fusion
  141.7 4.7 %all-to-all-start.1 = ((f32[128,8,128]{2,1,0:T(8,128)}), f32[128,8,128]{2,1,0:T(8,128)}, u32[]{:S(2)}, u32[]{:S(2)}) async-start(f32[128,8,128]{2,1,0:T(8,128)} %select_bitcast_fusion), calls=%async_computation.1 | async-start | bytes 1048576 | tf_op jit(solution)/shard_map/all_to_all | solution.py:287
  146.4 2.2 %fusion.1 = (bf16[2,2,256,384]{3,2,1,0:T(8,128)(2,1)}, bf16[2,2,256,384]{3,2,1,0:T(8,128)(2,1)S(1)}) fusion(s32[]{:T(128)S(6)} %select_n.15, bf16[1,2,2,256,384]{4,3,2,1,0:T(8,128)(2,1)S(1)} %bitcast.37, bf16[1,2,2,256,384]{4,3,2,1,0:T(8,128)(2,1)} %bitcast.38, s32[]{:T(128)S(6)} %select_n.14), kind=kLoop, calls=%fused_computation.15 | loop fusion | flops 786432 | bytes 3145736 | tf_op jit(solution)/shard_map/jit(dynamic_index_in_dim)/squeeze | solution.py:301
  148.6 1.1 collective-permute-start.11
  149.6 10.2 %all-to-all-done.1 = f32[128,8,128]{2,1,0:T(8,128)} async-done(((f32[128,8,128]{2,1,0:T(8,128)}), f32[128,8,128]{2,1,0:T(8,128)}, u32[]{:S(2)}, u32[]{:S(2)}) %all-to-all-start.1) | async-done | bytes 524320 | tf_op jit(solution)/shard_map/all_to_all | solution.py:287
  159.8 1.2 reduce_sum.29
  161.0 0.8 broadcast_in_dim.16
  161.8 5.2 %all-to-all-start.2 = ((f32[128,8,128]{2,1,0:T(8,128)}), f32[128,8,128]{2,1,0:T(8,128)}, u32[]{:S(2)}, u32[]{:S(2)}) async-start(f32[128,8,128]{2,1,0:T(8,128)} %broadcast_in_dim.16), calls=%async_computation.2 | async-start | bytes 1048576 | tf_op jit(solution)/shard_map/all_to_all | solution.py:291
  167.0 7.4 %outer.1 = bf16[2,1024,256]{2,1,0:T(8,128)(2,1)} custom-call(bf16[2,1024,384]{2,1,0:T(8,128)(2,1)S(1)} %pad_maximum_fusion.lat_own, bf16[2,1024,384]{2,1,0:T(8,128)(2,1)} %collective-permute-done.4.lat_other, bf16[2,2,256,384]{3,2,1,0:T(8,128)(2,1)S(1)} %get-tuple-element.45.c_own, bf16[2,2,256,384]{3,2,1,0:T(8,128)(2,1)S(1)} %collective-permute-done.11.c_other), custom_call_target="tpu_custom_call" | custom-call | tf_op jit(solution)/shard_map/outer/pallas_call | solution.py:233
  174.4 6.2 %all-to-all-done.2 = f32[128,8,128]{2,1,0:T(8,128)} async-done(((f32[128,8,128]{2,1,0:T(8,128)}), f32[128,8,128]{2,1,0:T(8,128)}, u32[]{:S(2)}, u32[]{:S(2)}) %all-to-all-start.2) | async-done | bytes 524320 | tf_op jit(solution)/shard_map/all_to_all | solution.py:291
  180.7 4.7 %all-to-all-start = ((bf16[64,32,256]{2,1,0:T(8,128)(2,1)}), bf16[64,32,256]{2,1,0:T(8,128)(2,1)S(1)}, u32[]{:S(2)}, u32[]{:S(2)}) async-start(bf16[64,32,256]{2,1,0:T(8,128)(2,1)} %bitcast.15), calls=%async_computation | async-start | bytes 2097152 | tf_op jit(solution)/shard_map/all_to_all | solution.py:305
  185.3 1.1 slice_bitcast_fusion
  186.4 1.0 copy.50
  187.4 1.3 constant_dynamic-slice_fusion
  188.6 2.0 slice_reduce_fusion
  190.6 11.3 %all-to-all-done = bf16[64,32,256]{2,1,0:T(8,128)(2,1)S(1)} async-done(((bf16[64,32,256]{2,1,0:T(8,128)(2,1)}), bf16[64,32,256]{2,1,0:T(8,128)(2,1)S(1)}, u32[]{:S(2)}, u32[]{:S(2)}) %all-to-all-start) | async-done | bytes 1048608 | tf_op jit(solution)/shard_map/all_to_all | solution.py:305
  202.1 7.7 %all_gather.3 = f32[32,1024]{1,0:T(8,128)S(1)} all-gather(f32[32,256]{1,0:T(8,128)S(1)} %convert_reduce_fusion), channel_id=1, replica_groups=mesh['ylo'=2,'core'=2,'z'=4,'yhi'=2,'x'=4] {'ylo','core'}, dimensions={1}, use_global_device_ids=true | all-gather | bytes 163840 | tf_op jit(solution)/shard_map/all_gather | solution.py:309
  209.8 0.7 copy.59
  (57 shorter events, 1.1 us)
Async XLA Ops:
  0.6 19.8 %copy-start.24 = (f32[1024]{0:T(1024)S(1)}, f32[1024]{0:T(1024)}, u32[]{:S(2)}) copy-start(f32[1024]{0:T(1024)} %param.10) | copy-start | bytes 12292
  0.6 20.1 %copy-start.3 = (bf16[100,1024]{1,0:T(8,128)(2,1)S(1)}, bf16[100,1024]{1,0:T(8,128)(2,1)}, u32[]{:S(2)}) copy-start(bf16[100,1024]{1,0:T(8,128)(2,1)} %w_out.3) | copy-start | bytes 614404
  0.7 20.3 %copy-start.17 = (s32[2048,3]{0,1:T(4,128)S(1)}, s32[2048,3]{0,1:T(4,128)}, u32[]{:S(2)}) copy-start(s32[2048,3]{0,1:T(4,128)} %param.12) | copy-start | bytes 73732
  0.7 20.3 %copy-start.18 = (f32[2048,3]{0,1:T(4,128)S(1)}, f32[2048,3]{0,1:T(4,128)}, u32[]{:S(2)}) copy-start(f32[2048,3]{0,1:T(4,128)} %param.13) | copy-start | bytes 73732
  2.9 27.4 %copy-start.20 = (bf16[1,128,1024]{1,2,0:T(8,128)(2,1)}, bf16[1,128,1024]{1,2,0:T(8,128)(2,1)S(1)}, u32[]{:S(2)}) copy-start(bf16[1,128,1024]{1,2,0:T(8,128)(2,1)S(1)} %copy.53) | copy-start | bytes 786436
  2.9 24.7 %collective-permute-start.2 = (bf16[128,1024]{0,1:T(8,128)(2,1)S(1)}, bf16[128,1024]{0,1:T(8,128)(2,1)S(1)}, u32[]{:S(2)}, u32[]{:S(2)}) collective-permute-start(bf16[128,1024]{0,1:T(8,128)(2,1)S(1)} %bitcast.42), channel_id=1, source_target_pairs={{0,1},{1,2},{2,3},{3,4},{4,5},{5,6},{6,7},{7,8},{8,9},{9,10},{10,1... | collective-permute-start | bytes 786440 | tf_op jit(solution)/shard_map/ppermute | solution.py:254
  5.0 23.5 %collective-permute-start.3 = (bf16[128,1024]{0,1:T(8,128)(2,1)S(1)}, bf16[128,1024]{0,1:T(8,128)(2,1)}, u32[]{:S(2)}, u32[]{:S(2)}) collective-permute-start(bf16[128,1024]{0,1:T(8,128)(2,1)S(1)} %bitcast.43), channel_id=1, source_target_pairs={{1,0},{2,1},{3,2},{4,3},{5,4},{6,5},{7,6},{8,7},{9,8},{10,9},{11,1... | collective-permute-start | bytes 786440 | tf_op jit(solution)/shard_map/ppermute | solution.py:255
  13.3 49.2 %collective-permute-start = (bf16[128,1024]{0,1:T(8,128)(2,1)}, bf16[128,1024]{0,1:T(8,128)(2,1)}, u32[]{:S(2)}, u32[]{:S(2)}) collective-permute-start(bf16[128,1024]{0,1:T(8,128)(2,1)} %bitcast), channel_id=1, source_target_pairs={{0,1},{1,2},{2,3},{3,4},{4,5},{5,6},{6,7},{7,8},{8,9},{9,10},{10,1... | collective-permute-start | bytes 786440 | tf_op jit(solution)/shard_map/ppermute | solution.py:254
  13.3 51.0 %collective-permute-start.1 = (bf16[128,1024]{0,1:T(8,128)(2,1)}, bf16[128,1024]{0,1:T(8,128)(2,1)}, u32[]{:S(2)}, u32[]{:S(2)}) collective-permute-start(bf16[128,1024]{0,1:T(8,128)(2,1)} %bitcast), channel_id=1, source_target_pairs={{1,0},{2,1},{3,2},{4,3},{5,4},{6,5},{7,6},{8,7},{9,8},{10,9},{11,1... | collective-permute-start | bytes 786440 | tf_op jit(solution)/shard_map/ppermute | solution.py:255
  25.2 1.1 copy-start
  26.3 1.2 copy-start.4
  27.6 2.7 %copy-start.22 = (bf16[128,1024]{0,1:T(8,128)(2,1)}, bf16[128,1024]{0,1:T(8,128)(2,1)S(1)}, u32[]{:S(2)}) copy-start(bf16[128,1024]{0,1:T(8,128)(2,1)S(1)} %collective-permute-done.2) | copy-start | bytes 786436
  30.2 1.2 copy-start.1
  31.4 0.9 copy-start.8
  32.3 0.9 copy-start.9
  33.3 0.9 copy-start.11
  60.3 39.3 %collective-permute-start.8 = (f16[100,2048]{1,0:T(8,128)(2,1)}, f16[100,2048]{1,0:T(8,128)(2,1)}, u32[]{:S(2)}, u32[]{:S(2)}) collective-permute-start(f16[100,2048]{1,0:T(8,128)(2,1)} %multiply_convert_fusion), channel_id=1, source_target_pairs={{0,64},{64,0},{1,65},{65,1},{2,66},{66,2},{3,67},{67,3},{4,68},{68... | collective-permute-start | bytes 1228808 | tf_op jit(solution)/shard_map/ppermute | solution.py:269
  60.7 47.0 %collective-permute-start.6 = (f16[100,2048]{1,0:T(8,128)(2,1)}, f16[100,2048]{1,0:T(8,128)(2,1)}, u32[]{:S(2)}, u32[]{:S(2)}) collective-permute-start(f16[100,2048]{1,0:T(8,128)(2,1)} %multiply_convert_fusion), channel_id=1, source_target_pairs={{0,32},{32,0},{1,33},{33,1},{2,34},{34,2},{3,35},{35,3},{4,36},{36... | collective-permute-start | bytes 1228808 | tf_op jit(solution)/shard_map/ppermute | solution.py:270
  66.1 1.2 copy-start.2
  67.2 0.9 copy-start.6
  68.2 0.9 copy-start.7
  69.1 0.9 copy-start.10
  95.2 2.7 %copy-start.21 = (bf16[1,128,1024]{1,2,0:T(8,128)(2,1)S(1)}, bf16[1,128,1024]{1,2,0:T(8,128)(2,1)}, u32[]{:S(2)}) copy-start(bf16[1,128,1024]{1,2,0:T(8,128)(2,1)} %copy-done.20) | copy-start | bytes 786436
  95.2 2.7 %copy-start.23 = (bf16[128,1024]{0,1:T(8,128)(2,1)S(1)}, bf16[128,1024]{0,1:T(8,128)(2,1)}, u32[]{:S(2)}) copy-start(bf16[128,1024]{0,1:T(8,128)(2,1)} %copy-done.22) | copy-start | bytes 786436
  95.3 11.5 %collective-permute-start.7 = (f16[100,2048]{1,0:T(8,128)(2,1)S(1)}, f16[100,2048]{1,0:T(8,128)(2,1)S(1)}, u32[]{:S(2)}, u32[]{:S(2)}) collective-permute-start(f16[100,2048]{1,0:T(8,128)(2,1)S(1)} %multiply_convert_fusion.1), channel_id=1, source_target_pairs={{0,64},{64,0},{1,65},{65,1},{2,66},{66,2},{3,67},{67,3},{4,68},{68... | collective-permute-start | bytes 1228808 | tf_op jit(solution)/shard_map/ppermute | solution.py:269
  96.5 12.4 %collective-permute-start.5 = (f16[100,2048]{1,0:T(8,128)(2,1)S(1)}, f16[100,2048]{1,0:T(8,128)(2,1)S(1)}, u32[]{:S(2)}, u32[]{:S(2)}) collective-permute-start(f16[100,2048]{1,0:T(8,128)(2,1)S(1)} %multiply_convert_fusion.1), channel_id=1, source_target_pairs={{0,32},{32,0},{1,33},{33,1},{2,34},{34,2},{3,35},{35,3},{4,36},{36... | collective-permute-start | bytes 1228808 | tf_op jit(solution)/shard_map/ppermute | solution.py:270
  99.3 67.7 %collective-permute-start.4 = (bf16[2,1024,384]{2,1,0:T(8,128)(2,1)S(1)}, bf16[2,1024,384]{2,1,0:T(8,128)(2,1)}, u32[]{:S(2)}, u32[]{:S(2)}) collective-permute-start(bf16[2,1024,384]{2,1,0:T(8,128)(2,1)S(1)} %pad_maximum_fusion.lat_own), channel_id=1, source_target_pairs={{0,32},{32,0},{1,33},{33,1},{2,34},{34,2},{3,35},{35,3},{4,36},{36... | collective-permute-start | bytes 4718600 | tf_op jit(solution)/shard_map/ppermute | solution.py:277
  99.6 9.4 %collective-permute-start.10 = (f16[100,2048]{1,0:T(8,128)(2,1)}, f16[100,2048]{1,0:T(8,128)(2,1)S(1)}, u32[]{:S(2)}, u32[]{:S(2)}) collective-permute-start(f16[100,2048]{1,0:T(8,128)(2,1)} %collective-permute-done.8), channel_id=1, source_target_pairs={{0,32},{32,0},{1,33},{33,1},{2,34},{34,2},{3,35},{35,3},{4,36},{36... | collective-permute-start | bytes 1228808 | tf_op jit(solution)/shard_map/ppermute | solution.py:272
  106.8 3.2 %collective-permute-start.9 = (f16[100,2048]{1,0:T(8,128)(2,1)S(1)}, f16[100,2048]{1,0:T(8,128)(2,1)S(1)}, u32[]{:S(2)}, u32[]{:S(2)}) collective-permute-start(f16[100,2048]{1,0:T(8,128)(2,1)S(1)} %collective-permute-done.7), channel_id=1, source_target_pairs={{0,32},{32,0},{1,33},{33,1},{2,34},{34,2},{3,35},{35,3},{4,36},{36... | collective-permute-start | bytes 1228808 | tf_op jit(solution)/shard_map/ppermute | solution.py:272
  109.0 2.0 copy-start.19
  117.2 0.8 copy-start.13
  118.0 0.8 copy-start.15
  119.4 1.4 copy-start.5
  120.8 1.0 copy-start.14
  121.9 1.0 copy-start.16
  140.0 6.4 %copy-start.12 = (bf16[1024,384]{1,0:T(8,128)(2,1)}, bf16[1024,384]{1,0:T(8,128)(2,1)S(1)}, u32[]{:S(2)}) copy-start(bf16[1024,384]{1,0:T(8,128)(2,1)S(1)} %get-tuple-element.33) | copy-start | bytes 2359300
  141.7 18.1 %all-to-all-start.1 = ((f32[128,8,128]{2,1,0:T(8,128)}), f32[128,8,128]{2,1,0:T(8,128)}, u32[]{:S(2)}, u32[]{:S(2)}) async-start(f32[128,8,128]{2,1,0:T(8,128)} %select_bitcast_fusion), calls=%async_computation.1 | async-start | bytes 1048576 | tf_op jit(solution)/shard_map/all_to_all | solution.py:287
  148.6 18.4 %collective-permute-start.11 = (bf16[2,2,256,384]{3,2,1,0:T(8,128)(2,1)}, bf16[2,2,256,384]{3,2,1,0:T(8,128)(2,1)S(1)}, u32[]{:S(2)}, u32[]{:S(2)}) collective-permute-start(bf16[2,2,256,384]{3,2,1,0:T(8,128)(2,1)} %get-tuple-element.44), channel_id=1, source_target_pairs={{0,32},{32,0},{1,33},{33,1},{2,34},{34,2},{3,35},{35,3},{4,36},{36... | collective-permute-start | bytes 2359304 | tf_op jit(solution)/shard_map/ppermute | solution.py:302
  161.8 18.8 %all-to-all-start.2 = ((f32[128,8,128]{2,1,0:T(8,128)}), f32[128,8,128]{2,1,0:T(8,128)}, u32[]{:S(2)}, u32[]{:S(2)}) async-start(f32[128,8,128]{2,1,0:T(8,128)} %broadcast_in_dim.16), calls=%async_computation.2 | async-start | bytes 1048576 | tf_op jit(solution)/shard_map/all_to_all | solution.py:291
  180.7 21.2 %all-to-all-start = ((bf16[64,32,256]{2,1,0:T(8,128)(2,1)}), bf16[64,32,256]{2,1,0:T(8,128)(2,1)S(1)}, u32[]{:S(2)}, u32[]{:S(2)}) async-start(bf16[64,32,256]{2,1,0:T(8,128)(2,1)} %bitcast.15), calls=%async_computation | async-start | bytes 2097152 | tf_op jit(solution)/shard_map/all_to_all | solution.py:305
where the time goes:
time: 212 us; the launch traced here: 210 us
  Pallas kernels  85.3 us (40%)
  starting transfers between devices  37.4 us (18%)
  waiting for transfers between devices  33.5 us (16%)
  local copies, waits for them, and re-layouts  32 us (15%)
  other arithmetic  13.6 us (6%)
  blocking collectives  7.69 us (4%)
    pallas_call x2, Pallas kernels, forward(): pl.pallas_call(forward_kernel, grid=(width // WIDE,), in_specs=[whole(low...  50.4 us
    unnamed x55, local copies, waits for them, and re-layouts  18.3 us
    pallas_call x1, Pallas kernels, backward(): pl.pallas_call(lambda *refs: backward_kernel(variables, *refs), grid=(wid...  17.1 us
    ppermute x2, starting transfers between devices, local(): high = [lax.ppermute(latent[m], REGION, behind) for m in range(members)]  14.6 us
    all_to_all x1, waiting for transfers between devices, local(): lax.all_to_all(part.reshape(chips, width // regions, width // 4), CHIPS,...  11.3 us
    all_to_all x1, waiting for transfers between devices, local(): lax.all_to_all(heads.reshape(every, width // every, PAD), EVERY, split_ax...  10.2 us
    all_gather x1, blocking collectives, local(): grad_node = lax.all_gather(own, MEMBER, axis=1, tiled=True)  7.69 us
    pallas_call x1, Pallas kernels, outer(): pl.pallas_call(outer_kernel, grid=(halves, inputs // WIDE), in_specs=[lat...  7.38 us
  transfers between devices with their start and end apart: 15, of which 4 were waited for; matrix products, arithmetic and copies ran while one was open for 13% of the time, Pallas kernels for 41%

commit v1 on v0

v1 whole, which is shorter than its diff:
```python
import jax
import jax.numpy as jnp
from jax import lax
from jax.experimental import pallas as pl
from jax.experimental.pallas import tpu as pltpu
from jax.sharding import Mesh
from jax.sharding import PartitionSpec as P

REGION = ("z", "yhi", "x")
MEMBER = ("ylo", "core")
CHIPS = ("ylo", "z", "yhi", "x")
EVERY = ("ylo", "core", "z", "yhi", "x")

SMOOTH_SQ = 0.01
C0 = 0.7978845608028654
C1 = 0.044715
WIDE = 256
PAD = 128
bf16 = jnp.bfloat16
f32 = jnp.float32
f16 = jnp.float16
EDGE = 16


def dot(a, b, ca=1, cb=0):
    return lax.dot_general(a, b, (((ca,), (cb,)), ((), ())), preferred_element_type=f32)


def params(semantics, mib):
    return pltpu.CompilerParams(dimension_semantics=semantics, vmem_limit_bytes=mib << 20)


def whole(a):
    return pl.BlockSpec(a.shape, lambda *i: (0,) * a.ndim)


def prep_kernel(src, weight, at):
    nodes, wide = at.shape[0] - EDGE, at.shape[1]
    place = lax.broadcasted_iota(jnp.int32, (nodes, wide), 0)
    total = jnp.zeros((nodes, wide), f32)
    for k in range(src.shape[0]):
        total = total + jnp.where(src[k : k + 1, :] == place, weight[k : k + 1, :], 0.0)
    at[:nodes, :] = total.astype(bf16)
    first = lax.broadcasted_iota(jnp.int32, (EDGE, wide), 0) == 0
    at[nodes:, :] = jnp.where(first, 1.0, 0.0).astype(bf16)


def prep(src, weight, nodes):
    fan, points = src.shape
    row = pl.BlockSpec((fan, WIDE), lambda i: (0, i))
    return pl.pallas_call(
        prep_kernel,
        grid=(points // WIDE,),
        in_specs=[row, row],
        out_specs=pl.BlockSpec((nodes + EDGE, WIDE), lambda i: (0, i)),
        out_shape=jax.ShapeDtypeStruct((nodes + EDGE, points), bf16),
        compiler_params=params(("arbitrary",), 8),
        name="prep",
    )(src, weight)


def turn_kernel(*refs):
    blocks, out = refs[:-1], refs[-1]
    for b, block in enumerate(blocks):
        nodes = block.shape[0]
        out[:, b * nodes : (b + 1) * nodes] = block[...].T


def turn(blocks):
    nodes, width = blocks[0].shape
    return pl.pallas_call(
        turn_kernel,
        grid=(width // WIDE,),
        in_specs=[pl.BlockSpec((nodes, WIDE), lambda i: (0, i))] * len(blocks),
        out_specs=pl.BlockSpec((WIDE, nodes * len(blocks)), lambda i: (i, 0)),
        out_shape=jax.ShapeDtypeStruct((width, nodes * len(blocks)), bf16),
        compiler_params=params(("arbitrary",), 8),
        name="turn",
    )(*blocks)


def forward_kernel(low, own, high, w_node, at, bias, w_out, target, hid, slope, err, proj):
    nodes = low.shape[0]

    @pl.when(pl.program_id(0) == 0)
    def _():
        for b, block in enumerate((low, own, high)):
            proj[:, b * nodes : (b + 1) * nodes] = dot(block[...], w_node[...]).T.astype(bf16)

    for g in range(target.shape[1] // WIDE):
        cols = slice(g * WIDE, (g + 1) * WIDE)
        total = -target[:, cols]
        for r in range(proj.shape[0] // WIDE):
            rows = slice(r * WIDE, (r + 1) * WIDE)
            x = dot(proj[rows, :], at[: 3 * nodes, cols]) + bias[rows, :]
            sq = x * x
            u = 0.5 + 0.5 * jnp.tanh(x * (C0 + (C0 * C1) * sq))
            h = x * u
            hb = h.astype(bf16)
            hid[rows, cols] = hb
            slope[rows, cols] = (u + h * (1.0 - u) * (2.0 * C0 + (6.0 * C0 * C1) * sq)).astype(bf16)
            total = total + dot(w_out[:, rows], hb)
        err[:, cols] = total


def forward(low, own, high, w_node, at, bias, w_out, target):
    width = w_node.shape[1]
    points = at.shape[1]
    variables = target.shape[0]
    nodes = low.shape[0]
    wide = 512

    def cut(rows):
        return pl.BlockSpec((rows, wide), lambda i: (0, i))

    return pl.pallas_call(
        forward_kernel,
        grid=(points // wide,),
        in_specs=[whole(low), whole(own), whole(high), whole(w_node), cut(at.shape[0]), whole(bias), whole(w_out), cut(variables)],
        out_specs=[cut(width), cut(width), cut(variables)],
        out_shape=[
            jax.ShapeDtypeStruct((width, points), bf16),
            jax.ShapeDtypeStruct((width, points), bf16),
            jax.ShapeDtypeStruct((variables, points), f32),
        ],
        scratch_shapes=[pltpu.VMEM((width, 3 * nodes), bf16)],
        compiler_params=params(("arbitrary",), 28),
        name="forward",
    )(low, own, high, w_node, at, bias, w_out, target)


def apart(d):
    q = d * d + SMOOTH_SQ
    r = lax.rsqrt(q)
    return q * r, d * r


def near_kernel(count, scale, own_0, own_1, *rest):
    others, (area, p_0, p_1, loss) = rest[:-4], rest[-4:]
    pairs = count * (count - 1)

    @pl.when(pl.program_id(0) == 0)
    def _():
        loss[...] = jnp.zeros_like(loss)

    for c in range(own_0.shape[1] // PAD):
        at = slice(c * PAD, (c + 1) * PAD)
        a, b = own_0[:, at], own_1[:, at]
        own_a, slope_a = apart(a)
        own_b, slope_b = apart(b)
        dist, t = apart(a - b)
        dist = 2.0 * dist
        sum_a, sum_b = t, -t
        for other in others:
            o = other[:, at]
            s, t = apart(a - o)
            dist = dist + s
            sum_a = sum_a + t
            s, t = apart(b - o)
            dist = dist + s
            sum_b = sum_b + t
        value = (own_a + own_b) * (1.0 / count) - dist * (0.5 / pairs)
        loss[...] += jnp.sum(value, axis=0, keepdims=True) * area[:, at] * (1.0 / scale)
        p_0[:, at] = slope_a * (1.0 / count) - sum_a * (1.0 / pairs)
        p_1[:, at] = slope_b * (1.0 / count) - sum_b * (1.0 / pairs)


def far_kernel(count, scale, own_0, own_1, *rest):
    others, (p_0, p_1, area, before, d_0, d_1, loss) = rest[:-7], rest[-7:]
    variables = own_0.shape[0]
    pairs = count * (count - 1)

    @pl.when(pl.program_id(0) == 0)
    def _():
        loss[...] = before[...]

    for c in range(own_0.shape[1] // PAD):
        at = slice(c * PAD, (c + 1) * PAD)
        a, b = own_0[:, at], own_1[:, at]
        dist, sum_a, sum_b = 0.0, 0.0, 0.0
        for other in others:
            o = other[:, at]
            s, t = apart(a - o)
            dist = dist + s
            sum_a = sum_a + t
            s, t = apart(b - o)
            dist = dist + s
            sum_b = sum_b + t
        where = area[:, at]
        loss[...] -= jnp.sum(dist, axis=0, keepdims=True) * where * (0.5 / pairs / scale)
        fold = where * (1.0 / variables)
        for ref, p, t in ((d_0, p_0, sum_a), (d_1, p_1, sum_b)):
            ref[:variables, at] = ((p[:, at] - t * (1.0 / pairs)) * fold).astype(bf16)
            ref[variables:, at] = jnp.zeros((PAD - variables, PAD), bf16)


def crps_near(own, others, area, count):
    variables, points = own[0].shape
    wide = 512
    field = pl.BlockSpec((variables, wide), lambda i: (0, i))
    row = pl.BlockSpec((1, wide), lambda i: (0, i))
    return pl.pallas_call(
        lambda *refs: near_kernel(count, variables * points, *refs),
        grid=(points // wide,),
        in_specs=[field] * (2 + len(others)) + [row],
        out_specs=[field, field, pl.BlockSpec((1, PAD), lambda i: (0, 0))],
        out_shape=[jax.ShapeDtypeStruct((variables, points), f32)] * 2 + [jax.ShapeDtypeStruct((1, PAD), f32)],
        compiler_params=params(("arbitrary",), 16),
        name="crps_near",
    )(*own, *others, area)


def crps_far(own, others, partial, area, before, count):
    variables, points = own[0].shape
    wide = 512
    field = pl.BlockSpec((variables, wide), lambda i: (0, i))
    padded = pl.BlockSpec((PAD, wide), lambda i: (0, i))
    row = pl.BlockSpec((1, wide), lambda i: (0, i))
    one = pl.BlockSpec((1, PAD), lambda i: (0, 0))
    return pl.pallas_call(
        lambda *refs: far_kernel(count, variables * points, *refs),
        grid=(points // wide,),
        in_specs=[field] * (4 + len(others)) + [row, one],
        out_specs=[padded, padded, one],
        out_shape=[jax.ShapeDtypeStruct((PAD, points), bf16)] * 2 + [jax.ShapeDtypeStruct((1, PAD), f32)],
        compiler_params=params(("arbitrary",), 16),
        name="crps_far",
    )(*own, *others, *partial, area, before)


def backward_kernel(variables, who, d_0, d_1, w_out_t, s_0, s_1, h_0, h_1, at, loss, contrib, heads, dpre):
    quarter = 2 * pl.program_id(0) + who[0]
    nodes = at.shape[0] - EDGE
    shape = (PAD, WIDE)
    row = lax.broadcasted_iota(jnp.int32, shape, 0)
    spot = lax.broadcasted_iota(jnp.int32, shape, 1) + quarter * WIDE
    total = jnp.where((row == variables + 1) & (spot == who[1]), jnp.sum(loss[...]), 0.0)
    for m, (d, slope, hid) in enumerate(((d_0, s_0, h_0), (d_1, s_1, h_1))):
        for g in range(d.shape[1] // WIDE):
            cut = slice(g * WIDE, (g + 1) * WIDE)
            dpre[m, :, cut] = (dot(w_out_t[...], d[:, cut]) * slope[:, cut].astype(f32)).astype(bf16)
        total = total + dot(d[...], hid[...], 1, 1)
        part = dot(at[...], dpre[m], 1, 1)
        contrib[m * nodes : (m + 1) * nodes, :] = part[:nodes].astype(bf16)
        total = total + jnp.where(row == variables, part[nodes : nodes + 1], 0.0)
    for i in range(PAD // 8):
        for j in range(WIDE // 128):
            heads[i, j] = total[i * 8 : (i + 1) * 8, j * 128 : (j + 1) * 128]


def backward(who, variables, dpred, w_out_t, slope, hid, at, loss):
    width, points = hid[0].shape
    nodes = at.shape[0] - EDGE
    count = width // WIDE // 2

    def fixed(a):
        return pl.BlockSpec(a.shape, lambda y, w: (0,) * a.ndim)

    rows = pl.BlockSpec((WIDE, points), lambda y, w: (2 * y + w[0], 0))
    narrow = pl.BlockSpec((WIDE, PAD), lambda y, w: (2 * y + w[0], 0))
    return pl.pallas_call(
        lambda *refs: backward_kernel(variables, *refs),
        grid_spec=pltpu.PrefetchScalarGridSpec(
            num_scalar_prefetch=1,
            grid=(count,),
            in_specs=[fixed(dpred[0]), fixed(dpred[1]), narrow, rows, rows, rows, rows, fixed(at), fixed(loss)],
            out_specs=[
                pl.BlockSpec((None, 2 * nodes, WIDE), lambda y, w: (y, 0, 0)),
                pl.BlockSpec((None, PAD // 8, WIDE // 128, 8, 128), lambda y, w: (y, 0, 0, 0, 0)),
            ],
            scratch_shapes=[pltpu.VMEM((2, WIDE, points), bf16)],
        ),
        out_shape=[
            jax.ShapeDtypeStruct((count, 2 * nodes, WIDE), bf16),
            jax.ShapeDtypeStruct((count, PAD // 8, WIDE // 128, 8, 128), f32),
        ],
        compiler_params=params(("arbitrary",), 28),
        name="backward",
    )(who, *dpred, w_out_t, *slope, *hid, at, loss)


def outer_kernel(lat_own, lat_other, c_own, c_other, out):
    for y in range(c_own.shape[0]):
        out[y] = (dot(lat_own[...], c_own[y]) + dot(lat_other[...], c_other[y])).astype(bf16)


def outer(lat_own, lat_other, c_own, c_other):
    inputs, nodes = lat_own.shape
    halves, _, quarter = c_own.shape
    lat = pl.BlockSpec((WIDE, nodes), lambda i: (i, 0))
    return pl.pallas_call(
        outer_kernel,
        grid=(inputs // WIDE,),
        in_specs=[lat, lat, whole(c_own), whole(c_own)],
        out_specs=pl.BlockSpec((halves, WIDE, quarter), lambda i: (0, i, 0)),
        out_shape=jax.ShapeDtypeStruct((halves, inputs, quarter), bf16),
        compiler_params=params(("arbitrary",), 16),
        name="outer",
    )(lat_own, lat_other, c_own, c_other)


def finish_kernel(width, order, pieces, out):
    quarters = width // WIDE
    for k in range(quarters):
        for i in range(PAD // 8):
            for j in range(WIDE // 128):
                left = k * WIDE + j * 128
                out[i * 8 : (i + 1) * 8, left : left + 128] = pieces[k, i, j]


def finish(pieces, width):
    return pl.pallas_call(
        lambda *refs: finish_kernel(width, None, *refs),
        out_shape=jax.ShapeDtypeStruct((PAD, width), f32),
        compiler_params=pltpu.CompilerParams(vmem_limit_bytes=8 << 20),
        name="finish",
    )(pieces)


def local(latent, w_node, bias, w_out, edge_src, edge_weight, target, area):
    members, nodes, width = latent.shape
    points = edge_src.shape[0]
    variables = target.shape[0]
    regions = lax.axis_size(REGION)
    count = members * lax.axis_size(MEMBER)
    ahead = [(i, (i + 1) % regions) for i in range(regions)]
    behind = [(t, s) for s, t in ahead]
    swap = [(0, 1), (1, 0)]
    core = lax.axis_index("core")
    where = lax.axis_index(REGION)

    mine = [latent[m] for m in range(members)]
    low, high = [], []
    low.append(lax.ppermute(mine[0], REGION, ahead))
    high.append(lax.ppermute(mine[0], REGION, behind))
    at = prep(edge_src.T, edge_weight.T, 3 * nodes)
    at, second = lax.optimization_barrier((at, mine[1]))
    low.append(lax.ppermute(second, REGION, ahead))
    high.append(lax.ppermute(second, REGION, behind))
    w_out_t = jnp.pad(w_out, ((0, PAD - variables), (0, 0))).T
    bias_col = bias[:, None]

    hid, slope, err, near, far, beside = [], [], [], [], [], []
    for m in range(members):
        h, s, e = forward(low[m], mine[m], high[m], w_node, at, bias_col, w_out, target)
        hid.append(h)
        slope.append(s)
        err.append(e)
        over = lax.ppermute((e * 0.125).astype(f16), "ylo", swap)
        near.append(lax.ppermute(e, "core", swap))
        far.append(over.astype(f32) * 8.0)
        beside.append(lax.ppermute(over, "core", swap).astype(f32) * 8.0)

    first, err[1] = lax.optimization_barrier((mine[0], err[1]))
    lat_t = turn((low[0], first, high[0], low[1], mine[1], high[1]))
    lat_t_other = lax.ppermute(lat_t, "core", swap)

    area_row = area[None, :]
    p_0, p_1, loss = crps_near(err, near + [far[0], beside[0]], area_row, count)
    d_0, d_1, loss = crps_far(err, [far[1], beside[1]], (p_0, p_1), area_row, loss, count)

    def back(side):
        who = jnp.stack([side, where]).astype(jnp.int32)
        return backward(who, variables, (d_0, d_1), w_out_t, slope, hid, at, loss)

    given, heads_given = back(1 - core)
    taken = lax.ppermute(given, "core", swap)
    kept, heads_kept = back(core)

    every = lax.axis_size(EVERY)
    even = core == 0
    heads = jnp.stack(
        [jnp.where(even, heads_kept, heads_given), jnp.where(even, heads_given, heads_kept)], axis=1
    )
    pieces = lax.all_to_all(heads.reshape(every, 8, 128), EVERY, split_axis=0, concat_axis=0, tiled=True)
    part = outer(lat_t, lat_t_other, kept, taken)
    pieces, part = lax.optimization_barrier((pieces, part))
    chips = lax.axis_size(CHIPS)
    shares = lax.all_to_all(
        part.reshape(chips, width // regions, width // 4), CHIPS, split_axis=0, concat_axis=0, tiled=True
    )
    table = lax.all_to_all(
        jnp.broadcast_to(pieces.sum(axis=0), pieces.shape), EVERY, split_axis=0, concat_axis=0, tiled=True
    )
    own = shares.astype(f32).sum(axis=0)
    grad_node = lax.all_gather(own, MEMBER, axis=1, tiled=True)
    full = finish(table.reshape(width // WIDE, PAD // 8, WIDE // 128, 8, 128), width)
    grad_out = full[:variables]
    grad_bias = full[variables]
    loss_here = lax.dynamic_slice(full, (variables + 1, where), (1, 1)).reshape(1)
    return grad_node, grad_out, grad_bias, loss_here


def solution(mesh):
    finer = Mesh(mesh.devices.reshape(2, 2, 4, 2, 4), EVERY)
    in_specs = (
        P(MEMBER, REGION, None),
        P(),
        P(),
        P(),
        P(REGION, None),
        P(REGION, None),
        P(None, REGION),
        P(REGION),
    )
    out_specs = (P(REGION, None), P(), P(), P(REGION))
    return jax.shard_map(local, mesh=finer, in_specs=in_specs, out_specs=out_specs, check_vma=False)
```

time: 212 us -> 160 us (0.75)
  Pallas kernels: 85.3 us -> 48.1 us
  local copies, waits for them, and re-layouts: 32 us -> 13.3 us
  blocking collectives: 7.69 us -> 25.2 us
  other arithmetic: 13.6 us -> 2 us
  starting transfers between devices: 37.4 us -> 34.6 us
    pallas_call x5 -> x9, Pallas kernels: 81 us -> 47 us  [the longest x2 22.9 us: forward(): pl.pallas_call(forward_kernel, grid=(points // wide,), in_specs=[whole(lo...]
    all_to_all x0 -> x1, blocking collectives: none -> 17.5 us  [local(): lax.all_to_all(jnp.broadcast_to(pieces.sum(axis=0), pieces.shape), EVERY,...]
    unnamed x55 -> x18, local copies, waits for them, and re-layouts: 18.3 us -> 6.63 us
    all_to_all x2 -> x1, waiting for transfers between devices: 16.4 us -> 7.53 us  [local(): lax.all_to_all(heads.reshape(every, 8, 128), EVERY, split_axis=0, concat_...]
    ppermute x10, waiting for transfers between devices: 5.86 us -> 12.7 us  [the longest x2 12.6 us: local(): over = lax.ppermute((e * 0.125).astype(f16), 'ylo', swap)]
    ppermute x4 -> x0, local copies, waits for them, and re-layouts: 6.24 us -> none  [the longest x2 3.57 us: local(): high = [lax.ppermute(latent[m], REGION, behind) for m in range(members)]]
    all_to_all x2 -> x1, starting transfers between devices: 9.84 us -> 5.38 us  [local(): lax.all_to_all(heads.reshape(every, 8, 128), EVERY, split_axis=0, concat_...]
    mul x6 -> x4, other arithmetic: 4.36 us -> 0.35 us  [the longest x2 0.18 us: local(): beside.append(lax.ppermute(over, 'core', swap).astype(f32) * 8.0)]
  transfers between devices with their start and end apart: 15 -> 14, of which waited for: 4 -> 4; matrix products, arithmetic and copies ran while one was open for 13% -> 4% of each run, Pallas kernels for 41% -> 30%
where the time goes in v1:
time: 160 us; the launch traced here: 159 us
  Pallas kernels  48.1 us (30%)
  waiting for transfers between devices  34.8 us (22%)
  starting transfers between devices  34.6 us (22%)
  blocking collectives  25.2 us (16%)
  local copies, waits for them, and re-layouts  13.3 us (8%)
  other arithmetic  2 us (1%)
    pallas_call x2, Pallas kernels, forward(): pl.pallas_call(forward_kernel, grid=(points // wide,), in_specs=[whole(lo...  22.9 us
    all_to_all x1, blocking collectives, local(): lax.all_to_all(jnp.broadcast_to(pieces.sum(axis=0), pieces.shape), EVERY,...  17.5 us
    all_to_all x1, waiting for transfers between devices, local(): lax.all_to_all(part.reshape(chips, width // regions, width // 4), CHIPS,...  14.6 us
    ppermute x2, waiting for transfers between devices, local(): over = lax.ppermute((e * 0.125).astype(f16), 'ylo', swap)  12.6 us
    pallas_call x2, Pallas kernels, backward(): pl.pallas_call(lambda *refs: backward_kernel(variables, *refs), grid_spec...  10.8 us
    all_gather x1, blocking collectives, local(): grad_node = lax.all_gather(own, MEMBER, axis=1, tiled=True)  7.69 us
    all_to_all x1, waiting for transfers between devices, local(): lax.all_to_all(heads.reshape(every, 8, 128), EVERY, split_axis=0, concat_...  7.53 us
    ppermute x1, starting transfers between devices, local(): high.append(lax.ppermute(second, REGION, behind))  7.45 us
  transfers between devices with their start and end apart: 14, of which 4 were waited for; matrix products, arithmetic and copies ran while one was open for 4% of the time, Pallas kernels for 30%

profile of v1, /device:TPU:1, one launch (start us, length us, event | category | flops | bytes accessed | tf_op | source)
XLA Modules:
  0.0 158.9 jit_solution(16621091795151164737)
XLA Ops:
  0.7 1.9 %slice_bitcast_fusion = (bf16[128,1024]{1,0:T(8,128)(2,1)S(1)}, bf16[128,1024]{1,0:T(8,128)(2,1)}) fusion(bf16[2,128,1024]{2,1,0:T(8,128)(2,1)} %param.8), kind=kLoop, calls=%fused_computation.11 | loop fusion | bytes 1048576 | tf_op jit(solution)/shard_map/squeeze | solution.py:332
  2.5 0.8 copy-done.6
  3.3 0.8 copy-done.7
  4.0 1.1 prep.1.at.refs_8_
  5.1 2.1 %collective-permute-start.2 = (bf16[128,1024]{1,0:T(8,128)(2,1)S(1)}, bf16[128,1024]{1,0:T(8,128)(2,1)}, u32[]{:S(2)}, u32[]{:S(2)}) collective-permute-start(bf16[128,1024]{1,0:T(8,128)(2,1)S(1)} %get-tuple-element.28.own.refs_4_), channel_id=1, source_target_pairs={{0,1},{1,2},{2,3},{3,4},{4,5},{5,6},{6,7},{7,8},{8,9},{9,10},{10,1... | collective-permute-start | bytes 786440 | tf_op jit(solution)/shard_map/ppermute | solution.py:338
  7.2 7.5 %collective-permute-start.3 = (bf16[128,1024]{1,0:T(8,128)(2,1)S(1)}, bf16[128,1024]{1,0:T(8,128)(2,1)}, u32[]{:S(2)}, u32[]{:S(2)}) collective-permute-start(bf16[128,1024]{1,0:T(8,128)(2,1)S(1)} %get-tuple-element.28.own.refs_4_), channel_id=1, source_target_pairs={{1,0},{2,1},{3,2},{4,3},{5,4},{6,5},{7,6},{8,7},{9,8},{10,9},{11,1... | collective-permute-start | bytes 786440 | tf_op jit(solution)/shard_map/ppermute | solution.py:339
  14.7 0.0 collective-permute-start
  14.7 7.2 %collective-permute-start.1 = (bf16[128,1024]{1,0:T(8,128)(2,1)}, bf16[128,1024]{1,0:T(8,128)(2,1)}, u32[]{:S(2)}, u32[]{:S(2)}) collective-permute-start(bf16[128,1024]{1,0:T(8,128)(2,1)} %get-tuple-element.43.own.refs_1_), channel_id=1, source_target_pairs={{1,0},{2,1},{3,2},{4,3},{5,4},{6,5},{7,6},{8,7},{9,8},{10,9},{11,1... | collective-permute-start | bytes 786440 | tf_op jit(solution)/shard_map/ppermute | solution.py:335
  21.9 0.9 copy.13.bias
  22.8 0.8 copy.15
  23.7 0.1 pad_add_fusion
  23.7 1.0 pad_bitcast_fusion.refs_3_
  24.7 0.0 collective-permute-done.2.low.refs_3_
  24.7 0.0 collective-permute-done.3.high.refs_5_
  24.8 0.0 copy-start
  24.8 1.6 copy-done
  26.4 11.4 %forward.3 = (bf16[1024,2048]{1,0:T(8,128)(2,1)S(1)}, bf16[1024,2048]{1,0:T(8,128)(2,1)S(1)}, f32[100,2048]{1,0:T(8,128)S(1)}) custom-call(bf16[128,1024]{1,0:T(8,128)(2,1)} %collective-permute-done.2.low.refs_3_, bf16[128,1024]{1,0:T(8,128)(2,1)S(1)} %get-tuple-element.28.own.refs_4_, bf16[128,1024]{1,0:T(8,128)(2,1)} %collective-permute-done.3.high.refs_5_, ...), custom_call_target="tpu_custom_call" | custom-call | tf_op jit(solution)/shard_map/forward/pallas_call | solution.py:116
  37.8 1.6 %collective-permute-start.7 = (f32[100,2048]{1,0:T(8,128)S(1)}, f32[100,2048]{1,0:T(8,128)S(1)}, u32[]{:S(2)}, u32[]{:S(2)}) collective-permute-start(f32[100,2048]{1,0:T(8,128)S(1)} %get-tuple-element.30.refs_1_), channel_id=1, source_target_pairs={{0,32},{32,0},{1,33},{33,1},{2,34},{34,2},{3,35},{35,3},{4,36},{36... | collective-permute-start | bytes 2457608 | tf_op jit(solution)/shard_map/ppermute | solution.py:350
  39.4 0.0 collective-permute-done.low.refs_0_
  39.4 0.0 collective-permute-done.1.high.refs_2_
  39.4 11.5 %forward.2 = (bf16[1024,2048]{1,0:T(8,128)(2,1)S(1)}, bf16[1024,2048]{1,0:T(8,128)(2,1)S(1)}, f32[100,2048]{1,0:T(8,128)S(1)}) custom-call(bf16[128,1024]{1,0:T(8,128)(2,1)} %collective-permute-done.low.refs_0_, bf16[128,1024]{1,0:T(8,128)(2,1)} %get-tuple-element.43.own.refs_1_, bf16[128,1024]{1,0:T(8,128)(2,1)} %collective-permute-done.1.high.refs_2_, ...), custom_call_target="tpu_custom_call" | custom-call | tf_op jit(solution)/shard_map/forward/pallas_call | solution.py:116
  50.9 0.1 multiply_convert_fusion
  51.0 0.1 collective-permute-start.6
  51.1 0.5 collective-permute-start.8
  51.6 0.1 multiply_convert_fusion.1
  51.7 1.1 collective-permute-start.4
  52.8 2.5 %turn.1.lat_own = bf16[1024,768]{1,0:T(8,128)(2,1)S(1)} custom-call(bf16[128,1024]{1,0:T(8,128)(2,1)} %collective-permute-done.low.refs_0_, bf16[128,1024]{1,0:T(8,128)(2,1)} %get-tuple-element.43.own.refs_1_, bf16[128,1024]{1,0:T(8,128)(2,1)} %collective-permute-done.1.high.refs_2_, bf16[128,1024]{1,0:T(8,128)(2,1)} %collective-permute-done.2.low.refs_3_, ...), custom_call_target="tpu_custom_call" | custom-call | tf_op jit(solution)/shard_map/turn/pallas_call | solution.py:71
  55.3 0.0 copy-start.5
  55.3 1.1 collective-permute-start.10
  56.4 5.8 %collective-permute-done.8 = f16[100,2048]{1,0:T(8,128)(2,1)S(1)} collective-permute-done((f16[100,2048]{1,0:T(8,128)(2,1)S(1)}, f16[100,2048]{1,0:T(8,128)(2,1)S(1)}, u32[]{:S(2)}, u32[]{:S(2)}) %collective-permute-start.8) | collective-permute-done | bytes 409632 | tf_op jit(solution)/shard_map/ppermute | solution.py:349
  62.1 2.1 %collective-permute-start.9 = (f16[100,2048]{1,0:T(8,128)(2,1)S(1)}, f16[100,2048]{1,0:T(8,128)(2,1)S(1)}, u32[]{:S(2)}, u32[]{:S(2)}) collective-permute-start(f16[100,2048]{1,0:T(8,128)(2,1)S(1)} %collective-permute-done.8), channel_id=1, source_target_pairs={{0,32},{32,0},{1,33},{33,1},{2,34},{34,2},{3,35},{35,3},{4,36},{36... | collective-permute-start | bytes 1228808 | tf_op jit(solution)/shard_map/ppermute | solution.py:352
  64.3 0.1 convert_multiply_fusion.1.refs_4_
  64.4 6.9 %collective-permute-done.4 = f16[100,2048]{1,0:T(8,128)(2,1)S(1)} collective-permute-done((f16[100,2048]{1,0:T(8,128)(2,1)S(1)}, f16[100,2048]{1,0:T(8,128)(2,1)S(1)}, u32[]{:S(2)}, u32[]{:S(2)}) %collective-permute-start.4) | collective-permute-done | bytes 409632 | tf_op jit(solution)/shard_map/ppermute | solution.py:349
  71.2 1.3 collective-permute-start.5
  72.5 0.1 convert_multiply_fusion.3.refs_2_
  72.6 0.0 collective-permute-done.9
  72.6 0.1 convert_multiply_fusion.refs_5_
  72.7 0.0 collective-permute-done.7.refs_3_
  72.7 0.0 collective-permute-done.6.refs_2_
  72.7 4.0 %crps_near.1 = (f32[100,2048]{1,0:T(8,128)S(1)}, f32[100,2048]{1,0:T(8,128)S(1)}, f32[1,128]{1,0:T(1,128)S(1)}) custom-call(f32[100,2048]{1,0:T(8,128)S(1)} %get-tuple-element.27.refs_0_, f32[100,2048]{1,0:T(8,128)S(1)} %get-tuple-element.30.refs_1_, f32[100,2048]{1,0:T(8,128)S(1)} %collective-permute-done.6.refs_2_, ...), custom_call_target="tpu_custom_call" | custom-call | tf_op jit(solution)/shard_map/crps_near/pallas_call | solution.py:202
  76.7 0.0 collective-permute-done.5
  76.8 0.1 convert_multiply_fusion.2.refs_3_
  76.9 1.9 %crps_far.1 = (bf16[128,2048]{1,0:T(8,128)(2,1)S(1)}, bf16[128,2048]{1,0:T(8,128)(2,1)S(1)}, f32[1,128]{1,0:T(1,128)S(1)}) custom-call(f32[100,2048]{1,0:T(8,128)S(1)} %get-tuple-element.27.refs_0_, f32[100,2048]{1,0:T(8,128)S(1)} %get-tuple-element.30.refs_1_, f32[100,2048]{1,0:T(8,128)S(1)} %convert_multiply_fusion.3.refs_2_, ...), custom_call_target="tpu_custom_call" | custom-call | tf_op jit(solution)/shard_map/crps_far/pallas_call | solution.py:220
  78.8 5.8 %backward.3 = (bf16[2,768,256]{2,1,0:T(8,128)(2,1)}, f32[2,16,2,8,128]{4,3,2,1,0:T(8,128)S(1)}) custom-call(s32[2]{0:T(128)S(1)} %get-tuple-element.53.refs_0_, bf16[128,2048]{1,0:T(8,128)(2,1)S(1)} %get-tuple-element.34.refs_1_, bf16[128,2048]{1,0:T(8,128)(2,1)S(1)} %get-tuple-element.35.refs_2_, bf16[1024,128]{1,0:T(8,128)(2,1)S(1)} %pad_bitcast_fusion.refs_3_, ...), custom_call_target="tpu_custom_call" | custom-call | tf_op jit(solution)/shard_map/backward/pallas_call | solution.py:261
  84.6 0.0 collective-permute-start.11
  84.6 5.0 %backward.2 = (bf16[2,768,256]{2,1,0:T(8,128)(2,1)S(1)}, f32[2,16,2,8,128]{4,3,2,1,0:T(8,128)S(1)}) custom-call(s32[2]{0:T(128)S(1)} %get-tuple-element.52.refs_0_, bf16[128,2048]{1,0:T(8,128)(2,1)S(1)} %get-tuple-element.34.refs_1_, bf16[128,2048]{1,0:T(8,128)(2,1)S(1)} %get-tuple-element.35.refs_2_, bf16[1024,128]{1,0:T(8,128)(2,1)S(1)} %pad_bitcast_fusion.refs_3_, ...), custom_call_target="tpu_custom_call" | custom-call | tf_op jit(solution)/shard_map/backward/pallas_call | solution.py:261
  89.6 0.9 copy-done.3
  90.6 0.9 copy.16
  91.5 5.4 %all-to-all-start = ((f32[128,8,128]{2,1,0:T(8,128)}), f32[128,8,128]{2,1,0:T(8,128)}, u32[]{:S(2)}, u32[]{:S(2)}) async-start(f32[128,8,128]{2,1,0:T(8,128)} %bitcast.12), calls=%async_computation | async-start | bytes 1048576 | tf_op jit(solution)/shard_map/all_to_all | solution.py:375
  96.8 0.0 collective-permute-done.10.lat_other
  96.9 0.0 collective-permute-done.11.c_other
  96.9 1.1 copy-done.4
  98.0 4.8 %outer.1 = bf16[2,1024,256]{2,1,0:T(8,128)(2,1)} custom-call(bf16[1024,768]{1,0:T(8,128)(2,1)S(1)} %turn.1.lat_own, bf16[1024,768]{1,0:T(8,128)(2,1)} %collective-permute-done.10.lat_other, bf16[2,768,256]{2,1,0:T(8,128)(2,1)S(1)} %copy-done.4, bf16[2,768,256]{2,1,0:T(8,128)(2,1)} %collective-permute-done.11.c_other), custom_call_target="tpu_custom_call" | custom-call | tf_op jit(solution)/shard_map/outer/pallas_call | solution.py:291
  102.8 7.5 %all-to-all-done = f32[128,8,128]{2,1,0:T(8,128)} async-done(((f32[128,8,128]{2,1,0:T(8,128)}), f32[128,8,128]{2,1,0:T(8,128)}, u32[]{:S(2)}, u32[]{:S(2)}) %all-to-all-start) | async-done | bytes 524320 | tf_op jit(solution)/shard_map/all_to_all | solution.py:375
  110.4 1.2 reduce_sum.19
  111.6 17.5 %all_to_all.15 = f32[128,8,128]{2,1,0:T(8,128)S(1)} all-to-all(f32[128,8,128]{2,1,0:T(8,128)S(1)} %broadcast_in_dim.11), channel_id=1, replica_groups=mesh['ylo'=2,'core'=2,'z'=4,'yhi'=2,'x'=4] {'ylo','core','z','yhi','x'}, dimensions={0} | all-to-all | bytes 1048576 | tf_op jit(solution)/shard_map/all_to_all | solution.py:382
  129.1 4.7 %all-to-all-start.1 = ((bf16[64,32,256]{2,1,0:T(8,128)(2,1)}), bf16[64,32,256]{2,1,0:T(8,128)(2,1)S(1)}, u32[]{:S(2)}, u32[]{:S(2)}) async-start(bf16[64,32,256]{2,1,0:T(8,128)(2,1)} %bitcast.13), calls=%async_computation.1 | async-start | bytes 2097152 | tf_op jit(solution)/shard_map/all_to_all | solution.py:379
  133.8 0.8 slice.16
  134.6 0.6 slice.17
  135.2 0.6 constant_dynamic-slice_fusion
  135.8 14.6 %all-to-all-done.1 = bf16[64,32,256]{2,1,0:T(8,128)(2,1)S(1)} async-done(((bf16[64,32,256]{2,1,0:T(8,128)(2,1)}), bf16[64,32,256]{2,1,0:T(8,128)(2,1)S(1)}, u32[]{:S(2)}, u32[]{:S(2)}) %all-to-all-start.1) | async-done | bytes 1048608 | tf_op jit(solution)/shard_map/all_to_all | solution.py:379
  150.4 0.2 convert_reduce_fusion
  150.5 7.7 %all_gather.3 = f32[32,1024]{1,0:T(8,128)S(1)} all-gather(f32[32,256]{1,0:T(8,128)S(1)} %convert_reduce_fusion), channel_id=1, replica_groups=mesh['ylo'=2,'core'=2,'z'=4,'yhi'=2,'x'=4] {'ylo','core'}, dimensions={1}, use_global_device_ids=true | all-gather | bytes 163840 | tf_op jit(solution)/shard_map/all_gather | solution.py:386
  158.2 0.7 copy.18
  (13 shorter events, 0.2 us)
Async XLA Ops:
  0.6 22.2 %copy-start.2 = (bf16[100,1024]{1,0:T(8,128)(2,1)S(1)}, bf16[100,1024]{1,0:T(8,128)(2,1)}, u32[]{:S(2)}) copy-start(bf16[100,1024]{1,0:T(8,128)(2,1)} %w_out.3) | copy-start | bytes 614404
  0.6 24.1 %copy-start.1 = (f32[100,2048]{1,0:T(8,128)S(1)}, f32[100,2048]{1,0:T(8,128)}, u32[]{:S(2)}) copy-start(f32[100,2048]{1,0:T(8,128)} %target.3) | copy-start | bytes 2457604
  2.5 0.8 copy-start.6
  3.3 0.8 copy-start.7
  5.1 19.6 %collective-permute-start.2 = (bf16[128,1024]{1,0:T(8,128)(2,1)S(1)}, bf16[128,1024]{1,0:T(8,128)(2,1)}, u32[]{:S(2)}, u32[]{:S(2)}) collective-permute-start(bf16[128,1024]{1,0:T(8,128)(2,1)S(1)} %get-tuple-element.28.own.refs_4_), channel_id=1, source_target_pairs={{0,1},{1,2},{2,3},{3,4},{4,5},{5,6},{6,7},{7,8},{8,9},{9,10},{10,1... | collective-permute-start | bytes 786440 | tf_op jit(solution)/shard_map/ppermute | solution.py:338
  7.2 17.5 %collective-permute-start.3 = (bf16[128,1024]{1,0:T(8,128)(2,1)S(1)}, bf16[128,1024]{1,0:T(8,128)(2,1)}, u32[]{:S(2)}, u32[]{:S(2)}) collective-permute-start(bf16[128,1024]{1,0:T(8,128)(2,1)S(1)} %get-tuple-element.28.own.refs_4_), channel_id=1, source_target_pairs={{1,0},{2,1},{3,2},{4,3},{5,4},{6,5},{7,6},{8,7},{9,8},{10,9},{11,1... | collective-permute-start | bytes 786440 | tf_op jit(solution)/shard_map/ppermute | solution.py:339
  14.7 24.7 %collective-permute-start = (bf16[128,1024]{1,0:T(8,128)(2,1)}, bf16[128,1024]{1,0:T(8,128)(2,1)}, u32[]{:S(2)}, u32[]{:S(2)}) collective-permute-start(bf16[128,1024]{1,0:T(8,128)(2,1)} %get-tuple-element.43.own.refs_1_), channel_id=1, source_target_pairs={{0,1},{1,2},{2,3},{3,4},{4,5},{5,6},{6,7},{7,8},{8,9},{9,10},{10,1... | collective-permute-start | bytes 786440 | tf_op jit(solution)/shard_map/ppermute | solution.py:334
  14.7 24.7 %collective-permute-start.1 = (bf16[128,1024]{1,0:T(8,128)(2,1)}, bf16[128,1024]{1,0:T(8,128)(2,1)}, u32[]{:S(2)}, u32[]{:S(2)}) collective-permute-start(bf16[128,1024]{1,0:T(8,128)(2,1)} %get-tuple-element.43.own.refs_1_), channel_id=1, source_target_pairs={{1,0},{2,1},{3,2},{4,3},{5,4},{6,5},{7,6},{8,7},{9,8},{10,9},{11,1... | collective-permute-start | bytes 786440 | tf_op jit(solution)/shard_map/ppermute | solution.py:335
  24.8 1.6 %copy-start = (bf16[1024,1024]{1,0:T(8,128)(2,1)S(1)}, bf16[1024,1024]{1,0:T(8,128)(2,1)}, u32[]{:S(2)}) copy-start(bf16[1024,1024]{1,0:T(8,128)(2,1)} %w_node.3) | copy-start | bytes 6291460
  37.8 34.9 %collective-permute-start.7 = (f32[100,2048]{1,0:T(8,128)S(1)}, f32[100,2048]{1,0:T(8,128)S(1)}, u32[]{:S(2)}, u32[]{:S(2)}) collective-permute-start(f32[100,2048]{1,0:T(8,128)S(1)} %get-tuple-element.30.refs_1_), channel_id=1, source_target_pairs={{0,32},{32,0},{1,33},{33,1},{2,34},{34,2},{3,35},{35,3},{4,36},{36... | collective-permute-start | bytes 2457608 | tf_op jit(solution)/shard_map/ppermute | solution.py:350
  51.0 21.8 %collective-permute-start.6 = (f32[100,2048]{1,0:T(8,128)S(1)}, f32[100,2048]{1,0:T(8,128)S(1)}, u32[]{:S(2)}, u32[]{:S(2)}) collective-permute-start(f32[100,2048]{1,0:T(8,128)S(1)} %get-tuple-element.27.refs_0_), channel_id=1, source_target_pairs={{0,32},{32,0},{1,33},{33,1},{2,34},{34,2},{3,35},{35,3},{4,36},{36... | collective-permute-start | bytes 2457608 | tf_op jit(solution)/shard_map/ppermute | solution.py:350
  51.1 11.0 %collective-permute-start.8 = (f16[100,2048]{1,0:T(8,128)(2,1)S(1)}, f16[100,2048]{1,0:T(8,128)(2,1)S(1)}, u32[]{:S(2)}, u32[]{:S(2)}) collective-permute-start(f16[100,2048]{1,0:T(8,128)(2,1)S(1)} %multiply_convert_fusion), channel_id=1, source_target_pairs={{0,64},{64,0},{1,65},{65,1},{2,66},{66,2},{3,67},{67,3},{4,68},{68... | collective-permute-start | bytes 1228808 | tf_op jit(solution)/shard_map/ppermute | solution.py:349
  51.7 19.6 %collective-permute-start.4 = (f16[100,2048]{1,0:T(8,128)(2,1)S(1)}, f16[100,2048]{1,0:T(8,128)(2,1)S(1)}, u32[]{:S(2)}, u32[]{:S(2)}) collective-permute-start(f16[100,2048]{1,0:T(8,128)(2,1)S(1)} %multiply_convert_fusion.1), channel_id=1, source_target_pairs={{0,64},{64,0},{1,65},{65,1},{2,66},{66,2},{3,67},{67,3},{4,68},{68... | collective-permute-start | bytes 1228808 | tf_op jit(solution)/shard_map/ppermute | solution.py:349
  55.3 17.5 %copy-start.5 = (f32[2048]{0:T(1024)S(1)}, f32[2048]{0:T(1024)}, u32[]{:S(2)}) copy-start(f32[2048]{0:T(1024)} %param.15) | copy-start | bytes 24580
  55.3 41.5 %collective-permute-start.10 = (bf16[1024,768]{1,0:T(8,128)(2,1)S(1)}, bf16[1024,768]{1,0:T(8,128)(2,1)}, u32[]{:S(2)}, u32[]{:S(2)}) collective-permute-start(bf16[1024,768]{1,0:T(8,128)(2,1)S(1)} %turn.1.lat_own), channel_id=1, source_target_pairs={{0,32},{32,0},{1,33},{33,1},{2,34},{34,2},{3,35},{35,3},{4,36},{36... | collective-permute-start | bytes 4718600 | tf_op jit(solution)/shard_map/ppermute | solution.py:356
  62.1 10.5 %collective-permute-start.9 = (f16[100,2048]{1,0:T(8,128)(2,1)S(1)}, f16[100,2048]{1,0:T(8,128)(2,1)S(1)}, u32[]{:S(2)}, u32[]{:S(2)}) collective-permute-start(f16[100,2048]{1,0:T(8,128)(2,1)S(1)} %collective-permute-done.8), channel_id=1, source_target_pairs={{0,32},{32,0},{1,33},{33,1},{2,34},{34,2},{3,35},{35,3},{4,36},{36... | collective-permute-start | bytes 1228808 | tf_op jit(solution)/shard_map/ppermute | solution.py:352
  71.2 5.5 %collective-permute-start.5 = (f16[100,2048]{1,0:T(8,128)(2,1)S(1)}, f16[100,2048]{1,0:T(8,128)(2,1)S(1)}, u32[]{:S(2)}, u32[]{:S(2)}) collective-permute-start(f16[100,2048]{1,0:T(8,128)(2,1)S(1)} %collective-permute-done.4), channel_id=1, source_target_pairs={{0,32},{32,0},{1,33},{33,1},{2,34},{34,2},{3,35},{35,3},{4,36},{36... | collective-permute-start | bytes 1228808 | tf_op jit(solution)/shard_map/ppermute | solution.py:352
  84.6 12.3 %collective-permute-start.11 = (bf16[2,768,256]{2,1,0:T(8,128)(2,1)}, bf16[2,768,256]{2,1,0:T(8,128)(2,1)}, u32[]{:S(2)}, u32[]{:S(2)}) collective-permute-start(bf16[2,768,256]{2,1,0:T(8,128)(2,1)} %get-tuple-element.45), channel_id=1, source_target_pairs={{0,32},{32,0},{1,33},{33,1},{2,34},{34,2},{3,35},{35,3},{4,36},{36... | collective-permute-start | bytes 2359304 | tf_op jit(solution)/shard_map/ppermute | solution.py:367
  89.6 0.9 copy-start.3
  91.5 18.9 %all-to-all-start = ((f32[128,8,128]{2,1,0:T(8,128)}), f32[128,8,128]{2,1,0:T(8,128)}, u32[]{:S(2)}, u32[]{:S(2)}) async-start(f32[128,8,128]{2,1,0:T(8,128)} %bitcast.12), calls=%async_computation | async-start | bytes 1048576 | tf_op jit(solution)/shard_map/all_to_all | solution.py:375
  96.9 1.1 copy-start.4
  129.1 21.2 %all-to-all-start.1 = ((bf16[64,32,256]{2,1,0:T(8,128)(2,1)}), bf16[64,32,256]{2,1,0:T(8,128)(2,1)S(1)}, u32[]{:S(2)}, u32[]{:S(2)}) async-start(bf16[64,32,256]{2,1,0:T(8,128)(2,1)} %bitcast.13), calls=%async_computation.1 | async-start | bytes 2097152 | tf_op jit(solution)/shard_map/all_to_all | solution.py:379

commit v2 on v1

--- a/solution.py
+++ b/solution.py
@@ -5,6 +5,7 @@
 from jax.experimental.pallas import tpu as pltpu
 from jax.sharding import Mesh
 from jax.sharding import PartitionSpec as P
+
 
 REGION = ("z", "yhi", "x")
 MEMBER = ("ylo", "core")
@@ -20,6 +21,8 @@
 f32 = jnp.float32
 f16 = jnp.float16
 EDGE = 16
+DEEP = 128
+SPLIT = 3
 
 
 def dot(a, b, ca=1, cb=0):
@@ -35,13 +38,13 @@
 
 
 def prep_kernel(src, weight, at):
-    nodes, wide = at.shape[0] - EDGE, at.shape[1]
+    nodes, wide = at.shape[0] - DEEP, at.shape[1]
     place = lax.broadcasted_iota(jnp.int32, (nodes, wide), 0)
     total = jnp.zeros((nodes, wide), f32)
     for k in range(src.shape[0]):
         total = total + jnp.where(src[k : k + 1, :] == place, weight[k : k + 1, :], 0.0)
     at[:nodes, :] = total.astype(bf16)
-    first = lax.broadcasted_iota(jnp.int32, (EDGE, wide), 0) == 0
+    first = lax.broadcasted_iota(jnp.int32, (DEEP, wide), 0) < SPLIT
     at[nodes:, :] = jnp.where(first, 1.0, 0.0).astype(bf16)
 
 
@@ -52,8 +55,8 @@
         prep_kernel,
         grid=(points // WIDE,),
         in_specs=[row, row],
-        out_specs=pl.BlockSpec((nodes + EDGE, WIDE), lambda i: (0, i)),
-        out_shape=jax.ShapeDtypeStruct((nodes + EDGE, points), bf16),
+        out_specs=pl.BlockSpec((nodes + DEEP, WIDE), lambda i: (0, i)),
+        out_shape=jax.ShapeDtypeStruct((nodes + DEEP, points), bf16),
         compiler_params=params(("arbitrary",), 8),
         name="prep",
     )(src, weight)
@@ -79,26 +82,25 @@
     )(*blocks)
 
 
-def forward_kernel(low, own, high, w_node, at, bias, w_out, target, hid, slope, err, proj):
-    nodes = low.shape[0]
+def forward_kernel(low, own, high, w_node, at, bias, w_out, target, hid, pre, err, proj):
+    nodes = 3 * low.shape[0]
 
     @pl.when(pl.program_id(0) == 0)
     def _():
-        for b, block in enumerate((low, own, high)):
-            proj[:, b * nodes : (b + 1) * nodes] = dot(block[...], w_node[...]).T.astype(bf16)
+        stacked = jnp.concatenate([low[...], own[...], high[...]], axis=0)
+        proj[:, :nodes] = dot(stacked, w_node[...]).astype(bf16).T
+        proj[:, nodes:] = bias[...]
 
     for g in range(target.shape[1] // WIDE):
         cols = slice(g * WIDE, (g + 1) * WIDE)
         total = -target[:, cols]
         for r in range(proj.shape[0] // WIDE):
             rows = slice(r * WIDE, (r + 1) * WIDE)
-            x = dot(proj[rows, :], at[: 3 * nodes, cols]) + bias[rows, :]
-            sq = x * x
-            u = 0.5 + 0.5 * jnp.tanh(x * (C0 + (C0 * C1) * sq))
-            h = x * u
-            hb = h.astype(bf16)
+            x = dot(proj[rows, :], at[:, cols])
+            pre[rows, cols] = x.astype(bf16)
+            u = 0.5 + 0.5 * jnp.tanh(x * (C0 + (C0 * C1) * (x * x)))
+            hb = (x * u).astype(bf16)
             hid[rows, cols] = hb
-            slope[rows, cols] = (u + h * (1.0 - u) * (2.0 * C0 + (6.0 * C0 * C1) * sq)).astype(bf16)
             total = total + dot(w_out[:, rows], hb)
         err[:, cols] = total
 
@@ -107,7 +109,6 @@
     width = w_node.shape[1]
     points = at.shape[1]
     variables = target.shape[0]
-    nodes = low.shape[0]
     wide = 512
 
     def cut(rows):
@@ -123,10 +124,34 @@
             jax.ShapeDtypeStruct((width, points), bf16),
             jax.ShapeDtypeStruct((variables, points), f32),
         ],
-        scratch_shapes=[pltpu.VMEM((width, 3 * nodes), bf16)],
-        compiler_params=params(("arbitrary",), 28),
+        scratch_shapes=[pltpu.VMEM((width, at.shape[0]), bf16)],
+        compiler_params=params(("arbitrary",), 24),
         name="forward",
     )(low, own, high, w_node, at, bias, w_out, target)
+
+
+def slope_kernel(pre_0, pre_1, out_0, out_1):
+    for pre, out in ((pre_0, out_0), (pre_1, out_1)):
+        for g in range(pre.shape[1] // WIDE):
+            cols = slice(g * WIDE, (g + 1) * WIDE)
+            x = pre[:, cols].astype(f32)
+            sq = x * x
+            u = 0.5 + 0.5 * jnp.tanh(x * (C0 + (C0 * C1) * sq))
+            out[:, cols] = (u + (x * u) * (1.0 - u) * (2.0 * C0 + (6.0 * C0 * C1) * sq)).astype(bf16)
+
+
+def slopes(pre):
+    width, points = pre[0].shape
+    rows = pl.BlockSpec((128, points), lambda i: (i, 0))
+    return pl.pallas_call(
+        slope_kernel,
+        grid=(width // 128,),
+        in_specs=[rows, rows],
+        out_specs=[rows, rows],
+        out_shape=[jax.ShapeDtypeStruct((width, points), bf16)] * 2,
+        compiler_params=params(("arbitrary",), 8),
+        name="slope",
+    )(*pre)
 
 
 def apart(d):
@@ -230,7 +255,7 @@
 
 def backward_kernel(variables, who, d_0, d_1, w_out_t, s_0, s_1, h_0, h_1, at, loss, contrib, heads, dpre):
     quarter = 2 * pl.program_id(0) + who[0]
-    nodes = at.shape[0] - EDGE
+    nodes = at.shape[0] - DEEP
     shape = (PAD, WIDE)
     row = lax.broadcasted_iota(jnp.int32, shape, 0)
     spot = lax.broadcasted_iota(jnp.int32, shape, 1) + quarter * WIDE
@@ -240,7 +265,7 @@
             cut = slice(g * WIDE, (g + 1) * WIDE)
             dpre[m, :, cut] = (dot(w_out_t[...], d[:, cut]) * slope[:, cut].astype(f32)).astype(bf16)
         total = total + dot(d[...], hid[...], 1, 1)
-        part = dot(at[...], dpre[m], 1, 1)
+        part = dot(at[: nodes + EDGE], dpre[m], 1, 1)
         contrib[m * nodes : (m + 1) * nodes, :] = part[:nodes].astype(bf16)
         total = total + jnp.where(row == variables, part[nodes : nodes + 1], 0.0)
     for i in range(PAD // 8):
@@ -250,7 +275,7 @@
 
 def backward(who, variables, dpred, w_out_t, slope, hid, at, loss):
     width, points = hid[0].shape
-    nodes = at.shape[0] - EDGE
+    nodes = at.shape[0] - DEEP
     count = width // WIDE // 2
 
     def fixed(a):
@@ -299,18 +324,20 @@
     )(lat_own, lat_other, c_own, c_other)
 
 
-def finish_kernel(width, order, pieces, out):
-    quarters = width // WIDE
-    for k in range(quarters):
-        for i in range(PAD // 8):
-            for j in range(WIDE // 128):
-                left = k * WIDE + j * 128
-                out[i * 8 : (i + 1) * 8, left : left + 128] = pieces[k, i, j]
+def finish_kernel(pieces, out):
+    per_row = WIDE // 128
+    down = PAD // 8
+    for at in range(pieces.shape[0]):
+        core, z, x, yhi, ylo = at // 64, at // 16 % 4, at // 4 % 4, at // 2 % 2, at % 2
+        piece = (((ylo * 2 + core) * 4 + z) * 2 + yhi) * 4 + x
+        quarter, i, j = piece // (down * per_row), piece // per_row % down, piece % per_row
+        left = quarter * WIDE + j * 128
+        out[i * 8 : (i + 1) * 8, left : left + 128] = pieces[at]
 
 
 def finish(pieces, width):
     return pl.pallas_call(
-        lambda *refs: finish_kernel(width, None, *refs),
+        finish_kernel,
         out_shape=jax.ShapeDtypeStruct((PAD, width), f32),
         compiler_params=pltpu.CompilerParams(vmem_limit_bytes=8 << 20),
         name="finish",
@@ -319,7 +346,6 @@
 
 def local(latent, w_node, bias, w_out, edge_src, edge_weight, target, area):
     members, nodes, width = latent.shape
-    points = edge_src.shape[0]
     variables = target.shape[0]
     regions = lax.axis_size(REGION)
     count = members * lax.axis_size(MEMBER)
@@ -330,21 +356,28 @@
     where = lax.axis_index(REGION)
 
     mine = [latent[m] for m in range(members)]
-    low, high = [], []
-    low.append(lax.ppermute(mine[0], REGION, ahead))
-    high.append(lax.ppermute(mine[0], REGION, behind))
+
+    def halo(block):
+        before = lax.ppermute(block, REGION, ahead)
+        return before, lax.ppermute(block, REGION, behind)
+
+    low, high = [None] * members, [None] * members
+    low[0], high[0] = halo(mine[0])
     at = prep(edge_src.T, edge_weight.T, 3 * nodes)
-    at, second = lax.optimization_barrier((at, mine[1]))
-    low.append(lax.ppermute(second, REGION, ahead))
-    high.append(lax.ppermute(second, REGION, behind))
+    parts, rest = [], bias
+    for _ in range(SPLIT):
+        parts.append(rest.astype(bf16))
+        rest = rest - parts[-1].astype(f32)
+    bias_cols = jnp.pad(jnp.stack(parts, axis=1), ((0, 0), (0, DEEP - SPLIT)))
+    low[0], high[0], second = lax.optimization_barrier((low[0], high[0], mine[1]))
+    low[1], high[1] = halo(second)
     w_out_t = jnp.pad(w_out, ((0, PAD - variables), (0, 0))).T
-    bias_col = bias[:, None]
-
-    hid, slope, err, near, far, beside = [], [], [], [], [], []
+
+    hid, pre, err, near, far, beside = [], [], [], [], [], []
     for m in range(members):
-        h, s, e = forward(low[m], mine[m], high[m], w_node, at, bias_col, w_out, target)
+        h, s, e = forward(low[m], mine[m], high[m], w_node, at, bias_cols, w_out, target)
         hid.append(h)
-        slope.append(s)
+        pre.append(s)
         err.append(e)
         over = lax.ppermute((e * 0.125).astype(f16), "ylo", swap)
         near.append(lax.ppermute(e, "core", swap))
@@ -354,6 +387,7 @@
     first, err[1] = lax.optimization_barrier((mine[0], err[1]))
     lat_t = turn((low[0], first, high[0], low[1], mine[1], high[1]))
     lat_t_other = lax.ppermute(lat_t, "core", swap)
+    slope = slopes(pre)
 
     area_row = area[None, :]
     p_0, p_1, loss = crps_near(err, near + [far[0], beside[0]], area_row, count)
@@ -374,17 +408,31 @@
     )
     pieces = lax.all_to_all(heads.reshape(every, 8, 128), EVERY, split_axis=0, concat_axis=0, tiled=True)
     part = outer(lat_t, lat_t_other, kept, taken)
-    pieces, part = lax.optimization_barrier((pieces, part))
     chips = lax.axis_size(CHIPS)
     shares = lax.all_to_all(
         part.reshape(chips, width // regions, width // 4), CHIPS, split_axis=0, concat_axis=0, tiled=True
     )
-    table = lax.all_to_all(
-        jnp.broadcast_to(pieces.sum(axis=0), pieces.shape), EVERY, split_axis=0, concat_axis=0, tiled=True
+    spread = pieces.sum(axis=0)[None]
+    ring = [(0, 3), (3, 0), (1, 2), (2, 1)]
+    pair = [(0, 1), (1, 0), (2, 3), (3, 2)]
+    x, z = lax.axis_index("x"), lax.axis_index("z")
+    steps = (
+        ("ylo", swap, lax.axis_index("ylo")),
+        (("ylo", "yhi"), ring, lax.axis_index("yhi")),
+        ("x", pair, x % 2),
+        ("x", ring, x // 2),
+        ("z", pair, z % 2),
+        ("z", ring, z // 2),
+        ("core", swap, core),
     )
+    for axis, moves, place in steps:
+        other = lax.ppermute(spread, axis, moves)
+        spread = jnp.where(
+            place == 0, jnp.concatenate([spread, other]), jnp.concatenate([other, spread])
+        )
     own = shares.astype(f32).sum(axis=0)
     grad_node = lax.all_gather(own, MEMBER, axis=1, tiled=True)
-    full = finish(table.reshape(width // WIDE, PAD // 8, WIDE // 128, 8, 128), width)
+    full = finish(spread, width)
     grad_out = full[:variables]
     grad_bias = full[variables]
     loss_here = lax.dynamic_slice(full, (variables + 1, where), (1, 1)).reshape(1)
@@ -404,4 +452,5 @@
         P(REGION),
     )
     out_specs = (P(REGION, None), P(), P(), P(REGION))
+
     return jax.shard_map(local, mesh=finer, in_specs=in_specs, out_specs=out_specs, check_vma=False)

time: 160 us -> 154 us (0.963)
  waiting for transfers between devices: 34.8 us -> 22.6 us
  Pallas kernels: 48.1 us -> 54.3 us
  starting transfers between devices: 34.6 us -> 39.1 us
  blocking collectives: 25.2 us -> 22.8 us
  local copies, waits for them, and re-layouts: 13.3 us -> 11.6 us
    ppermute x4 -> x11, waiting for transfers between devices: 0.01 us -> 21.8 us  [the longest x7 21.8 us: local(): other = lax.ppermute(spread, axis, moves)]
    all_to_all x1, waiting for transfers between devices: 14.6 us -> 0.01 us  [local(): lax.all_to_all(part.reshape(chips, width // regions, width // 4), CHIPS,...]
    ppermute x2, waiting for transfers between devices: 12.6 us -> 0.01 us  [local(): over = lax.ppermute((e * 0.125).astype(f16), 'ylo', swap)]
    ppermute x4 -> x11, starting transfers between devices: 16.7 us -> 28.9 us  [the longest x2 14.6 us: halo(): return (before, lax.ppermute(block, REGION, behind))]
    pallas_call x1 -> x2, Pallas kernels: 0.04 us -> 8.54 us  [the longest x1 8.51 us: slopes(): pl.pallas_call(slope_kernel, grid=(width // 128,), in_specs=[rows, rows],...]
    all_to_all x1 -> x0, waiting for transfers between devices: 7.53 us -> none  [local(): lax.all_to_all(heads.reshape(every, 8, 128), EVERY, split_axis=0, concat_...]
    all_to_all x1 -> x0, starting transfers between devices: 5.38 us -> none  [local(): lax.all_to_all(heads.reshape(every, 8, 128), EVERY, split_axis=0, concat_...]
    pallas_call x2, Pallas kernels: 22.9 us -> 19.3 us  [forward(): pl.pallas_call(forward_kernel, grid=(points // wide,), in_specs=[whole(lo...]
  transfers between devices with their start and end apart: 14 -> 20, of which waited for: 4 -> 7; matrix products, arithmetic and copies ran while one was open for 4% -> 4% of each run, Pallas kernels for 30% -> 35%
where the time goes in v2:
time: 154 us; the launch traced here: 153 us
  Pallas kernels  54.3 us (35%)
  starting transfers between devices  39.1 us (25%)
  blocking collectives  22.8 us (15%)
  waiting for transfers between devices  22.6 us (15%)
  local copies, waits for them, and re-layouts  11.6 us (8%)
  other arithmetic  1.83 us (1%)
    ppermute x7, waiting for transfers between devices, local(): other = lax.ppermute(spread, axis, moves)  21.8 us
    pallas_call x2, Pallas kernels, forward(): pl.pallas_call(forward_kernel, grid=(points // wide,), in_specs=[whole(lo...  19.3 us
    all_to_all x1, blocking collectives, local(): lax.all_to_all(heads.reshape(every, 8, 128), EVERY, split_axis=0, concat_...  17.2 us
    ppermute x2, starting transfers between devices, halo(): return (before, lax.ppermute(block, REGION, behind))  14.6 us
    ppermute x7, starting transfers between devices, local(): other = lax.ppermute(spread, axis, moves)  12.3 us
    pallas_call x2, Pallas kernels, backward(): pl.pallas_call(lambda *refs: backward_kernel(variables, *refs), grid_spec...  10.8 us
    pallas_call x1, Pallas kernels, slopes(): pl.pallas_call(slope_kernel, grid=(width // 128,), in_specs=[rows, rows],...  8.51 us
    unnamed x14, local copies, waits for them, and re-layouts  6.48 us
  transfers between devices with their start and end apart: 20, of which 7 were waited for; matrix products, arithmetic and copies ran while one was open for 4% of the time, Pallas kernels for 35%

profile of v2, /device:TPU:1, one launch (start us, length us, event | category | flops | bytes accessed | tf_op | source)
XLA Modules:
  0.0 153.2 jit_solution(4452106684318131230)
XLA Ops:
  0.6 1.8 %slice_bitcast_fusion = (bf16[128,1024]{1,0:T(8,128)(2,1)S(1)}, bf16[128,1024]{1,0:T(8,128)(2,1)}) fusion(bf16[2,128,1024]{2,1,0:T(8,128)(2,1)} %param.8), kind=kLoop, calls=%fused_computation.13 | loop fusion | bytes 1048576 | tf_op jit(solution)/shard_map/squeeze | solution.py:358
  2.5 2.0 %collective-permute-start = (bf16[128,1024]{1,0:T(8,128)(2,1)}, bf16[128,1024]{1,0:T(8,128)(2,1)}, u32[]{:S(2)}, u32[]{:S(2)}) collective-permute-start(bf16[128,1024]{1,0:T(8,128)(2,1)} %get-tuple-element.30.refs_1_.own), channel_id=1, source_target_pairs={{0,1},{1,2},{2,3},{3,4},{4,5},{5,6},{6,7},{7,8},{8,9},{9,10},{10,1... | collective-permute-start | bytes 786440 | tf_op jit(solution)/shard_map/ppermute | solution.py:361
  4.5 7.4 %collective-permute-start.1 = (bf16[128,1024]{1,0:T(8,128)(2,1)}, bf16[128,1024]{1,0:T(8,128)(2,1)}, u32[]{:S(2)}, u32[]{:S(2)}) collective-permute-start(bf16[128,1024]{1,0:T(8,128)(2,1)} %get-tuple-element.30.refs_1_.own), channel_id=1, source_target_pairs={{1,0},{2,1},{3,2},{4,3},{5,4},{6,5},{7,6},{8,7},{9,8},{10,9},{11,1... | collective-permute-start | bytes 786440 | tf_op jit(solution)/shard_map/ppermute | solution.py:362
  11.9 0.8 fusion.1
  12.7 0.2 copy.18
  12.9 1.8 %copy.19 = bf16[100,1024]{0,1:T(8,128)(2,1)} copy(bf16[100,1024]{1,0:T(8,128)(2,1)} %w_out.3) | data formatting | bytes 409600 | tf_op args[3]
  14.7 0.1 pad.8.bias
  14.8 0.0 copy-start.3
  14.8 0.7 copy-done.3
  15.5 0.8 copy-done.4
  16.3 1.2 prep.1.at.refs_8_
  17.5 0.1 pad_add_fusion
  17.6 1.0 pad_bitcast_fusion.refs_3_
  18.6 0.1 collective-permute-start.2
  18.7 7.2 %collective-permute-start.3 = (bf16[128,1024]{1,0:T(8,128)(2,1)S(1)}, bf16[128,1024]{1,0:T(8,128)(2,1)S(1)}, u32[]{:S(2)}, u32[]{:S(2)}) collective-permute-start(bf16[128,1024]{1,0:T(8,128)(2,1)S(1)} %get-tuple-element.28.own.refs_4_), channel_id=1, source_target_pairs={{1,0},{2,1},{3,2},{4,3},{5,4},{6,5},{7,6},{8,7},{9,8},{10,9},{11,1... | collective-permute-start | bytes 786440 | tf_op jit(solution)/shard_map/ppermute | solution.py:362
  25.9 1.6 %copy-done = bf16[1024,1024]{1,0:T(8,128)(2,1)S(1)} copy-done((bf16[1024,1024]{1,0:T(8,128)(2,1)S(1)}, bf16[1024,1024]{1,0:T(8,128)(2,1)}, u32[]{:S(2)}) %copy-start) | copy-done | bytes 2097176
  27.5 0.9 copy-done.2
  28.4 10.2 %forward.3 = (bf16[1024,2048]{1,0:T(8,128)(2,1)S(1)}, bf16[1024,2048]{1,0:T(8,128)(2,1)S(1)}, f32[100,2048]{1,0:T(8,128)S(1)}) custom-call(bf16[128,1024]{1,0:T(8,128)(2,1)} %collective-permute-done.refs_0_.low, bf16[128,1024]{1,0:T(8,128)(2,1)} %get-tuple-element.30.refs_1_.own, bf16[128,1024]{1,0:T(8,128)(2,1)} %collective-permute-done.1.refs_2_.high, ...), custom_call_target="tpu_custom_call" | custom-call | tf_op jit(solution)/shard_map/forward/pallas_call | solution.py:117
  38.6 1.6 %collective-permute-start.7 = (f32[100,2048]{1,0:T(8,128)S(1)}, f32[100,2048]{1,0:T(8,128)S(1)}, u32[]{:S(2)}, u32[]{:S(2)}) collective-permute-start(f32[100,2048]{1,0:T(8,128)S(1)} %get-tuple-element.32.refs_0_), channel_id=1, source_target_pairs={{0,32},{32,0},{1,33},{33,1},{2,34},{34,2},{3,35},{35,3},{4,36},{36... | collective-permute-start | bytes 2457608 | tf_op jit(solution)/shard_map/ppermute | solution.py:383
  40.2 0.1 multiply_convert_fusion
  40.3 0.5 collective-permute-start.9
  40.8 0.0 collective-permute-done.3.high.refs_5_
  40.8 9.1 %forward.2 = (bf16[1024,2048]{1,0:T(8,128)(2,1)S(1)}, bf16[1024,2048]{1,0:T(8,128)(2,1)S(1)}, f32[100,2048]{1,0:T(8,128)S(1)}) custom-call(bf16[128,1024]{1,0:T(8,128)(2,1)S(1)} %collective-permute-done.2.low.refs_3_, bf16[128,1024]{1,0:T(8,128)(2,1)S(1)} %get-tuple-element.28.own.refs_4_, bf16[128,1024]{1,0:T(8,128)(2,1)S(1)} %collective-permute-done.3.high.refs_5_, ...), custom_call_target="tpu_custom_call" | custom-call | tf_op jit(solution)/shard_map/forward/pallas_call | solution.py:117
  49.9 0.4 collective-permute-start.8
  50.3 0.1 multiply_convert_fusion.1
  50.4 1.1 collective-permute-start.5
  51.5 3.6 %turn.1.lat_own = bf16[1024,768]{1,0:T(8,128)(2,1)} custom-call(bf16[128,1024]{1,0:T(8,128)(2,1)} %collective-permute-done.refs_0_.low, bf16[128,1024]{1,0:T(8,128)(2,1)} %get-tuple-element.30.refs_1_.own, bf16[128,1024]{1,0:T(8,128)(2,1)} %collective-permute-done.1.refs_2_.high, bf16[128,1024]{1,0:T(8,128)(2,1)S(1)} %collective-permute-done.2.low.refs_3_, ...), custom_call_target="tpu_custom_call" | custom-call | tf_op jit(solution)/shard_map/turn/pallas_call | solution.py:74
  55.2 0.5 collective-permute-start.4
  55.7 8.5 %slope.1 = (bf16[1024,2048]{1,0:T(8,128)(2,1)S(1)}, bf16[1024,2048]{1,0:T(8,128)(2,1)S(1)}) custom-call(bf16[1024,2048]{1,0:T(8,128)(2,1)S(1)} %get-tuple-element.39.pre_0, bf16[1024,2048]{1,0:T(8,128)(2,1)S(1)} %get-tuple-element.40.pre_1), custom_call_target="tpu_custom_call" | custom-call | tf_op jit(solution)/shard_map/slope/pallas_call | solution.py:146
  64.2 0.1 collective-permute-start.10
  64.3 0.1 convert_multiply_fusion.1.refs_4_
  64.4 0.7 collective-permute-start.6
  65.1 0.1 convert_multiply_fusion.3.refs_2_
  65.2 0.8 collective-permute-done.10
  66.0 0.1 convert_multiply_fusion.refs_5_
  66.2 4.0 %crps_near.1 = (f32[100,2048]{1,0:T(8,128)S(1)}, f32[100,2048]{1,0:T(8,128)S(1)}, f32[1,128]{1,0:T(1,128)S(1)}) custom-call(f32[100,2048]{1,0:T(8,128)S(1)} %get-tuple-element.32.refs_0_, f32[100,2048]{1,0:T(8,128)S(1)} %get-tuple-element.33.refs_1_, f32[100,2048]{1,0:T(8,128)S(1)} %collective-permute-done.7.refs_2_, ...), custom_call_target="tpu_custom_call" | custom-call | tf_op jit(solution)/shard_map/crps_near/pallas_call | solution.py:227
  70.2 0.1 convert_multiply_fusion.2.refs_3_
  70.3 1.9 %crps_far.1 = (bf16[128,2048]{1,0:T(8,128)(2,1)S(1)}, bf16[128,2048]{1,0:T(8,128)(2,1)S(1)}, f32[1,128]{1,0:T(1,128)S(1)}) custom-call(f32[100,2048]{1,0:T(8,128)S(1)} %get-tuple-element.32.refs_0_, f32[100,2048]{1,0:T(8,128)S(1)} %get-tuple-element.33.refs_1_, f32[100,2048]{1,0:T(8,128)S(1)} %convert_multiply_fusion.3.refs_2_, ...), custom_call_target="tpu_custom_call" | custom-call | tf_op jit(solution)/shard_map/crps_far/pallas_call | solution.py:245
  72.2 5.8 %backward.3 = (bf16[2,768,256]{2,1,0:T(8,128)(2,1)}, f32[2,16,2,8,128]{4,3,2,1,0:T(8,128)S(1)}) custom-call(s32[2]{0:T(128)S(1)} %get-tuple-element.58.refs_0_, bf16[128,2048]{1,0:T(8,128)(2,1)S(1)} %get-tuple-element.37.refs_1_, bf16[128,2048]{1,0:T(8,128)(2,1)S(1)} %get-tuple-element.38.refs_2_, bf16[1024,128]{1,0:T(8,128)(2,1)S(1)} %pad_bitcast_fusion.refs_3_, ...), custom_call_target="tpu_custom_call" | custom-call | tf_op jit(solution)/shard_map/backward/pallas_call | solution.py:286
  77.9 5.0 %backward.2 = (bf16[2,768,256]{2,1,0:T(8,128)(2,1)S(1)}, f32[2,16,2,8,128]{4,3,2,1,0:T(8,128)S(1)}) custom-call(s32[2]{0:T(128)S(1)} %get-tuple-element.57.refs_0_, bf16[128,2048]{1,0:T(8,128)(2,1)S(1)} %get-tuple-element.37.refs_1_, bf16[128,2048]{1,0:T(8,128)(2,1)S(1)} %get-tuple-element.38.refs_2_, bf16[1024,128]{1,0:T(8,128)(2,1)S(1)} %pad_bitcast_fusion.refs_3_, ...), custom_call_target="tpu_custom_call" | custom-call | tf_op jit(solution)/shard_map/backward/pallas_call | solution.py:286
  83.0 0.2 collective-permute-start.11
  83.3 17.2 %all_to_all.10 = f32[128,8,128]{2,1,0:T(8,128)S(1)} all-to-all(f32[128,8,128]{2,1,0:T(8,128)S(1)} %bitcast.25), channel_id=1, replica_groups=mesh['ylo'=2,'core'=2,'z'=4,'yhi'=2,'x'=4] {'ylo','core','z','yhi','x'}, dimensions={0} | all-to-all | bytes 1048576 | tf_op jit(solution)/shard_map/all_to_all | solution.py:409
  100.5 0.1 reduce_sum.19
  100.6 0.3 collective-permute-start.12
  100.9 2.2 %collective-permute-done.12 = f32[1,8,128]{2,1,0:T(8,128)S(1)} collective-permute-done((f32[1,8,128]{2,1,0:T(8,128)S(1)}, f32[1,8,128]{2,1,0:T(8,128)S(1)}, u32[]{:S(2)}, u32[]{:S(2)}) %collective-permute-start.12) | collective-permute-done | bytes 4128 | tf_op jit(solution)/shard_map/ppermute | solution.py:429
  103.1 0.4 collective-permute-start.13
  103.5 3.3 %collective-permute-done.13 = f32[2,8,128]{2,1,0:T(8,128)S(1)} collective-permute-done((f32[2,8,128]{2,1,0:T(8,128)S(1)}, f32[2,8,128]{2,1,0:T(8,128)S(1)}, u32[]{:S(2)}, u32[]{:S(2)}) %collective-permute-start.13) | collective-permute-done | bytes 8224 | tf_op jit(solution)/shard_map/ppermute | solution.py:429
  106.9 0.3 collective-permute-start.14
  107.2 4.9 %outer.1 = bf16[2,1024,256]{2,1,0:T(8,128)(2,1)} custom-call(bf16[1024,768]{1,0:T(8,128)(2,1)} %turn.1.lat_own, bf16[1024,768]{1,0:T(8,128)(2,1)} %collective-permute-done.4.lat_other, bf16[2,768,256]{2,1,0:T(8,128)(2,1)S(1)} %get-tuple-element.46.c_own, bf16[2,768,256]{2,1,0:T(8,128)(2,1)S(1)} %collective-permute-done.11.c_other), custom_call_target="tpu_custom_call" | custom-call | tf_op jit(solution)/shard_map/outer/pallas_call | solution.py:316
  112.1 5.0 %all-to-all-start = ((bf16[64,32,256]{2,1,0:T(8,128)(2,1)}), bf16[64,32,256]{2,1,0:T(8,128)(2,1)S(1)}, u32[]{:S(2)}, u32[]{:S(2)}) async-start(bf16[64,32,256]{2,1,0:T(8,128)(2,1)} %bitcast.9), calls=%async_computation | async-start | bytes 2097152 | tf_op jit(solution)/shard_map/all_to_all | solution.py:412
  117.1 2.3 %collective-permute-start.15 = (f32[8,8,128]{2,1,0:T(8,128)S(1)}, f32[8,8,128]{2,1,0:T(8,128)S(1)}, u32[]{:S(2)}, u32[]{:S(2)}) collective-permute-start(f32[8,8,128]{2,1,0:T(8,128)S(1)} %maximum_select_fusion.4), channel_id=1, source_target_pairs={{0,3},{3,0},{1,2},{2,1},{4,7},{7,4},{5,6},{6,5},{8,11},{11,8},{9,1... | collective-permute-start | bytes 98312 | tf_op jit(solution)/shard_map/ppermute | solution.py:429
  119.4 9.0 %collective-permute-done.15 = f32[8,8,128]{2,1,0:T(8,128)S(1)} collective-permute-done((f32[8,8,128]{2,1,0:T(8,128)S(1)}, f32[8,8,128]{2,1,0:T(8,128)S(1)}, u32[]{:S(2)}, u32[]{:S(2)}) %collective-permute-start.15) | collective-permute-done | bytes 32800 | tf_op jit(solution)/shard_map/ppermute | solution.py:429
  128.5 1.3 collective-permute-start.16
  129.8 3.3 %collective-permute-done.16 = f32[16,8,128]{2,1,0:T(8,128)S(1)} collective-permute-done((f32[16,8,128]{2,1,0:T(8,128)S(1)}, f32[16,8,128]{2,1,0:T(8,128)S(1)}, u32[]{:S(2)}, u32[]{:S(2)}) %collective-permute-start.16) | collective-permute-done | bytes 65568 | tf_op jit(solution)/shard_map/ppermute | solution.py:429
  133.1 2.4 %collective-permute-start.17 = (f32[32,8,128]{2,1,0:T(8,128)S(1)}, f32[32,8,128]{2,1,0:T(8,128)S(1)}, u32[]{:S(2)}, u32[]{:S(2)}) collective-permute-start(f32[32,8,128]{2,1,0:T(8,128)S(1)} %maximum_select_fusion.2), channel_id=1, source_target_pairs={{0,24},{24,0},{8,16},{16,8},{1,25},{25,1},{9,17},{17,9},{2,26},{26... | collective-permute-start | bytes 393224 | tf_op jit(solution)/shard_map/ppermute | solution.py:429
  135.5 2.7 %collective-permute-done.17 = f32[32,8,128]{2,1,0:T(8,128)S(1)} collective-permute-done((f32[32,8,128]{2,1,0:T(8,128)S(1)}, f32[32,8,128]{2,1,0:T(8,128)S(1)}, u32[]{:S(2)}, u32[]{:S(2)}) %collective-permute-start.17) | collective-permute-done | bytes 131104 | tf_op jit(solution)/shard_map/ppermute | solution.py:429
  138.2 5.3 %collective-permute-start.18 = (f32[64,8,128]{2,1,0:T(8,128)S(1)}, f32[64,8,128]{2,1,0:T(8,128)S(1)}, u32[]{:S(2)}, u32[]{:S(2)}) collective-permute-start(f32[64,8,128]{2,1,0:T(8,128)S(1)} %maximum_select_fusion.1), channel_id=1, source_target_pairs={{0,32},{32,0},{1,33},{33,1},{2,34},{34,2},{3,35},{35,3},{4,36},{36... | collective-permute-start | bytes 786440 | tf_op jit(solution)/shard_map/ppermute | solution.py:429
  143.5 1.2 collective-permute-done.18
  144.7 0.8 slice.16
  145.5 0.6 slice.17
  146.1 0.6 constant_dynamic-slice_fusion
  146.7 0.2 convert_reduce_fusion
  146.9 5.6 %all_gather.3 = f32[32,1024]{1,0:T(8,128)S(1)} all-gather(f32[32,256]{1,0:T(8,128)S(1)} %convert_reduce_fusion), channel_id=1, replica_groups=mesh['ylo'=2,'core'=2,'z'=4,'yhi'=2,'x'=4] {'ylo','core'}, dimensions={1}, use_global_device_ids=true | all-gather | bytes 163840 | tf_op jit(solution)/shard_map/all_gather | solution.py:434
  152.5 0.7 copy.22
  (34 shorter events, 0.3 us)
Async XLA Ops:
  0.6 25.2 %copy-start.1 = (f32[100,2048]{1,0:T(8,128)S(1)}, f32[100,2048]{1,0:T(8,128)}, u32[]{:S(2)}) copy-start(f32[100,2048]{1,0:T(8,128)} %target.3) | copy-start | bytes 2457604
  2.5 16.1 %collective-permute-start = (bf16[128,1024]{1,0:T(8,128)(2,1)}, bf16[128,1024]{1,0:T(8,128)(2,1)}, u32[]{:S(2)}, u32[]{:S(2)}) collective-permute-start(bf16[128,1024]{1,0:T(8,128)(2,1)} %get-tuple-element.30.refs_1_.own), channel_id=1, source_target_pairs={{0,1},{1,2},{2,3},{3,4},{4,5},{5,6},{6,7},{7,8},{8,9},{9,10},{10,1... | collective-permute-start | bytes 786440 | tf_op jit(solution)/shard_map/ppermute | solution.py:361
  4.5 14.1 %collective-permute-start.1 = (bf16[128,1024]{1,0:T(8,128)(2,1)}, bf16[128,1024]{1,0:T(8,128)(2,1)}, u32[]{:S(2)}, u32[]{:S(2)}) collective-permute-start(bf16[128,1024]{1,0:T(8,128)(2,1)} %get-tuple-element.30.refs_1_.own), channel_id=1, source_target_pairs={{1,0},{2,1},{3,2},{4,3},{5,4},{6,5},{7,6},{8,7},{9,8},{10,9},{11,1... | collective-permute-start | bytes 786440 | tf_op jit(solution)/shard_map/ppermute | solution.py:362
  14.8 0.8 copy-start.3
  15.5 0.8 copy-start.4
  18.6 22.2 %collective-permute-start.2 = (bf16[128,1024]{1,0:T(8,128)(2,1)S(1)}, bf16[128,1024]{1,0:T(8,128)(2,1)S(1)}, u32[]{:S(2)}, u32[]{:S(2)}) collective-permute-start(bf16[128,1024]{1,0:T(8,128)(2,1)S(1)} %get-tuple-element.28.own.refs_4_), channel_id=1, source_target_pairs={{0,1},{1,2},{2,3},{3,4},{4,5},{5,6},{6,7},{7,8},{8,9},{9,10},{10,1... | collective-permute-start | bytes 786440 | tf_op jit(solution)/shard_map/ppermute | solution.py:361
  18.7 22.1 %collective-permute-start.3 = (bf16[128,1024]{1,0:T(8,128)(2,1)S(1)}, bf16[128,1024]{1,0:T(8,128)(2,1)S(1)}, u32[]{:S(2)}, u32[]{:S(2)}) collective-permute-start(bf16[128,1024]{1,0:T(8,128)(2,1)S(1)} %get-tuple-element.28.own.refs_4_), channel_id=1, source_target_pairs={{1,0},{2,1},{3,2},{4,3},{5,4},{6,5},{7,6},{8,7},{9,8},{10,9},{11,1... | collective-permute-start | bytes 786440 | tf_op jit(solution)/shard_map/ppermute | solution.py:362
  25.9 1.6 %copy-start = (bf16[1024,1024]{1,0:T(8,128)(2,1)S(1)}, bf16[1024,1024]{1,0:T(8,128)(2,1)}, u32[]{:S(2)}) copy-start(bf16[1024,1024]{1,0:T(8,128)(2,1)} %w_node.3) | copy-start | bytes 6291460
  27.5 0.9 copy-start.2
  38.6 27.5 %collective-permute-start.7 = (f32[100,2048]{1,0:T(8,128)S(1)}, f32[100,2048]{1,0:T(8,128)S(1)}, u32[]{:S(2)}, u32[]{:S(2)}) collective-permute-start(f32[100,2048]{1,0:T(8,128)S(1)} %get-tuple-element.32.refs_0_), channel_id=1, source_target_pairs={{0,32},{32,0},{1,33},{33,1},{2,34},{34,2},{3,35},{35,3},{4,36},{36... | collective-permute-start | bytes 2457608 | tf_op jit(solution)/shard_map/ppermute | solution.py:383
  40.3 23.9 %collective-permute-start.9 = (f16[100,2048]{1,0:T(8,128)(2,1)S(1)}, f16[100,2048]{1,0:T(8,128)(2,1)S(1)}, u32[]{:S(2)}, u32[]{:S(2)}) collective-permute-start(f16[100,2048]{1,0:T(8,128)(2,1)S(1)} %multiply_convert_fusion), channel_id=1, source_target_pairs={{0,64},{64,0},{1,65},{65,1},{2,66},{66,2},{3,67},{67,3},{4,68},{68... | collective-permute-start | bytes 1228808 | tf_op jit(solution)/shard_map/ppermute | solution.py:382
  49.9 16.2 %collective-permute-start.8 = (f32[100,2048]{1,0:T(8,128)S(1)}, f32[100,2048]{1,0:T(8,128)S(1)}, u32[]{:S(2)}, u32[]{:S(2)}) collective-permute-start(f32[100,2048]{1,0:T(8,128)S(1)} %get-tuple-element.33.refs_1_), channel_id=1, source_target_pairs={{0,32},{32,0},{1,33},{33,1},{2,34},{34,2},{3,35},{35,3},{4,36},{36... | collective-permute-start | bytes 2457608 | tf_op jit(solution)/shard_map/ppermute | solution.py:383
  50.4 14.0 %collective-permute-start.5 = (f16[100,2048]{1,0:T(8,128)(2,1)S(1)}, f16[100,2048]{1,0:T(8,128)(2,1)S(1)}, u32[]{:S(2)}, u32[]{:S(2)}) collective-permute-start(f16[100,2048]{1,0:T(8,128)(2,1)S(1)} %multiply_convert_fusion.1), channel_id=1, source_target_pairs={{0,64},{64,0},{1,65},{65,1},{2,66},{66,2},{3,67},{67,3},{4,68},{68... | collective-permute-start | bytes 1228808 | tf_op jit(solution)/shard_map/ppermute | solution.py:382
  55.2 52.1 %collective-permute-start.4 = (bf16[1024,768]{1,0:T(8,128)(2,1)}, bf16[1024,768]{1,0:T(8,128)(2,1)}, u32[]{:S(2)}, u32[]{:S(2)}) collective-permute-start(bf16[1024,768]{1,0:T(8,128)(2,1)} %turn.1.lat_own), channel_id=1, source_target_pairs={{0,32},{32,0},{1,33},{33,1},{2,34},{34,2},{3,35},{35,3},{4,36},{36... | collective-permute-start | bytes 4718600 | tf_op jit(solution)/shard_map/ppermute | solution.py:389
  55.7 10.5 %copy-start.5 = (f32[2048]{0:T(1024)S(1)}, f32[2048]{0:T(1024)}, u32[]{:S(2)}) copy-start(f32[2048]{0:T(1024)} %param.15) | copy-start | bytes 24580
  64.2 1.8 %collective-permute-start.10 = (f16[100,2048]{1,0:T(8,128)(2,1)S(1)}, f16[100,2048]{1,0:T(8,128)(2,1)S(1)}, u32[]{:S(2)}, u32[]{:S(2)}) collective-permute-start(f16[100,2048]{1,0:T(8,128)(2,1)S(1)} %collective-permute-done.9), channel_id=1, source_target_pairs={{0,32},{32,0},{1,33},{33,1},{2,34},{34,2},{3,35},{35,3},{4,36},{36... | collective-permute-start | bytes 1228808 | tf_op jit(solution)/shard_map/ppermute | solution.py:385
  64.4 5.8 %collective-permute-start.6 = (f16[100,2048]{1,0:T(8,128)(2,1)S(1)}, f16[100,2048]{1,0:T(8,128)(2,1)S(1)}, u32[]{:S(2)}, u32[]{:S(2)}) collective-permute-start(f16[100,2048]{1,0:T(8,128)(2,1)S(1)} %collective-permute-done.5), channel_id=1, source_target_pairs={{0,32},{32,0},{1,33},{33,1},{2,34},{34,2},{3,35},{35,3},{4,36},{36... | collective-permute-start | bytes 1228808 | tf_op jit(solution)/shard_map/ppermute | solution.py:385
  83.0 24.2 %collective-permute-start.11 = (bf16[2,768,256]{2,1,0:T(8,128)(2,1)}, bf16[2,768,256]{2,1,0:T(8,128)(2,1)S(1)}, u32[]{:S(2)}, u32[]{:S(2)}) collective-permute-start(bf16[2,768,256]{2,1,0:T(8,128)(2,1)} %get-tuple-element.47), channel_id=1, source_target_pairs={{0,32},{32,0},{1,33},{33,1},{2,34},{34,2},{3,35},{35,3},{4,36},{36... | collective-permute-start | bytes 2359304 | tf_op jit(solution)/shard_map/ppermute | solution.py:401
  100.6 2.5 %collective-permute-start.12 = (f32[1,8,128]{2,1,0:T(8,128)S(1)}, f32[1,8,128]{2,1,0:T(8,128)S(1)}, u32[]{:S(2)}, u32[]{:S(2)}) collective-permute-start(f32[1,8,128]{2,1,0:T(8,128)S(1)} %bitcast.26), channel_id=1, source_target_pairs={{0,64},{64,0},{1,65},{65,1},{2,66},{66,2},{3,67},{67,3},{4,68},{68... | collective-permute-start | bytes 12296 | tf_op jit(solution)/shard_map/ppermute | solution.py:429
  103.1 3.7 %collective-permute-start.13 = (f32[2,8,128]{2,1,0:T(8,128)S(1)}, f32[2,8,128]{2,1,0:T(8,128)S(1)}, u32[]{:S(2)}, u32[]{:S(2)}) collective-permute-start(f32[2,8,128]{2,1,0:T(8,128)S(1)} %maximum_select_fusion.6), channel_id=1, source_target_pairs={{0,68},{68,0},{4,64},{64,4},{1,69},{69,1},{5,65},{65,5},{2,70},{70... | collective-permute-start | bytes 24584 | tf_op jit(solution)/shard_map/ppermute | solution.py:429
  106.9 10.3 %collective-permute-start.14 = (f32[4,8,128]{2,1,0:T(8,128)S(1)}, f32[4,8,128]{2,1,0:T(8,128)S(1)}, u32[]{:S(2)}, u32[]{:S(2)}) collective-permute-start(f32[4,8,128]{2,1,0:T(8,128)S(1)} %maximum_select_fusion.5), channel_id=1, source_target_pairs={{0,1},{1,0},{2,3},{3,2},{4,5},{5,4},{6,7},{7,6},{8,9},{9,8},{10,11... | collective-permute-start | bytes 49160 | tf_op jit(solution)/shard_map/ppermute | solution.py:429
  112.1 34.6 %all-to-all-start = ((bf16[64,32,256]{2,1,0:T(8,128)(2,1)}), bf16[64,32,256]{2,1,0:T(8,128)(2,1)S(1)}, u32[]{:S(2)}, u32[]{:S(2)}) async-start(bf16[64,32,256]{2,1,0:T(8,128)(2,1)} %bitcast.9), calls=%async_computation | async-start | bytes 2097152 | tf_op jit(solution)/shard_map/all_to_all | solution.py:412
  117.1 11.3 %collective-permute-start.15 = (f32[8,8,128]{2,1,0:T(8,128)S(1)}, f32[8,8,128]{2,1,0:T(8,128)S(1)}, u32[]{:S(2)}, u32[]{:S(2)}) collective-permute-start(f32[8,8,128]{2,1,0:T(8,128)S(1)} %maximum_select_fusion.4), channel_id=1, source_target_pairs={{0,3},{3,0},{1,2},{2,1},{4,7},{7,4},{5,6},{6,5},{8,11},{11,8},{9,1... | collective-permute-start | bytes 98312 | tf_op jit(solution)/shard_map/ppermute | solution.py:429
  128.5 4.6 %collective-permute-start.16 = (f32[16,8,128]{2,1,0:T(8,128)S(1)}, f32[16,8,128]{2,1,0:T(8,128)S(1)}, u32[]{:S(2)}, u32[]{:S(2)}) collective-permute-start(f32[16,8,128]{2,1,0:T(8,128)S(1)} %maximum_select_fusion.3), channel_id=1, source_target_pairs={{0,8},{8,0},{16,24},{24,16},{1,9},{9,1},{17,25},{25,17},{2,10},{10... | collective-permute-start | bytes 196616 | tf_op jit(solution)/shard_map/ppermute | solution.py:429
  133.1 5.1 %collective-permute-start.17 = (f32[32,8,128]{2,1,0:T(8,128)S(1)}, f32[32,8,128]{2,1,0:T(8,128)S(1)}, u32[]{:S(2)}, u32[]{:S(2)}) collective-permute-start(f32[32,8,128]{2,1,0:T(8,128)S(1)} %maximum_select_fusion.2), channel_id=1, source_target_pairs={{0,24},{24,0},{8,16},{16,8},{1,25},{25,1},{9,17},{17,9},{2,26},{26... | collective-permute-start | bytes 393224 | tf_op jit(solution)/shard_map/ppermute | solution.py:429
  138.2 6.4 %collective-permute-start.18 = (f32[64,8,128]{2,1,0:T(8,128)S(1)}, f32[64,8,128]{2,1,0:T(8,128)S(1)}, u32[]{:S(2)}, u32[]{:S(2)}) collective-permute-start(f32[64,8,128]{2,1,0:T(8,128)S(1)} %maximum_select_fusion.1), channel_id=1, source_target_pairs={{0,32},{32,0},{1,33},{33,1},{2,34},{34,2},{3,35},{35,3},{4,36},{36... | collective-permute-start | bytes 786440 | tf_op jit(solution)/shard_map/ppermute | solution.py:429

commit v3 on v2

--- a/solution.py
+++ b/solution.py
@@ -33,6 +33,10 @@
     return pltpu.CompilerParams(dimension_semantics=semantics, vmem_limit_bytes=mib << 20)
 
 
+def parked(a):
+    return pltpu.with_memory_space_constraint(a, pltpu.HBM)
+
+
 def whole(a):
     return pl.BlockSpec(a.shape, lambda *i: (0,) * a.ndim)
 
@@ -89,7 +93,13 @@
     def _():
         stacked = jnp.concatenate([low[...], own[...], high[...]], axis=0)
         proj[:, :nodes] = dot(stacked, w_node[...]).astype(bf16).T
-        proj[:, nodes:] = bias[...]
+        row = lax.broadcasted_iota(jnp.int32, (DEEP, proj.shape[0]), 0)
+        block, rest = jnp.zeros(row.shape, f32), bias[...]
+        for k in range(SPLIT):
+            part = rest.astype(bf16).astype(f32)
+            block = jnp.where(row == k, part, block)
+            rest = rest - part
+        proj[:, nodes:] = block.T.astype(bf16)
 
     for g in range(target.shape[1] // WIDE):
         cols = slice(g * WIDE, (g + 1) * WIDE)
@@ -120,14 +130,14 @@
         in_specs=[whole(low), whole(own), whole(high), whole(w_node), cut(at.shape[0]), whole(bias), whole(w_out), cut(variables)],
         out_specs=[cut(width), cut(width), cut(variables)],
         out_shape=[
-            jax.ShapeDtypeStruct((width, points), bf16),
-            jax.ShapeDtypeStruct((width, points), bf16),
+            pltpu.HBM((width, points), bf16),
+            pltpu.HBM((width, points), bf16),
             jax.ShapeDtypeStruct((variables, points), f32),
         ],
         scratch_shapes=[pltpu.VMEM((width, at.shape[0]), bf16)],
         compiler_params=params(("arbitrary",), 24),
         name="forward",
-    )(low, own, high, w_node, at, bias, w_out, target)
+    )(low, own, high, parked(w_node), at, bias, w_out, parked(target))
 
 
 def slope_kernel(pre_0, pre_1, out_0, out_1):
@@ -148,10 +158,10 @@
         grid=(width // 128,),
         in_specs=[rows, rows],
         out_specs=[rows, rows],
-        out_shape=[jax.ShapeDtypeStruct((width, points), bf16)] * 2,
+        out_shape=[pltpu.HBM((width, points), bf16)] * 2,
         compiler_params=params(("arbitrary",), 8),
         name="slope",
-    )(*pre)
+    )(*map(parked, pre))
 
 
 def apart(d):
@@ -253,28 +263,57 @@
     )(*own, *others, *partial, area, before)
 
 
-def backward_kernel(variables, who, d_0, d_1, w_out_t, s_0, s_1, h_0, h_1, at, loss, contrib, heads, dpre):
-    quarter = 2 * pl.program_id(0) + who[0]
-    nodes = at.shape[0] - DEEP
+def heads_kernel(variables, where, d_0, d_1, h_0, h_1, loss, heads):
     shape = (PAD, WIDE)
     row = lax.broadcasted_iota(jnp.int32, shape, 0)
-    spot = lax.broadcasted_iota(jnp.int32, shape, 1) + quarter * WIDE
-    total = jnp.where((row == variables + 1) & (spot == who[1]), jnp.sum(loss[...]), 0.0)
-    for m, (d, slope, hid) in enumerate(((d_0, s_0, h_0), (d_1, s_1, h_1))):
-        for g in range(d.shape[1] // WIDE):
-            cut = slice(g * WIDE, (g + 1) * WIDE)
-            dpre[m, :, cut] = (dot(w_out_t[...], d[:, cut]) * slope[:, cut].astype(f32)).astype(bf16)
-        total = total + dot(d[...], hid[...], 1, 1)
-        part = dot(at[: nodes + EDGE], dpre[m], 1, 1)
-        contrib[m * nodes : (m + 1) * nodes, :] = part[:nodes].astype(bf16)
-        total = total + jnp.where(row == variables, part[nodes : nodes + 1], 0.0)
+    spot = lax.broadcasted_iota(jnp.int32, shape, 1) + pl.program_id(0) * WIDE
+    total = jnp.where((row == variables + 1) & (spot == where[0]), jnp.sum(loss[...]), 0.0)
+    total = total + dot(d_0[...], h_0[...], 1, 1) + dot(d_1[...], h_1[...], 1, 1)
     for i in range(PAD // 8):
         for j in range(WIDE // 128):
             heads[i, j] = total[i * 8 : (i + 1) * 8, j * 128 : (j + 1) * 128]
 
 
-def backward(who, variables, dpred, w_out_t, slope, hid, at, loss):
+def head_parts(where, variables, dpred, hid, loss):
     width, points = hid[0].shape
+    quarters = width // WIDE
+
+    def fixed(a):
+        return pl.BlockSpec(a.shape, lambda q, w: (0,) * a.ndim)
+
+    rows = pl.BlockSpec((WIDE, points), lambda q, w: (q, 0))
+    return pl.pallas_call(
+        lambda *refs: heads_kernel(variables, *refs),
+        grid_spec=pltpu.PrefetchScalarGridSpec(
+            num_scalar_prefetch=1,
+            grid=(quarters,),
+            in_specs=[fixed(dpred[0]), fixed(dpred[1]), rows, rows, fixed(loss)],
+            out_specs=pl.BlockSpec((None, PAD // 8, WIDE // 128, 8, 128), lambda q, w: (q, 0, 0, 0, 0)),
+        ),
+        out_shape=pltpu.HBM((quarters, PAD // 8, WIDE // 128, 8, 128), f32),
+        compiler_params=params(("arbitrary",), 16),
+        name="heads",
+    )(where, *dpred, *map(parked, hid), loss)
+
+
+def backward_kernel(who, d_0, d_1, w_out, s_0, s_1, at, contrib, summed, dpre):
+    nodes = at.shape[0] - DEEP
+    variables = w_out.shape[0]
+    turned = w_out[...].T
+    total = None
+    for m, (d, slope) in enumerate(((d_0, s_0), (d_1, s_1))):
+        for g in range(d.shape[1] // WIDE):
+            cut = slice(g * WIDE, (g + 1) * WIDE)
+            dpre[m, :, cut] = (dot(turned, d[:variables, cut]) * slope[:, cut].astype(f32)).astype(bf16)
+        part = dot(at[: nodes + EDGE], dpre[m], 1, 1)
+        contrib[m * nodes : (m + 1) * nodes, :] = part[:nodes].astype(bf16)
+        edge = part[nodes : nodes + 8]
+        total = edge if total is None else total + edge
+    summed[...] = total
+
+
+def backward(who, dpred, w_out, slope, at):
+    width, points = slope[0].shape
     nodes = at.shape[0] - DEEP
     count = width // WIDE // 2
 
@@ -282,26 +321,26 @@
         return pl.BlockSpec(a.shape, lambda y, w: (0,) * a.ndim)
 
     rows = pl.BlockSpec((WIDE, points), lambda y, w: (2 * y + w[0], 0))
-    narrow = pl.BlockSpec((WIDE, PAD), lambda y, w: (2 * y + w[0], 0))
-    return pl.pallas_call(
-        lambda *refs: backward_kernel(variables, *refs),
+    narrow = pl.BlockSpec((w_out.shape[0], WIDE), lambda y, w: (0, 2 * y + w[0]))
+    return pl.pallas_call(
+        backward_kernel,
         grid_spec=pltpu.PrefetchScalarGridSpec(
             num_scalar_prefetch=1,
             grid=(count,),
-            in_specs=[fixed(dpred[0]), fixed(dpred[1]), narrow, rows, rows, rows, rows, fixed(at), fixed(loss)],
+            in_specs=[fixed(dpred[0]), fixed(dpred[1]), narrow, rows, rows, fixed(at)],
             out_specs=[
                 pl.BlockSpec((None, 2 * nodes, WIDE), lambda y, w: (y, 0, 0)),
-                pl.BlockSpec((None, PAD // 8, WIDE // 128, 8, 128), lambda y, w: (y, 0, 0, 0, 0)),
+                pl.BlockSpec((None, 8, WIDE), lambda y, w: (y, 0, 0)),
             ],
             scratch_shapes=[pltpu.VMEM((2, WIDE, points), bf16)],
         ),
         out_shape=[
-            jax.ShapeDtypeStruct((count, 2 * nodes, WIDE), bf16),
-            jax.ShapeDtypeStruct((count, PAD // 8, WIDE // 128, 8, 128), f32),
+            pltpu.HBM((count, 2 * nodes, WIDE), bf16),
+            jax.ShapeDtypeStruct((count, 8, WIDE), f32),
         ],
-        compiler_params=params(("arbitrary",), 28),
+        compiler_params=params(("arbitrary",), 20),
         name="backward",
-    )(who, *dpred, w_out_t, *slope, *hid, at, loss)
+    )(who, *dpred, w_out, *map(parked, slope), at)
 
 
 def outer_kernel(lat_own, lat_other, c_own, c_other, out):
@@ -321,27 +360,49 @@
         out_shape=jax.ShapeDtypeStruct((halves, inputs, quarter), bf16),
         compiler_params=params(("arbitrary",), 16),
         name="outer",
-    )(lat_own, lat_other, c_own, c_other)
-
-
-def finish_kernel(pieces, out):
+    )(parked(lat_own), parked(lat_other), parked(c_own), parked(c_other))
+
+
+def finish_kernel(where, pieces, grad_out, grad_bias, loss):
+    variables, width = grad_out.shape
     per_row = WIDE // 128
     down = PAD // 8
-    for at in range(pieces.shape[0]):
-        core, z, x, yhi, ylo = at // 64, at // 16 % 4, at // 4 % 4, at // 2 % 2, at % 2
-        piece = (((ylo * 2 + core) * 4 + z) * 2 + yhi) * 4 + x
-        quarter, i, j = piece // (down * per_row), piece // per_row % down, piece % per_row
-        left = quarter * WIDE + j * 128
-        out[i * 8 : (i + 1) * 8, left : left + 128] = pieces[at]
-
-
-def finish(pieces, width):
+    groups, held = pieces.shape[0], pieces.shape[1] - 1
+    total = pieces[0, held]
+    for group in range(1, groups):
+        total = total + pieces[group, held]
+    for k in range(width // 128):
+        grad_bias[:, k * 128 : (k + 1) * 128] = total[k : k + 1]
+    for group in range(groups):
+        core, z = group // 4, group % 4
+        for at in range(held):
+            x, yhi, ylo = at // 4, at // 2 % 2, at % 2
+            piece = (((ylo * 2 + core) * 4 + z) * 2 + yhi) * 4 + x
+            quarter, i, j = piece // (down * per_row), piece // per_row % down, piece % per_row
+            left = quarter * WIDE + j * 128
+            top = i * 8
+            rows = max(0, min(8, variables - top))
+            if rows:
+                grad_out[top : top + rows, left : left + 128] = pieces[group, at, :rows]
+            line = variables + 1 - top
+            if left == 0 and 0 <= line < 8:
+                values = pieces[group, at, line : line + 1]
+                spot = lax.broadcasted_iota(jnp.int32, values.shape, 1)
+                loss[...] = jnp.sum(jnp.where(spot == where[0], values, 0.0), axis=1, keepdims=True)
+
+
+def finish(where, pieces, variables, width):
     return pl.pallas_call(
         finish_kernel,
-        out_shape=jax.ShapeDtypeStruct((PAD, width), f32),
+        in_specs=[pl.BlockSpec(memory_space=pltpu.SMEM), pl.BlockSpec(memory_space=pltpu.VMEM)],
+        out_shape=[
+            jax.ShapeDtypeStruct((variables, width), f32),
+            jax.ShapeDtypeStruct((1, width), f32),
+            jax.ShapeDtypeStruct((1, 1), f32),
+        ],
         compiler_params=pltpu.CompilerParams(vmem_limit_bytes=8 << 20),
         name="finish",
-    )(pieces)
+    )(where, pieces)
 
 
 def local(latent, w_node, bias, w_out, edge_src, edge_weight, target, area):
@@ -357,25 +418,16 @@
 
     mine = [latent[m] for m in range(members)]
 
-    def halo(block):
-        before = lax.ppermute(block, REGION, ahead)
-        return before, lax.ppermute(block, REGION, behind)
-
-    low, high = [None] * members, [None] * members
-    low[0], high[0] = halo(mine[0])
+    low, high = [], []
+    for m in range(members):
+        low.append(lax.ppermute(mine[m], REGION, ahead))
+        high.append(lax.ppermute(mine[m], REGION, behind))
     at = prep(edge_src.T, edge_weight.T, 3 * nodes)
-    parts, rest = [], bias
-    for _ in range(SPLIT):
-        parts.append(rest.astype(bf16))
-        rest = rest - parts[-1].astype(f32)
-    bias_cols = jnp.pad(jnp.stack(parts, axis=1), ((0, 0), (0, DEEP - SPLIT)))
-    low[0], high[0], second = lax.optimization_barrier((low[0], high[0], mine[1]))
-    low[1], high[1] = halo(second)
-    w_out_t = jnp.pad(w_out, ((0, PAD - variables), (0, 0))).T
+    bias_row = bias[None, :]
 
     hid, pre, err, near, far, beside = [], [], [], [], [], []
     for m in range(members):
-        h, s, e = forward(low[m], mine[m], high[m], w_node, at, bias_cols, w_out, target)
+        h, s, e = forward(low[m], mine[m], high[m], w_node, at, bias_row, w_out, target)
         hid.append(h)
         pre.append(s)
         err.append(e)
@@ -393,49 +445,53 @@
     p_0, p_1, loss = crps_near(err, near + [far[0], beside[0]], area_row, count)
     d_0, d_1, loss = crps_far(err, [far[1], beside[1]], (p_0, p_1), area_row, loss, count)
 
+    spot = where[None].astype(jnp.int32)
+    every = lax.axis_size(EVERY)
+    heads = head_parts(spot, variables, (d_0, d_1), hid, loss)
+    pieces = lax.all_to_all(heads.reshape(every, 8, 128), EVERY, split_axis=0, concat_axis=0, tiled=True)
+
     def back(side):
-        who = jnp.stack([side, where]).astype(jnp.int32)
-        return backward(who, variables, (d_0, d_1), w_out_t, slope, hid, at, loss)
-
-    given, heads_given = back(1 - core)
+        return backward(side[None].astype(jnp.int32), (d_0, d_1), w_out, slope, at)
+
+    given, bias_given = back(1 - core)
     taken = lax.ppermute(given, "core", swap)
-    kept, heads_kept = back(core)
-
-    every = lax.axis_size(EVERY)
-    even = core == 0
-    heads = jnp.stack(
-        [jnp.where(even, heads_kept, heads_given), jnp.where(even, heads_given, heads_kept)], axis=1
-    )
-    pieces = lax.all_to_all(heads.reshape(every, 8, 128), EVERY, split_axis=0, concat_axis=0, tiled=True)
+    kept, bias_kept = back(core)
     part = outer(lat_t, lat_t_other, kept, taken)
     chips = lax.axis_size(CHIPS)
     shares = lax.all_to_all(
         part.reshape(chips, width // regions, width // 4), CHIPS, split_axis=0, concat_axis=0, tiled=True
     )
+    even = core == 0
+    summed = jnp.stack(
+        [jnp.where(even, bias_kept, bias_given)[:, 0], jnp.where(even, bias_given, bias_kept)[:, 0]], axis=1
+    ).reshape(1, 8, 128)
     spread = pieces.sum(axis=0)[None]
     ring = [(0, 3), (3, 0), (1, 2), (2, 1)]
     pair = [(0, 1), (1, 0), (2, 3), (3, 2)]
-    x, z = lax.axis_index("x"), lax.axis_index("z")
+    x = lax.axis_index("x")
     steps = (
         ("ylo", swap, lax.axis_index("ylo")),
         (("ylo", "yhi"), ring, lax.axis_index("yhi")),
         ("x", pair, x % 2),
         ("x", ring, x // 2),
-        ("z", pair, z % 2),
-        ("z", ring, z // 2),
-        ("core", swap, core),
     )
     for axis, moves, place in steps:
-        other = lax.ppermute(spread, axis, moves)
+        other = lax.ppermute(jnp.concatenate([spread, summed]), axis, moves)
+        summed = summed + other[-1:]
+        other = other[:-1]
         spread = jnp.where(
             place == 0, jnp.concatenate([spread, other]), jnp.concatenate([other, spread])
         )
+    spread = jnp.concatenate([spread, summed])
+    rest = ("core", "z")
+    table = lax.all_to_all(
+        jnp.broadcast_to(spread, (lax.axis_size(rest), *spread.shape)), rest, split_axis=0, concat_axis=0, tiled=True
+    )
     own = shares.astype(f32).sum(axis=0)
     grad_node = lax.all_gather(own, MEMBER, axis=1, tiled=True)
-    full = finish(spread, width)
-    grad_out = full[:variables]
-    grad_bias = full[variables]
-    loss_here = lax.dynamic_slice(full, (variables + 1, where), (1, 1)).reshape(1)
+    grad_out, grad_bias, loss_here = finish(spot, table, variables, width)
+    grad_bias = grad_bias.reshape(width)
+    loss_here = loss_here.reshape(1)
     return grad_node, grad_out, grad_bias, loss_here
 
 

time: 154 us -> 184 us (1.19)
  waiting for transfers between devices: 22.6 us -> 38.8 us
  Pallas kernels: 54.3 us -> 69.7 us
  blocking collectives: 22.8 us -> 8.21 us
  starting transfers between devices: 39.1 us -> 52.5 us
    ppermute x11 -> x8, waiting for transfers between devices: 21.8 us -> 2.7 us  [the longest x4 2.68 us: local(): other = lax.ppermute(jnp.concatenate([spread, summed]), axis, moves)]
    all_to_all x1 -> x0, blocking collectives: 17.2 us -> none  [local(): lax.all_to_all(heads.reshape(every, 8, 128), EVERY, split_axis=0, concat_...]
    ppermute x2, waiting for transfers between devices: 0.01 us -> 16.2 us  [local(): over = lax.ppermute((e * 0.125).astype(f16), 'ylo', swap)]
    all_to_all x1, waiting for transfers between devices: 0.01 us -> 15.3 us  [local(): lax.all_to_all(part.reshape(chips, width // regions, width // 4), CHIPS,...]
    all_to_all x0 -> x2, starting transfers between devices: none -> 12.3 us  [the longest x1 7.12 us: local(): lax.all_to_all(jnp.broadcast_to(spread, (lax.axis_size(rest), *spread.sha...]
    pallas_call x3 -> x4, Pallas kernels: 10.8 us -> 20.2 us  [the longest x2 13 us: backward(): pl.pallas_call(backward_kernel, grid_spec=pltpu.PrefetchScalarGridSpec(nu...]
    ppermute x11 -> x8, starting transfers between devices: 28.9 us -> 24.7 us  [the longest x2 14.6 us: local(): high.append(lax.ppermute(mine[m], REGION, behind))]
    pallas_call x2, Pallas kernels: 19.3 us -> 22.9 us  [forward(): pl.pallas_call(forward_kernel, grid=(points // wide,), in_specs=[whole(lo...]
  transfers between devices with their start and end apart: 20 -> 19, of which waited for: 7 -> 8; matrix products, arithmetic and copies ran while one was open for 4% -> 1% of each run, Pallas kernels for 35% -> 31%
where the time goes in v3:
time: 184 us; the launch traced here: 183 us
  Pallas kernels  69.7 us (38%)
  starting transfers between devices  52.5 us (29%)
  waiting for transfers between devices  38.8 us (21%)
  local copies, waits for them, and re-layouts  10.6 us (6%)
  blocking collectives  8.21 us (4%)
  other arithmetic  1.93 us (1%)
    pallas_call x2, Pallas kernels, forward(): pl.pallas_call(forward_kernel, grid=(points // wide,), in_specs=[whole(lo...  22.9 us
    ppermute x2, waiting for transfers between devices, local(): over = lax.ppermute((e * 0.125).astype(f16), 'ylo', swap)  16.2 us
    all_to_all x1, waiting for transfers between devices, local(): lax.all_to_all(part.reshape(chips, width // regions, width // 4), CHIPS,...  15.3 us
    ppermute x2, starting transfers between devices, local(): high.append(lax.ppermute(mine[m], REGION, behind))  14.6 us
    pallas_call x2, Pallas kernels, backward(): pl.pallas_call(backward_kernel, grid_spec=pltpu.PrefetchScalarGridSpec(nu...  13 us
    pallas_call x1, Pallas kernels, slopes(): pl.pallas_call(slope_kernel, grid=(width // 128,), in_specs=[rows, rows],...  11.7 us
    unnamed x35, local copies, waits for them, and re-layouts  8.67 us
    all_gather x1, blocking collectives, local(): grad_node = lax.all_gather(own, MEMBER, axis=1, tiled=True)  8.21 us
  transfers between devices with their start and end apart: 19, of which 8 were waited for; matrix products, arithmetic and copies ran while one was open for 1% of the time, Pallas kernels for 31%

profile of v3, /device:TPU:1, one launch (start us, length us, event | category | flops | bytes accessed | tf_op | source)
XLA Modules:
  0.0 182.8 jit_solution(7454546578671364246)
XLA Ops:
  0.6 1.1 slice_bitcast_fusion
  1.7 2.1 %collective-permute-start = (bf16[128,1024]{1,0:T(8,128)(2,1)S(1)}, bf16[128,1024]{1,0:T(8,128)(2,1)S(1)}, u32[]{:S(2)}, u32[]{:S(2)}) collective-permute-start(bf16[128,1024]{1,0:T(8,128)(2,1)S(1)} %get-tuple-element.28.refs_1_.own), channel_id=1, source_target_pairs={{0,1},{1,2},{2,3},{3,4},{4,5},{5,6},{6,7},{7,8},{8,9},{9,10},{10,1... | collective-permute-start | bytes 786440 | tf_op jit(solution)/shard_map/ppermute | solution.py:423
  3.8 7.5 %collective-permute-start.3 = (bf16[128,1024]{1,0:T(8,128)(2,1)S(1)}, bf16[128,1024]{1,0:T(8,128)(2,1)S(1)}, u32[]{:S(2)}, u32[]{:S(2)}) collective-permute-start(bf16[128,1024]{1,0:T(8,128)(2,1)S(1)} %get-tuple-element.28.refs_1_.own), channel_id=1, source_target_pairs={{1,0},{2,1},{3,2},{4,3},{5,4},{6,5},{7,6},{8,7},{9,8},{10,9},{11,1... | collective-permute-start | bytes 786440 | tf_op jit(solution)/shard_map/ppermute | solution.py:424
  11.3 0.0 collective-permute-start.1
  11.3 7.2 %collective-permute-start.2 = (bf16[128,1024]{1,0:T(8,128)(2,1)S(1)}, bf16[128,1024]{1,0:T(8,128)(2,1)}, u32[]{:S(2)}, u32[]{:S(2)}) collective-permute-start(bf16[128,1024]{1,0:T(8,128)(2,1)S(1)} %get-tuple-element.50.own.refs_4_), channel_id=1, source_target_pairs={{1,0},{2,1},{3,2},{4,3},{5,4},{6,5},{7,6},{8,7},{9,8},{10,9},{11,1... | collective-permute-start | bytes 786440 | tf_op jit(solution)/shard_map/ppermute | solution.py:424
  18.5 0.8 copy-done.11
  19.2 0.8 copy-done.12
  20.0 1.2 prep.1.at
  21.2 0.0 copy-start.15
  21.2 0.0 copy-start.7
  21.3 0.0 copy-start.1
  21.3 1.1 copy-done.1
  22.4 0.7 copy-done.14
  23.1 11.4 %forward.3 = (bf16[1024,2048]{1,0:T(8,128)(2,1)}, bf16[1024,2048]{1,0:T(8,128)(2,1)}, f32[100,2048]{1,0:T(8,128)S(1)}) custom-call(bf16[128,1024]{1,0:T(8,128)(2,1)S(1)} %collective-permute-done.refs_0_.low, bf16[128,1024]{1,0:T(8,128)(2,1)S(1)} %get-tuple-element.28.refs_1_.own, bf16[128,1024]{1,0:T(8,128)(2,1)S(1)} %collective-permute-done.3.refs_2_.high, ...), custom_call_target="tpu_custom_call" | custom-call | tf_op jit(solution)/shard_map/forward/pallas_call | solution.py:127
  34.4 1.5 collective-permute-start.7
  36.0 0.1 multiply_convert_fusion
  36.1 11.5 %forward.2 = (bf16[1024,2048]{1,0:T(8,128)(2,1)}, bf16[1024,2048]{1,0:T(8,128)(2,1)}, f32[100,2048]{1,0:T(8,128)S(1)}) custom-call(bf16[128,1024]{1,0:T(8,128)(2,1)} %collective-permute-done.1.low.refs_3_, bf16[128,1024]{1,0:T(8,128)(2,1)S(1)} %get-tuple-element.50.own.refs_4_, bf16[128,1024]{1,0:T(8,128)(2,1)} %collective-permute-done.2.high.refs_5_, ...), custom_call_target="tpu_custom_call" | custom-call | tf_op jit(solution)/shard_map/forward/pallas_call | solution.py:127
  47.7 0.0 copy-start.13
  47.7 0.1 collective-permute-start.8
  47.8 0.5 collective-permute-start.9
  48.2 0.1 multiply_convert_fusion.1
  48.3 1.1 collective-permute-start.5
  49.5 9.3 %collective-permute-done.9 = f16[100,2048]{1,0:T(8,128)(2,1)S(1)} collective-permute-done((f16[100,2048]{1,0:T(8,128)(2,1)S(1)}, f16[100,2048]{1,0:T(8,128)(2,1)S(1)}, u32[]{:S(2)}, u32[]{:S(2)}) %collective-permute-start.9) | collective-permute-done | bytes 409632 | tf_op jit(solution)/shard_map/ppermute | solution.py:434
  58.8 2.1 %collective-permute-start.10 = (f16[100,2048]{1,0:T(8,128)(2,1)S(1)}, f16[100,2048]{1,0:T(8,128)(2,1)S(1)}, u32[]{:S(2)}, u32[]{:S(2)}) collective-permute-start(f16[100,2048]{1,0:T(8,128)(2,1)S(1)} %collective-permute-done.9), channel_id=1, source_target_pairs={{0,32},{32,0},{1,33},{33,1},{2,34},{34,2},{3,35},{35,3},{4,36},{36... | collective-permute-start | bytes 1228808 | tf_op jit(solution)/shard_map/ppermute | solution.py:437
  60.9 0.1 convert_multiply_fusion.1.refs_4_
  61.0 6.9 %collective-permute-done.5 = f16[100,2048]{1,0:T(8,128)(2,1)S(1)} collective-permute-done((f16[100,2048]{1,0:T(8,128)(2,1)S(1)}, f16[100,2048]{1,0:T(8,128)(2,1)S(1)}, u32[]{:S(2)}, u32[]{:S(2)}) %collective-permute-start.5) | collective-permute-done | bytes 409632 | tf_op jit(solution)/shard_map/ppermute | solution.py:434
  67.9 1.3 collective-permute-start.6
  69.2 0.1 convert_multiply_fusion.3.refs_2_
  69.3 0.1 convert_multiply_fusion.refs_5_
  69.4 1.2 collective-permute-done.6
  70.6 0.1 convert_multiply_fusion.2.refs_3_
  70.7 4.0 %crps_near.1 = (f32[100,2048]{1,0:T(8,128)S(1)}, f32[100,2048]{1,0:T(8,128)S(1)}, f32[1,128]{1,0:T(1,128)S(1)}) custom-call(f32[100,2048]{1,0:T(8,128)S(1)} %get-tuple-element.29.refs_0_, f32[100,2048]{1,0:T(8,128)S(1)} %get-tuple-element.30.refs_1_, f32[100,2048]{1,0:T(8,128)S(1)} %collective-permute-done.7.refs_2_, ...), custom_call_target="tpu_custom_call" | custom-call | tf_op jit(solution)/shard_map/crps_near/pallas_call | solution.py:237
  74.7 1.9 %crps_far.1 = (bf16[128,2048]{1,0:T(8,128)(2,1)S(1)}, bf16[128,2048]{1,0:T(8,128)(2,1)S(1)}, f32[1,128]{1,0:T(1,128)S(1)}) custom-call(f32[100,2048]{1,0:T(8,128)S(1)} %get-tuple-element.29.refs_0_, f32[100,2048]{1,0:T(8,128)S(1)} %get-tuple-element.30.refs_1_, f32[100,2048]{1,0:T(8,128)S(1)} %convert_multiply_fusion.3.refs_2_, ...), custom_call_target="tpu_custom_call" | custom-call | tf_op jit(solution)/shard_map/crps_far/pallas_call | solution.py:255
  76.6 6.4 %heads.1 = f32[4,16,2,8,128]{4,3,2,1,0:T(8,128)} custom-call(s32[1]{0:T(128)} %bitcast.9.refs_0_.where, bf16[128,2048]{1,0:T(8,128)(2,1)S(1)} %get-tuple-element.34.d_0.refs_1_, bf16[128,2048]{1,0:T(8,128)(2,1)S(1)} %get-tuple-element.35.d_1.refs_2_, bf16[1024,2048]{1,0:T(8,128)(2,1)} %get-tuple-element.42.refs_3_, ...), custom_call_target="tpu_custom_call" | custom-call | tf_op jit(solution)/shard_map/heads/pallas_call | solution.py:285
  83.1 5.2 %all-to-all-start.1 = ((f32[128,8,128]{2,1,0:T(8,128)}), f32[128,8,128]{2,1,0:T(8,128)}, u32[]{:S(2)}, u32[]{:S(2)}) async-start(f32[128,8,128]{2,1,0:T(8,128)} %bitcast.22), calls=%async_computation.1 | async-start | bytes 1048576 | tf_op jit(solution)/shard_map/all_to_all | solution.py:451
  88.3 11.7 %slope.1 = (bf16[1024,2048]{1,0:T(8,128)(2,1)}, bf16[1024,2048]{1,0:T(8,128)(2,1)}) custom-call(bf16[1024,2048]{1,0:T(8,128)(2,1)} %get-tuple-element.36.pre_0, bf16[1024,2048]{1,0:T(8,128)(2,1)} %get-tuple-element.37.pre_1), custom_call_target="tpu_custom_call" | custom-call | tf_op jit(solution)/shard_map/slope/pallas_call | solution.py:156
  100.0 6.5 %backward.3 = (bf16[2,768,256]{2,1,0:T(8,128)(2,1)}, f32[2,8,256]{2,1,0:T(8,128)S(1)}) custom-call(s32[1]{0:T(128)} %bitcast.7.who, bf16[128,2048]{1,0:T(8,128)(2,1)S(1)} %get-tuple-element.34.d_0.refs_1_, bf16[128,2048]{1,0:T(8,128)(2,1)S(1)} %get-tuple-element.35.d_1.refs_2_, bf16[100,1024]{1,0:T(8,128)(2,1)S(1)} %copy-done.2, ...), custom_call_target="tpu_custom_call" | custom-call | tf_op jit(solution)/shard_map/backward/pallas_call | solution.py:325
  106.4 6.5 %backward.2 = (bf16[2,768,256]{2,1,0:T(8,128)(2,1)}, f32[2,8,256]{2,1,0:T(8,128)S(1)}) custom-call(s32[1]{0:T(128)} %bitcast.5.who, bf16[128,2048]{1,0:T(8,128)(2,1)S(1)} %get-tuple-element.34.d_0.refs_1_, bf16[128,2048]{1,0:T(8,128)(2,1)S(1)} %get-tuple-element.35.d_1.refs_2_, bf16[100,1024]{1,0:T(8,128)(2,1)S(1)} %copy-done.2, ...), custom_call_target="tpu_custom_call" | custom-call | tf_op jit(solution)/shard_map/backward/pallas_call | solution.py:325
  113.0 1.2 reduce_sum.19
  114.2 1.4 collective-permute-start.12
  115.6 1.1 collective-permute-done.12
  116.8 2.7 %collective-permute-start.13 = (f32[3,8,128]{2,1,0:T(8,128)S(1)}, f32[3,8,128]{2,1,0:T(8,128)S(1)}, u32[]{:S(2)}, u32[]{:S(2)}) collective-permute-start(f32[3,8,128]{2,1,0:T(8,128)S(1)} %pad_maximum_fusion.3), channel_id=1, source_target_pairs={{0,68},{68,0},{4,64},{64,4},{1,69},{69,1},{5,65},{65,5},{2,70},{70... | collective-permute-start | bytes 36872 | tf_op jit(solution)/shard_map/ppermute | solution.py:479
  119.5 0.9 copy-done.4
  120.4 0.9 copy-done.6
  121.4 0.9 copy-done.8
  122.3 0.9 copy-done.10
  123.3 2.4 %turn.1.lat_own = bf16[1024,768]{1,0:T(8,128)(2,1)S(1)} custom-call(bf16[128,1024]{1,0:T(8,128)(2,1)S(1)} %copy-done.8, bf16[128,1024]{1,0:T(8,128)(2,1)S(1)} %copy-done.6, bf16[128,1024]{1,0:T(8,128)(2,1)S(1)} %copy-done.10, bf16[128,1024]{1,0:T(8,128)(2,1)} %collective-permute-done.1.low.refs_3_, bf16[128,1024]{1,0:T(8,128)(2,1)S(1)} %copy-done.4, ...), custom_call_target="tpu_custom_call" | custom-call | tf_op jit(solution)/shard_map/turn/pallas_call | solution.py:78
  125.7 1.9 %collective-permute-start.4 = (bf16[1024,768]{1,0:T(8,128)(2,1)S(1)}, bf16[1024,768]{1,0:T(8,128)(2,1)}, u32[]{:S(2)}, u32[]{:S(2)}) collective-permute-start(bf16[1024,768]{1,0:T(8,128)(2,1)S(1)} %turn.1.lat_own), channel_id=1, source_target_pairs={{0,32},{32,0},{1,33},{33,1},{2,34},{34,2},{3,35},{35,3},{4,36},{36... | collective-permute-start | bytes 4718600 | tf_op jit(solution)/shard_map/ppermute | solution.py:441
  127.6 1.3 collective-permute-start.14
  128.9 1.4 collective-permute-done.14
  130.3 2.5 %collective-permute-start.15 = (f32[9,8,128]{2,1,0:T(8,128)S(1)}, f32[9,8,128]{2,1,0:T(8,128)S(1)}, u32[]{:S(2)}, u32[]{:S(2)}) collective-permute-start(f32[9,8,128]{2,1,0:T(8,128)S(1)} %pad_maximum_fusion.1), channel_id=1, source_target_pairs={{0,3},{3,0},{1,2},{2,1},{4,7},{7,4},{5,6},{6,5},{8,11},{11,8},{9,1... | collective-permute-start | bytes 110600 | tf_op jit(solution)/shard_map/ppermute | solution.py:479
  132.9 1.5 collective-permute-start.11
  134.3 0.1 collective-permute-done.15
  134.5 0.8 broadcast_in_dim.27
  135.3 7.1 %all-to-all-start.2 = ((f32[8,17,8,128]{3,2,1,0:T(8,128)}), f32[8,17,8,128]{3,2,1,0:T(8,128)S(1)}, u32[]{:S(2)}, u32[]{:S(2)}) async-start(f32[8,17,8,128]{3,2,1,0:T(8,128)} %broadcast_in_dim.27), calls=%async_computation.2 | async-start | bytes 1114112 | tf_op jit(solution)/shard_map/all_to_all | solution.py:487
  142.5 0.9 copy-done.16
  143.4 5.3 %outer.1 = bf16[2,1024,256]{2,1,0:T(8,128)(2,1)} custom-call(bf16[1024,768]{1,0:T(8,128)(2,1)} %copy-done, bf16[1024,768]{1,0:T(8,128)(2,1)} %collective-permute-done.4.lat_other, bf16[2,768,256]{2,1,0:T(8,128)(2,1)} %get-tuple-element.40.c_own, bf16[2,768,256]{2,1,0:T(8,128)(2,1)} %copy-done.16), custom_call_target="tpu_custom_call" | custom-call | tf_op jit(solution)/shard_map/outer/pallas_call | solution.py:355
  148.7 3.5 %all-to-all-done.2.pieces = f32[8,17,8,128]{3,2,1,0:T(8,128)S(1)} async-done(((f32[8,17,8,128]{3,2,1,0:T(8,128)}), f32[8,17,8,128]{3,2,1,0:T(8,128)S(1)}, u32[]{:S(2)}, u32[]{:S(2)}) %all-to-all-start.2) | async-done | bytes 557088 | tf_op jit(solution)/shard_map/all_to_all | solution.py:487
  152.1 5.5 %all-to-all-start = ((bf16[64,32,256]{2,1,0:T(8,128)(2,1)}), bf16[64,32,256]{2,1,0:T(8,128)(2,1)S(1)}, u32[]{:S(2)}, u32[]{:S(2)}) async-start(bf16[64,32,256]{2,1,0:T(8,128)(2,1)} %bitcast.8), calls=%async_computation | async-start | bytes 2097152 | tf_op jit(solution)/shard_map/all_to_all | solution.py:461
  157.7 0.8 finish.1
  158.5 15.3 %all-to-all-done = bf16[64,32,256]{2,1,0:T(8,128)(2,1)S(1)} async-done(((bf16[64,32,256]{2,1,0:T(8,128)(2,1)}), bf16[64,32,256]{2,1,0:T(8,128)(2,1)S(1)}, u32[]{:S(2)}, u32[]{:S(2)}) %all-to-all-start) | async-done | bytes 1048608 | tf_op jit(solution)/shard_map/all_to_all | solution.py:461
  173.7 0.2 convert_reduce_fusion
  173.9 8.2 %all_gather.3 = f32[32,1024]{1,0:T(8,128)S(1)} all-gather(f32[32,256]{1,0:T(8,128)S(1)} %convert_reduce_fusion), channel_id=1, replica_groups=mesh['ylo'=2,'core'=2,'z'=4,'yhi'=2,'x'=4] {'ylo','core'}, dimensions={1}, use_global_device_ids=true | all-gather | bytes 163840 | tf_op jit(solution)/shard_map/all_gather | solution.py:491
  182.1 0.7 copy.13
  (51 shorter events, 0.2 us)
Async XLA Ops:
  1.7 34.3 %copy-start.5 = (bf16[128,1024]{1,0:T(8,128)(2,1)}, bf16[128,1024]{1,0:T(8,128)(2,1)S(1)}, u32[]{:S(2)}) copy-start(bf16[128,1024]{1,0:T(8,128)(2,1)S(1)} %get-tuple-element.28.refs_1_.own) | copy-start | bytes 786436
  1.7 34.4 %copy-start.3 = (bf16[128,1024]{1,0:T(8,128)(2,1)}, bf16[128,1024]{1,0:T(8,128)(2,1)S(1)}, u32[]{:S(2)}) copy-start(bf16[128,1024]{1,0:T(8,128)(2,1)S(1)} %get-tuple-element.50.own.refs_4_) | copy-start | bytes 786436
  1.7 19.5 %collective-permute-start = (bf16[128,1024]{1,0:T(8,128)(2,1)S(1)}, bf16[128,1024]{1,0:T(8,128)(2,1)S(1)}, u32[]{:S(2)}, u32[]{:S(2)}) collective-permute-start(bf16[128,1024]{1,0:T(8,128)(2,1)S(1)} %get-tuple-element.28.refs_1_.own), channel_id=1, source_target_pairs={{0,1},{1,2},{2,3},{3,4},{4,5},{5,6},{6,7},{7,8},{8,9},{9,10},{10,1... | collective-permute-start | bytes 786440 | tf_op jit(solution)/shard_map/ppermute | solution.py:423
  3.8 17.4 %collective-permute-start.3 = (bf16[128,1024]{1,0:T(8,128)(2,1)S(1)}, bf16[128,1024]{1,0:T(8,128)(2,1)S(1)}, u32[]{:S(2)}, u32[]{:S(2)}) collective-permute-start(bf16[128,1024]{1,0:T(8,128)(2,1)S(1)} %get-tuple-element.28.refs_1_.own), channel_id=1, source_target_pairs={{1,0},{2,1},{3,2},{4,3},{5,4},{6,5},{7,6},{8,7},{9,8},{10,9},{11,1... | collective-permute-start | bytes 786440 | tf_op jit(solution)/shard_map/ppermute | solution.py:424
  11.3 24.8 %collective-permute-start.1 = (bf16[128,1024]{1,0:T(8,128)(2,1)S(1)}, bf16[128,1024]{1,0:T(8,128)(2,1)}, u32[]{:S(2)}, u32[]{:S(2)}) collective-permute-start(bf16[128,1024]{1,0:T(8,128)(2,1)S(1)} %get-tuple-element.50.own.refs_4_), channel_id=1, source_target_pairs={{0,1},{1,2},{2,3},{3,4},{4,5},{5,6},{6,7},{7,8},{8,9},{9,10},{10,1... | collective-permute-start | bytes 786440 | tf_op jit(solution)/shard_map/ppermute | solution.py:423
  11.3 24.8 %collective-permute-start.2 = (bf16[128,1024]{1,0:T(8,128)(2,1)S(1)}, bf16[128,1024]{1,0:T(8,128)(2,1)}, u32[]{:S(2)}, u32[]{:S(2)}) collective-permute-start(bf16[128,1024]{1,0:T(8,128)(2,1)S(1)} %get-tuple-element.50.own.refs_4_), channel_id=1, source_target_pairs={{1,0},{2,1},{3,2},{4,3},{5,4},{6,5},{7,6},{8,7},{9,8},{10,9},{11,1... | collective-permute-start | bytes 786440 | tf_op jit(solution)/shard_map/ppermute | solution.py:424
  18.5 0.8 copy-start.11
  19.2 0.8 copy-start.12
  20.0 16.1 %copy-start.2 = (bf16[100,1024]{1,0:T(8,128)(2,1)S(1)}, bf16[100,1024]{1,0:T(8,128)(2,1)}, u32[]{:S(2)}) copy-start(bf16[100,1024]{1,0:T(8,128)(2,1)} %w_out.7) | copy-start | bytes 614404
  21.2 14.9 %copy-start.15 = (f32[1024]{0:T(1024)S(1)}, f32[1024]{0:T(1024)}, u32[]{:S(2)}) copy-start(f32[1024]{0:T(1024)} %param.10) | copy-start | bytes 12292
  21.2 26.4 %copy-start.7 = (bf16[128,1024]{1,0:T(8,128)(2,1)}, bf16[128,1024]{1,0:T(8,128)(2,1)S(1)}, u32[]{:S(2)}) copy-start(bf16[128,1024]{1,0:T(8,128)(2,1)S(1)} %collective-permute-done.refs_0_.low) | copy-start | bytes 786436
  21.2 26.4 %copy-start.9 = (bf16[128,1024]{1,0:T(8,128)(2,1)}, bf16[128,1024]{1,0:T(8,128)(2,1)S(1)}, u32[]{:S(2)}) copy-start(bf16[128,1024]{1,0:T(8,128)(2,1)S(1)} %collective-permute-done.3.refs_2_.high) | copy-start | bytes 786436
  21.3 1.1 copy-start.1
  22.4 0.7 copy-start.14
  34.4 36.3 %collective-permute-start.7 = (f32[100,2048]{1,0:T(8,128)S(1)}, f32[100,2048]{1,0:T(8,128)S(1)}, u32[]{:S(2)}, u32[]{:S(2)}) collective-permute-start(f32[100,2048]{1,0:T(8,128)S(1)} %get-tuple-element.29.refs_0_), channel_id=1, source_target_pairs={{0,32},{32,0},{1,33},{33,1},{2,34},{34,2},{3,35},{35,3},{4,36},{36... | collective-permute-start | bytes 2457608 | tf_op jit(solution)/shard_map/ppermute | solution.py:435
  47.7 23.1 %copy-start.13 = (f32[2048]{0:T(1024)S(1)}, f32[2048]{0:T(1024)}, u32[]{:S(2)}) copy-start(f32[2048]{0:T(1024)} %param.15) | copy-start | bytes 24580
  47.7 23.0 %collective-permute-start.8 = (f32[100,2048]{1,0:T(8,128)S(1)}, f32[100,2048]{1,0:T(8,128)S(1)}, u32[]{:S(2)}, u32[]{:S(2)}) collective-permute-start(f32[100,2048]{1,0:T(8,128)S(1)} %get-tuple-element.30.refs_1_), channel_id=1, source_target_pairs={{0,32},{32,0},{1,33},{33,1},{2,34},{34,2},{3,35},{35,3},{4,36},{36... | collective-permute-start | bytes 2457608 | tf_op jit(solution)/shard_map/ppermute | solution.py:435
  47.8 11.0 %collective-permute-start.9 = (f16[100,2048]{1,0:T(8,128)(2,1)S(1)}, f16[100,2048]{1,0:T(8,128)(2,1)S(1)}, u32[]{:S(2)}, u32[]{:S(2)}) collective-permute-start(f16[100,2048]{1,0:T(8,128)(2,1)S(1)} %multiply_convert_fusion), channel_id=1, source_target_pairs={{0,64},{64,0},{1,65},{65,1},{2,66},{66,2},{3,67},{67,3},{4,68},{68... | collective-permute-start | bytes 1228808 | tf_op jit(solution)/shard_map/ppermute | solution.py:434
  48.3 19.6 %collective-permute-start.5 = (f16[100,2048]{1,0:T(8,128)(2,1)S(1)}, f16[100,2048]{1,0:T(8,128)(2,1)S(1)}, u32[]{:S(2)}, u32[]{:S(2)}) collective-permute-start(f16[100,2048]{1,0:T(8,128)(2,1)S(1)} %multiply_convert_fusion.1), channel_id=1, source_target_pairs={{0,64},{64,0},{1,65},{65,1},{2,66},{66,2},{3,67},{67,3},{4,68},{68... | collective-permute-start | bytes 1228808 | tf_op jit(solution)/shard_map/ppermute | solution.py:434
  58.8 10.5 %collective-permute-start.10 = (f16[100,2048]{1,0:T(8,128)(2,1)S(1)}, f16[100,2048]{1,0:T(8,128)(2,1)S(1)}, u32[]{:S(2)}, u32[]{:S(2)}) collective-permute-start(f16[100,2048]{1,0:T(8,128)(2,1)S(1)} %collective-permute-done.9), channel_id=1, source_target_pairs={{0,32},{32,0},{1,33},{33,1},{2,34},{34,2},{3,35},{35,3},{4,36},{36... | collective-permute-start | bytes 1228808 | tf_op jit(solution)/shard_map/ppermute | solution.py:437
  67.9 2.7 %collective-permute-start.6 = (f16[100,2048]{1,0:T(8,128)(2,1)S(1)}, f16[100,2048]{1,0:T(8,128)(2,1)S(1)}, u32[]{:S(2)}, u32[]{:S(2)}) collective-permute-start(f16[100,2048]{1,0:T(8,128)(2,1)S(1)} %collective-permute-done.5), channel_id=1, source_target_pairs={{0,32},{32,0},{1,33},{33,1},{2,34},{34,2},{3,35},{35,3},{4,36},{36... | collective-permute-start | bytes 1228808 | tf_op jit(solution)/shard_map/ppermute | solution.py:437
  83.1 29.9 %all-to-all-start.1 = ((f32[128,8,128]{2,1,0:T(8,128)}), f32[128,8,128]{2,1,0:T(8,128)}, u32[]{:S(2)}, u32[]{:S(2)}) async-start(f32[128,8,128]{2,1,0:T(8,128)} %bitcast.22), calls=%async_computation.1 | async-start | bytes 1048576 | tf_op jit(solution)/shard_map/all_to_all | solution.py:451
  114.2 2.6 %collective-permute-start.12 = (f32[2,8,128]{2,1,0:T(8,128)S(1)}, f32[2,8,128]{2,1,0:T(8,128)S(1)}, u32[]{:S(2)}, u32[]{:S(2)}) collective-permute-start(f32[2,8,128]{2,1,0:T(8,128)S(1)} %pad_maximum_fusion.4), channel_id=1, source_target_pairs={{0,64},{64,0},{1,65},{65,1},{2,66},{66,2},{3,67},{67,3},{4,68},{68... | collective-permute-start | bytes 24584 | tf_op jit(solution)/shard_map/ppermute | solution.py:479
  116.8 10.8 %collective-permute-start.13 = (f32[3,8,128]{2,1,0:T(8,128)S(1)}, f32[3,8,128]{2,1,0:T(8,128)S(1)}, u32[]{:S(2)}, u32[]{:S(2)}) collective-permute-start(f32[3,8,128]{2,1,0:T(8,128)S(1)} %pad_maximum_fusion.3), channel_id=1, source_target_pairs={{0,68},{68,0},{4,64},{64,4},{1,69},{69,1},{5,65},{65,5},{2,70},{70... | collective-permute-start | bytes 36872 | tf_op jit(solution)/shard_map/ppermute | solution.py:479
  119.5 0.9 copy-start.4
  120.4 0.9 copy-start.6
  121.4 0.9 copy-start.8
  122.3 0.9 copy-start.10
  125.7 16.8 %copy-start = (bf16[1024,768]{1,0:T(8,128)(2,1)}, bf16[1024,768]{1,0:T(8,128)(2,1)S(1)}, u32[]{:S(2)}) copy-start(bf16[1024,768]{1,0:T(8,128)(2,1)S(1)} %turn.1.lat_own) | copy-start | bytes 4718596
  125.7 16.8 %collective-permute-start.4 = (bf16[1024,768]{1,0:T(8,128)(2,1)S(1)}, bf16[1024,768]{1,0:T(8,128)(2,1)}, u32[]{:S(2)}, u32[]{:S(2)}) collective-permute-start(bf16[1024,768]{1,0:T(8,128)(2,1)S(1)} %turn.1.lat_own), channel_id=1, source_target_pairs={{0,32},{32,0},{1,33},{33,1},{2,34},{34,2},{3,35},{35,3},{4,36},{36... | collective-permute-start | bytes 4718600 | tf_op jit(solution)/shard_map/ppermute | solution.py:441
  127.6 2.7 %collective-permute-start.14 = (f32[5,8,128]{2,1,0:T(8,128)S(1)}, f32[5,8,128]{2,1,0:T(8,128)S(1)}, u32[]{:S(2)}, u32[]{:S(2)}) collective-permute-start(f32[5,8,128]{2,1,0:T(8,128)S(1)} %pad_maximum_fusion.2), channel_id=1, source_target_pairs={{0,1},{1,0},{2,3},{3,2},{4,5},{5,4},{6,7},{7,6},{8,9},{9,8},{10,11... | collective-permute-start | bytes 61448 | tf_op jit(solution)/shard_map/ppermute | solution.py:479
  130.3 4.1 %collective-permute-start.15 = (f32[9,8,128]{2,1,0:T(8,128)S(1)}, f32[9,8,128]{2,1,0:T(8,128)S(1)}, u32[]{:S(2)}, u32[]{:S(2)}) collective-permute-start(f32[9,8,128]{2,1,0:T(8,128)S(1)} %pad_maximum_fusion.1), channel_id=1, source_target_pairs={{0,3},{3,0},{1,2},{2,1},{4,7},{7,4},{5,6},{6,5},{8,11},{11,8},{9,1... | collective-permute-start | bytes 110600 | tf_op jit(solution)/shard_map/ppermute | solution.py:479
  132.9 9.6 %collective-permute-start.11 = (bf16[2,768,256]{2,1,0:T(8,128)(2,1)}, bf16[2,768,256]{2,1,0:T(8,128)(2,1)S(1)}, u32[]{:S(2)}, u32[]{:S(2)}) collective-permute-start(bf16[2,768,256]{2,1,0:T(8,128)(2,1)} %get-tuple-element.41), channel_id=1, source_target_pairs={{0,32},{32,0},{1,33},{33,1},{2,34},{34,2},{3,35},{35,3},{4,36},{36... | collective-permute-start | bytes 2359304 | tf_op jit(solution)/shard_map/ppermute | solution.py:457
  135.3 16.8 %all-to-all-start.2 = ((f32[8,17,8,128]{3,2,1,0:T(8,128)}), f32[8,17,8,128]{3,2,1,0:T(8,128)S(1)}, u32[]{:S(2)}, u32[]{:S(2)}) async-start(f32[8,17,8,128]{3,2,1,0:T(8,128)} %broadcast_in_dim.27), calls=%async_computation.2 | async-start | bytes 1114112 | tf_op jit(solution)/shard_map/all_to_all | solution.py:487
  142.5 0.9 copy-start.16
  152.1 21.6 %all-to-all-start = ((bf16[64,32,256]{2,1,0:T(8,128)(2,1)}), bf16[64,32,256]{2,1,0:T(8,128)(2,1)S(1)}, u32[]{:S(2)}, u32[]{:S(2)}) async-start(bf16[64,32,256]{2,1,0:T(8,128)(2,1)} %bitcast.8), calls=%async_computation | async-start | bytes 2097152 | tf_op jit(solution)/shard_map/all_to_all | solution.py:461

commit v4 on v2

--- a/solution.py
+++ b/solution.py
@@ -33,6 +33,10 @@
     return pltpu.CompilerParams(dimension_semantics=semantics, vmem_limit_bytes=mib << 20)
 
 
+def parked(a):
+    return pltpu.with_memory_space_constraint(a, pltpu.VMEM)
+
+
 def whole(a):
     return pl.BlockSpec(a.shape, lambda *i: (0,) * a.ndim)
 
@@ -56,7 +60,7 @@
         grid=(points // WIDE,),
         in_specs=[row, row],
         out_specs=pl.BlockSpec((nodes + DEEP, WIDE), lambda i: (0, i)),
-        out_shape=jax.ShapeDtypeStruct((nodes + DEEP, points), bf16),
+        out_shape=pltpu.VMEM((nodes + DEEP, points), bf16),
         compiler_params=params(("arbitrary",), 8),
         name="prep",
     )(src, weight)
@@ -76,7 +80,7 @@
         grid=(width // WIDE,),
         in_specs=[pl.BlockSpec((nodes, WIDE), lambda i: (0, i))] * len(blocks),
         out_specs=pl.BlockSpec((WIDE, nodes * len(blocks)), lambda i: (i, 0)),
-        out_shape=jax.ShapeDtypeStruct((width, nodes * len(blocks)), bf16),
+        out_shape=pltpu.VMEM((width, nodes * len(blocks)), bf16),
         compiler_params=params(("arbitrary",), 8),
         name="turn",
     )(*blocks)
@@ -89,7 +93,13 @@
     def _():
         stacked = jnp.concatenate([low[...], own[...], high[...]], axis=0)
         proj[:, :nodes] = dot(stacked, w_node[...]).astype(bf16).T
-        proj[:, nodes:] = bias[...]
+        row = lax.broadcasted_iota(jnp.int32, (DEEP, proj.shape[0]), 0)
+        block, rest = jnp.zeros(row.shape, f32), bias[...]
+        for k in range(SPLIT):
+            part = rest.astype(bf16).astype(f32)
+            block = jnp.where(row == k, part, block)
+            rest = rest - part
+        proj[:, nodes:] = block.T.astype(bf16)
 
     for g in range(target.shape[1] // WIDE):
         cols = slice(g * WIDE, (g + 1) * WIDE)
@@ -120,14 +130,14 @@
         in_specs=[whole(low), whole(own), whole(high), whole(w_node), cut(at.shape[0]), whole(bias), whole(w_out), cut(variables)],
         out_specs=[cut(width), cut(width), cut(variables)],
         out_shape=[
-            jax.ShapeDtypeStruct((width, points), bf16),
-            jax.ShapeDtypeStruct((width, points), bf16),
-            jax.ShapeDtypeStruct((variables, points), f32),
+            pltpu.VMEM((width, points), bf16),
+            pltpu.VMEM((width, points), bf16),
+            pltpu.VMEM((variables, points), f32),
         ],
         scratch_shapes=[pltpu.VMEM((width, at.shape[0]), bf16)],
         compiler_params=params(("arbitrary",), 24),
         name="forward",
-    )(low, own, high, w_node, at, bias, w_out, target)
+    )(low, own, high, parked(w_node), parked(at), bias, parked(w_out), parked(target))
 
 
 def slope_kernel(pre_0, pre_1, out_0, out_1):
@@ -148,10 +158,10 @@
         grid=(width // 128,),
         in_specs=[rows, rows],
         out_specs=[rows, rows],
-        out_shape=[jax.ShapeDtypeStruct((width, points), bf16)] * 2,
+        out_shape=[pltpu.VMEM((width, points), bf16)] * 2,
         compiler_params=params(("arbitrary",), 8),
         name="slope",
-    )(*pre)
+    )(*map(parked, pre))
 
 
 def apart(d):
@@ -229,10 +239,10 @@
         grid=(points // wide,),
         in_specs=[field] * (2 + len(others)) + [row],
         out_specs=[field, field, pl.BlockSpec((1, PAD), lambda i: (0, 0))],
-        out_shape=[jax.ShapeDtypeStruct((variables, points), f32)] * 2 + [jax.ShapeDtypeStruct((1, PAD), f32)],
+        out_shape=[pltpu.VMEM((variables, points), f32)] * 2 + [jax.ShapeDtypeStruct((1, PAD), f32)],
         compiler_params=params(("arbitrary",), 16),
         name="crps_near",
-    )(*own, *others, area)
+    )(*map(parked, own), *others, area)
 
 
 def crps_far(own, others, partial, area, before, count):
@@ -247,23 +257,24 @@
         grid=(points // wide,),
         in_specs=[field] * (4 + len(others)) + [row, one],
         out_specs=[padded, padded, one],
-        out_shape=[jax.ShapeDtypeStruct((PAD, points), bf16)] * 2 + [jax.ShapeDtypeStruct((1, PAD), f32)],
+        out_shape=[pltpu.VMEM((PAD, points), bf16)] * 2 + [jax.ShapeDtypeStruct((1, PAD), f32)],
         compiler_params=params(("arbitrary",), 16),
         name="crps_far",
-    )(*own, *others, *partial, area, before)
-
-
-def backward_kernel(variables, who, d_0, d_1, w_out_t, s_0, s_1, h_0, h_1, at, loss, contrib, heads, dpre):
-    quarter = 2 * pl.program_id(0) + who[0]
+    )(*map(parked, own), *others, *map(parked, partial), area, before)
+
+
+def backward_kernel(who, d_0, d_1, w_out, s_0, s_1, h_0, h_1, at, loss, contrib, heads, dpre):
     nodes = at.shape[0] - DEEP
+    variables = w_out.shape[0]
     shape = (PAD, WIDE)
     row = lax.broadcasted_iota(jnp.int32, shape, 0)
-    spot = lax.broadcasted_iota(jnp.int32, shape, 1) + quarter * WIDE
+    spot = lax.broadcasted_iota(jnp.int32, shape, 1) + (2 * pl.program_id(0) + who[0]) * WIDE
     total = jnp.where((row == variables + 1) & (spot == who[1]), jnp.sum(loss[...]), 0.0)
+    turned = w_out[...].T
     for m, (d, slope, hid) in enumerate(((d_0, s_0, h_0), (d_1, s_1, h_1))):
         for g in range(d.shape[1] // WIDE):
             cut = slice(g * WIDE, (g + 1) * WIDE)
-            dpre[m, :, cut] = (dot(w_out_t[...], d[:, cut]) * slope[:, cut].astype(f32)).astype(bf16)
+            dpre[m, :, cut] = (dot(turned, d[:variables, cut]) * slope[:, cut].astype(f32)).astype(bf16)
         total = total + dot(d[...], hid[...], 1, 1)
         part = dot(at[: nodes + EDGE], dpre[m], 1, 1)
         contrib[m * nodes : (m + 1) * nodes, :] = part[:nodes].astype(bf16)
@@ -273,8 +284,8 @@
             heads[i, j] = total[i * 8 : (i + 1) * 8, j * 128 : (j + 1) * 128]
 
 
-def backward(who, variables, dpred, w_out_t, slope, hid, at, loss):
-    width, points = hid[0].shape
+def backward(who, dpred, w_out, slope, hid, at, loss):
+    width, points = slope[0].shape
     nodes = at.shape[0] - DEEP
     count = width // WIDE // 2
 
@@ -282,9 +293,9 @@
         return pl.BlockSpec(a.shape, lambda y, w: (0,) * a.ndim)
 
     rows = pl.BlockSpec((WIDE, points), lambda y, w: (2 * y + w[0], 0))
-    narrow = pl.BlockSpec((WIDE, PAD), lambda y, w: (2 * y + w[0], 0))
-    return pl.pallas_call(
-        lambda *refs: backward_kernel(variables, *refs),
+    narrow = pl.BlockSpec((w_out.shape[0], WIDE), lambda y, w: (0, 2 * y + w[0]))
+    return pl.pallas_call(
+        backward_kernel,
         grid_spec=pltpu.PrefetchScalarGridSpec(
             num_scalar_prefetch=1,
             grid=(count,),
@@ -296,52 +307,74 @@
             scratch_shapes=[pltpu.VMEM((2, WIDE, points), bf16)],
         ),
         out_shape=[
-            jax.ShapeDtypeStruct((count, 2 * nodes, WIDE), bf16),
-            jax.ShapeDtypeStruct((count, PAD // 8, WIDE // 128, 8, 128), f32),
+            pltpu.VMEM((count, 2 * nodes, WIDE), bf16),
+            pltpu.VMEM((count, PAD // 8, WIDE // 128, 8, 128), f32),
         ],
         compiler_params=params(("arbitrary",), 28),
         name="backward",
-    )(who, *dpred, w_out_t, *slope, *hid, at, loss)
-
-
-def outer_kernel(lat_own, lat_other, c_own, c_other, out):
+    )(who, *map(parked, dpred), parked(w_out), *map(parked, slope), *map(parked, hid), parked(at), loss)
+
+
+def outer_kernel(lat_own, lat_other, c_own, c_other, h_own, h_other, out):
+    regions, rows, _ = out.shape[1:]
+    share = rows - 8
     for y in range(c_own.shape[0]):
-        out[y] = (dot(lat_own[...], c_own[y]) + dot(lat_other[...], c_other[y])).astype(bf16)
-
-
-def outer(lat_own, lat_other, c_own, c_other):
+        part = (dot(lat_own[...], c_own[y]) + dot(lat_other[...], c_other[y])).astype(bf16)
+        for r in range(regions):
+            out[y, r, :share] = part[r * share : (r + 1) * share]
+            piece = (h_own[y, r] + h_other[y, r]).astype(bf16)
+            out[y, r, share:] = jnp.concatenate([piece, jnp.zeros_like(piece)], axis=1)
+
+
+def outer(lat_own, lat_other, c_own, c_other, h_own, h_other, regions):
     inputs, nodes = lat_own.shape
     halves, _, quarter = c_own.shape
+    share = inputs // regions
+    here = WIDE // share
     lat = pl.BlockSpec((WIDE, nodes), lambda i: (i, 0))
+    piece = pl.BlockSpec((halves, here, 8, 128), lambda i: (0, i, 0, 0))
     return pl.pallas_call(
         outer_kernel,
         grid=(inputs // WIDE,),
-        in_specs=[lat, lat, whole(c_own), whole(c_own)],
-        out_specs=pl.BlockSpec((halves, WIDE, quarter), lambda i: (0, i, 0)),
-        out_shape=jax.ShapeDtypeStruct((halves, inputs, quarter), bf16),
+        in_specs=[lat, lat, whole(c_own), whole(c_own), piece, piece],
+        out_specs=pl.BlockSpec((halves, here, share + 8, quarter), lambda i: (0, i, 0, 0)),
+        out_shape=pltpu.VMEM((halves, regions, share + 8, quarter), bf16),
         compiler_params=params(("arbitrary",), 16),
         name="outer",
-    )(lat_own, lat_other, c_own, c_other)
-
-
-def finish_kernel(pieces, out):
+    )(parked(lat_own), lat_other, parked(c_own), c_other, parked(h_own), h_other)
+
+
+def finish_kernel(where, pieces, grad_out, grad_bias, loss):
+    variables, _ = grad_out.shape
     per_row = WIDE // 128
-    down = PAD // 8
     for at in range(pieces.shape[0]):
-        core, z, x, yhi, ylo = at // 64, at // 16 % 4, at // 4 % 4, at // 2 % 2, at % 2
-        piece = (((ylo * 2 + core) * 4 + z) * 2 + yhi) * 4 + x
-        quarter, i, j = piece // (down * per_row), piece // per_row % down, piece % per_row
-        left = quarter * WIDE + j * 128
-        out[i * 8 : (i + 1) * 8, left : left + 128] = pieces[at]
-
-
-def finish(pieces, width):
+        ylo, core, place = at // 64, at // 32 % 2, at % 32
+        i, j = place // per_row, place % per_row
+        left, top = (2 * ylo + core) * WIDE + j * 128, i * 8
+        rows = max(0, min(8, variables - top))
+        if rows:
+            grad_out[top : top + rows, left : left + 128] = pieces[at, :rows]
+        line = variables - top
+        if 0 <= line < 7:
+            grad_bias[:, left : left + 128] = pieces[at, line : line + 1]
+            if left == 0:
+                values = pieces[at, line + 1 : line + 2]
+                spot = lax.broadcasted_iota(jnp.int32, values.shape, 1)
+                loss[...] = jnp.sum(jnp.where(spot == where[0], values, 0.0), axis=1, keepdims=True)
+
+
+def finish(where, pieces, variables, width):
     return pl.pallas_call(
         finish_kernel,
-        out_shape=jax.ShapeDtypeStruct((PAD, width), f32),
+        in_specs=[pl.BlockSpec(memory_space=pltpu.SMEM), pl.BlockSpec(memory_space=pltpu.VMEM)],
+        out_shape=[
+            jax.ShapeDtypeStruct((variables, width), f32),
+            jax.ShapeDtypeStruct((1, width), f32),
+            jax.ShapeDtypeStruct((1, 1), f32),
+        ],
         compiler_params=pltpu.CompilerParams(vmem_limit_bytes=8 << 20),
         name="finish",
-    )(pieces)
+    )(where, pieces)
 
 
 def local(latent, w_node, bias, w_out, edge_src, edge_weight, target, area):
@@ -357,25 +390,16 @@
 
     mine = [latent[m] for m in range(members)]
 
-    def halo(block):
-        before = lax.ppermute(block, REGION, ahead)
-        return before, lax.ppermute(block, REGION, behind)
-
-    low, high = [None] * members, [None] * members
-    low[0], high[0] = halo(mine[0])
+    low, high = [], []
+    for m in range(members):
+        low.append(lax.ppermute(mine[m], REGION, ahead))
+        high.append(lax.ppermute(mine[m], REGION, behind))
     at = prep(edge_src.T, edge_weight.T, 3 * nodes)
-    parts, rest = [], bias
-    for _ in range(SPLIT):
-        parts.append(rest.astype(bf16))
-        rest = rest - parts[-1].astype(f32)
-    bias_cols = jnp.pad(jnp.stack(parts, axis=1), ((0, 0), (0, DEEP - SPLIT)))
-    low[0], high[0], second = lax.optimization_barrier((low[0], high[0], mine[1]))
-    low[1], high[1] = halo(second)
-    w_out_t = jnp.pad(w_out, ((0, PAD - variables), (0, 0))).T
+    bias_row = bias[None, :]
 
     hid, pre, err, near, far, beside = [], [], [], [], [], []
     for m in range(members):
-        h, s, e = forward(low[m], mine[m], high[m], w_node, at, bias_cols, w_out, target)
+        h, s, e = forward(low[m], mine[m], high[m], w_node, at, bias_row, w_out, target)
         hid.append(h)
         pre.append(s)
         err.append(e)
@@ -393,49 +417,30 @@
     p_0, p_1, loss = crps_near(err, near + [far[0], beside[0]], area_row, count)
     d_0, d_1, loss = crps_far(err, [far[1], beside[1]], (p_0, p_1), area_row, loss, count)
 
+    spot = where[None].astype(jnp.int32)
+    every = lax.axis_size(EVERY)
+
     def back(side):
         who = jnp.stack([side, where]).astype(jnp.int32)
-        return backward(who, variables, (d_0, d_1), w_out_t, slope, hid, at, loss)
+        return backward(who, (d_0, d_1), w_out, slope, hid, at, loss)
 
     given, heads_given = back(1 - core)
     taken = lax.ppermute(given, "core", swap)
+    heads_taken = lax.ppermute(heads_given, "core", swap)
     kept, heads_kept = back(core)
-
-    every = lax.axis_size(EVERY)
-    even = core == 0
-    heads = jnp.stack(
-        [jnp.where(even, heads_kept, heads_given), jnp.where(even, heads_given, heads_kept)], axis=1
+    tiles = (2, regions, 8, 128)
+    part = outer(lat_t, lat_t_other, kept, taken, heads_kept.reshape(tiles), heads_taken.reshape(tiles), regions)
+    chips = lax.axis_size(CHIPS)
+    share = width // regions
+    shares = lax.all_to_all(part.reshape(chips, share + 8, width // 4), CHIPS, split_axis=0, concat_axis=0, tiled=True)
+    summed = shares.astype(f32).sum(axis=0)
+    table = lax.all_to_all(
+        jnp.broadcast_to(summed[share:, :128], (every, 8, 128)), EVERY, split_axis=0, concat_axis=0, tiled=True
     )
-    pieces = lax.all_to_all(heads.reshape(every, 8, 128), EVERY, split_axis=0, concat_axis=0, tiled=True)
-    part = outer(lat_t, lat_t_other, kept, taken)
-    chips = lax.axis_size(CHIPS)
-    shares = lax.all_to_all(
-        part.reshape(chips, width // regions, width // 4), CHIPS, split_axis=0, concat_axis=0, tiled=True
-    )
-    spread = pieces.sum(axis=0)[None]
-    ring = [(0, 3), (3, 0), (1, 2), (2, 1)]
-    pair = [(0, 1), (1, 0), (2, 3), (3, 2)]
-    x, z = lax.axis_index("x"), lax.axis_index("z")
-    steps = (
-        ("ylo", swap, lax.axis_index("ylo")),
-        (("ylo", "yhi"), ring, lax.axis_index("yhi")),
-        ("x", pair, x % 2),
-        ("x", ring, x // 2),
-        ("z", pair, z % 2),
-        ("z", ring, z // 2),
-        ("core", swap, core),
-    )
-    for axis, moves, place in steps:
-        other = lax.ppermute(spread, axis, moves)
-        spread = jnp.where(
-            place == 0, jnp.concatenate([spread, other]), jnp.concatenate([other, spread])
-        )
-    own = shares.astype(f32).sum(axis=0)
-    grad_node = lax.all_gather(own, MEMBER, axis=1, tiled=True)
-    full = finish(spread, width)
-    grad_out = full[:variables]
-    grad_bias = full[variables]
-    loss_here = lax.dynamic_slice(full, (variables + 1, where), (1, 1)).reshape(1)
+    grad_node = lax.all_gather(summed[:share], MEMBER, axis=1, tiled=True)
+    grad_out, grad_bias, loss_here = finish(spot, table, variables, width)
+    grad_bias = grad_bias.reshape(width)
+    loss_here = loss_here.reshape(1)
     return grad_node, grad_out, grad_bias, loss_here
 
 

time: 154 us -> 136 us (0.88)
  blocking collectives: 22.8 us -> 33.1 us
  waiting for transfers between devices: 22.6 us -> 12.3 us
  starting transfers between devices: 39.1 us -> 29.5 us
  local copies, waits for them, and re-layouts: 11.6 us -> 6.48 us
  Pallas kernels: 54.3 us -> 51.9 us
    ppermute x11 -> x5, waiting for transfers between devices: 21.8 us -> 0.01 us  [the longest x2 0.01 us: local(): high.append(lax.ppermute(mine[m], REGION, behind))]
    ppermute x11 -> x5, starting transfers between devices: 28.9 us -> 17.1 us  [the longest x2 14.6 us: local(): high.append(lax.ppermute(mine[m], REGION, behind))]
    all_to_all x1, blocking collectives: 17.2 us -> 25.3 us  [local(): lax.all_to_all(part.reshape(chips, share + 8, width // 4), CHIPS, split_a...]
    ppermute x2, waiting for transfers between devices: 0.01 us -> 6.16 us  [local(): over = lax.ppermute((e * 0.125).astype(f16), 'ylo', swap)]
    all_to_all x1, waiting for transfers between devices: 0.01 us -> 6.14 us  [local(): lax.all_to_all(jnp.broadcast_to(summed[share:, :128], (every, 8, 128)), E...]
    unnamed x14 -> x15, local copies, waits for them, and re-layouts: 6.48 us -> 3.78 us
    pallas_call x1, Pallas kernels: 4.87 us -> 2.45 us  [outer(): pl.pallas_call(outer_kernel, grid=(inputs // WIDE,), in_specs=[lat, lat,...]
    all_gather x1, blocking collectives: 5.62 us -> 7.72 us  [local(): grad_node = lax.all_gather(summed[:share], MEMBER, axis=1, tiled=True)]
  transfers between devices with their start and end apart: 20 -> 14, of which waited for: 7 -> 2; matrix products, arithmetic and copies ran while one was open for 4% -> 0% of each run, Pallas kernels for 35% -> 36%
where the time goes in v4:
time: 136 us; the launch traced here: 135 us
  Pallas kernels  51.9 us (38%)
  blocking collectives  33.1 us (24%)
  starting transfers between devices  29.5 us (22%)
  waiting for transfers between devices  12.3 us (9%)
  local copies, waits for them, and re-layouts  6.48 us (5%)
    all_to_all x1, blocking collectives, local(): lax.all_to_all(part.reshape(chips, share + 8, width // 4), CHIPS, split_a...  25.3 us
    pallas_call x2, Pallas kernels, forward(): pl.pallas_call(forward_kernel, grid=(points // wide,), in_specs=[whole(lo...  20.4 us
    ppermute x2, starting transfers between devices, local(): high.append(lax.ppermute(mine[m], REGION, behind))  14.6 us
    pallas_call x2, Pallas kernels, backward(): pl.pallas_call(backward_kernel, grid_spec=pltpu.PrefetchScalarGridSpec(nu...  10.1 us
    pallas_call x1, Pallas kernels, slopes(): pl.pallas_call(slope_kernel, grid=(width // 128,), in_specs=[rows, rows],...  8.51 us
    all_gather x1, blocking collectives, local(): grad_node = lax.all_gather(summed[:share], MEMBER, axis=1, tiled=True)  7.72 us
    all_to_all x1, starting transfers between devices, local(): lax.all_to_all(jnp.broadcast_to(summed[share:, :128], (every, 8, 128)), E...  6.61 us
    ppermute x2, waiting for transfers between devices, local(): over = lax.ppermute((e * 0.125).astype(f16), 'ylo', swap)  6.16 us
  transfers between devices with their start and end apart: 14, of which 2 were waited for; matrix products, arithmetic and copies ran while one was open for 0% of the time, Pallas kernels for 36%

profile of v4, /device:TPU:1, one launch (start us, length us, event | category | flops | bytes accessed | tf_op | source)
XLA Modules:
  0.0 135.0 jit_solution(6308292668450863641)
XLA Ops:
  0.6 0.0 copy-start.6
  0.6 0.0 copy-start.2
  0.7 0.0 copy-start.1
  0.7 1.9 %slice_bitcast_fusion = (bf16[128,1024]{1,0:T(8,128)(2,1)S(1)}, bf16[128,1024]{1,0:T(8,128)(2,1)}) fusion(bf16[2,128,1024]{2,1,0:T(8,128)(2,1)} %param.8), kind=kLoop, calls=%fused_computation.7 | loop fusion | bytes 1048576 | tf_op jit(solution)/shard_map/squeeze | solution.py:391
  2.5 2.0 %collective-permute-start = (bf16[128,1024]{1,0:T(8,128)(2,1)}, bf16[128,1024]{1,0:T(8,128)(2,1)}, u32[]{:S(2)}, u32[]{:S(2)}) collective-permute-start(bf16[128,1024]{1,0:T(8,128)(2,1)} %get-tuple-element.28.refs_1_.own), channel_id=1, source_target_pairs={{0,1},{1,2},{2,3},{3,4},{4,5},{5,6},{6,7},{7,8},{8,9},{9,10},{10,1... | collective-permute-start | bytes 786440 | tf_op jit(solution)/shard_map/ppermute | solution.py:395
  4.5 7.4 %collective-permute-start.3 = (bf16[128,1024]{1,0:T(8,128)(2,1)}, bf16[128,1024]{1,0:T(8,128)(2,1)}, u32[]{:S(2)}, u32[]{:S(2)}) collective-permute-start(bf16[128,1024]{1,0:T(8,128)(2,1)} %get-tuple-element.28.refs_1_.own), channel_id=1, source_target_pairs={{1,0},{2,1},{3,2},{4,3},{5,4},{6,5},{7,6},{8,7},{9,8},{10,9},{11,1... | collective-permute-start | bytes 786440 | tf_op jit(solution)/shard_map/ppermute | solution.py:396
  11.9 0.0 collective-permute-start.1
  11.9 7.2 %collective-permute-start.2 = (bf16[128,1024]{1,0:T(8,128)(2,1)S(1)}, bf16[128,1024]{1,0:T(8,128)(2,1)}, u32[]{:S(2)}, u32[]{:S(2)}) collective-permute-start(bf16[128,1024]{1,0:T(8,128)(2,1)S(1)} %get-tuple-element.50.own.refs_4_), channel_id=1, source_target_pairs={{1,0},{2,1},{3,2},{4,3},{5,4},{6,5},{7,6},{8,7},{9,8},{10,9},{11,1... | collective-permute-start | bytes 786440 | tf_op jit(solution)/shard_map/ppermute | solution.py:396
  19.1 0.8 copy-done.3
  19.9 0.8 copy-done.4
  20.6 1.2 prep.1.at
  21.9 0.1 pad_add_fusion
  21.9 0.0 collective-permute-done.refs_0_.low
  21.9 0.0 collective-permute-done.3.refs_2_.high
  21.9 0.0 copy-done.6
  21.9 0.0 copy-done.2
  21.9 0.0 copy-done.1
  22.0 0.0 copy-start
  22.0 1.6 %copy-done = bf16[1024,1024]{1,0:T(8,128)(2,1)S(1)} copy-done((bf16[1024,1024]{1,0:T(8,128)(2,1)S(1)}, bf16[1024,1024]{1,0:T(8,128)(2,1)}, u32[]{:S(2)}) %copy-start) | copy-done | bytes 2097176
  23.6 10.2 %forward.3 = (bf16[1024,2048]{1,0:T(8,128)(2,1)S(1)}, bf16[1024,2048]{1,0:T(8,128)(2,1)S(1)}, f32[100,2048]{1,0:T(8,128)S(1)}) custom-call(bf16[128,1024]{1,0:T(8,128)(2,1)} %collective-permute-done.refs_0_.low, bf16[128,1024]{1,0:T(8,128)(2,1)} %get-tuple-element.28.refs_1_.own, bf16[128,1024]{1,0:T(8,128)(2,1)} %collective-permute-done.3.refs_2_.high, ...), custom_call_target="tpu_custom_call" | custom-call | tf_op jit(solution)/shard_map/forward/pallas_call | solution.py:127
  33.8 1.6 %collective-permute-start.7 = (f32[100,2048]{1,0:T(8,128)S(1)}, f32[100,2048]{1,0:T(8,128)S(1)}, u32[]{:S(2)}, u32[]{:S(2)}) collective-permute-start(f32[100,2048]{1,0:T(8,128)S(1)} %get-tuple-element.29.refs_0_), channel_id=1, source_target_pairs={{0,32},{32,0},{1,33},{33,1},{2,34},{34,2},{3,35},{35,3},{4,36},{36... | collective-permute-start | bytes 2457608 | tf_op jit(solution)/shard_map/ppermute | solution.py:407
  35.4 0.1 multiply_convert_fusion
  35.5 0.0 collective-permute-done.1.low.refs_3_
  35.5 0.0 collective-permute-done.2.high.refs_5_
  35.5 10.2 %forward.2 = (bf16[1024,2048]{1,0:T(8,128)(2,1)S(1)}, bf16[1024,2048]{1,0:T(8,128)(2,1)S(1)}, f32[100,2048]{1,0:T(8,128)S(1)}) custom-call(bf16[128,1024]{1,0:T(8,128)(2,1)} %collective-permute-done.1.low.refs_3_, bf16[128,1024]{1,0:T(8,128)(2,1)S(1)} %get-tuple-element.50.own.refs_4_, bf16[128,1024]{1,0:T(8,128)(2,1)} %collective-permute-done.2.high.refs_5_, ...), custom_call_target="tpu_custom_call" | custom-call | tf_op jit(solution)/shard_map/forward/pallas_call | solution.py:127
  45.7 0.1 collective-permute-start.8
  45.8 0.5 collective-permute-start.9
  46.2 0.1 multiply_convert_fusion.1
  46.3 1.1 collective-permute-start.5
  47.5 2.5 %turn.1.lat_own = bf16[1024,768]{1,0:T(8,128)(2,1)S(1)} custom-call(bf16[128,1024]{1,0:T(8,128)(2,1)} %collective-permute-done.refs_0_.low, bf16[128,1024]{1,0:T(8,128)(2,1)} %get-tuple-element.28.refs_1_.own, bf16[128,1024]{1,0:T(8,128)(2,1)} %collective-permute-done.3.refs_2_.high, bf16[128,1024]{1,0:T(8,128)(2,1)} %collective-permute-done.1.low.refs_3_, ...), custom_call_target="tpu_custom_call" | custom-call | tf_op jit(solution)/shard_map/turn/pallas_call | solution.py:78
  50.0 1.1 collective-permute-start.4
  51.0 8.5 %slope.1 = (bf16[1024,2048]{1,0:T(8,128)(2,1)S(1)}, bf16[1024,2048]{1,0:T(8,128)(2,1)S(1)}) custom-call(bf16[1024,2048]{1,0:T(8,128)(2,1)S(1)} %get-tuple-element.36.pre_0, bf16[1024,2048]{1,0:T(8,128)(2,1)S(1)} %get-tuple-element.37.pre_1), custom_call_target="tpu_custom_call" | custom-call | tf_op jit(solution)/shard_map/slope/pallas_call | solution.py:156
  59.6 0.0 copy-start.5
  59.6 0.0 collective-permute-done.9
  59.6 0.1 collective-permute-start.10
  59.7 0.1 convert_multiply_fusion.1.refs_4_
  59.8 6.2 %collective-permute-done.5 = f16[100,2048]{1,0:T(8,128)(2,1)S(1)} collective-permute-done((f16[100,2048]{1,0:T(8,128)(2,1)S(1)}, f16[100,2048]{1,0:T(8,128)(2,1)S(1)}, u32[]{:S(2)}, u32[]{:S(2)}) %collective-permute-start.5) | collective-permute-done | bytes 409632 | tf_op jit(solution)/shard_map/ppermute | solution.py:406
  65.9 1.3 collective-permute-start.6
  67.2 0.1 convert_multiply_fusion.3.refs_2_
  67.3 0.0 collective-permute-done.10
  67.3 0.1 convert_multiply_fusion.refs_5_
  67.4 0.0 collective-permute-done.7.refs_2_
  67.4 0.0 collective-permute-done.8.refs_3_
  67.4 0.0 copy-done.5
  67.4 4.0 %crps_near.1 = (f32[100,2048]{1,0:T(8,128)S(1)}, f32[100,2048]{1,0:T(8,128)S(1)}, f32[1,128]{1,0:T(1,128)S(1)}) custom-call(f32[100,2048]{1,0:T(8,128)S(1)} %get-tuple-element.29.refs_0_, f32[100,2048]{1,0:T(8,128)S(1)} %get-tuple-element.30.refs_1_, f32[100,2048]{1,0:T(8,128)S(1)} %collective-permute-done.7.refs_2_, ...), custom_call_target="tpu_custom_call" | custom-call | tf_op jit(solution)/shard_map/crps_near/pallas_call | solution.py:237
  71.4 0.0 collective-permute-done.6
  71.4 0.1 convert_multiply_fusion.2.refs_3_
  71.5 1.9 %crps_far.1 = (bf16[128,2048]{1,0:T(8,128)(2,1)S(1)}, bf16[128,2048]{1,0:T(8,128)(2,1)S(1)}, f32[1,128]{1,0:T(1,128)S(1)}) custom-call(f32[100,2048]{1,0:T(8,128)S(1)} %get-tuple-element.29.refs_0_, f32[100,2048]{1,0:T(8,128)S(1)} %get-tuple-element.30.refs_1_, f32[100,2048]{1,0:T(8,128)S(1)} %convert_multiply_fusion.3.refs_2_, ...), custom_call_target="tpu_custom_call" | custom-call | tf_op jit(solution)/shard_map/crps_far/pallas_call | solution.py:255
  73.5 5.1 %backward.3 = (bf16[2,768,256]{2,1,0:T(8,128)(2,1)S(1)}, f32[2,16,2,8,128]{4,3,2,1,0:T(8,128)S(1)}) custom-call(s32[2]{0:T(128)S(1)} %get-tuple-element.53.who, bf16[128,2048]{1,0:T(8,128)(2,1)S(1)} %get-tuple-element.34.d_0, bf16[128,2048]{1,0:T(8,128)(2,1)S(1)} %get-tuple-element.35.d_1, bf16[100,1024]{1,0:T(8,128)(2,1)S(1)} %copy-done.2, ...), custom_call_target="tpu_custom_call" | custom-call | tf_op jit(solution)/shard_map/backward/pallas_call | solution.py:297
  78.5 0.1 collective-permute-start.11
  78.6 0.5 collective-permute-start.12
  79.1 5.1 %backward.2 = (bf16[2,768,256]{2,1,0:T(8,128)(2,1)S(1)}, f32[2,16,2,8,128]{4,3,2,1,0:T(8,128)S(1)}) custom-call(s32[2]{0:T(128)S(1)} %get-tuple-element.52.who, bf16[128,2048]{1,0:T(8,128)(2,1)S(1)} %get-tuple-element.34.d_0, bf16[128,2048]{1,0:T(8,128)(2,1)S(1)} %get-tuple-element.35.d_1, bf16[100,1024]{1,0:T(8,128)(2,1)S(1)} %copy-done.2, ...), custom_call_target="tpu_custom_call" | custom-call | tf_op jit(solution)/shard_map/backward/pallas_call | solution.py:297
  84.2 0.0 collective-permute-done.12
  84.2 0.0 collective-permute-done.4.lat_other
  84.2 0.0 collective-permute-done.11.c_other
  84.2 2.5 %outer.1 = bf16[2,32,40,256]{3,2,1,0:T(8,128)(2,1)S(1)} custom-call(bf16[1024,768]{1,0:T(8,128)(2,1)S(1)} %turn.1.lat_own, bf16[1024,768]{1,0:T(8,128)(2,1)S(1)} %collective-permute-done.4.lat_other, bf16[2,768,256]{2,1,0:T(8,128)(2,1)S(1)} %get-tuple-element.43.c_own, bf16[2,768,256]{2,1,0:T(8,128)(2,1)S(1)} %collective-permute-done.11.c_other, ...), custom_call_target="tpu_custom_call" | custom-call | tf_op jit(solution)/shard_map/outer/pallas_call | solution.py:336
  86.7 25.3 %all_to_all.10 = bf16[64,40,256]{2,1,0:T(8,128)(2,1)S(1)} all-to-all(bf16[64,40,256]{2,1,0:T(8,128)(2,1)S(1)} %bitcast.16), channel_id=1, replica_groups=mesh['ylo'=2,'core'=2,'z'=4,'yhi'=2,'x'=4] {'ylo','z','yhi','x'}, dimensions={0} | all-to-all | bytes 2621440 | tf_op jit(solution)/shard_map/all_to_all | solution.py:435
  112.0 0.2 convert_reduce_fusion
  112.2 0.8 broadcast_in_dim.12
  113.1 6.6 %all-to-all-start.1 = ((f32[128,8,128]{2,1,0:T(8,128)}), f32[128,8,128]{2,1,0:T(8,128)S(1)}, u32[]{:S(2)}, u32[]{:S(2)}) async-start(f32[128,8,128]{2,1,0:T(8,128)} %broadcast_in_dim.12), calls=%async_computation.1 | async-start | bytes 1048576 | tf_op jit(solution)/shard_map/all_to_all | solution.py:437
  119.7 7.7 %all_gather.3 = f32[32,1024]{1,0:T(8,128)S(1)} all-gather(f32[32,256]{1,0:T(8,128)S(1)} %slice.16), channel_id=1, replica_groups=mesh['ylo'=2,'core'=2,'z'=4,'yhi'=2,'x'=4] {'ylo','core'}, dimensions={1}, use_global_device_ids=true | all-gather | bytes 163840 | tf_op jit(solution)/shard_map/all_gather | solution.py:440
  127.4 6.1 %all-to-all-done.1.pieces = f32[128,8,128]{2,1,0:T(8,128)S(1)} async-done(((f32[128,8,128]{2,1,0:T(8,128)}), f32[128,8,128]{2,1,0:T(8,128)S(1)}, u32[]{:S(2)}, u32[]{:S(2)}) %all-to-all-start.1) | async-done | bytes 524320 | tf_op jit(solution)/shard_map/all_to_all | solution.py:437
  133.6 0.8 finish.1
  134.4 0.7 copy.13
  (4 shorter events, 0.0 us)
Async XLA Ops:
  0.6 21.3 %copy-start.6 = (f32[1024]{0:T(1024)S(1)}, f32[1024]{0:T(1024)}, u32[]{:S(2)}) copy-start(f32[1024]{0:T(1024)} %param.10) | copy-start | bytes 12292
  0.6 21.3 %copy-start.2 = (bf16[100,1024]{1,0:T(8,128)(2,1)S(1)}, bf16[100,1024]{1,0:T(8,128)(2,1)}, u32[]{:S(2)}) copy-start(bf16[100,1024]{1,0:T(8,128)(2,1)} %w_out.7) | copy-start | bytes 614404
  0.7 21.3 %copy-start.1 = (f32[100,2048]{1,0:T(8,128)S(1)}, f32[100,2048]{1,0:T(8,128)}, u32[]{:S(2)}) copy-start(f32[100,2048]{1,0:T(8,128)} %target.3) | copy-start | bytes 2457604
  2.5 19.4 %collective-permute-start = (bf16[128,1024]{1,0:T(8,128)(2,1)}, bf16[128,1024]{1,0:T(8,128)(2,1)}, u32[]{:S(2)}, u32[]{:S(2)}) collective-permute-start(bf16[128,1024]{1,0:T(8,128)(2,1)} %get-tuple-element.28.refs_1_.own), channel_id=1, source_target_pairs={{0,1},{1,2},{2,3},{3,4},{4,5},{5,6},{6,7},{7,8},{8,9},{9,10},{10,1... | collective-permute-start | bytes 786440 | tf_op jit(solution)/shard_map/ppermute | solution.py:395
  4.5 17.4 %collective-permute-start.3 = (bf16[128,1024]{1,0:T(8,128)(2,1)}, bf16[128,1024]{1,0:T(8,128)(2,1)}, u32[]{:S(2)}, u32[]{:S(2)}) collective-permute-start(bf16[128,1024]{1,0:T(8,128)(2,1)} %get-tuple-element.28.refs_1_.own), channel_id=1, source_target_pairs={{1,0},{2,1},{3,2},{4,3},{5,4},{6,5},{7,6},{8,7},{9,8},{10,9},{11,1... | collective-permute-start | bytes 786440 | tf_op jit(solution)/shard_map/ppermute | solution.py:396
  11.9 23.6 %collective-permute-start.1 = (bf16[128,1024]{1,0:T(8,128)(2,1)S(1)}, bf16[128,1024]{1,0:T(8,128)(2,1)}, u32[]{:S(2)}, u32[]{:S(2)}) collective-permute-start(bf16[128,1024]{1,0:T(8,128)(2,1)S(1)} %get-tuple-element.50.own.refs_4_), channel_id=1, source_target_pairs={{0,1},{1,2},{2,3},{3,4},{4,5},{5,6},{6,7},{7,8},{8,9},{9,10},{10,1... | collective-permute-start | bytes 786440 | tf_op jit(solution)/shard_map/ppermute | solution.py:395
  11.9 23.6 %collective-permute-start.2 = (bf16[128,1024]{1,0:T(8,128)(2,1)S(1)}, bf16[128,1024]{1,0:T(8,128)(2,1)}, u32[]{:S(2)}, u32[]{:S(2)}) collective-permute-start(bf16[128,1024]{1,0:T(8,128)(2,1)S(1)} %get-tuple-element.50.own.refs_4_), channel_id=1, source_target_pairs={{1,0},{2,1},{3,2},{4,3},{5,4},{6,5},{7,6},{8,7},{9,8},{10,9},{11,1... | collective-permute-start | bytes 786440 | tf_op jit(solution)/shard_map/ppermute | solution.py:396
  19.1 0.8 copy-start.3
  19.9 0.8 copy-start.4
  22.0 1.6 %copy-start = (bf16[1024,1024]{1,0:T(8,128)(2,1)S(1)}, bf16[1024,1024]{1,0:T(8,128)(2,1)}, u32[]{:S(2)}) copy-start(bf16[1024,1024]{1,0:T(8,128)(2,1)} %w_node.3) | copy-start | bytes 6291460
  33.8 33.6 %collective-permute-start.7 = (f32[100,2048]{1,0:T(8,128)S(1)}, f32[100,2048]{1,0:T(8,128)S(1)}, u32[]{:S(2)}, u32[]{:S(2)}) collective-permute-start(f32[100,2048]{1,0:T(8,128)S(1)} %get-tuple-element.29.refs_0_), channel_id=1, source_target_pairs={{0,32},{32,0},{1,33},{33,1},{2,34},{34,2},{3,35},{35,3},{4,36},{36... | collective-permute-start | bytes 2457608 | tf_op jit(solution)/shard_map/ppermute | solution.py:407
  45.7 21.7 %collective-permute-start.8 = (f32[100,2048]{1,0:T(8,128)S(1)}, f32[100,2048]{1,0:T(8,128)S(1)}, u32[]{:S(2)}, u32[]{:S(2)}) collective-permute-start(f32[100,2048]{1,0:T(8,128)S(1)} %get-tuple-element.30.refs_1_), channel_id=1, source_target_pairs={{0,32},{32,0},{1,33},{33,1},{2,34},{34,2},{3,35},{35,3},{4,36},{36... | collective-permute-start | bytes 2457608 | tf_op jit(solution)/shard_map/ppermute | solution.py:407
  45.8 13.8 %collective-permute-start.9 = (f16[100,2048]{1,0:T(8,128)(2,1)S(1)}, f16[100,2048]{1,0:T(8,128)(2,1)S(1)}, u32[]{:S(2)}, u32[]{:S(2)}) collective-permute-start(f16[100,2048]{1,0:T(8,128)(2,1)S(1)} %multiply_convert_fusion), channel_id=1, source_target_pairs={{0,64},{64,0},{1,65},{65,1},{2,66},{66,2},{3,67},{67,3},{4,68},{68... | collective-permute-start | bytes 1228808 | tf_op jit(solution)/shard_map/ppermute | solution.py:406
  46.3 19.6 %collective-permute-start.5 = (f16[100,2048]{1,0:T(8,128)(2,1)S(1)}, f16[100,2048]{1,0:T(8,128)(2,1)S(1)}, u32[]{:S(2)}, u32[]{:S(2)}) collective-permute-start(f16[100,2048]{1,0:T(8,128)(2,1)S(1)} %multiply_convert_fusion.1), channel_id=1, source_target_pairs={{0,64},{64,0},{1,65},{65,1},{2,66},{66,2},{3,67},{67,3},{4,68},{68... | collective-permute-start | bytes 1228808 | tf_op jit(solution)/shard_map/ppermute | solution.py:406
  50.0 34.2 %collective-permute-start.4 = (bf16[1024,768]{1,0:T(8,128)(2,1)S(1)}, bf16[1024,768]{1,0:T(8,128)(2,1)S(1)}, u32[]{:S(2)}, u32[]{:S(2)}) collective-permute-start(bf16[1024,768]{1,0:T(8,128)(2,1)S(1)} %turn.1.lat_own), channel_id=1, source_target_pairs={{0,32},{32,0},{1,33},{33,1},{2,34},{34,2},{3,35},{35,3},{4,36},{36... | collective-permute-start | bytes 4718600 | tf_op jit(solution)/shard_map/ppermute | solution.py:413
  59.6 7.9 %copy-start.5 = (f32[2048]{0:T(1024)S(1)}, f32[2048]{0:T(1024)}, u32[]{:S(2)}) copy-start(f32[2048]{0:T(1024)} %param.15) | copy-start | bytes 24580
  59.6 7.7 %collective-permute-start.10 = (f16[100,2048]{1,0:T(8,128)(2,1)S(1)}, f16[100,2048]{1,0:T(8,128)(2,1)S(1)}, u32[]{:S(2)}, u32[]{:S(2)}) collective-permute-start(f16[100,2048]{1,0:T(8,128)(2,1)S(1)} %collective-permute-done.9), channel_id=1, source_target_pairs={{0,32},{32,0},{1,33},{33,1},{2,34},{34,2},{3,35},{35,3},{4,36},{36... | collective-permute-start | bytes 1228808 | tf_op jit(solution)/shard_map/ppermute | solution.py:409
  65.9 5.5 %collective-permute-start.6 = (f16[100,2048]{1,0:T(8,128)(2,1)S(1)}, f16[100,2048]{1,0:T(8,128)(2,1)S(1)}, u32[]{:S(2)}, u32[]{:S(2)}) collective-permute-start(f16[100,2048]{1,0:T(8,128)(2,1)S(1)} %collective-permute-done.5), channel_id=1, source_target_pairs={{0,32},{32,0},{1,33},{33,1},{2,34},{34,2},{3,35},{35,3},{4,36},{36... | collective-permute-start | bytes 1228808 | tf_op jit(solution)/shard_map/ppermute | solution.py:409
  78.5 5.7 %collective-permute-start.11 = (bf16[2,768,256]{2,1,0:T(8,128)(2,1)S(1)}, bf16[2,768,256]{2,1,0:T(8,128)(2,1)S(1)}, u32[]{:S(2)}, u32[]{:S(2)}) collective-permute-start(bf16[2,768,256]{2,1,0:T(8,128)(2,1)S(1)} %get-tuple-element.44), channel_id=1, source_target_pairs={{0,32},{32,0},{1,33},{33,1},{2,34},{34,2},{3,35},{35,3},{4,36},{36... | collective-permute-start | bytes 2359304 | tf_op jit(solution)/shard_map/ppermute | solution.py:428
  78.6 5.6 %collective-permute-start.12 = (f32[2,16,2,8,128]{4,3,2,1,0:T(8,128)S(1)}, f32[2,16,2,8,128]{4,3,2,1,0:T(8,128)S(1)}, u32[]{:S(2)}, u32[]{:S(2)}) collective-permute-start(f32[2,16,2,8,128]{4,3,2,1,0:T(8,128)S(1)} %get-tuple-element.46), channel_id=1, source_target_pairs={{0,32},{32,0},{1,33},{33,1},{2,34},{34,2},{3,35},{35,3},{4,36},{36... | collective-permute-start | bytes 786440 | tf_op jit(solution)/shard_map/ppermute | solution.py:429
  113.1 20.5 %all-to-all-start.1 = ((f32[128,8,128]{2,1,0:T(8,128)}), f32[128,8,128]{2,1,0:T(8,128)S(1)}, u32[]{:S(2)}, u32[]{:S(2)}) async-start(f32[128,8,128]{2,1,0:T(8,128)} %broadcast_in_dim.12), calls=%async_computation.1 | async-start | bytes 1048576 | tf_op jit(solution)/shard_map/all_to_all | solution.py:437

commit v5 on v4

--- a/solution.py
+++ b/solution.py
@@ -89,79 +89,68 @@
 def forward_kernel(low, own, high, w_node, at, bias, w_out, target, hid, pre, err, proj):
     nodes = 3 * low.shape[0]
 
-    @pl.when(pl.program_id(0) == 0)
-    def _():
-        stacked = jnp.concatenate([low[...], own[...], high[...]], axis=0)
-        proj[:, :nodes] = dot(stacked, w_node[...]).astype(bf16).T
-        row = lax.broadcasted_iota(jnp.int32, (DEEP, proj.shape[0]), 0)
-        block, rest = jnp.zeros(row.shape, f32), bias[...]
-        for k in range(SPLIT):
-            part = rest.astype(bf16).astype(f32)
-            block = jnp.where(row == k, part, block)
-            rest = rest - part
-        proj[:, nodes:] = block.T.astype(bf16)
-
-    for g in range(target.shape[1] // WIDE):
-        cols = slice(g * WIDE, (g + 1) * WIDE)
-        total = -target[:, cols]
-        for r in range(proj.shape[0] // WIDE):
-            rows = slice(r * WIDE, (r + 1) * WIDE)
+    stacked = jnp.concatenate([low[...], own[...], high[...]], axis=0)
+    proj[:, :nodes] = dot(stacked, w_node[...]).astype(bf16).T
+    row = lax.broadcasted_iota(jnp.int32, (DEEP, proj.shape[0]), 0)
+    block, rest = jnp.zeros(row.shape, f32), bias[...]
+    for k in range(SPLIT):
+        part = rest.astype(bf16).astype(f32)
+        block = jnp.where(row == k, part, block)
+        rest = rest - part
+    proj[:, nodes:] = block.T.astype(bf16)
+
+    for g in range(target.shape[1] // 256):
+        cols = slice(g * 256, (g + 1) * 256)
+        for r in range(proj.shape[0] // 256):
+            rows = slice(r * 256, (r + 1) * 256)
             x = dot(proj[rows, :], at[:, cols])
             pre[rows, cols] = x.astype(bf16)
             u = 0.5 + 0.5 * jnp.tanh(x * (C0 + (C0 * C1) * (x * x)))
-            hb = (x * u).astype(bf16)
-            hid[rows, cols] = hb
-            total = total + dot(w_out[:, rows], hb)
-        err[:, cols] = total
+            hid[rows, cols] = (x * u).astype(bf16)
+    err[...] = dot(w_out[...], hid[...]) - target[...]
 
 
 def forward(low, own, high, w_node, at, bias, w_out, target):
     width = w_node.shape[1]
     points = at.shape[1]
     variables = target.shape[0]
-    wide = 512
-
-    def cut(rows):
-        return pl.BlockSpec((rows, wide), lambda i: (0, i))
-
+    vm = pl.BlockSpec(memory_space=pltpu.VMEM)
     return pl.pallas_call(
         forward_kernel,
-        grid=(points // wide,),
-        in_specs=[whole(low), whole(own), whole(high), whole(w_node), cut(at.shape[0]), whole(bias), whole(w_out), cut(variables)],
-        out_specs=[cut(width), cut(width), cut(variables)],
+        in_specs=[vm] * 8,
+        out_specs=[vm] * 3,
         out_shape=[
             pltpu.VMEM((width, points), bf16),
             pltpu.VMEM((width, points), bf16),
             pltpu.VMEM((variables, points), f32),
         ],
         scratch_shapes=[pltpu.VMEM((width, at.shape[0]), bf16)],
-        compiler_params=params(("arbitrary",), 24),
+        compiler_params=pltpu.CompilerParams(vmem_limit_bytes=24 << 20),
         name="forward",
-    )(low, own, high, parked(w_node), parked(at), bias, parked(w_out), parked(target))
-
-
-def slope_kernel(pre_0, pre_1, out_0, out_1):
-    for pre, out in ((pre_0, out_0), (pre_1, out_1)):
-        for g in range(pre.shape[1] // WIDE):
-            cols = slice(g * WIDE, (g + 1) * WIDE)
-            x = pre[:, cols].astype(f32)
-            sq = x * x
-            u = 0.5 + 0.5 * jnp.tanh(x * (C0 + (C0 * C1) * sq))
-            out[:, cols] = (u + (x * u) * (1.0 - u) * (2.0 * C0 + (6.0 * C0 * C1) * sq)).astype(bf16)
+    )(parked(low), parked(own), parked(high), parked(w_node), parked(at), parked(bias), parked(w_out), parked(target))
+
+
+def slope_kernel(pre, out):
+    for g in range(pre.shape[1] // WIDE):
+        cols = slice(g * WIDE, (g + 1) * WIDE)
+        x = pre[:, cols].astype(f32)
+        sq = x * x
+        u = 0.5 + 0.5 * jnp.tanh(x * (C0 + (C0 * C1) * sq))
+        out[:, cols] = (u + (x * u) * (1.0 - u) * (2.0 * C0 + (6.0 * C0 * C1) * sq)).astype(bf16)
 
 
 def slopes(pre):
-    width, points = pre[0].shape
+    width, points = pre.shape
     rows = pl.BlockSpec((128, points), lambda i: (i, 0))
     return pl.pallas_call(
         slope_kernel,
         grid=(width // 128,),
-        in_specs=[rows, rows],
-        out_specs=[rows, rows],
-        out_shape=[pltpu.VMEM((width, points), bf16)] * 2,
+        in_specs=[rows],
+        out_specs=rows,
+        out_shape=pltpu.VMEM((width, points), bf16),
         compiler_params=params(("arbitrary",), 8),
         name="slope",
-    )(*map(parked, pre))
+    )(parked(pre))
 
 
 def apart(d):
@@ -268,67 +257,59 @@
     variables = w_out.shape[0]
     shape = (PAD, WIDE)
     row = lax.broadcasted_iota(jnp.int32, shape, 0)
-    spot = lax.broadcasted_iota(jnp.int32, shape, 1) + (2 * pl.program_id(0) + who[0]) * WIDE
-    total = jnp.where((row == variables + 1) & (spot == who[1]), jnp.sum(loss[...]), 0.0)
-    turned = w_out[...].T
-    for m, (d, slope, hid) in enumerate(((d_0, s_0, h_0), (d_1, s_1, h_1))):
-        for g in range(d.shape[1] // WIDE):
-            cut = slice(g * WIDE, (g + 1) * WIDE)
-            dpre[m, :, cut] = (dot(turned, d[:variables, cut]) * slope[:, cut].astype(f32)).astype(bf16)
-        total = total + dot(d[...], hid[...], 1, 1)
-        part = dot(at[: nodes + EDGE], dpre[m], 1, 1)
-        contrib[m * nodes : (m + 1) * nodes, :] = part[:nodes].astype(bf16)
-        total = total + jnp.where(row == variables, part[nodes : nodes + 1], 0.0)
-    for i in range(PAD // 8):
-        for j in range(WIDE // 128):
-            heads[i, j] = total[i * 8 : (i + 1) * 8, j * 128 : (j + 1) * 128]
+    lane = lax.broadcasted_iota(jnp.int32, shape, 1)
+    for y in range(contrib.shape[0]):
+        first = pl.multiple_of((2 * y + who[0]) * WIDE, WIDE)
+        rows = pl.ds(first, WIDE)
+        total = jnp.where((row == variables + 1) & (lane + first == who[1]), jnp.sum(loss[...]), 0.0)
+        turned = w_out[:, rows].T
+        for m, (d, slope, hid) in enumerate(((d_0, s_0, h_0), (d_1, s_1, h_1))):
+            for g in range(d.shape[1] // WIDE):
+                cut = slice(g * WIDE, (g + 1) * WIDE)
+                part = dot(turned, d[:variables, cut]) * slope[rows, cut].astype(f32)
+                dpre[y, m, :, cut] = part.astype(bf16)
+            total = total + dot(d[...], hid[rows, :], 1, 1)
+            part = dot(at[: nodes + EDGE], dpre[y, m], 1, 1)
+            contrib[y, m * nodes : (m + 1) * nodes, :] = part[:nodes].astype(bf16)
+            total = total + jnp.where(row == variables, part[nodes : nodes + 1], 0.0)
+        for i in range(PAD // 8):
+            for j in range(WIDE // 128):
+                heads[y, i, j] = total[i * 8 : (i + 1) * 8, j * 128 : (j + 1) * 128]
 
 
 def backward(who, dpred, w_out, slope, hid, at, loss):
     width, points = slope[0].shape
     nodes = at.shape[0] - DEEP
     count = width // WIDE // 2
-
-    def fixed(a):
-        return pl.BlockSpec(a.shape, lambda y, w: (0,) * a.ndim)
-
-    rows = pl.BlockSpec((WIDE, points), lambda y, w: (2 * y + w[0], 0))
-    narrow = pl.BlockSpec((w_out.shape[0], WIDE), lambda y, w: (0, 2 * y + w[0]))
+    vm = pl.BlockSpec(memory_space=pltpu.VMEM)
     return pl.pallas_call(
         backward_kernel,
-        grid_spec=pltpu.PrefetchScalarGridSpec(
-            num_scalar_prefetch=1,
-            grid=(count,),
-            in_specs=[fixed(dpred[0]), fixed(dpred[1]), narrow, rows, rows, rows, rows, fixed(at), fixed(loss)],
-            out_specs=[
-                pl.BlockSpec((None, 2 * nodes, WIDE), lambda y, w: (y, 0, 0)),
-                pl.BlockSpec((None, PAD // 8, WIDE // 128, 8, 128), lambda y, w: (y, 0, 0, 0, 0)),
-            ],
-            scratch_shapes=[pltpu.VMEM((2, WIDE, points), bf16)],
-        ),
+        in_specs=[pl.BlockSpec(memory_space=pltpu.SMEM)] + [vm] * 9,
+        out_specs=[vm, vm],
         out_shape=[
             pltpu.VMEM((count, 2 * nodes, WIDE), bf16),
             pltpu.VMEM((count, PAD // 8, WIDE // 128, 8, 128), f32),
         ],
-        compiler_params=params(("arbitrary",), 28),
+        scratch_shapes=[pltpu.VMEM((count, 2, WIDE, points), bf16)],
+        compiler_params=pltpu.CompilerParams(vmem_limit_bytes=24 << 20),
         name="backward",
-    )(who, *map(parked, dpred), parked(w_out), *map(parked, slope), *map(parked, hid), parked(at), loss)
+    )(who, *map(parked, dpred), parked(w_out), *map(parked, slope), *map(parked, hid), parked(at), parked(loss))
 
 
 def outer_kernel(lat_own, lat_other, c_own, c_other, h_own, h_other, out):
-    regions, rows, _ = out.shape[1:]
-    share = rows - 8
+    regions = out.shape[1]
+    share = lat_own.shape[0] // regions
     for y in range(c_own.shape[0]):
         part = (dot(lat_own[...], c_own[y]) + dot(lat_other[...], c_other[y])).astype(bf16)
         for r in range(regions):
-            out[y, r, :share] = part[r * share : (r + 1) * share]
-            piece = (h_own[y, r] + h_other[y, r]).astype(bf16)
-            out[y, r, share:] = jnp.concatenate([piece, jnp.zeros_like(piece)], axis=1)
+            for j in range(part.shape[1] // 128):
+                out[y, r, j * share : (j + 1) * share] = part[r * share : (r + 1) * share, j * 128 : (j + 1) * 128]
+            out[y, r, 2 * share :] = (h_own[y, r] + h_other[y, r]).astype(bf16)
 
 
 def outer(lat_own, lat_other, c_own, c_other, h_own, h_other, regions):
     inputs, nodes = lat_own.shape
-    halves, _, quarter = c_own.shape
+    halves, _, _ = c_own.shape
     share = inputs // regions
     here = WIDE // share
     lat = pl.BlockSpec((WIDE, nodes), lambda i: (i, 0))
@@ -337,8 +318,8 @@
         outer_kernel,
         grid=(inputs // WIDE,),
         in_specs=[lat, lat, whole(c_own), whole(c_own), piece, piece],
-        out_specs=pl.BlockSpec((halves, here, share + 8, quarter), lambda i: (0, i, 0, 0)),
-        out_shape=pltpu.VMEM((halves, regions, share + 8, quarter), bf16),
+        out_specs=pl.BlockSpec((halves, here, 2 * share + 8, 128), lambda i: (0, i, 0, 0)),
+        out_shape=pltpu.VMEM((halves, regions, 2 * share + 8, 128), bf16),
         compiler_params=params(("arbitrary",), 16),
         name="outer",
     )(parked(lat_own), lat_other, parked(c_own), c_other, parked(h_own), h_other)
@@ -397,11 +378,11 @@
     at = prep(edge_src.T, edge_weight.T, 3 * nodes)
     bias_row = bias[None, :]
 
-    hid, pre, err, near, far, beside = [], [], [], [], [], []
+    hid, slope, err, near, far, beside = [], [], [], [], [], []
     for m in range(members):
         h, s, e = forward(low[m], mine[m], high[m], w_node, at, bias_row, w_out, target)
         hid.append(h)
-        pre.append(s)
+        slope.append(slopes(s))
         err.append(e)
         over = lax.ppermute((e * 0.125).astype(f16), "ylo", swap)
         near.append(lax.ppermute(e, "core", swap))
@@ -411,7 +392,6 @@
     first, err[1] = lax.optimization_barrier((mine[0], err[1]))
     lat_t = turn((low[0], first, high[0], low[1], mine[1], high[1]))
     lat_t_other = lax.ppermute(lat_t, "core", swap)
-    slope = slopes(pre)
 
     area_row = area[None, :]
     p_0, p_1, loss = crps_near(err, near + [far[0], beside[0]], area_row, count)
@@ -432,12 +412,15 @@
     part = outer(lat_t, lat_t_other, kept, taken, heads_kept.reshape(tiles), heads_taken.reshape(tiles), regions)
     chips = lax.axis_size(CHIPS)
     share = width // regions
-    shares = lax.all_to_all(part.reshape(chips, share + 8, width // 4), CHIPS, split_axis=0, concat_axis=0, tiled=True)
+    shares = lax.all_to_all(
+        part.reshape(chips, 2 * share + 8, 128), CHIPS, split_axis=0, concat_axis=0, tiled=True
+    )
     summed = shares.astype(f32).sum(axis=0)
     table = lax.all_to_all(
-        jnp.broadcast_to(summed[share:, :128], (every, 8, 128)), EVERY, split_axis=0, concat_axis=0, tiled=True
+        jnp.broadcast_to(summed[2 * share :], (every, 8, 128)), EVERY, split_axis=0, concat_axis=0, tiled=True
     )
-    grad_node = lax.all_gather(summed[:share], MEMBER, axis=1, tiled=True)
+    own = jnp.concatenate([summed[:share], summed[share : 2 * share]], axis=1)
+    grad_node = lax.all_gather(own, MEMBER, axis=1, tiled=True)
     grad_out, grad_bias, loss_here = finish(spot, table, variables, width)
     grad_bias = grad_bias.reshape(width)
     loss_here = loss_here.reshape(1)

time: 136 us -> 125 us (0.919)
  Pallas kernels: 51.9 us -> 43.2 us
  blocking collectives: 33.1 us -> 31.7 us
    pallas_call x5 -> x6, Pallas kernels: 39 us -> 30.3 us  [the longest x2 12.2 us: forward(): pl.pallas_call(forward_kernel, in_specs=[vm] * 8, out_specs=[vm] * 3, out...]
  transfers between devices with their start and end apart: 14 -> 14, of which waited for: 2 -> 2; matrix products, arithmetic and copies ran while one was open for 0% -> 0% of each run, Pallas kernels for 36% -> 32%
where the time goes in v5:
time: 125 us
  Pallas kernels  43.2 us (35%)
  blocking collectives  31.7 us (25%)
  starting transfers between devices  29.7 us (24%)
  waiting for transfers between devices  12 us (10%)
  local copies, waits for them, and re-layouts  6.49 us (5%)
    all_to_all x1, blocking collectives, local(): lax.all_to_all(part.reshape(chips, 2 * share + 8, 128), CHIPS, split_axis...  24 us
    ppermute x2, starting transfers between devices, local(): high.append(lax.ppermute(mine[m], REGION, behind))  14.6 us
    pallas_call x2, Pallas kernels, forward(): pl.pallas_call(forward_kernel, in_specs=[vm] * 8, out_specs=[vm] * 3, out...  12.2 us
    pallas_call x2, Pallas kernels, backward(): pl.pallas_call(backward_kernel, in_specs=[pl.BlockSpec(memory_space=pltpu...  9.49 us
    pallas_call x2, Pallas kernels, slopes(): pl.pallas_call(slope_kernel, grid=(width // 128,), in_specs=[rows], out_s...  8.66 us
    all_gather x1, blocking collectives, local(): grad_node = lax.all_gather(own, MEMBER, axis=1, tiled=True)  7.71 us
    all_to_all x1, starting transfers between devices, local(): lax.all_to_all(jnp.broadcast_to(summed[2 * share:], (every, 8, 128)), EVE...  6.56 us
    all_to_all x1, waiting for transfers between devices, local(): lax.all_to_all(jnp.broadcast_to(summed[2 * share:], (every, 8, 128)), EVE...  6.14 us
  transfers between devices with their start and end apart: 14, of which 2 were waited for; matrix products, arithmetic and copies ran while one was open for 0% of the time, Pallas kernels for 32%

profile of v5, /device:TPU:1, one launch (start us, length us, event | category | flops | bytes accessed | tf_op | source)
XLA Modules:
  0.0 124.7 jit_solution(16300405469422385066)
XLA Ops:
  0.6 0.0 copy-start.6
  0.6 0.0 copy-start.2
  0.7 0.0 copy-start.1
  0.7 1.9 %slice_bitcast_fusion = (bf16[128,1024]{1,0:T(8,128)(2,1)S(1)}, bf16[128,1024]{1,0:T(8,128)(2,1)}) fusion(bf16[2,128,1024]{2,1,0:T(8,128)(2,1)} %param.8), kind=kLoop, calls=%fused_computation.7 | loop fusion | bytes 1048576 | tf_op jit(solution)/shard_map/squeeze | solution.py:372
  2.5 2.0 %collective-permute-start = (bf16[128,1024]{1,0:T(8,128)(2,1)}, bf16[128,1024]{1,0:T(8,128)(2,1)}, u32[]{:S(2)}, u32[]{:S(2)}) collective-permute-start(bf16[128,1024]{1,0:T(8,128)(2,1)} %get-tuple-element.26.refs_1_.own), channel_id=1, source_target_pairs={{0,1},{1,2},{2,3},{3,4},{4,5},{5,6},{6,7},{7,8},{8,9},{9,10},{10,1... | collective-permute-start | bytes 786440 | tf_op jit(solution)/shard_map/ppermute | solution.py:376
  4.5 7.4 %collective-permute-start.3 = (bf16[128,1024]{1,0:T(8,128)(2,1)}, bf16[128,1024]{1,0:T(8,128)(2,1)}, u32[]{:S(2)}, u32[]{:S(2)}) collective-permute-start(bf16[128,1024]{1,0:T(8,128)(2,1)} %get-tuple-element.26.refs_1_.own), channel_id=1, source_target_pairs={{1,0},{2,1},{3,2},{4,3},{5,4},{6,5},{7,6},{8,7},{9,8},{10,9},{11,1... | collective-permute-start | bytes 786440 | tf_op jit(solution)/shard_map/ppermute | solution.py:377
  11.9 0.0 collective-permute-start.1
  11.9 7.2 %collective-permute-start.2 = (bf16[128,1024]{1,0:T(8,128)(2,1)S(1)}, bf16[128,1024]{1,0:T(8,128)(2,1)}, u32[]{:S(2)}, u32[]{:S(2)}) collective-permute-start(bf16[128,1024]{1,0:T(8,128)(2,1)S(1)} %get-tuple-element.46.own.refs_4_), channel_id=1, source_target_pairs={{1,0},{2,1},{3,2},{4,3},{5,4},{6,5},{7,6},{8,7},{9,8},{10,9},{11,1... | collective-permute-start | bytes 786440 | tf_op jit(solution)/shard_map/ppermute | solution.py:377
  19.1 0.8 copy-done.3
  19.9 0.8 copy-done.4
  20.6 1.2 prep.1.at
  21.9 0.1 pad_add_fusion
  21.9 0.0 collective-permute-done.refs_0_.low
  21.9 0.0 collective-permute-done.3.refs_2_.high
  21.9 0.0 copy-done.2
  21.9 0.0 copy-done.1
  22.0 0.0 copy-start
  22.0 1.6 %copy-done = bf16[1024,1024]{1,0:T(8,128)(2,1)S(1)} copy-done((bf16[1024,1024]{1,0:T(8,128)(2,1)S(1)}, bf16[1024,1024]{1,0:T(8,128)(2,1)}, u32[]{:S(2)}) %copy-start) | copy-done | bytes 2097176
  23.6 6.1 %forward.3 = (bf16[1024,2048]{1,0:T(8,128)(2,1)S(1)}, bf16[1024,2048]{1,0:T(8,128)(2,1)S(1)}, f32[100,2048]{1,0:T(8,128)S(1)}) custom-call(bf16[128,1024]{1,0:T(8,128)(2,1)} %collective-permute-done.refs_0_.low, bf16[128,1024]{1,0:T(8,128)(2,1)} %get-tuple-element.26.refs_1_.own, bf16[128,1024]{1,0:T(8,128)(2,1)} %collective-permute-done.3.refs_2_.high, ...), custom_call_target="tpu_custom_call" | custom-call | tf_op jit(solution)/shard_map/forward/pallas_call | solution.py:118
  29.7 1.6 %collective-permute-start.7 = (f32[100,2048]{1,0:T(8,128)S(1)}, f32[100,2048]{1,0:T(8,128)S(1)}, u32[]{:S(2)}, u32[]{:S(2)}) collective-permute-start(f32[100,2048]{1,0:T(8,128)S(1)} %get-tuple-element.27.refs_0_), channel_id=1, source_target_pairs={{0,32},{32,0},{1,33},{33,1},{2,34},{34,2},{3,35},{35,3},{4,36},{36... | collective-permute-start | bytes 2457608 | tf_op jit(solution)/shard_map/ppermute | solution.py:388
  31.3 0.1 multiply_convert_fusion
  31.4 0.0 collective-permute-done.1.low.refs_3_
  31.4 0.0 collective-permute-done.2.high.refs_5_
  31.4 6.0 %forward.2 = (bf16[1024,2048]{1,0:T(8,128)(2,1)S(1)}, bf16[1024,2048]{1,0:T(8,128)(2,1)S(1)}, f32[100,2048]{1,0:T(8,128)S(1)}) custom-call(bf16[128,1024]{1,0:T(8,128)(2,1)} %collective-permute-done.1.low.refs_3_, bf16[128,1024]{1,0:T(8,128)(2,1)S(1)} %get-tuple-element.46.own.refs_4_, bf16[128,1024]{1,0:T(8,128)(2,1)} %collective-permute-done.2.high.refs_5_, ...), custom_call_target="tpu_custom_call" | custom-call | tf_op jit(solution)/shard_map/forward/pallas_call | solution.py:118
  37.4 0.1 collective-permute-start.8
  37.5 0.5 collective-permute-start.9
  38.0 0.1 multiply_convert_fusion.1
  38.1 1.3 %collective-permute-start.5 = (f16[100,2048]{1,0:T(8,128)(2,1)S(1)}, f16[100,2048]{1,0:T(8,128)(2,1)S(1)}, u32[]{:S(2)}, u32[]{:S(2)}) collective-permute-start(f16[100,2048]{1,0:T(8,128)(2,1)S(1)} %multiply_convert_fusion.1), channel_id=1, source_target_pairs={{0,64},{64,0},{1,65},{65,1},{2,66},{66,2},{3,67},{67,3},{4,68},{68... | collective-permute-start | bytes 1228808 | tf_op jit(solution)/shard_map/ppermute | solution.py:387
  39.4 4.3 %slope.2.s_0 = bf16[1024,2048]{1,0:T(8,128)(2,1)S(1)} custom-call(bf16[1024,2048]{1,0:T(8,128)(2,1)S(1)} %get-tuple-element.34.pre), custom_call_target="tpu_custom_call" | custom-call | tf_op jit(solution)/shard_map/slope/pallas_call | solution.py:145
  43.7 4.3 %slope.3.s_1 = bf16[1024,2048]{1,0:T(8,128)(2,1)S(1)} custom-call(bf16[1024,2048]{1,0:T(8,128)(2,1)S(1)} %get-tuple-element.35.pre), custom_call_target="tpu_custom_call" | custom-call | tf_op jit(solution)/shard_map/slope/pallas_call | solution.py:145
  48.1 2.5 %turn.1.lat_own = bf16[1024,768]{1,0:T(8,128)(2,1)S(1)} custom-call(bf16[128,1024]{1,0:T(8,128)(2,1)} %collective-permute-done.refs_0_.low, bf16[128,1024]{1,0:T(8,128)(2,1)} %get-tuple-element.26.refs_1_.own, bf16[128,1024]{1,0:T(8,128)(2,1)} %collective-permute-done.3.refs_2_.high, bf16[128,1024]{1,0:T(8,128)(2,1)} %collective-permute-done.1.low.refs_3_, ...), custom_call_target="tpu_custom_call" | custom-call | tf_op jit(solution)/shard_map/turn/pallas_call | solution.py:78
  50.6 0.0 copy-start.5
  50.6 1.1 collective-permute-start.4
  51.7 0.0 collective-permute-done.9
  51.7 0.1 collective-permute-start.10
  51.8 0.1 convert_multiply_fusion.1.refs_4_
  51.9 5.8 %collective-permute-done.5 = f16[100,2048]{1,0:T(8,128)(2,1)S(1)} collective-permute-done((f16[100,2048]{1,0:T(8,128)(2,1)S(1)}, f16[100,2048]{1,0:T(8,128)(2,1)S(1)}, u32[]{:S(2)}, u32[]{:S(2)}) %collective-permute-start.5) | collective-permute-done | bytes 409632 | tf_op jit(solution)/shard_map/ppermute | solution.py:387
  57.7 1.3 %collective-permute-start.6 = (f16[100,2048]{1,0:T(8,128)(2,1)S(1)}, f16[100,2048]{1,0:T(8,128)(2,1)S(1)}, u32[]{:S(2)}, u32[]{:S(2)}) collective-permute-start(f16[100,2048]{1,0:T(8,128)(2,1)S(1)} %collective-permute-done.5), channel_id=1, source_target_pairs={{0,32},{32,0},{1,33},{33,1},{2,34},{34,2},{3,35},{35,3},{4,36},{36... | collective-permute-start | bytes 1228808 | tf_op jit(solution)/shard_map/ppermute | solution.py:390
  59.0 0.1 convert_multiply_fusion.3.refs_2_
  59.1 0.0 collective-permute-done.10
  59.1 0.1 convert_multiply_fusion.refs_5_
  59.2 0.0 collective-permute-done.7.refs_2_
  59.2 0.0 collective-permute-done.8.refs_3_
  59.2 0.0 copy-done.5
  59.2 4.0 %crps_near.1 = (f32[100,2048]{1,0:T(8,128)S(1)}, f32[100,2048]{1,0:T(8,128)S(1)}, f32[1,128]{1,0:T(1,128)S(1)}) custom-call(f32[100,2048]{1,0:T(8,128)S(1)} %get-tuple-element.27.refs_0_, f32[100,2048]{1,0:T(8,128)S(1)} %get-tuple-element.28.refs_1_, f32[100,2048]{1,0:T(8,128)S(1)} %collective-permute-done.7.refs_2_, ...), custom_call_target="tpu_custom_call" | custom-call | tf_op jit(solution)/shard_map/crps_near/pallas_call | solution.py:226
  63.2 0.0 collective-permute-done.6
  63.2 0.1 convert_multiply_fusion.2.refs_3_
  63.3 1.9 %crps_far.1 = (bf16[128,2048]{1,0:T(8,128)(2,1)S(1)}, bf16[128,2048]{1,0:T(8,128)(2,1)S(1)}, f32[1,128]{1,0:T(1,128)S(1)}) custom-call(f32[100,2048]{1,0:T(8,128)S(1)} %get-tuple-element.27.refs_0_, f32[100,2048]{1,0:T(8,128)S(1)} %get-tuple-element.28.refs_1_, f32[100,2048]{1,0:T(8,128)S(1)} %convert_multiply_fusion.3.refs_2_, ...), custom_call_target="tpu_custom_call" | custom-call | tf_op jit(solution)/shard_map/crps_far/pallas_call | solution.py:244
  65.2 4.7 %backward.3 = (bf16[2,768,256]{2,1,0:T(8,128)(2,1)S(1)}, f32[2,16,2,8,128]{4,3,2,1,0:T(8,128)S(1)}) custom-call(s32[2]{0:T(128)S(1)} %get-tuple-element.51.who, bf16[128,2048]{1,0:T(8,128)(2,1)S(1)} %get-tuple-element.32.d_0, bf16[128,2048]{1,0:T(8,128)(2,1)S(1)} %get-tuple-element.33.d_1, bf16[100,1024]{1,0:T(8,128)(2,1)S(1)} %copy-done.2, ...), custom_call_target="tpu_custom_call" | custom-call | tf_op jit(solution)/shard_map/backward/pallas_call | solution.py:285
  70.0 0.1 collective-permute-start.11
  70.1 0.5 collective-permute-start.12
  70.6 4.7 %backward.2 = (bf16[2,768,256]{2,1,0:T(8,128)(2,1)S(1)}, f32[2,16,2,8,128]{4,3,2,1,0:T(8,128)S(1)}) custom-call(s32[2]{0:T(128)S(1)} %get-tuple-element.50.who, bf16[128,2048]{1,0:T(8,128)(2,1)S(1)} %get-tuple-element.32.d_0, bf16[128,2048]{1,0:T(8,128)(2,1)S(1)} %get-tuple-element.33.d_1, bf16[100,1024]{1,0:T(8,128)(2,1)S(1)} %copy-done.2, ...), custom_call_target="tpu_custom_call" | custom-call | tf_op jit(solution)/shard_map/backward/pallas_call | solution.py:285
  75.3 0.0 collective-permute-done.12
  75.3 0.0 collective-permute-done.4.lat_other
  75.3 0.0 collective-permute-done.11.c_other
  75.3 2.5 %outer.1 = bf16[2,32,72,128]{3,2,1,0:T(8,128)(2,1)S(1)} custom-call(bf16[1024,768]{1,0:T(8,128)(2,1)S(1)} %turn.1.lat_own, bf16[1024,768]{1,0:T(8,128)(2,1)S(1)} %collective-permute-done.4.lat_other, bf16[2,768,256]{2,1,0:T(8,128)(2,1)S(1)} %get-tuple-element.39.c_own, bf16[2,768,256]{2,1,0:T(8,128)(2,1)S(1)} %collective-permute-done.11.c_other, ...), custom_call_target="tpu_custom_call" | custom-call | tf_op jit(solution)/shard_map/outer/pallas_call | solution.py:317
  77.8 24.0 %all_to_all.10 = bf16[64,72,128]{2,1,0:T(8,128)(2,1)S(1)} all-to-all(bf16[64,72,128]{2,1,0:T(8,128)(2,1)S(1)} %bitcast.16), channel_id=1, replica_groups=mesh['ylo'=2,'core'=2,'z'=4,'yhi'=2,'x'=4] {'ylo','z','yhi','x'}, dimensions={0} | all-to-all | bytes 2359296 | tf_op jit(solution)/shard_map/all_to_all | solution.py:415
  101.8 0.2 convert_reduce_fusion
  102.0 0.8 broadcast_in_dim.12
  102.9 6.6 %all-to-all-start.1 = ((f32[128,8,128]{2,1,0:T(8,128)}), f32[128,8,128]{2,1,0:T(8,128)S(1)}, u32[]{:S(2)}, u32[]{:S(2)}) async-start(f32[128,8,128]{2,1,0:T(8,128)} %broadcast_in_dim.12), calls=%async_computation.1 | async-start | bytes 1048576 | tf_op jit(solution)/shard_map/all_to_all | solution.py:419
  109.5 7.7 %all_gather.3 = f32[32,1024]{1,0:T(8,128)S(1)} all-gather(f32[32,256]{1,0:T(8,128)S(1)} %pad_maximum_fusion), channel_id=1, replica_groups=mesh['ylo'=2,'core'=2,'z'=4,'yhi'=2,'x'=4] {'ylo','core'}, dimensions={1}, use_global_device_ids=true | all-gather | bytes 163840 | tf_op jit(solution)/shard_map/all_gather | solution.py:423
  117.2 6.1 %all-to-all-done.1.pieces = f32[128,8,128]{2,1,0:T(8,128)S(1)} async-done(((f32[128,8,128]{2,1,0:T(8,128)}), f32[128,8,128]{2,1,0:T(8,128)S(1)}, u32[]{:S(2)}, u32[]{:S(2)}) %all-to-all-start.1) | async-done | bytes 524320 | tf_op jit(solution)/shard_map/all_to_all | solution.py:419
  123.3 0.8 finish.1
  124.1 0.7 copy.13
  (6 shorter events, 0.0 us)
Async XLA Ops:
  0.6 21.3 %copy-start.6 = (f32[1024]{0:T(1024)S(1)}, f32[1024]{0:T(1024)}, u32[]{:S(2)}) copy-start(f32[1024]{0:T(1024)} %param.10) | copy-start | bytes 12292
  0.6 21.3 %copy-start.2 = (bf16[100,1024]{1,0:T(8,128)(2,1)S(1)}, bf16[100,1024]{1,0:T(8,128)(2,1)}, u32[]{:S(2)}) copy-start(bf16[100,1024]{1,0:T(8,128)(2,1)} %w_out.7) | copy-start | bytes 614404
  0.7 21.3 %copy-start.1 = (f32[100,2048]{1,0:T(8,128)S(1)}, f32[100,2048]{1,0:T(8,128)}, u32[]{:S(2)}) copy-start(f32[100,2048]{1,0:T(8,128)} %target.3) | copy-start | bytes 2457604
  2.5 19.4 %collective-permute-start = (bf16[128,1024]{1,0:T(8,128)(2,1)}, bf16[128,1024]{1,0:T(8,128)(2,1)}, u32[]{:S(2)}, u32[]{:S(2)}) collective-permute-start(bf16[128,1024]{1,0:T(8,128)(2,1)} %get-tuple-element.26.refs_1_.own), channel_id=1, source_target_pairs={{0,1},{1,2},{2,3},{3,4},{4,5},{5,6},{6,7},{7,8},{8,9},{9,10},{10,1... | collective-permute-start | bytes 786440 | tf_op jit(solution)/shard_map/ppermute | solution.py:376
  4.5 17.4 %collective-permute-start.3 = (bf16[128,1024]{1,0:T(8,128)(2,1)}, bf16[128,1024]{1,0:T(8,128)(2,1)}, u32[]{:S(2)}, u32[]{:S(2)}) collective-permute-start(bf16[128,1024]{1,0:T(8,128)(2,1)} %get-tuple-element.26.refs_1_.own), channel_id=1, source_target_pairs={{1,0},{2,1},{3,2},{4,3},{5,4},{6,5},{7,6},{8,7},{9,8},{10,9},{11,1... | collective-permute-start | bytes 786440 | tf_op jit(solution)/shard_map/ppermute | solution.py:377
  11.9 19.5 %collective-permute-start.1 = (bf16[128,1024]{1,0:T(8,128)(2,1)S(1)}, bf16[128,1024]{1,0:T(8,128)(2,1)}, u32[]{:S(2)}, u32[]{:S(2)}) collective-permute-start(bf16[128,1024]{1,0:T(8,128)(2,1)S(1)} %get-tuple-element.46.own.refs_4_), channel_id=1, source_target_pairs={{0,1},{1,2},{2,3},{3,4},{4,5},{5,6},{6,7},{7,8},{8,9},{9,10},{10,1... | collective-permute-start | bytes 786440 | tf_op jit(solution)/shard_map/ppermute | solution.py:376
  11.9 19.5 %collective-permute-start.2 = (bf16[128,1024]{1,0:T(8,128)(2,1)S(1)}, bf16[128,1024]{1,0:T(8,128)(2,1)}, u32[]{:S(2)}, u32[]{:S(2)}) collective-permute-start(bf16[128,1024]{1,0:T(8,128)(2,1)S(1)} %get-tuple-element.46.own.refs_4_), channel_id=1, source_target_pairs={{1,0},{2,1},{3,2},{4,3},{5,4},{6,5},{7,6},{8,7},{9,8},{10,9},{11,1... | collective-permute-start | bytes 786440 | tf_op jit(solution)/shard_map/ppermute | solution.py:377
  19.1 0.8 copy-start.3
  19.9 0.8 copy-start.4
  22.0 1.6 %copy-start = (bf16[1024,1024]{1,0:T(8,128)(2,1)S(1)}, bf16[1024,1024]{1,0:T(8,128)(2,1)}, u32[]{:S(2)}) copy-start(bf16[1024,1024]{1,0:T(8,128)(2,1)} %w_node.3) | copy-start | bytes 6291460
  29.7 29.5 %collective-permute-start.7 = (f32[100,2048]{1,0:T(8,128)S(1)}, f32[100,2048]{1,0:T(8,128)S(1)}, u32[]{:S(2)}, u32[]{:S(2)}) collective-permute-start(f32[100,2048]{1,0:T(8,128)S(1)} %get-tuple-element.27.refs_0_), channel_id=1, source_target_pairs={{0,32},{32,0},{1,33},{33,1},{2,34},{34,2},{3,35},{35,3},{4,36},{36... | collective-permute-start | bytes 2457608 | tf_op jit(solution)/shard_map/ppermute | solution.py:388
  37.4 21.7 %collective-permute-start.8 = (f32[100,2048]{1,0:T(8,128)S(1)}, f32[100,2048]{1,0:T(8,128)S(1)}, u32[]{:S(2)}, u32[]{:S(2)}) collective-permute-start(f32[100,2048]{1,0:T(8,128)S(1)} %get-tuple-element.28.refs_1_), channel_id=1, source_target_pairs={{0,32},{32,0},{1,33},{33,1},{2,34},{34,2},{3,35},{35,3},{4,36},{36... | collective-permute-start | bytes 2457608 | tf_op jit(solution)/shard_map/ppermute | solution.py:388
  37.5 14.1 %collective-permute-start.9 = (f16[100,2048]{1,0:T(8,128)(2,1)S(1)}, f16[100,2048]{1,0:T(8,128)(2,1)S(1)}, u32[]{:S(2)}, u32[]{:S(2)}) collective-permute-start(f16[100,2048]{1,0:T(8,128)(2,1)S(1)} %multiply_convert_fusion), channel_id=1, source_target_pairs={{0,64},{64,0},{1,65},{65,1},{2,66},{66,2},{3,67},{67,3},{4,68},{68... | collective-permute-start | bytes 1228808 | tf_op jit(solution)/shard_map/ppermute | solution.py:387
  38.1 19.6 %collective-permute-start.5 = (f16[100,2048]{1,0:T(8,128)(2,1)S(1)}, f16[100,2048]{1,0:T(8,128)(2,1)S(1)}, u32[]{:S(2)}, u32[]{:S(2)}) collective-permute-start(f16[100,2048]{1,0:T(8,128)(2,1)S(1)} %multiply_convert_fusion.1), channel_id=1, source_target_pairs={{0,64},{64,0},{1,65},{65,1},{2,66},{66,2},{3,67},{67,3},{4,68},{68... | collective-permute-start | bytes 1228808 | tf_op jit(solution)/shard_map/ppermute | solution.py:387
  50.6 8.6 %copy-start.5 = (f32[2048]{0:T(1024)S(1)}, f32[2048]{0:T(1024)}, u32[]{:S(2)}) copy-start(f32[2048]{0:T(1024)} %param.15) | copy-start | bytes 24580
  50.6 24.7 %collective-permute-start.4 = (bf16[1024,768]{1,0:T(8,128)(2,1)S(1)}, bf16[1024,768]{1,0:T(8,128)(2,1)S(1)}, u32[]{:S(2)}, u32[]{:S(2)}) collective-permute-start(bf16[1024,768]{1,0:T(8,128)(2,1)S(1)} %turn.1.lat_own), channel_id=1, source_target_pairs={{0,32},{32,0},{1,33},{33,1},{2,34},{34,2},{3,35},{35,3},{4,36},{36... | collective-permute-start | bytes 4718600 | tf_op jit(solution)/shard_map/ppermute | solution.py:394
  51.7 7.4 %collective-permute-start.10 = (f16[100,2048]{1,0:T(8,128)(2,1)S(1)}, f16[100,2048]{1,0:T(8,128)(2,1)S(1)}, u32[]{:S(2)}, u32[]{:S(2)}) collective-permute-start(f16[100,2048]{1,0:T(8,128)(2,1)S(1)} %collective-permute-done.9), channel_id=1, source_target_pairs={{0,32},{32,0},{1,33},{33,1},{2,34},{34,2},{3,35},{35,3},{4,36},{36... | collective-permute-start | bytes 1228808 | tf_op jit(solution)/shard_map/ppermute | solution.py:390
  57.7 5.5 %collective-permute-start.6 = (f16[100,2048]{1,0:T(8,128)(2,1)S(1)}, f16[100,2048]{1,0:T(8,128)(2,1)S(1)}, u32[]{:S(2)}, u32[]{:S(2)}) collective-permute-start(f16[100,2048]{1,0:T(8,128)(2,1)S(1)} %collective-permute-done.5), channel_id=1, source_target_pairs={{0,32},{32,0},{1,33},{33,1},{2,34},{34,2},{3,35},{35,3},{4,36},{36... | collective-permute-start | bytes 1228808 | tf_op jit(solution)/shard_map/ppermute | solution.py:390
  70.0 5.4 %collective-permute-start.11 = (bf16[2,768,256]{2,1,0:T(8,128)(2,1)S(1)}, bf16[2,768,256]{2,1,0:T(8,128)(2,1)S(1)}, u32[]{:S(2)}, u32[]{:S(2)}) collective-permute-start(bf16[2,768,256]{2,1,0:T(8,128)(2,1)S(1)} %get-tuple-element.40), channel_id=1, source_target_pairs={{0,32},{32,0},{1,33},{33,1},{2,34},{34,2},{3,35},{35,3},{4,36},{36... | collective-permute-start | bytes 2359304 | tf_op jit(solution)/shard_map/ppermute | solution.py:408
  70.1 5.3 %collective-permute-start.12 = (f32[2,16,2,8,128]{4,3,2,1,0:T(8,128)S(1)}, f32[2,16,2,8,128]{4,3,2,1,0:T(8,128)S(1)}, u32[]{:S(2)}, u32[]{:S(2)}) collective-permute-start(f32[2,16,2,8,128]{4,3,2,1,0:T(8,128)S(1)} %get-tuple-element.42), channel_id=1, source_target_pairs={{0,32},{32,0},{1,33},{33,1},{2,34},{34,2},{3,35},{35,3},{4,36},{36... | collective-permute-start | bytes 786440 | tf_op jit(solution)/shard_map/ppermute | solution.py:409
  102.9 20.4 %all-to-all-start.1 = ((f32[128,8,128]{2,1,0:T(8,128)}), f32[128,8,128]{2,1,0:T(8,128)S(1)}, u32[]{:S(2)}, u32[]{:S(2)}) async-start(f32[128,8,128]{2,1,0:T(8,128)} %broadcast_in_dim.12), calls=%async_computation.1 | async-start | bytes 1048576 | tf_op jit(solution)/shard_map/all_to_all | solution.py:419

commit v6 on v5

--- a/solution.py
+++ b/solution.py
@@ -41,7 +41,8 @@
     return pl.BlockSpec(a.shape, lambda *i: (0,) * a.ndim)
 
 
-def prep_kernel(src, weight, at):
+def prep_kernel(src, weight, bias, *rest):
+    at, lift = rest[-2:]
     nodes, wide = at.shape[0] - DEEP, at.shape[1]
     place = lax.broadcasted_iota(jnp.int32, (nodes, wide), 0)
     total = jnp.zeros((nodes, wide), f32)
@@ -50,20 +51,32 @@
     at[:nodes, :] = total.astype(bf16)
     first = lax.broadcasted_iota(jnp.int32, (DEEP, wide), 0) < SPLIT
     at[nodes:, :] = jnp.where(first, 1.0, 0.0).astype(bf16)
-
-
-def prep(src, weight, nodes):
+    row = lax.broadcasted_iota(jnp.int32, lift.shape, 0)
+    block, rest = jnp.zeros(lift.shape, f32), bias[...]
+    for k in range(SPLIT):
+        part = rest.astype(bf16).astype(f32)
+        block = jnp.where(row == k, part, block)
+        rest = rest - part
+    lift[...] = block.astype(bf16)
+
+
+def prep(src, weight, bias, nodes, later):
     fan, points = src.shape
+    width = bias.shape[1]
+    steps = points // WIDE
     row = pl.BlockSpec((fan, WIDE), lambda i: (0, i))
     return pl.pallas_call(
         prep_kernel,
-        grid=(points // WIDE,),
-        in_specs=[row, row],
-        out_specs=pl.BlockSpec((nodes + DEEP, WIDE), lambda i: (0, i)),
-        out_shape=pltpu.VMEM((nodes + DEEP, points), bf16),
+        grid=(steps,),
+        in_specs=[row, row, pl.BlockSpec((1, width // steps), lambda i: (0, i))] + [pl.BlockSpec(memory_space=pltpu.VMEM)] * len(later),
+        out_specs=[
+            pl.BlockSpec((nodes + DEEP, WIDE), lambda i: (0, i)),
+            pl.BlockSpec((DEEP, width // steps), lambda i: (0, i)),
+        ],
+        out_shape=[pltpu.VMEM((nodes + DEEP, points), bf16), pltpu.VMEM((DEEP, width), bf16)],
         compiler_params=params(("arbitrary",), 8),
         name="prep",
-    )(src, weight)
+    )(src, weight, bias, *map(parked, later))
 
 
 def turn_kernel(*refs):
@@ -91,13 +104,7 @@
 
     stacked = jnp.concatenate([low[...], own[...], high[...]], axis=0)
     proj[:, :nodes] = dot(stacked, w_node[...]).astype(bf16).T
-    row = lax.broadcasted_iota(jnp.int32, (DEEP, proj.shape[0]), 0)
-    block, rest = jnp.zeros(row.shape, f32), bias[...]
-    for k in range(SPLIT):
-        part = rest.astype(bf16).astype(f32)
-        block = jnp.where(row == k, part, block)
-        rest = rest - part
-    proj[:, nodes:] = block.T.astype(bf16)
+    proj[:, nodes:] = bias[...].T
 
     for g in range(target.shape[1] // 256):
         cols = slice(g * 256, (g + 1) * 256)
@@ -369,18 +376,17 @@
     core = lax.axis_index("core")
     where = lax.axis_index(REGION)
 
-    mine = [latent[m] for m in range(members)]
+    mine = [latent[0]] + [lax.optimization_barrier(latent)[m] for m in range(1, members)]
 
     low, high = [], []
     for m in range(members):
         low.append(lax.ppermute(mine[m], REGION, ahead))
         high.append(lax.ppermute(mine[m], REGION, behind))
-    at = prep(edge_src.T, edge_weight.T, 3 * nodes)
-    bias_row = bias[None, :]
+    at, lift = prep(edge_src.T, edge_weight.T, bias[None, :], 3 * nodes, (w_node, w_out, target))
 
     hid, slope, err, near, far, beside = [], [], [], [], [], []
     for m in range(members):
-        h, s, e = forward(low[m], mine[m], high[m], w_node, at, bias_row, w_out, target)
+        h, s, e = forward(low[m], mine[m], high[m], w_node, at, lift, w_out, target)
         hid.append(h)
         slope.append(slopes(s))
         err.append(e)

time: 125 us -> 125 us (level)
  Pallas kernels: 43.2 us -> 39.7 us
  local copies, waits for them, and re-layouts: 6.49 us -> 9.59 us
  blocking collectives: 31.7 us -> 30.1 us
    unnamed x15 -> x21, local copies, waits for them, and re-layouts: 3.78 us -> 6.71 us
    pallas_call x2, Pallas kernels: 12.2 us -> 10.2 us  [forward(): pl.pallas_call(forward_kernel, in_specs=[vm] * 8, out_specs=[vm] * 3, out...]
    all_to_all x1, blocking collectives: 24 us -> 22.4 us  [local(): lax.all_to_all(part.reshape(chips, 2 * share + 8, 128), CHIPS, split_axis...]
    pallas_call x1, Pallas kernels: 2.52 us -> 0.93 us  [turn(): pl.pallas_call(turn_kernel, grid=(width // WIDE,), in_specs=[pl.BlockSpec...]
  transfers between devices with their start and end apart: 14 -> 14, of which waited for: 2 -> 2; matrix products, arithmetic and copies ran while one was open for 0% -> 1% of each run, Pallas kernels for 32% -> 29%
where the time goes in v6:
time: 125 us; the launch traced here: 124 us
  Pallas kernels  39.7 us (32%)
  starting transfers between devices  30.1 us (24%)
  blocking collectives  30.1 us (24%)
  waiting for transfers between devices  13.1 us (10%)
  local copies, waits for them, and re-layouts  9.59 us (8%)
    all_to_all x1, blocking collectives, local(): lax.all_to_all(part.reshape(chips, 2 * share + 8, 128), CHIPS, split_axis...  22.4 us
    ppermute x2, starting transfers between devices, local(): high.append(lax.ppermute(mine[m], REGION, behind))  14.6 us
    pallas_call x2, Pallas kernels, forward(): pl.pallas_call(forward_kernel, in_specs=[vm] * 8, out_specs=[vm] * 3, out...  10.2 us
    pallas_call x2, Pallas kernels, backward(): pl.pallas_call(backward_kernel, in_specs=[pl.BlockSpec(memory_space=pltpu...  9.51 us
    pallas_call x2, Pallas kernels, slopes(): pl.pallas_call(slope_kernel, grid=(width // 128,), in_specs=[rows], out_s...  8.66 us
    all_gather x1, blocking collectives, local(): grad_node = lax.all_gather(own, MEMBER, axis=1, tiled=True)  7.71 us
    ppermute x2, waiting for transfers between devices, local(): over = lax.ppermute((e * 0.125).astype(f16), 'ylo', swap)  6.89 us
    unnamed x21, local copies, waits for them, and re-layouts  6.71 us
  transfers between devices with their start and end apart: 14, of which 2 were waited for; matrix products, arithmetic and copies ran while one was open for 1% of the time, Pallas kernels for 29%

profile of v6, /device:TPU:1, one launch (start us, length us, event | category | flops | bytes accessed | tf_op | source)
XLA Modules:
  0.0 124.3 jit_solution(9247014197837436342)
XLA Ops:
  0.6 0.0 copy-start.5
  0.6 0.0 copy-start.3
  0.7 1.1 slice_bitcast_fusion.1.refs_1_.own
  1.7 2.1 %collective-permute-start = (bf16[128,1024]{1,0:T(8,128)(2,1)S(1)}, bf16[128,1024]{1,0:T(8,128)(2,1)S(1)}, u32[]{:S(2)}, u32[]{:S(2)}) collective-permute-start(bf16[128,1024]{1,0:T(8,128)(2,1)S(1)} %slice_bitcast_fusion.1.refs_1_.own), channel_id=1, source_target_pairs={{0,1},{1,2},{2,3},{3,4},{4,5},{5,6},{6,7},{7,8},{8,9},{9,10},{10,1... | collective-permute-start | bytes 786440 | tf_op jit(solution)/shard_map/ppermute | solution.py:383
  3.8 7.5 %collective-permute-start.3 = (bf16[128,1024]{1,0:T(8,128)(2,1)S(1)}, bf16[128,1024]{1,0:T(8,128)(2,1)S(1)}, u32[]{:S(2)}, u32[]{:S(2)}) collective-permute-start(bf16[128,1024]{1,0:T(8,128)(2,1)S(1)} %slice_bitcast_fusion.1.refs_1_.own), channel_id=1, source_target_pairs={{1,0},{2,1},{3,2},{4,3},{5,4},{6,5},{7,6},{8,7},{9,8},{10,9},{11,1... | collective-permute-start | bytes 786440 | tf_op jit(solution)/shard_map/ppermute | solution.py:384
  11.3 1.0 slice_bitcast_fusion.own.refs_4_
  12.2 0.1 collective-permute-start.1
  12.3 7.2 %collective-permute-start.2 = (bf16[128,1024]{1,0:T(8,128)(2,1)S(1)}, bf16[128,1024]{1,0:T(8,128)(2,1)S(1)}, u32[]{:S(2)}, u32[]{:S(2)}) collective-permute-start(bf16[128,1024]{1,0:T(8,128)(2,1)S(1)} %slice_bitcast_fusion.own.refs_4_), channel_id=1, source_target_pairs={{1,0},{2,1},{3,2},{4,3},{5,4},{6,5},{7,6},{8,7},{9,8},{10,9},{11,1... | collective-permute-start | bytes 786440 | tf_op jit(solution)/shard_map/ppermute | solution.py:384
  19.5 1.6 %copy-done = bf16[1024,1024]{1,0:T(8,128)(2,1)S(1)} copy-done((bf16[1024,1024]{1,0:T(8,128)(2,1)S(1)}, bf16[1024,1024]{1,0:T(8,128)(2,1)}, u32[]{:S(2)}) %copy-start) | copy-done | bytes 2097176
  21.1 1.2 copy-done.2
  22.2 0.9 copy-done.4
  23.2 0.8 copy-done.6
  23.9 0.8 copy-done.7
  24.7 0.7 copy-done.9
  25.4 1.3 %prep.1 = (bf16[512,2048]{1,0:T(8,128)(2,1)S(1)}, bf16[128,1024]{1,0:T(8,128)(2,1)S(1)}) custom-call(s32[3,2048]{1,0:T(4,128)S(1)} %bitcast.19, f32[3,2048]{1,0:T(4,128)S(1)} %bitcast.20, f32[1,1024]{1,0:T(1,128)S(1)} %bitcast.23, bf16[1024,1024]{1,0:T(8,128)(2,1)S(1)} %copy-done, bf16[100,1024]{1,0:T(8,128)(2,1)S(1)} %copy-done.4, f32[100,2048]{1,0:T(8,128)S(1)} %copy-done.2), custom_call_target="tpu_custom_call" | custom-call | tf_op jit(solution)/shard_map/prep/pallas_call | solution.py:68
  26.7 0.1 pad_add_fusion
  26.8 0.0 collective-permute-done.refs_0_.low
  26.8 0.0 collective-permute-done.3.refs_2_.high
  26.8 0.2 copy-done.1
  27.0 5.1 %forward.3 = (bf16[1024,2048]{1,0:T(8,128)(2,1)S(1)}, bf16[1024,2048]{1,0:T(8,128)(2,1)S(1)}, f32[100,2048]{1,0:T(8,128)S(1)}) custom-call(bf16[128,1024]{1,0:T(8,128)(2,1)S(1)} %collective-permute-done.refs_0_.low, bf16[128,1024]{1,0:T(8,128)(2,1)S(1)} %slice_bitcast_fusion.1.refs_1_.own, bf16[128,1024]{1,0:T(8,128)(2,1)S(1)} %collective-permute-done.3.refs_2_.high, ...), custom_call_target="tpu_custom_call" | custom-call | tf_op jit(solution)/shard_map/forward/pallas_call | solution.py:125
  32.1 1.6 %collective-permute-start.7 = (f32[100,2048]{1,0:T(8,128)S(1)}, f32[100,2048]{1,0:T(8,128)S(1)}, u32[]{:S(2)}, u32[]{:S(2)}) collective-permute-start(f32[100,2048]{1,0:T(8,128)S(1)} %get-tuple-element.31.refs_0_), channel_id=1, source_target_pairs={{0,32},{32,0},{1,33},{33,1},{2,34},{34,2},{3,35},{35,3},{4,36},{36... | collective-permute-start | bytes 2457608 | tf_op jit(solution)/shard_map/ppermute | solution.py:394
  33.7 0.1 multiply_convert_fusion
  33.7 0.0 collective-permute-done.1.low.refs_3_
  33.7 0.0 collective-permute-done.2.high.refs_5_
  33.7 5.1 %forward.2 = (bf16[1024,2048]{1,0:T(8,128)(2,1)S(1)}, bf16[1024,2048]{1,0:T(8,128)(2,1)S(1)}, f32[100,2048]{1,0:T(8,128)S(1)}) custom-call(bf16[128,1024]{1,0:T(8,128)(2,1)S(1)} %collective-permute-done.1.low.refs_3_, bf16[128,1024]{1,0:T(8,128)(2,1)S(1)} %slice_bitcast_fusion.own.refs_4_, bf16[128,1024]{1,0:T(8,128)(2,1)S(1)} %collective-permute-done.2.high.refs_5_, ...), custom_call_target="tpu_custom_call" | custom-call | tf_op jit(solution)/shard_map/forward/pallas_call | solution.py:125
  38.8 0.1 collective-permute-start.8
  38.9 0.5 collective-permute-start.9
  39.4 0.1 multiply_convert_fusion.1
  39.5 1.3 %collective-permute-start.5 = (f16[100,2048]{1,0:T(8,128)(2,1)S(1)}, f16[100,2048]{1,0:T(8,128)(2,1)S(1)}, u32[]{:S(2)}, u32[]{:S(2)}) collective-permute-start(f16[100,2048]{1,0:T(8,128)(2,1)S(1)} %multiply_convert_fusion.1), channel_id=1, source_target_pairs={{0,64},{64,0},{1,65},{65,1},{2,66},{66,2},{3,67},{67,3},{4,68},{68... | collective-permute-start | bytes 1228808 | tf_op jit(solution)/shard_map/ppermute | solution.py:393
  40.8 4.3 %slope.2.s_0 = bf16[1024,2048]{1,0:T(8,128)(2,1)S(1)} custom-call(bf16[1024,2048]{1,0:T(8,128)(2,1)S(1)} %get-tuple-element.38.pre), custom_call_target="tpu_custom_call" | custom-call | tf_op jit(solution)/shard_map/slope/pallas_call | solution.py:152
  45.1 4.3 %slope.3.s_1 = bf16[1024,2048]{1,0:T(8,128)(2,1)S(1)} custom-call(bf16[1024,2048]{1,0:T(8,128)(2,1)S(1)} %get-tuple-element.39.pre), custom_call_target="tpu_custom_call" | custom-call | tf_op jit(solution)/shard_map/slope/pallas_call | solution.py:152
  49.5 0.9 turn.1.lat_own
  50.4 0.0 copy-start.8
  50.4 1.1 collective-permute-start.4
  51.5 0.0 collective-permute-done.9
  51.5 0.6 collective-permute-start.10
  52.1 0.1 convert_multiply_fusion.1.refs_4_
  52.2 6.9 %collective-permute-done.5 = f16[100,2048]{1,0:T(8,128)(2,1)S(1)} collective-permute-done((f16[100,2048]{1,0:T(8,128)(2,1)S(1)}, f16[100,2048]{1,0:T(8,128)(2,1)S(1)}, u32[]{:S(2)}, u32[]{:S(2)}) %collective-permute-start.5) | collective-permute-done | bytes 409632 | tf_op jit(solution)/shard_map/ppermute | solution.py:393
  59.1 1.3 %collective-permute-start.6 = (f16[100,2048]{1,0:T(8,128)(2,1)S(1)}, f16[100,2048]{1,0:T(8,128)(2,1)S(1)}, u32[]{:S(2)}, u32[]{:S(2)}) collective-permute-start(f16[100,2048]{1,0:T(8,128)(2,1)S(1)} %collective-permute-done.5), channel_id=1, source_target_pairs={{0,32},{32,0},{1,33},{33,1},{2,34},{34,2},{3,35},{35,3},{4,36},{36... | collective-permute-start | bytes 1228808 | tf_op jit(solution)/shard_map/ppermute | solution.py:396
  60.4 0.1 convert_multiply_fusion.3.refs_2_
  60.5 0.0 collective-permute-done.10
  60.5 0.1 convert_multiply_fusion.refs_5_
  60.6 0.0 collective-permute-done.7.refs_2_
  60.6 0.0 collective-permute-done.8.refs_3_
  60.6 4.0 %crps_near.1 = (f32[100,2048]{1,0:T(8,128)S(1)}, f32[100,2048]{1,0:T(8,128)S(1)}, f32[1,128]{1,0:T(1,128)S(1)}) custom-call(f32[100,2048]{1,0:T(8,128)S(1)} %get-tuple-element.31.refs_0_, f32[100,2048]{1,0:T(8,128)S(1)} %get-tuple-element.32.refs_1_, f32[100,2048]{1,0:T(8,128)S(1)} %collective-permute-done.7.refs_2_, ...), custom_call_target="tpu_custom_call" | custom-call | tf_op jit(solution)/shard_map/crps_near/pallas_call | solution.py:233
  64.6 0.0 collective-permute-done.6
  64.6 0.1 convert_multiply_fusion.2.refs_3_
  64.7 1.9 %crps_far.1 = (bf16[128,2048]{1,0:T(8,128)(2,1)S(1)}, bf16[128,2048]{1,0:T(8,128)(2,1)S(1)}, f32[1,128]{1,0:T(1,128)S(1)}) custom-call(f32[100,2048]{1,0:T(8,128)S(1)} %get-tuple-element.31.refs_0_, f32[100,2048]{1,0:T(8,128)S(1)} %get-tuple-element.32.refs_1_, f32[100,2048]{1,0:T(8,128)S(1)} %convert_multiply_fusion.3.refs_2_, ...), custom_call_target="tpu_custom_call" | custom-call | tf_op jit(solution)/shard_map/crps_far/pallas_call | solution.py:251
  66.6 4.8 %backward.3 = (bf16[2,768,256]{2,1,0:T(8,128)(2,1)S(1)}, f32[2,16,2,8,128]{4,3,2,1,0:T(8,128)S(1)}) custom-call(s32[2]{0:T(128)S(1)} %get-tuple-element.53.who, bf16[128,2048]{1,0:T(8,128)(2,1)S(1)} %get-tuple-element.36.d_0, bf16[128,2048]{1,0:T(8,128)(2,1)S(1)} %get-tuple-element.37.d_1, bf16[100,1024]{1,0:T(8,128)(2,1)S(1)} %copy-done.5, ...), custom_call_target="tpu_custom_call" | custom-call | tf_op jit(solution)/shard_map/backward/pallas_call | solution.py:292
  71.4 0.1 collective-permute-start.11
  71.5 0.5 collective-permute-start.12
  72.0 4.8 %backward.2 = (bf16[2,768,256]{2,1,0:T(8,128)(2,1)S(1)}, f32[2,16,2,8,128]{4,3,2,1,0:T(8,128)S(1)}) custom-call(s32[2]{0:T(128)S(1)} %get-tuple-element.52.who, bf16[128,2048]{1,0:T(8,128)(2,1)S(1)} %get-tuple-element.36.d_0, bf16[128,2048]{1,0:T(8,128)(2,1)S(1)} %get-tuple-element.37.d_1, bf16[100,1024]{1,0:T(8,128)(2,1)S(1)} %copy-done.5, ...), custom_call_target="tpu_custom_call" | custom-call | tf_op jit(solution)/shard_map/backward/pallas_call | solution.py:292
  76.7 0.0 collective-permute-done.12
  76.7 0.0 collective-permute-done.4.lat_other
  76.8 0.0 collective-permute-done.11.c_other
  76.8 2.5 %outer.1 = bf16[2,32,72,128]{3,2,1,0:T(8,128)(2,1)S(1)} custom-call(bf16[1024,768]{1,0:T(8,128)(2,1)S(1)} %turn.1.lat_own, bf16[1024,768]{1,0:T(8,128)(2,1)S(1)} %collective-permute-done.4.lat_other, bf16[2,768,256]{2,1,0:T(8,128)(2,1)S(1)} %get-tuple-element.43.c_own, bf16[2,768,256]{2,1,0:T(8,128)(2,1)S(1)} %collective-permute-done.11.c_other, ...), custom_call_target="tpu_custom_call" | custom-call | tf_op jit(solution)/shard_map/outer/pallas_call | solution.py:324
  79.2 22.4 %all_to_all.10 = bf16[64,72,128]{2,1,0:T(8,128)(2,1)S(1)} all-to-all(bf16[64,72,128]{2,1,0:T(8,128)(2,1)S(1)} %bitcast.16), channel_id=1, replica_groups=mesh['ylo'=2,'core'=2,'z'=4,'yhi'=2,'x'=4] {'ylo','z','yhi','x'}, dimensions={0} | all-to-all | bytes 2359296 | tf_op jit(solution)/shard_map/all_to_all | solution.py:421
  101.6 0.2 convert_reduce_fusion
  101.8 0.8 broadcast_in_dim.12
  102.7 6.3 %all-to-all-start.1 = ((f32[128,8,128]{2,1,0:T(8,128)}), f32[128,8,128]{2,1,0:T(8,128)S(1)}, u32[]{:S(2)}, u32[]{:S(2)}) async-start(f32[128,8,128]{2,1,0:T(8,128)} %broadcast_in_dim.12), calls=%async_computation.1 | async-start | bytes 1048576 | tf_op jit(solution)/shard_map/all_to_all | solution.py:425
  109.0 7.7 %all_gather.3 = f32[32,1024]{1,0:T(8,128)S(1)} all-gather(f32[32,256]{1,0:T(8,128)S(1)} %pad_maximum_fusion), channel_id=1, replica_groups=mesh['ylo'=2,'core'=2,'z'=4,'yhi'=2,'x'=4] {'ylo','core'}, dimensions={1}, use_global_device_ids=true | all-gather | bytes 163840 | tf_op jit(solution)/shard_map/all_gather | solution.py:429
  116.7 6.1 %all-to-all-done.1.pieces = f32[128,8,128]{2,1,0:T(8,128)S(1)} async-done(((f32[128,8,128]{2,1,0:T(8,128)}), f32[128,8,128]{2,1,0:T(8,128)S(1)}, u32[]{:S(2)}, u32[]{:S(2)}) %all-to-all-start.1) | async-done | bytes 524320 | tf_op jit(solution)/shard_map/all_to_all | solution.py:425
  122.8 0.8 finish.1
  123.6 0.7 copy.13
  (13 shorter events, 0.0 us)
Async XLA Ops:
  0.6 26.2 %copy-start.5 = (bf16[100,1024]{1,0:T(8,128)(2,1)S(1)}, bf16[100,1024]{1,0:T(8,128)(2,1)}, u32[]{:S(2)}) copy-start(bf16[100,1024]{1,0:T(8,128)(2,1)} %w_out.7) | copy-start | bytes 614404
  0.6 26.2 %copy-start.3 = (f32[100,2048]{1,0:T(8,128)S(1)}, f32[100,2048]{1,0:T(8,128)}, u32[]{:S(2)}) copy-start(f32[100,2048]{1,0:T(8,128)} %target.3) | copy-start | bytes 2457604
  1.7 25.1 %collective-permute-start = (bf16[128,1024]{1,0:T(8,128)(2,1)S(1)}, bf16[128,1024]{1,0:T(8,128)(2,1)S(1)}, u32[]{:S(2)}, u32[]{:S(2)}) collective-permute-start(bf16[128,1024]{1,0:T(8,128)(2,1)S(1)} %slice_bitcast_fusion.1.refs_1_.own), channel_id=1, source_target_pairs={{0,1},{1,2},{2,3},{3,4},{4,5},{5,6},{6,7},{7,8},{8,9},{9,10},{10,1... | collective-permute-start | bytes 786440 | tf_op jit(solution)/shard_map/ppermute | solution.py:383
  3.8 23.0 %collective-permute-start.3 = (bf16[128,1024]{1,0:T(8,128)(2,1)S(1)}, bf16[128,1024]{1,0:T(8,128)(2,1)S(1)}, u32[]{:S(2)}, u32[]{:S(2)}) collective-permute-start(bf16[128,1024]{1,0:T(8,128)(2,1)S(1)} %slice_bitcast_fusion.1.refs_1_.own), channel_id=1, source_target_pairs={{1,0},{2,1},{3,2},{4,3},{5,4},{6,5},{7,6},{8,7},{9,8},{10,9},{11,1... | collective-permute-start | bytes 786440 | tf_op jit(solution)/shard_map/ppermute | solution.py:384
  12.2 21.5 %collective-permute-start.1 = (bf16[128,1024]{1,0:T(8,128)(2,1)S(1)}, bf16[128,1024]{1,0:T(8,128)(2,1)S(1)}, u32[]{:S(2)}, u32[]{:S(2)}) collective-permute-start(bf16[128,1024]{1,0:T(8,128)(2,1)S(1)} %slice_bitcast_fusion.own.refs_4_), channel_id=1, source_target_pairs={{0,1},{1,2},{2,3},{3,4},{4,5},{5,6},{6,7},{7,8},{8,9},{9,10},{10,1... | collective-permute-start | bytes 786440 | tf_op jit(solution)/shard_map/ppermute | solution.py:383
  12.3 21.4 %collective-permute-start.2 = (bf16[128,1024]{1,0:T(8,128)(2,1)S(1)}, bf16[128,1024]{1,0:T(8,128)(2,1)S(1)}, u32[]{:S(2)}, u32[]{:S(2)}) collective-permute-start(bf16[128,1024]{1,0:T(8,128)(2,1)S(1)} %slice_bitcast_fusion.own.refs_4_), channel_id=1, source_target_pairs={{1,0},{2,1},{3,2},{4,3},{5,4},{6,5},{7,6},{8,7},{9,8},{10,9},{11,1... | collective-permute-start | bytes 786440 | tf_op jit(solution)/shard_map/ppermute | solution.py:384
  19.5 1.6 %copy-start = (bf16[1024,1024]{1,0:T(8,128)(2,1)S(1)}, bf16[1024,1024]{1,0:T(8,128)(2,1)}, u32[]{:S(2)}) copy-start(bf16[1024,1024]{1,0:T(8,128)(2,1)} %w_node.3) | copy-start | bytes 6291460
  21.1 1.2 copy-start.2
  22.2 0.9 copy-start.4
  23.2 0.8 copy-start.6
  23.9 0.8 copy-start.7
  24.7 0.7 copy-start.9
  25.4 1.6 %copy-start.1 = (bf16[1024,1024]{1,0:T(8,128)(2,1)S(1)}, bf16[1024,1024]{1,0:T(8,128)(2,1)}, u32[]{:S(2)}) copy-start(bf16[1024,1024]{1,0:T(8,128)(2,1)} %w_node.3) | copy-start | bytes 6291460
  32.1 28.5 %collective-permute-start.7 = (f32[100,2048]{1,0:T(8,128)S(1)}, f32[100,2048]{1,0:T(8,128)S(1)}, u32[]{:S(2)}, u32[]{:S(2)}) collective-permute-start(f32[100,2048]{1,0:T(8,128)S(1)} %get-tuple-element.31.refs_0_), channel_id=1, source_target_pairs={{0,32},{32,0},{1,33},{33,1},{2,34},{34,2},{3,35},{35,3},{4,36},{36... | collective-permute-start | bytes 2457608 | tf_op jit(solution)/shard_map/ppermute | solution.py:394
  38.8 21.7 %collective-permute-start.8 = (f32[100,2048]{1,0:T(8,128)S(1)}, f32[100,2048]{1,0:T(8,128)S(1)}, u32[]{:S(2)}, u32[]{:S(2)}) collective-permute-start(f32[100,2048]{1,0:T(8,128)S(1)} %get-tuple-element.32.refs_1_), channel_id=1, source_target_pairs={{0,32},{32,0},{1,33},{33,1},{2,34},{34,2},{3,35},{35,3},{4,36},{36... | collective-permute-start | bytes 2457608 | tf_op jit(solution)/shard_map/ppermute | solution.py:394
  38.9 12.6 %collective-permute-start.9 = (f16[100,2048]{1,0:T(8,128)(2,1)S(1)}, f16[100,2048]{1,0:T(8,128)(2,1)S(1)}, u32[]{:S(2)}, u32[]{:S(2)}) collective-permute-start(f16[100,2048]{1,0:T(8,128)(2,1)S(1)} %multiply_convert_fusion), channel_id=1, source_target_pairs={{0,64},{64,0},{1,65},{65,1},{2,66},{66,2},{3,67},{67,3},{4,68},{68... | collective-permute-start | bytes 1228808 | tf_op jit(solution)/shard_map/ppermute | solution.py:393
  39.5 19.6 %collective-permute-start.5 = (f16[100,2048]{1,0:T(8,128)(2,1)S(1)}, f16[100,2048]{1,0:T(8,128)(2,1)S(1)}, u32[]{:S(2)}, u32[]{:S(2)}) collective-permute-start(f16[100,2048]{1,0:T(8,128)(2,1)S(1)} %multiply_convert_fusion.1), channel_id=1, source_target_pairs={{0,64},{64,0},{1,65},{65,1},{2,66},{66,2},{3,67},{67,3},{4,68},{68... | collective-permute-start | bytes 1228808 | tf_op jit(solution)/shard_map/ppermute | solution.py:393
  50.4 10.2 %copy-start.8 = (f32[2048]{0:T(1024)S(1)}, f32[2048]{0:T(1024)}, u32[]{:S(2)}) copy-start(f32[2048]{0:T(1024)} %param.15) | copy-start | bytes 24580
  50.4 26.3 %collective-permute-start.4 = (bf16[1024,768]{1,0:T(8,128)(2,1)S(1)}, bf16[1024,768]{1,0:T(8,128)(2,1)S(1)}, u32[]{:S(2)}, u32[]{:S(2)}) collective-permute-start(bf16[1024,768]{1,0:T(8,128)(2,1)S(1)} %turn.1.lat_own), channel_id=1, source_target_pairs={{0,32},{32,0},{1,33},{33,1},{2,34},{34,2},{3,35},{35,3},{4,36},{36... | collective-permute-start | bytes 4718600 | tf_op jit(solution)/shard_map/ppermute | solution.py:400
  51.5 9.0 %collective-permute-start.10 = (f16[100,2048]{1,0:T(8,128)(2,1)S(1)}, f16[100,2048]{1,0:T(8,128)(2,1)S(1)}, u32[]{:S(2)}, u32[]{:S(2)}) collective-permute-start(f16[100,2048]{1,0:T(8,128)(2,1)S(1)} %collective-permute-done.9), channel_id=1, source_target_pairs={{0,32},{32,0},{1,33},{33,1},{2,34},{34,2},{3,35},{35,3},{4,36},{36... | collective-permute-start | bytes 1228808 | tf_op jit(solution)/shard_map/ppermute | solution.py:396
  59.1 5.5 %collective-permute-start.6 = (f16[100,2048]{1,0:T(8,128)(2,1)S(1)}, f16[100,2048]{1,0:T(8,128)(2,1)S(1)}, u32[]{:S(2)}, u32[]{:S(2)}) collective-permute-start(f16[100,2048]{1,0:T(8,128)(2,1)S(1)} %collective-permute-done.5), channel_id=1, source_target_pairs={{0,32},{32,0},{1,33},{33,1},{2,34},{34,2},{3,35},{35,3},{4,36},{36... | collective-permute-start | bytes 1228808 | tf_op jit(solution)/shard_map/ppermute | solution.py:396
  71.4 5.4 %collective-permute-start.11 = (bf16[2,768,256]{2,1,0:T(8,128)(2,1)S(1)}, bf16[2,768,256]{2,1,0:T(8,128)(2,1)S(1)}, u32[]{:S(2)}, u32[]{:S(2)}) collective-permute-start(bf16[2,768,256]{2,1,0:T(8,128)(2,1)S(1)} %get-tuple-element.44), channel_id=1, source_target_pairs={{0,32},{32,0},{1,33},{33,1},{2,34},{34,2},{3,35},{35,3},{4,36},{36... | collective-permute-start | bytes 2359304 | tf_op jit(solution)/shard_map/ppermute | solution.py:414
  71.5 5.3 %collective-permute-start.12 = (f32[2,16,2,8,128]{4,3,2,1,0:T(8,128)S(1)}, f32[2,16,2,8,128]{4,3,2,1,0:T(8,128)S(1)}, u32[]{:S(2)}, u32[]{:S(2)}) collective-permute-start(f32[2,16,2,8,128]{4,3,2,1,0:T(8,128)S(1)} %get-tuple-element.46), channel_id=1, source_target_pairs={{0,32},{32,0},{1,33},{33,1},{2,34},{34,2},{3,35},{35,3},{4,36},{36... | collective-permute-start | bytes 786440 | tf_op jit(solution)/shard_map/ppermute | solution.py:415
  102.7 20.2 %all-to-all-start.1 = ((f32[128,8,128]{2,1,0:T(8,128)}), f32[128,8,128]{2,1,0:T(8,128)S(1)}, u32[]{:S(2)}, u32[]{:S(2)}) async-start(f32[128,8,128]{2,1,0:T(8,128)} %broadcast_in_dim.12), calls=%async_computation.1 | async-start | bytes 1048576 | tf_op jit(solution)/shard_map/all_to_all | solution.py:425

commit v7 on v6

--- a/solution.py
+++ b/solution.py
@@ -35,6 +35,10 @@
 
 def parked(a):
     return pltpu.with_memory_space_constraint(a, pltpu.VMEM)
+
+
+def settled(a):
+    return pltpu.with_memory_space_constraint(a, pltpu.HBM)
 
 
 def whole(a):
@@ -76,7 +80,7 @@
         out_shape=[pltpu.VMEM((nodes + DEEP, points), bf16), pltpu.VMEM((DEEP, width), bf16)],
         compiler_params=params(("arbitrary",), 8),
         name="prep",
-    )(src, weight, bias, *map(parked, later))
+    )(*map(settled, (src, weight, bias)), *map(parked, later))
 
 
 def turn_kernel(*refs):
@@ -332,37 +336,48 @@
     )(parked(lat_own), lat_other, parked(c_own), c_other, parked(h_own), h_other)
 
 
-def finish_kernel(where, pieces, grad_out, grad_bias, loss):
+def finish_kernel(where, mine, others, rows_mine, rows_others, grad_node, grad_out, grad_bias, loss):
     variables, _ = grad_out.shape
     per_row = WIDE // 128
-    for at in range(pieces.shape[0]):
-        ylo, core, place = at // 64, at // 32 % 2, at % 32
-        i, j = place // per_row, place % per_row
-        left, top = (2 * ylo + core) * WIDE + j * 128, i * 8
-        rows = max(0, min(8, variables - top))
-        if rows:
-            grad_out[top : top + rows, left : left + 128] = pieces[at, :rows]
-        line = variables - top
-        if 0 <= line < 7:
-            grad_bias[:, left : left + 128] = pieces[at, line : line + 1]
-            if left == 0:
-                values = pieces[at, line + 1 : line + 2]
-                spot = lax.broadcasted_iota(jnp.int32, values.shape, 1)
-                loss[...] = jnp.sum(jnp.where(spot == where[0], values, 0.0), axis=1, keepdims=True)
-
-
-def finish(where, pieces, variables, width):
+    lower = where[1] == 0
+    for core in range(2):
+        first = lower if core == 0 else jnp.logical_not(lower)
+        for ylo in range(rows_mine.shape[0]):
+            left = (2 * ylo + core) * WIDE
+            grad_node[:, left : left + WIDE] = jnp.where(first, rows_mine[ylo], rows_others[ylo])
+        for at in range(mine.shape[0]):
+            ylo, place = at // 32, at % 32
+            i, j = place // per_row, place % per_row
+            left, top = (2 * ylo + core) * WIDE + j * 128, i * 8
+            if top >= variables + 2:
+                continue
+            piece = jnp.where(first, mine[at], others[at])
+            rows = min(8, variables - top)
+            if rows > 0:
+                grad_out[top : top + rows, left : left + 128] = piece[:rows]
+            line = variables - top
+            if 0 <= line < 7:
+                grad_bias[:, left : left + 128] = piece[line : line + 1]
+                if left == 0:
+                    values = piece[line + 1 : line + 2]
+                    spot = lax.broadcasted_iota(jnp.int32, values.shape, 1)
+                    loss[...] = jnp.sum(jnp.where(spot == where[0], values, 0.0), axis=1, keepdims=True)
+
+
+def finish(where, mine, others, rows_mine, rows_others, variables, width):
+    vm = pl.BlockSpec(memory_space=pltpu.VMEM)
     return pl.pallas_call(
         finish_kernel,
-        in_specs=[pl.BlockSpec(memory_space=pltpu.SMEM), pl.BlockSpec(memory_space=pltpu.VMEM)],
+        in_specs=[pl.BlockSpec(memory_space=pltpu.SMEM)] + [vm] * 4,
         out_shape=[
+            jax.ShapeDtypeStruct((rows_mine.shape[1], width), f32),
             jax.ShapeDtypeStruct((variables, width), f32),
             jax.ShapeDtypeStruct((1, width), f32),
             jax.ShapeDtypeStruct((1, 1), f32),
         ],
         compiler_params=pltpu.CompilerParams(vmem_limit_bytes=8 << 20),
         name="finish",
-    )(where, pieces)
+    )(where, mine, others, rows_mine, rows_others)
 
 
 def local(latent, w_node, bias, w_out, edge_src, edge_weight, target, area):
@@ -382,7 +397,7 @@
     for m in range(members):
         low.append(lax.ppermute(mine[m], REGION, ahead))
         high.append(lax.ppermute(mine[m], REGION, behind))
-    at, lift = prep(edge_src.T, edge_weight.T, bias[None, :], 3 * nodes, (w_node, w_out, target))
+    at, lift = prep(edge_src.T, edge_weight.T, bias[None, :], 3 * nodes, (w_node,))
 
     hid, slope, err, near, far, beside = [], [], [], [], [], []
     for m in range(members):
@@ -403,8 +418,6 @@
     p_0, p_1, loss = crps_near(err, near + [far[0], beside[0]], area_row, count)
     d_0, d_1, loss = crps_far(err, [far[1], beside[1]], (p_0, p_1), area_row, loss, count)
 
-    spot = where[None].astype(jnp.int32)
-    every = lax.axis_size(EVERY)
 
     def back(side):
         who = jnp.stack([side, where]).astype(jnp.int32)
@@ -422,12 +435,17 @@
         part.reshape(chips, 2 * share + 8, 128), CHIPS, split_axis=0, concat_axis=0, tiled=True
     )
     summed = shares.astype(f32).sum(axis=0)
+    own = jnp.concatenate([summed[:share], summed[share : 2 * share]], axis=1)
     table = lax.all_to_all(
-        jnp.broadcast_to(summed[2 * share :], (every, 8, 128)), EVERY, split_axis=0, concat_axis=0, tiled=True
+        jnp.broadcast_to(summed[2 * share :], (chips, 8, 128)), CHIPS, split_axis=0, concat_axis=0, tiled=True
     )
-    own = jnp.concatenate([summed[:share], summed[share : 2 * share]], axis=1)
-    grad_node = lax.all_gather(own, MEMBER, axis=1, tiled=True)
-    grad_out, grad_bias, loss_here = finish(spot, table, variables, width)
+    across = lax.ppermute(own, "ylo", swap)
+    upper = lax.axis_index("ylo") == 1
+    rows = jnp.stack([jnp.where(upper, across, own), jnp.where(upper, own, across)])
+    rows_others = lax.ppermute(rows, "core", swap)
+    table_others = lax.ppermute(table, "core", swap)
+    who = jnp.stack([where, core]).astype(jnp.int32)
+    grad_node, grad_out, grad_bias, loss_here = finish(who, table, table_others, rows, rows_others, variables, width)
     grad_bias = grad_bias.reshape(width)
     loss_here = loss_here.reshape(1)
     return grad_node, grad_out, grad_bias, loss_here

time: 125 us -> 122 us (0.976)
  blocking collectives: 30.1 us -> 22.6 us
  local copies, waits for them, and re-layouts: 9.59 us -> 4.37 us
  starting transfers between devices: 30.1 us -> 34.2 us
  Pallas kernels: 39.7 us -> 42.9 us
  waiting for transfers between devices: 13.1 us -> 16.2 us
    all_gather x1 -> x0, blocking collectives: 7.71 us -> none  [local(): grad_node = lax.all_gather(own, MEMBER, axis=1, tiled=True)]
    unnamed x21 -> x10, local copies, waits for them, and re-layouts: 6.71 us -> 1.61 us
    ppermute x0 -> x3, starting transfers between devices: none -> 4.11 us  [the longest x1 2.83 us: local(): table_others = lax.ppermute(table, 'core', swap)]
    pallas_call x1, Pallas kernels: 1.33 us -> 3.82 us  [prep(): pl.pallas_call(prep_kernel, grid=(steps,), in_specs=[row, row, pl.BlockSp...]
    all_to_all x1, waiting for transfers between devices: 6.14 us -> 8.1 us  [local(): lax.all_to_all(jnp.broadcast_to(summed[2 * share:], (chips, 8, 128)), CHI...]
  transfers between devices with their start and end apart: 14 -> 17, of which waited for: 2 -> 3; matrix products, arithmetic and copies ran while one was open for 1% -> 1% of each run, Pallas kernels for 29% -> 32%
where the time goes in v7:
time: 122 us
  Pallas kernels  42.9 us (35%)
  starting transfers between devices  34.2 us (28%)
  blocking collectives  22.6 us (19%)
  waiting for transfers between devices  16.2 us (13%)
  local copies, waits for them, and re-layouts  4.37 us (4%)
    all_to_all x1, blocking collectives, local(): lax.all_to_all(part.reshape(chips, 2 * share + 8, 128), CHIPS, split_axis...  22.6 us
    ppermute x2, starting transfers between devices, local(): high.append(lax.ppermute(mine[m], REGION, behind))  14.6 us
    pallas_call x2, Pallas kernels, forward(): pl.pallas_call(forward_kernel, in_specs=[vm] * 8, out_specs=[vm] * 3, out...  10.2 us
    pallas_call x2, Pallas kernels, backward(): pl.pallas_call(backward_kernel, in_specs=[pl.BlockSpec(memory_space=pltpu...  9.55 us
    pallas_call x2, Pallas kernels, slopes(): pl.pallas_call(slope_kernel, grid=(width // 128,), in_specs=[rows], out_s...  8.66 us
    all_to_all x1, waiting for transfers between devices, local(): lax.all_to_all(jnp.broadcast_to(summed[2 * share:], (chips, 8, 128)), CHI...  8.1 us
    ppermute x2, waiting for transfers between devices, local(): over = lax.ppermute((e * 0.125).astype(f16), 'ylo', swap)  6.89 us
    all_to_all x1, starting transfers between devices, local(): lax.all_to_all(jnp.broadcast_to(summed[2 * share:], (chips, 8, 128)), CHI...  6.27 us
  transfers between devices with their start and end apart: 17, of which 3 were waited for; matrix products, arithmetic and copies ran while one was open for 1% of the time, Pallas kernels for 32%

profile of v7, /device:TPU:1, one launch (start us, length us, event | category | flops | bytes accessed | tf_op | source)
XLA Modules:
  0.0 122.1 jit_solution(8921296332042243087)
XLA Ops:
  0.7 1.1 slice_bitcast_fusion.1.refs_1_.own
  1.7 2.1 %collective-permute-start = (bf16[128,1024]{1,0:T(8,128)(2,1)S(1)}, bf16[128,1024]{1,0:T(8,128)(2,1)S(1)}, u32[]{:S(2)}, u32[]{:S(2)}) collective-permute-start(bf16[128,1024]{1,0:T(8,128)(2,1)S(1)} %slice_bitcast_fusion.1.refs_1_.own), channel_id=1, source_target_pairs={{0,1},{1,2},{2,3},{3,4},{4,5},{5,6},{6,7},{7,8},{8,9},{9,10},{10,1... | collective-permute-start | bytes 786440 | tf_op jit(solution)/shard_map/ppermute | solution.py:398
  3.8 7.5 %collective-permute-start.3 = (bf16[128,1024]{1,0:T(8,128)(2,1)S(1)}, bf16[128,1024]{1,0:T(8,128)(2,1)S(1)}, u32[]{:S(2)}, u32[]{:S(2)}) collective-permute-start(bf16[128,1024]{1,0:T(8,128)(2,1)S(1)} %slice_bitcast_fusion.1.refs_1_.own), channel_id=1, source_target_pairs={{1,0},{2,1},{3,2},{4,3},{5,4},{6,5},{7,6},{8,7},{9,8},{10,9},{11,1... | collective-permute-start | bytes 786440 | tf_op jit(solution)/shard_map/ppermute | solution.py:399
  11.3 1.0 slice_bitcast_fusion.own.refs_4_
  12.2 0.1 collective-permute-start.1
  12.3 7.2 %collective-permute-start.2 = (bf16[128,1024]{1,0:T(8,128)(2,1)S(1)}, bf16[128,1024]{1,0:T(8,128)(2,1)S(1)}, u32[]{:S(2)}, u32[]{:S(2)}) collective-permute-start(bf16[128,1024]{1,0:T(8,128)(2,1)S(1)} %slice_bitcast_fusion.own.refs_4_), channel_id=1, source_target_pairs={{1,0},{2,1},{3,2},{4,3},{5,4},{6,5},{7,6},{8,7},{9,8},{10,9},{11,1... | collective-permute-start | bytes 786440 | tf_op jit(solution)/shard_map/ppermute | solution.py:399
  19.5 1.6 %copy-done = bf16[1024,1024]{1,0:T(8,128)(2,1)S(1)} copy-done((bf16[1024,1024]{1,0:T(8,128)(2,1)S(1)}, bf16[1024,1024]{1,0:T(8,128)(2,1)}, u32[]{:S(2)}) %copy-start) | copy-done | bytes 2097176
  21.1 3.8 %prep.1 = (bf16[512,2048]{1,0:T(8,128)(2,1)S(1)}, bf16[128,1024]{1,0:T(8,128)(2,1)S(1)}) custom-call(s32[3,2048]{1,0:T(4,128)} %bitcast.25, f32[3,2048]{1,0:T(4,128)} %bitcast.26, f32[1,1024]{1,0:T(1,128)} %bitcast.27, bf16[1024,1024]{1,0:T(8,128)(2,1)S(1)} %copy-done), custom_call_target="tpu_custom_call" | custom-call | tf_op jit(solution)/shard_map/prep/pallas_call | solution.py:72
  24.9 0.1 pad_add_fusion.1
  25.0 0.0 collective-permute-done.refs_0_.low
  25.0 0.0 collective-permute-done.3.refs_2_.high
  25.0 0.0 copy-done.3
  25.0 0.0 copy-done.2
  25.0 0.0 copy-done.1
  25.0 5.1 %forward.3 = (bf16[1024,2048]{1,0:T(8,128)(2,1)S(1)}, bf16[1024,2048]{1,0:T(8,128)(2,1)S(1)}, f32[100,2048]{1,0:T(8,128)S(1)}) custom-call(bf16[128,1024]{1,0:T(8,128)(2,1)S(1)} %collective-permute-done.refs_0_.low, bf16[128,1024]{1,0:T(8,128)(2,1)S(1)} %slice_bitcast_fusion.1.refs_1_.own, bf16[128,1024]{1,0:T(8,128)(2,1)S(1)} %collective-permute-done.3.refs_2_.high, ...), custom_call_target="tpu_custom_call" | custom-call | tf_op jit(solution)/shard_map/forward/pallas_call | solution.py:129
  30.1 1.6 %collective-permute-start.7 = (f32[100,2048]{1,0:T(8,128)S(1)}, f32[100,2048]{1,0:T(8,128)S(1)}, u32[]{:S(2)}, u32[]{:S(2)}) collective-permute-start(f32[100,2048]{1,0:T(8,128)S(1)} %get-tuple-element.32.refs_0_), channel_id=1, source_target_pairs={{0,32},{32,0},{1,33},{33,1},{2,34},{34,2},{3,35},{35,3},{4,36},{36... | collective-permute-start | bytes 2457608 | tf_op jit(solution)/shard_map/ppermute | solution.py:409
  31.7 0.1 multiply_convert_fusion
  31.8 0.0 collective-permute-done.1.low.refs_3_
  31.8 0.0 collective-permute-done.2.high.refs_5_
  31.8 5.1 %forward.2 = (bf16[1024,2048]{1,0:T(8,128)(2,1)S(1)}, bf16[1024,2048]{1,0:T(8,128)(2,1)S(1)}, f32[100,2048]{1,0:T(8,128)S(1)}) custom-call(bf16[128,1024]{1,0:T(8,128)(2,1)S(1)} %collective-permute-done.1.low.refs_3_, bf16[128,1024]{1,0:T(8,128)(2,1)S(1)} %slice_bitcast_fusion.own.refs_4_, bf16[128,1024]{1,0:T(8,128)(2,1)S(1)} %collective-permute-done.2.high.refs_5_, ...), custom_call_target="tpu_custom_call" | custom-call | tf_op jit(solution)/shard_map/forward/pallas_call | solution.py:129
  36.9 0.1 collective-permute-start.8
  37.0 0.5 collective-permute-start.9
  37.5 0.1 multiply_convert_fusion.1
  37.5 1.3 %collective-permute-start.5 = (f16[100,2048]{1,0:T(8,128)(2,1)S(1)}, f16[100,2048]{1,0:T(8,128)(2,1)S(1)}, u32[]{:S(2)}, u32[]{:S(2)}) collective-permute-start(f16[100,2048]{1,0:T(8,128)(2,1)S(1)} %multiply_convert_fusion.1), channel_id=1, source_target_pairs={{0,64},{64,0},{1,65},{65,1},{2,66},{66,2},{3,67},{67,3},{4,68},{68... | collective-permute-start | bytes 1228808 | tf_op jit(solution)/shard_map/ppermute | solution.py:408
  38.9 4.3 %slope.2.s_0 = bf16[1024,2048]{1,0:T(8,128)(2,1)S(1)} custom-call(bf16[1024,2048]{1,0:T(8,128)(2,1)S(1)} %get-tuple-element.39.pre), custom_call_target="tpu_custom_call" | custom-call | tf_op jit(solution)/shard_map/slope/pallas_call | solution.py:156
  43.2 4.3 %slope.3.s_1 = bf16[1024,2048]{1,0:T(8,128)(2,1)S(1)} custom-call(bf16[1024,2048]{1,0:T(8,128)(2,1)S(1)} %get-tuple-element.40.pre), custom_call_target="tpu_custom_call" | custom-call | tf_op jit(solution)/shard_map/slope/pallas_call | solution.py:156
  47.6 0.9 turn.1.lat_own
  48.5 0.0 copy-start.4
  48.5 1.1 collective-permute-start.4
  49.6 0.0 collective-permute-done.9
  49.6 0.6 collective-permute-start.10
  50.2 0.1 convert_multiply_fusion.1.refs_4_
  50.3 6.9 %collective-permute-done.5 = f16[100,2048]{1,0:T(8,128)(2,1)S(1)} collective-permute-done((f16[100,2048]{1,0:T(8,128)(2,1)S(1)}, f16[100,2048]{1,0:T(8,128)(2,1)S(1)}, u32[]{:S(2)}, u32[]{:S(2)}) %collective-permute-start.5) | collective-permute-done | bytes 409632 | tf_op jit(solution)/shard_map/ppermute | solution.py:408
  57.2 1.3 %collective-permute-start.6 = (f16[100,2048]{1,0:T(8,128)(2,1)S(1)}, f16[100,2048]{1,0:T(8,128)(2,1)S(1)}, u32[]{:S(2)}, u32[]{:S(2)}) collective-permute-start(f16[100,2048]{1,0:T(8,128)(2,1)S(1)} %collective-permute-done.5), channel_id=1, source_target_pairs={{0,32},{32,0},{1,33},{33,1},{2,34},{34,2},{3,35},{35,3},{4,36},{36... | collective-permute-start | bytes 1228808 | tf_op jit(solution)/shard_map/ppermute | solution.py:411
  58.4 0.1 convert_multiply_fusion.3.refs_2_
  58.5 0.0 collective-permute-done.10
  58.5 0.1 convert_multiply_fusion.refs_5_
  58.6 0.0 collective-permute-done.7.refs_2_
  58.7 0.0 collective-permute-done.8.refs_3_
  58.7 4.0 %crps_near.1 = (f32[100,2048]{1,0:T(8,128)S(1)}, f32[100,2048]{1,0:T(8,128)S(1)}, f32[1,128]{1,0:T(1,128)S(1)}) custom-call(f32[100,2048]{1,0:T(8,128)S(1)} %get-tuple-element.32.refs_0_, f32[100,2048]{1,0:T(8,128)S(1)} %get-tuple-element.33.refs_1_, f32[100,2048]{1,0:T(8,128)S(1)} %collective-permute-done.7.refs_2_, ...), custom_call_target="tpu_custom_call" | custom-call | tf_op jit(solution)/shard_map/crps_near/pallas_call | solution.py:237
  62.7 0.0 collective-permute-done.6
  62.7 0.1 convert_multiply_fusion.2.refs_3_
  62.8 1.9 %crps_far.1 = (bf16[128,2048]{1,0:T(8,128)(2,1)S(1)}, bf16[128,2048]{1,0:T(8,128)(2,1)S(1)}, f32[1,128]{1,0:T(1,128)S(1)}) custom-call(f32[100,2048]{1,0:T(8,128)S(1)} %get-tuple-element.32.refs_0_, f32[100,2048]{1,0:T(8,128)S(1)} %get-tuple-element.33.refs_1_, f32[100,2048]{1,0:T(8,128)S(1)} %convert_multiply_fusion.3.refs_2_, ...), custom_call_target="tpu_custom_call" | custom-call | tf_op jit(solution)/shard_map/crps_far/pallas_call | solution.py:255
  64.7 4.8 %backward.3 = (bf16[2,768,256]{2,1,0:T(8,128)(2,1)S(1)}, f32[2,16,2,8,128]{4,3,2,1,0:T(8,128)S(1)}) custom-call(s32[2]{0:T(128)S(1)} %get-tuple-element.57.who, bf16[128,2048]{1,0:T(8,128)(2,1)S(1)} %get-tuple-element.37.d_0, bf16[128,2048]{1,0:T(8,128)(2,1)S(1)} %get-tuple-element.38.d_1, bf16[100,1024]{1,0:T(8,128)(2,1)S(1)} %copy-done.3, ...), custom_call_target="tpu_custom_call" | custom-call | tf_op jit(solution)/shard_map/backward/pallas_call | solution.py:296
  69.5 0.1 collective-permute-start.11
  69.6 0.5 collective-permute-start.12
  70.1 4.8 %backward.2 = (bf16[2,768,256]{2,1,0:T(8,128)(2,1)S(1)}, f32[2,16,2,8,128]{4,3,2,1,0:T(8,128)S(1)}) custom-call(s32[2]{0:T(128)S(1)} %get-tuple-element.56.who, bf16[128,2048]{1,0:T(8,128)(2,1)S(1)} %get-tuple-element.37.d_0, bf16[128,2048]{1,0:T(8,128)(2,1)S(1)} %get-tuple-element.38.d_1, bf16[100,1024]{1,0:T(8,128)(2,1)S(1)} %copy-done.3, ...), custom_call_target="tpu_custom_call" | custom-call | tf_op jit(solution)/shard_map/backward/pallas_call | solution.py:296
  74.8 0.0 collective-permute-done.12
  74.9 0.0 collective-permute-done.4.lat_other
  74.9 0.0 collective-permute-done.11.c_other
  74.9 2.5 %outer.1 = bf16[2,32,72,128]{3,2,1,0:T(8,128)(2,1)S(1)} custom-call(bf16[1024,768]{1,0:T(8,128)(2,1)S(1)} %turn.1.lat_own, bf16[1024,768]{1,0:T(8,128)(2,1)S(1)} %collective-permute-done.4.lat_other, bf16[2,768,256]{2,1,0:T(8,128)(2,1)S(1)} %get-tuple-element.44.c_own, bf16[2,768,256]{2,1,0:T(8,128)(2,1)S(1)} %collective-permute-done.11.c_other, ...), custom_call_target="tpu_custom_call" | custom-call | tf_op jit(solution)/shard_map/outer/pallas_call | solution.py:328
  77.3 22.6 %all_to_all.10 = bf16[64,72,128]{2,1,0:T(8,128)(2,1)S(1)} all-to-all(bf16[64,72,128]{2,1,0:T(8,128)(2,1)S(1)} %bitcast.20), channel_id=1, replica_groups=mesh['ylo'=2,'core'=2,'z'=4,'yhi'=2,'x'=4] {'ylo','z','yhi','x'}, dimensions={0} | all-to-all | bytes 2359296 | tf_op jit(solution)/shard_map/all_to_all | solution.py:434
  100.0 0.2 convert_reduce_fusion
  100.2 0.7 broadcast_in_dim.11
  100.9 6.3 %all-to-all-start.1 = ((f32[64,8,128]{2,1,0:T(8,128)}), f32[64,8,128]{2,1,0:T(8,128)S(1)}, u32[]{:S(2)}, u32[]{:S(2)}) async-start(f32[64,8,128]{2,1,0:T(8,128)} %broadcast_in_dim.11), calls=%async_computation.1 | async-start | bytes 524288 | tf_op jit(solution)/shard_map/all_to_all | solution.py:439
  107.2 1.2 collective-permute-start.14
  108.4 8.1 %all-to-all-done.1.mine = f32[64,8,128]{2,1,0:T(8,128)S(1)} async-done(((f32[64,8,128]{2,1,0:T(8,128)}), f32[64,8,128]{2,1,0:T(8,128)S(1)}, u32[]{:S(2)}, u32[]{:S(2)}) %all-to-all-start.1) | async-done | bytes 262176 | tf_op jit(solution)/shard_map/all_to_all | solution.py:439
  116.5 2.8 %collective-permute-start.13 = (f32[64,8,128]{2,1,0:T(8,128)S(1)}, f32[64,8,128]{2,1,0:T(8,128)S(1)}, u32[]{:S(2)}, u32[]{:S(2)}) collective-permute-start(f32[64,8,128]{2,1,0:T(8,128)S(1)} %all-to-all-done.1.mine), channel_id=1, source_target_pairs={{0,32},{32,0},{1,33},{33,1},{2,34},{34,2},{3,35},{35,3},{4,36},{36... | collective-permute-start | bytes 786440 | tf_op jit(solution)/shard_map/ppermute | solution.py:446
  119.3 0.0 collective-permute-done.14
  119.3 0.1 collective-permute-start.15
  119.4 0.1 pad_add_fusion.where
  119.5 1.2 collective-permute-done.15.rows_others
  120.7 0.0 collective-permute-done.13.others
  120.7 1.4 %finish.1 = (f32[32,1024]{1,0:T(8,128)}, f32[100,1024]{1,0:T(8,128)}, f32[1,1024]{1,0:T(1,128)}, f32[1,1]{1,0:T(1,128)}) custom-call(s32[2]{0:T(128)S(1)} %pad_add_fusion.where, f32[64,8,128]{2,1,0:T(8,128)S(1)} %all-to-all-done.1.mine, f32[64,8,128]{2,1,0:T(8,128)S(1)} %collective-permute-done.13.others, f32[2,32,256]{2,1,0:T(8,128)S(1)} %pad_maximum_fusion.rows_mine, ...), custom_call_target="tpu_custom_call" | custom-call | tf_op jit(solution)/shard_map/finish/pallas_call | solution.py:369
  (10 shorter events, 0.0 us)
Async XLA Ops:
  0.6 24.4 %copy-start.3 = (bf16[100,1024]{1,0:T(8,128)(2,1)S(1)}, bf16[100,1024]{1,0:T(8,128)(2,1)}, u32[]{:S(2)}) copy-start(bf16[100,1024]{1,0:T(8,128)(2,1)} %w_out.7) | copy-start | bytes 614404
  0.6 24.4 %copy-start.2 = (f32[100,2048]{1,0:T(8,128)S(1)}, f32[100,2048]{1,0:T(8,128)}, u32[]{:S(2)}) copy-start(f32[100,2048]{1,0:T(8,128)} %target.3) | copy-start | bytes 2457604
  1.7 23.3 %collective-permute-start = (bf16[128,1024]{1,0:T(8,128)(2,1)S(1)}, bf16[128,1024]{1,0:T(8,128)(2,1)S(1)}, u32[]{:S(2)}, u32[]{:S(2)}) collective-permute-start(bf16[128,1024]{1,0:T(8,128)(2,1)S(1)} %slice_bitcast_fusion.1.refs_1_.own), channel_id=1, source_target_pairs={{0,1},{1,2},{2,3},{3,4},{4,5},{5,6},{6,7},{7,8},{8,9},{9,10},{10,1... | collective-permute-start | bytes 786440 | tf_op jit(solution)/shard_map/ppermute | solution.py:398
  3.8 21.2 %collective-permute-start.3 = (bf16[128,1024]{1,0:T(8,128)(2,1)S(1)}, bf16[128,1024]{1,0:T(8,128)(2,1)S(1)}, u32[]{:S(2)}, u32[]{:S(2)}) collective-permute-start(bf16[128,1024]{1,0:T(8,128)(2,1)S(1)} %slice_bitcast_fusion.1.refs_1_.own), channel_id=1, source_target_pairs={{1,0},{2,1},{3,2},{4,3},{5,4},{6,5},{7,6},{8,7},{9,8},{10,9},{11,1... | collective-permute-start | bytes 786440 | tf_op jit(solution)/shard_map/ppermute | solution.py:399
  12.2 19.6 %collective-permute-start.1 = (bf16[128,1024]{1,0:T(8,128)(2,1)S(1)}, bf16[128,1024]{1,0:T(8,128)(2,1)S(1)}, u32[]{:S(2)}, u32[]{:S(2)}) collective-permute-start(bf16[128,1024]{1,0:T(8,128)(2,1)S(1)} %slice_bitcast_fusion.own.refs_4_), channel_id=1, source_target_pairs={{0,1},{1,2},{2,3},{3,4},{4,5},{5,6},{6,7},{7,8},{8,9},{9,10},{10,1... | collective-permute-start | bytes 786440 | tf_op jit(solution)/shard_map/ppermute | solution.py:398
  12.3 19.5 %collective-permute-start.2 = (bf16[128,1024]{1,0:T(8,128)(2,1)S(1)}, bf16[128,1024]{1,0:T(8,128)(2,1)S(1)}, u32[]{:S(2)}, u32[]{:S(2)}) collective-permute-start(bf16[128,1024]{1,0:T(8,128)(2,1)S(1)} %slice_bitcast_fusion.own.refs_4_), channel_id=1, source_target_pairs={{1,0},{2,1},{3,2},{4,3},{5,4},{6,5},{7,6},{8,7},{9,8},{10,9},{11,1... | collective-permute-start | bytes 786440 | tf_op jit(solution)/shard_map/ppermute | solution.py:399
  19.5 1.6 %copy-start = (bf16[1024,1024]{1,0:T(8,128)(2,1)S(1)}, bf16[1024,1024]{1,0:T(8,128)(2,1)}, u32[]{:S(2)}) copy-start(bf16[1024,1024]{1,0:T(8,128)(2,1)} %w_node.3) | copy-start | bytes 6291460
  21.1 3.9 %copy-start.1 = (bf16[1024,1024]{1,0:T(8,128)(2,1)S(1)}, bf16[1024,1024]{1,0:T(8,128)(2,1)}, u32[]{:S(2)}) copy-start(bf16[1024,1024]{1,0:T(8,128)(2,1)} %w_node.3) | copy-start | bytes 6291460
  30.1 28.5 %collective-permute-start.7 = (f32[100,2048]{1,0:T(8,128)S(1)}, f32[100,2048]{1,0:T(8,128)S(1)}, u32[]{:S(2)}, u32[]{:S(2)}) collective-permute-start(f32[100,2048]{1,0:T(8,128)S(1)} %get-tuple-element.32.refs_0_), channel_id=1, source_target_pairs={{0,32},{32,0},{1,33},{33,1},{2,34},{34,2},{3,35},{35,3},{4,36},{36... | collective-permute-start | bytes 2457608 | tf_op jit(solution)/shard_map/ppermute | solution.py:409
  36.9 21.7 %collective-permute-start.8 = (f32[100,2048]{1,0:T(8,128)S(1)}, f32[100,2048]{1,0:T(8,128)S(1)}, u32[]{:S(2)}, u32[]{:S(2)}) collective-permute-start(f32[100,2048]{1,0:T(8,128)S(1)} %get-tuple-element.33.refs_1_), channel_id=1, source_target_pairs={{0,32},{32,0},{1,33},{33,1},{2,34},{34,2},{3,35},{35,3},{4,36},{36... | collective-permute-start | bytes 2457608 | tf_op jit(solution)/shard_map/ppermute | solution.py:409
  37.0 12.6 %collective-permute-start.9 = (f16[100,2048]{1,0:T(8,128)(2,1)S(1)}, f16[100,2048]{1,0:T(8,128)(2,1)S(1)}, u32[]{:S(2)}, u32[]{:S(2)}) collective-permute-start(f16[100,2048]{1,0:T(8,128)(2,1)S(1)} %multiply_convert_fusion), channel_id=1, source_target_pairs={{0,64},{64,0},{1,65},{65,1},{2,66},{66,2},{3,67},{67,3},{4,68},{68... | collective-permute-start | bytes 1228808 | tf_op jit(solution)/shard_map/ppermute | solution.py:408
  37.5 19.6 %collective-permute-start.5 = (f16[100,2048]{1,0:T(8,128)(2,1)S(1)}, f16[100,2048]{1,0:T(8,128)(2,1)S(1)}, u32[]{:S(2)}, u32[]{:S(2)}) collective-permute-start(f16[100,2048]{1,0:T(8,128)(2,1)S(1)} %multiply_convert_fusion.1), channel_id=1, source_target_pairs={{0,64},{64,0},{1,65},{65,1},{2,66},{66,2},{3,67},{67,3},{4,68},{68... | collective-permute-start | bytes 1228808 | tf_op jit(solution)/shard_map/ppermute | solution.py:408
  48.5 10.2 %copy-start.4 = (f32[2048]{0:T(1024)S(1)}, f32[2048]{0:T(1024)}, u32[]{:S(2)}) copy-start(f32[2048]{0:T(1024)} %param.15) | copy-start | bytes 24580
  48.5 26.3 %collective-permute-start.4 = (bf16[1024,768]{1,0:T(8,128)(2,1)S(1)}, bf16[1024,768]{1,0:T(8,128)(2,1)S(1)}, u32[]{:S(2)}, u32[]{:S(2)}) collective-permute-start(bf16[1024,768]{1,0:T(8,128)(2,1)S(1)} %turn.1.lat_own), channel_id=1, source_target_pairs={{0,32},{32,0},{1,33},{33,1},{2,34},{34,2},{3,35},{35,3},{4,36},{36... | collective-permute-start | bytes 4718600 | tf_op jit(solution)/shard_map/ppermute | solution.py:415
  49.6 9.0 %collective-permute-start.10 = (f16[100,2048]{1,0:T(8,128)(2,1)S(1)}, f16[100,2048]{1,0:T(8,128)(2,1)S(1)}, u32[]{:S(2)}, u32[]{:S(2)}) collective-permute-start(f16[100,2048]{1,0:T(8,128)(2,1)S(1)} %collective-permute-done.9), channel_id=1, source_target_pairs={{0,32},{32,0},{1,33},{33,1},{2,34},{34,2},{3,35},{35,3},{4,36},{36... | collective-permute-start | bytes 1228808 | tf_op jit(solution)/shard_map/ppermute | solution.py:411
  57.2 5.5 %collective-permute-start.6 = (f16[100,2048]{1,0:T(8,128)(2,1)S(1)}, f16[100,2048]{1,0:T(8,128)(2,1)S(1)}, u32[]{:S(2)}, u32[]{:S(2)}) collective-permute-start(f16[100,2048]{1,0:T(8,128)(2,1)S(1)} %collective-permute-done.5), channel_id=1, source_target_pairs={{0,32},{32,0},{1,33},{33,1},{2,34},{34,2},{3,35},{35,3},{4,36},{36... | collective-permute-start | bytes 1228808 | tf_op jit(solution)/shard_map/ppermute | solution.py:411
  69.5 5.4 %collective-permute-start.11 = (bf16[2,768,256]{2,1,0:T(8,128)(2,1)S(1)}, bf16[2,768,256]{2,1,0:T(8,128)(2,1)S(1)}, u32[]{:S(2)}, u32[]{:S(2)}) collective-permute-start(bf16[2,768,256]{2,1,0:T(8,128)(2,1)S(1)} %get-tuple-element.45), channel_id=1, source_target_pairs={{0,32},{32,0},{1,33},{33,1},{2,34},{34,2},{3,35},{35,3},{4,36},{36... | collective-permute-start | bytes 2359304 | tf_op jit(solution)/shard_map/ppermute | solution.py:427
  69.6 5.3 %collective-permute-start.12 = (f32[2,16,2,8,128]{4,3,2,1,0:T(8,128)S(1)}, f32[2,16,2,8,128]{4,3,2,1,0:T(8,128)S(1)}, u32[]{:S(2)}, u32[]{:S(2)}) collective-permute-start(f32[2,16,2,8,128]{4,3,2,1,0:T(8,128)S(1)} %get-tuple-element.47), channel_id=1, source_target_pairs={{0,32},{32,0},{1,33},{33,1},{2,34},{34,2},{3,35},{35,3},{4,36},{36... | collective-permute-start | bytes 786440 | tf_op jit(solution)/shard_map/ppermute | solution.py:428
  100.9 15.6 %all-to-all-start.1 = ((f32[64,8,128]{2,1,0:T(8,128)}), f32[64,8,128]{2,1,0:T(8,128)S(1)}, u32[]{:S(2)}, u32[]{:S(2)}) async-start(f32[64,8,128]{2,1,0:T(8,128)} %broadcast_in_dim.11), calls=%async_computation.1 | async-start | bytes 524288 | tf_op jit(solution)/shard_map/all_to_all | solution.py:439
  107.2 12.1 %collective-permute-start.14 = (f32[32,256]{1,0:T(8,128)S(1)}, f32[32,256]{1,0:T(8,128)S(1)}, u32[]{:S(2)}, u32[]{:S(2)}) collective-permute-start(f32[32,256]{1,0:T(8,128)S(1)} %pad_maximum_fusion.1), channel_id=1, source_target_pairs={{0,64},{64,0},{1,65},{65,1},{2,66},{66,2},{3,67},{67,3},{4,68},{68... | collective-permute-start | bytes 98312 | tf_op jit(solution)/shard_map/ppermute | solution.py:442
  116.5 4.2 %collective-permute-start.13 = (f32[64,8,128]{2,1,0:T(8,128)S(1)}, f32[64,8,128]{2,1,0:T(8,128)S(1)}, u32[]{:S(2)}, u32[]{:S(2)}) collective-permute-start(f32[64,8,128]{2,1,0:T(8,128)S(1)} %all-to-all-done.1.mine), channel_id=1, source_target_pairs={{0,32},{32,0},{1,33},{33,1},{2,34},{34,2},{3,35},{35,3},{4,36},{36... | collective-permute-start | bytes 786440 | tf_op jit(solution)/shard_map/ppermute | solution.py:446
  119.3 1.3 %collective-permute-start.15 = (f32[2,32,256]{2,1,0:T(8,128)S(1)}, f32[2,32,256]{2,1,0:T(8,128)S(1)}, u32[]{:S(2)}, u32[]{:S(2)}) collective-permute-start(f32[2,32,256]{2,1,0:T(8,128)S(1)} %pad_maximum_fusion.rows_mine), channel_id=1, source_target_pairs={{0,32},{32,0},{1,33},{33,1},{2,34},{34,2},{3,35},{35,3},{4,36},{36... | collective-permute-start | bytes 196616 | tf_op jit(solution)/shard_map/ppermute | solution.py:445

commit v8 on v7

--- a/solution.py
+++ b/solution.py
@@ -39,10 +39,6 @@
 
 def settled(a):
     return pltpu.with_memory_space_constraint(a, pltpu.HBM)
-
-
-def whole(a):
-    return pl.BlockSpec(a.shape, lambda *i: (0,) * a.ndim)
 
 
 def prep_kernel(src, weight, bias, *rest):
@@ -103,7 +99,7 @@
     )(*blocks)
 
 
-def forward_kernel(low, own, high, w_node, at, bias, w_out, target, hid, pre, err, proj):
+def forward_kernel(low, own, high, w_node, at, bias, w_out, target, hid, slope, err, proj):
     nodes = 3 * low.shape[0]
 
     stacked = jnp.concatenate([low[...], own[...], high[...]], axis=0)
@@ -115,9 +111,11 @@
         for r in range(proj.shape[0] // 256):
             rows = slice(r * 256, (r + 1) * 256)
             x = dot(proj[rows, :], at[:, cols])
-            pre[rows, cols] = x.astype(bf16)
-            u = 0.5 + 0.5 * jnp.tanh(x * (C0 + (C0 * C1) * (x * x)))
-            hid[rows, cols] = (x * u).astype(bf16)
+            sq = x * x
+            u = 0.5 + 0.5 * jnp.tanh(x * (C0 + (C0 * C1) * sq))
+            h = x * u
+            hid[rows, cols] = h.astype(bf16)
+            slope[rows, cols] = (u + h * (1.0 - u) * (2.0 * C0 + (6.0 * C0 * C1) * sq)).astype(bf16)
     err[...] = dot(w_out[...], hid[...]) - target[...]
 
 
@@ -139,29 +137,6 @@
         compiler_params=pltpu.CompilerParams(vmem_limit_bytes=24 << 20),
         name="forward",
     )(parked(low), parked(own), parked(high), parked(w_node), parked(at), parked(bias), parked(w_out), parked(target))
-
-
-def slope_kernel(pre, out):
-    for g in range(pre.shape[1] // WIDE):
-        cols = slice(g * WIDE, (g + 1) * WIDE)
-        x = pre[:, cols].astype(f32)
-        sq = x * x
-        u = 0.5 + 0.5 * jnp.tanh(x * (C0 + (C0 * C1) * sq))
-        out[:, cols] = (u + (x * u) * (1.0 - u) * (2.0 * C0 + (6.0 * C0 * C1) * sq)).astype(bf16)
-
-
-def slopes(pre):
-    width, points = pre.shape
-    rows = pl.BlockSpec((128, points), lambda i: (i, 0))
-    return pl.pallas_call(
-        slope_kernel,
-        grid=(width // 128,),
-        in_specs=[rows],
-        out_specs=rows,
-        out_shape=pltpu.VMEM((width, points), bf16),
-        compiler_params=params(("arbitrary",), 8),
-        name="slope",
-    )(parked(pre))
 
 
 def apart(d):
@@ -310,33 +285,33 @@
 def outer_kernel(lat_own, lat_other, c_own, c_other, h_own, h_other, out):
     regions = out.shape[1]
     share = lat_own.shape[0] // regions
-    for y in range(c_own.shape[0]):
-        part = (dot(lat_own[...], c_own[y]) + dot(lat_other[...], c_other[y])).astype(bf16)
-        for r in range(regions):
-            for j in range(part.shape[1] // 128):
-                out[y, r, j * share : (j + 1) * share] = part[r * share : (r + 1) * share, j * 128 : (j + 1) * 128]
-            out[y, r, 2 * share :] = (h_own[y, r] + h_other[y, r]).astype(bf16)
+    for i in range(lat_own.shape[0] // WIDE):
+        rows = slice(i * WIDE, (i + 1) * WIDE)
+        for y in range(c_own.shape[0]):
+            part = (dot(lat_own[rows], c_own[y]) + dot(lat_other[rows], c_other[y])).astype(bf16)
+            for k in range(WIDE // share):
+                r = i * (WIDE // share) + k
+                for j in range(part.shape[1] // 128):
+                    out[y, r, j * share : (j + 1) * share] = part[k * share : (k + 1) * share, j * 128 : (j + 1) * 128]
+                out[y, r, 2 * share :] = (h_own[y, r] + h_other[y, r]).astype(bf16)
 
 
 def outer(lat_own, lat_other, c_own, c_other, h_own, h_other, regions):
-    inputs, nodes = lat_own.shape
-    halves, _, _ = c_own.shape
+    inputs = lat_own.shape[0]
+    halves = c_own.shape[0]
     share = inputs // regions
-    here = WIDE // share
-    lat = pl.BlockSpec((WIDE, nodes), lambda i: (i, 0))
-    piece = pl.BlockSpec((halves, here, 8, 128), lambda i: (0, i, 0, 0))
+    vm = pl.BlockSpec(memory_space=pltpu.VMEM)
     return pl.pallas_call(
         outer_kernel,
-        grid=(inputs // WIDE,),
-        in_specs=[lat, lat, whole(c_own), whole(c_own), piece, piece],
-        out_specs=pl.BlockSpec((halves, here, 2 * share + 8, 128), lambda i: (0, i, 0, 0)),
+        in_specs=[vm] * 6,
+        out_specs=vm,
         out_shape=pltpu.VMEM((halves, regions, 2 * share + 8, 128), bf16),
-        compiler_params=params(("arbitrary",), 16),
+        compiler_params=pltpu.CompilerParams(vmem_limit_bytes=12 << 20),
         name="outer",
-    )(parked(lat_own), lat_other, parked(c_own), c_other, parked(h_own), h_other)
-
-
-def finish_kernel(where, mine, others, rows_mine, rows_others, grad_node, grad_out, grad_bias, loss):
+    )(*map(parked, (lat_own, lat_other, c_own, c_other, h_own, h_other)))
+
+
+def finish_kernel(where, table, rows_mine, rows_others, grad_node, grad_out, grad_bias, loss):
     variables, _ = grad_out.shape
     per_row = WIDE // 128
     lower = where[1] == 0
@@ -345,13 +320,13 @@
         for ylo in range(rows_mine.shape[0]):
             left = (2 * ylo + core) * WIDE
             grad_node[:, left : left + WIDE] = jnp.where(first, rows_mine[ylo], rows_others[ylo])
-        for at in range(mine.shape[0]):
-            ylo, place = at // 32, at % 32
+        for at in range(table.shape[0]):
+            ylo, place = at // 64, at % 32
             i, j = place // per_row, place % per_row
             left, top = (2 * ylo + core) * WIDE + j * 128, i * 8
-            if top >= variables + 2:
+            if top >= variables + 2 or at // 32 % 2 != core:
                 continue
-            piece = jnp.where(first, mine[at], others[at])
+            piece = table[at]
             rows = min(8, variables - top)
             if rows > 0:
                 grad_out[top : top + rows, left : left + 128] = piece[:rows]
@@ -364,11 +339,11 @@
                     loss[...] = jnp.sum(jnp.where(spot == where[0], values, 0.0), axis=1, keepdims=True)
 
 
-def finish(where, mine, others, rows_mine, rows_others, variables, width):
+def finish(where, table, rows_mine, rows_others, variables, width):
     vm = pl.BlockSpec(memory_space=pltpu.VMEM)
     return pl.pallas_call(
         finish_kernel,
-        in_specs=[pl.BlockSpec(memory_space=pltpu.SMEM)] + [vm] * 4,
+        in_specs=[pl.BlockSpec(memory_space=pltpu.SMEM)] + [vm] * 3,
         out_shape=[
             jax.ShapeDtypeStruct((rows_mine.shape[1], width), f32),
             jax.ShapeDtypeStruct((variables, width), f32),
@@ -377,7 +352,7 @@
         ],
         compiler_params=pltpu.CompilerParams(vmem_limit_bytes=8 << 20),
         name="finish",
-    )(where, mine, others, rows_mine, rows_others)
+    )(where, table, rows_mine, rows_others)
 
 
 def local(latent, w_node, bias, w_out, edge_src, edge_weight, target, area):
@@ -403,7 +378,7 @@
     for m in range(members):
         h, s, e = forward(low[m], mine[m], high[m], w_node, at, lift, w_out, target)
         hid.append(h)
-        slope.append(slopes(s))
+        slope.append(s)
         err.append(e)
         over = lax.ppermute((e * 0.125).astype(f16), "ylo", swap)
         near.append(lax.ppermute(e, "core", swap))
@@ -429,7 +404,7 @@
     kept, heads_kept = back(core)
     tiles = (2, regions, 8, 128)
     part = outer(lat_t, lat_t_other, kept, taken, heads_kept.reshape(tiles), heads_taken.reshape(tiles), regions)
-    chips = lax.axis_size(CHIPS)
+    chips, every = lax.axis_size(CHIPS), lax.axis_size(EVERY)
     share = width // regions
     shares = lax.all_to_all(
         part.reshape(chips, 2 * share + 8, 128), CHIPS, split_axis=0, concat_axis=0, tiled=True
@@ -437,15 +412,14 @@
     summed = shares.astype(f32).sum(axis=0)
     own = jnp.concatenate([summed[:share], summed[share : 2 * share]], axis=1)
     table = lax.all_to_all(
-        jnp.broadcast_to(summed[2 * share :], (chips, 8, 128)), CHIPS, split_axis=0, concat_axis=0, tiled=True
+        jnp.broadcast_to(summed[2 * share :], (every, 8, 128)), EVERY, split_axis=0, concat_axis=0, tiled=True
     )
     across = lax.ppermute(own, "ylo", swap)
     upper = lax.axis_index("ylo") == 1
     rows = jnp.stack([jnp.where(upper, across, own), jnp.where(upper, own, across)])
     rows_others = lax.ppermute(rows, "core", swap)
-    table_others = lax.ppermute(table, "core", swap)
     who = jnp.stack([where, core]).astype(jnp.int32)
-    grad_node, grad_out, grad_bias, loss_here = finish(who, table, table_others, rows, rows_others, variables, width)
+    grad_node, grad_out, grad_bias, loss_here = finish(who, table, rows, rows_others, variables, width)
     grad_bias = grad_bias.reshape(width)
     loss_here = loss_here.reshape(1)
     return grad_node, grad_out, grad_bias, loss_here

time: 122 us -> 125 us (1.025)
  waiting for transfers between devices: 16.2 us -> 24.2 us
  Pallas kernels: 42.9 us -> 36.4 us
  starting transfers between devices: 34.2 us -> 35.5 us
    pallas_call x3 -> x1, Pallas kernels: 11.1 us -> 1.8 us  [outer(): pl.pallas_call(outer_kernel, in_specs=[vm] * 6, out_specs=vm, out_shape=p...]
    ppermute x2, waiting for transfers between devices: 6.89 us -> 14.2 us  [local(): over = lax.ppermute((e * 0.125).astype(f16), 'ylo', swap)]
    pallas_call x2, Pallas kernels: 10.2 us -> 13.1 us  [forward(): pl.pallas_call(forward_kernel, in_specs=[vm] * 8, out_specs=[vm] * 3, out...]
    ppermute x1 -> x0, starting transfers between devices: 2.83 us -> none  [local(): table_others = lax.ppermute(table, 'core', swap)]
    ppermute x1, waiting for transfers between devices: 0.01 us -> 2.62 us  [local(): across = lax.ppermute(own, 'ylo', swap)]
    ppermute x1, starting transfers between devices: 0.09 us -> 2.4 us  [local(): rows_others = lax.ppermute(rows, 'core', swap)]
    all_to_all x1, waiting for transfers between devices: 8.1 us -> 6.47 us  [local(): lax.all_to_all(jnp.broadcast_to(summed[2 * share:], (every, 8, 128)), EVE...]
    ppermute x2, starting transfers between devices: 1.88 us -> 3.42 us  [local(): beside.append(lax.ppermute(over, 'core', swap).astype(f32) * 8.0)]
  transfers between devices with their start and end apart: 17 -> 16, of which waited for: 3 -> 5; matrix products, arithmetic and copies ran while one was open for 1% -> 1% of each run, Pallas kernels for 32% -> 27%
where the time goes in v8:
time: 125 us
  Pallas kernels  36.4 us (29%)
  starting transfers between devices  35.5 us (28%)
  waiting for transfers between devices  24.2 us (19%)
  blocking collectives  22.4 us (18%)
  local copies, waits for them, and re-layouts  4.5 us (4%)
    all_to_all x1, blocking collectives, local(): lax.all_to_all(part.reshape(chips, 2 * share + 8, 128), CHIPS, split_axis...  22.4 us
    ppermute x2, starting transfers between devices, local(): high.append(lax.ppermute(mine[m], REGION, behind))  14.6 us
    ppermute x2, waiting for transfers between devices, local(): over = lax.ppermute((e * 0.125).astype(f16), 'ylo', swap)  14.2 us
    pallas_call x2, Pallas kernels, forward(): pl.pallas_call(forward_kernel, in_specs=[vm] * 8, out_specs=[vm] * 3, out...  13.1 us
    pallas_call x2, Pallas kernels, backward(): pl.pallas_call(backward_kernel, in_specs=[pl.BlockSpec(memory_space=pltpu...  9.49 us
    all_to_all x1, waiting for transfers between devices, local(): lax.all_to_all(jnp.broadcast_to(summed[2 * share:], (every, 8, 128)), EVE...  6.47 us
    all_to_all x1, starting transfers between devices, local(): lax.all_to_all(jnp.broadcast_to(summed[2 * share:], (every, 8, 128)), EVE...  6.29 us
    pallas_call x1, Pallas kernels, crps_near(): pl.pallas_call(lambda *refs: near_kernel(count, variables * points, *refs...  3.99 us
  transfers between devices with their start and end apart: 16, of which 5 were waited for; matrix products, arithmetic and copies ran while one was open for 1% of the time, Pallas kernels for 27%

profile of v8, /device:TPU:1, one launch (start us, length us, event | category | flops | bytes accessed | tf_op | source)
XLA Modules:
  0.0 124.7 jit_solution(18071379984352059484)
XLA Ops:
  0.6 0.0 copy-start.3
  0.6 0.0 copy-start.2
  0.7 1.1 slice_bitcast_fusion.1.refs_1_.own
  1.7 2.1 %collective-permute-start = (bf16[128,1024]{1,0:T(8,128)(2,1)S(1)}, bf16[128,1024]{1,0:T(8,128)(2,1)S(1)}, u32[]{:S(2)}, u32[]{:S(2)}) collective-permute-start(bf16[128,1024]{1,0:T(8,128)(2,1)S(1)} %slice_bitcast_fusion.1.refs_1_.own), channel_id=1, source_target_pairs={{0,1},{1,2},{2,3},{3,4},{4,5},{5,6},{6,7},{7,8},{8,9},{9,10},{10,1... | collective-permute-start | bytes 786440 | tf_op jit(solution)/shard_map/ppermute | solution.py:373
  3.8 7.5 %collective-permute-start.3 = (bf16[128,1024]{1,0:T(8,128)(2,1)S(1)}, bf16[128,1024]{1,0:T(8,128)(2,1)S(1)}, u32[]{:S(2)}, u32[]{:S(2)}) collective-permute-start(bf16[128,1024]{1,0:T(8,128)(2,1)S(1)} %slice_bitcast_fusion.1.refs_1_.own), channel_id=1, source_target_pairs={{1,0},{2,1},{3,2},{4,3},{5,4},{6,5},{7,6},{8,7},{9,8},{10,9},{11,1... | collective-permute-start | bytes 786440 | tf_op jit(solution)/shard_map/ppermute | solution.py:374
  11.3 1.0 slice_bitcast_fusion.own.refs_4_
  12.2 0.1 collective-permute-start.1
  12.3 7.2 %collective-permute-start.2 = (bf16[128,1024]{1,0:T(8,128)(2,1)S(1)}, bf16[128,1024]{1,0:T(8,128)(2,1)S(1)}, u32[]{:S(2)}, u32[]{:S(2)}) collective-permute-start(bf16[128,1024]{1,0:T(8,128)(2,1)S(1)} %slice_bitcast_fusion.own.refs_4_), channel_id=1, source_target_pairs={{1,0},{2,1},{3,2},{4,3},{5,4},{6,5},{7,6},{8,7},{9,8},{10,9},{11,1... | collective-permute-start | bytes 786440 | tf_op jit(solution)/shard_map/ppermute | solution.py:374
  19.5 0.0 copy-start
  19.5 1.6 %copy-done = bf16[1024,1024]{1,0:T(8,128)(2,1)S(1)} copy-done((bf16[1024,1024]{1,0:T(8,128)(2,1)S(1)}, bf16[1024,1024]{1,0:T(8,128)(2,1)}, u32[]{:S(2)}) %copy-start) | copy-done | bytes 2097176
  21.1 3.8 %prep.1 = (bf16[512,2048]{1,0:T(8,128)(2,1)S(1)}, bf16[128,1024]{1,0:T(8,128)(2,1)S(1)}) custom-call(s32[3,2048]{1,0:T(4,128)} %bitcast.25, f32[3,2048]{1,0:T(4,128)} %bitcast.26, f32[1,1024]{1,0:T(1,128)} %bitcast.27, bf16[1024,1024]{1,0:T(8,128)(2,1)S(1)} %copy-done), custom_call_target="tpu_custom_call" | custom-call | tf_op jit(solution)/shard_map/prep/pallas_call | solution.py:68
  24.9 0.1 pad_add_fusion.1
  25.0 0.0 collective-permute-done.refs_0_.low
  25.0 0.0 collective-permute-done.3.refs_2_.high
  25.0 0.0 copy-done.3
  25.0 0.0 copy-done.2
  25.0 0.0 copy-done.1
  25.0 6.6 %forward.3 = (bf16[1024,2048]{1,0:T(8,128)(2,1)S(1)}, bf16[1024,2048]{1,0:T(8,128)(2,1)S(1)}, f32[100,2048]{1,0:T(8,128)S(1)}) custom-call(bf16[128,1024]{1,0:T(8,128)(2,1)S(1)} %collective-permute-done.refs_0_.low, bf16[128,1024]{1,0:T(8,128)(2,1)S(1)} %slice_bitcast_fusion.1.refs_1_.own, bf16[128,1024]{1,0:T(8,128)(2,1)S(1)} %collective-permute-done.3.refs_2_.high, ...), custom_call_target="tpu_custom_call" | custom-call | tf_op jit(solution)/shard_map/forward/pallas_call | solution.py:127
  31.6 1.8 %collective-permute-start.7 = (f32[100,2048]{1,0:T(8,128)S(1)}, f32[100,2048]{1,0:T(8,128)S(1)}, u32[]{:S(2)}, u32[]{:S(2)}) collective-permute-start(f32[100,2048]{1,0:T(8,128)S(1)} %get-tuple-element.32.refs_0_), channel_id=1, source_target_pairs={{0,32},{32,0},{1,33},{33,1},{2,34},{34,2},{3,35},{35,3},{4,36},{36... | collective-permute-start | bytes 2457608 | tf_op jit(solution)/shard_map/ppermute | solution.py:384
  33.4 0.1 multiply_convert_fusion
  33.4 0.0 collective-permute-done.1.low.refs_3_
  33.4 0.0 collective-permute-done.2.high.refs_5_
  33.5 6.5 %forward.2 = (bf16[1024,2048]{1,0:T(8,128)(2,1)S(1)}, bf16[1024,2048]{1,0:T(8,128)(2,1)S(1)}, f32[100,2048]{1,0:T(8,128)S(1)}) custom-call(bf16[128,1024]{1,0:T(8,128)(2,1)S(1)} %collective-permute-done.1.low.refs_3_, bf16[128,1024]{1,0:T(8,128)(2,1)S(1)} %slice_bitcast_fusion.own.refs_4_, bf16[128,1024]{1,0:T(8,128)(2,1)S(1)} %collective-permute-done.2.high.refs_5_, ...), custom_call_target="tpu_custom_call" | custom-call | tf_op jit(solution)/shard_map/forward/pallas_call | solution.py:127
  40.0 0.1 collective-permute-start.8
  40.1 0.5 collective-permute-start.9
  40.5 0.1 multiply_convert_fusion.1
  40.6 1.1 collective-permute-start.5
  41.8 0.9 turn.1.lat_own
  42.7 0.0 copy-start.4
  42.7 1.1 collective-permute-start.4
  43.8 7.3 %collective-permute-done.9 = f16[100,2048]{1,0:T(8,128)(2,1)S(1)} collective-permute-done((f16[100,2048]{1,0:T(8,128)(2,1)S(1)}, f16[100,2048]{1,0:T(8,128)(2,1)S(1)}, u32[]{:S(2)}, u32[]{:S(2)}) %collective-permute-start.9) | collective-permute-done | bytes 409632 | tf_op jit(solution)/shard_map/ppermute | solution.py:383
  51.1 2.1 %collective-permute-start.10 = (f16[100,2048]{1,0:T(8,128)(2,1)S(1)}, f16[100,2048]{1,0:T(8,128)(2,1)S(1)}, u32[]{:S(2)}, u32[]{:S(2)}) collective-permute-start(f16[100,2048]{1,0:T(8,128)(2,1)S(1)} %collective-permute-done.9), channel_id=1, source_target_pairs={{0,32},{32,0},{1,33},{33,1},{2,34},{34,2},{3,35},{35,3},{4,36},{36... | collective-permute-start | bytes 1228808 | tf_op jit(solution)/shard_map/ppermute | solution.py:386
  53.3 0.1 convert_multiply_fusion.1.refs_4_
  53.4 6.9 %collective-permute-done.5 = f16[100,2048]{1,0:T(8,128)(2,1)S(1)} collective-permute-done((f16[100,2048]{1,0:T(8,128)(2,1)S(1)}, f16[100,2048]{1,0:T(8,128)(2,1)S(1)}, u32[]{:S(2)}, u32[]{:S(2)}) %collective-permute-start.5) | collective-permute-done | bytes 409632 | tf_op jit(solution)/shard_map/ppermute | solution.py:383
  60.2 1.3 %collective-permute-start.6 = (f16[100,2048]{1,0:T(8,128)(2,1)S(1)}, f16[100,2048]{1,0:T(8,128)(2,1)S(1)}, u32[]{:S(2)}, u32[]{:S(2)}) collective-permute-start(f16[100,2048]{1,0:T(8,128)(2,1)S(1)} %collective-permute-done.5), channel_id=1, source_target_pairs={{0,32},{32,0},{1,33},{33,1},{2,34},{34,2},{3,35},{35,3},{4,36},{36... | collective-permute-start | bytes 1228808 | tf_op jit(solution)/shard_map/ppermute | solution.py:386
  61.5 0.1 convert_multiply_fusion.3.refs_2_
  61.6 0.0 collective-permute-done.10
  61.6 0.1 convert_multiply_fusion.refs_5_
  61.7 0.0 collective-permute-done.7.refs_2_
  61.7 0.0 collective-permute-done.8.refs_3_
  61.7 0.0 copy-done.4
  61.7 4.0 %crps_near.1 = (f32[100,2048]{1,0:T(8,128)S(1)}, f32[100,2048]{1,0:T(8,128)S(1)}, f32[1,128]{1,0:T(1,128)S(1)}) custom-call(f32[100,2048]{1,0:T(8,128)S(1)} %get-tuple-element.32.refs_0_, f32[100,2048]{1,0:T(8,128)S(1)} %get-tuple-element.33.refs_1_, f32[100,2048]{1,0:T(8,128)S(1)} %collective-permute-done.7.refs_2_, ...), custom_call_target="tpu_custom_call" | custom-call | tf_op jit(solution)/shard_map/crps_near/pallas_call | solution.py:212
  65.7 0.0 collective-permute-done.6
  65.7 0.1 convert_multiply_fusion.2.refs_3_
  65.8 1.9 %crps_far.1 = (bf16[128,2048]{1,0:T(8,128)(2,1)S(1)}, bf16[128,2048]{1,0:T(8,128)(2,1)S(1)}, f32[1,128]{1,0:T(1,128)S(1)}) custom-call(f32[100,2048]{1,0:T(8,128)S(1)} %get-tuple-element.32.refs_0_, f32[100,2048]{1,0:T(8,128)S(1)} %get-tuple-element.33.refs_1_, f32[100,2048]{1,0:T(8,128)S(1)} %convert_multiply_fusion.3.refs_2_, ...), custom_call_target="tpu_custom_call" | custom-call | tf_op jit(solution)/shard_map/crps_far/pallas_call | solution.py:230
  67.8 4.7 %backward.3 = (bf16[2,768,256]{2,1,0:T(8,128)(2,1)S(1)}, f32[2,16,2,8,128]{4,3,2,1,0:T(8,128)S(1)}) custom-call(s32[2]{0:T(128)S(1)} %get-tuple-element.57.who, bf16[128,2048]{1,0:T(8,128)(2,1)S(1)} %get-tuple-element.37.d_0, bf16[128,2048]{1,0:T(8,128)(2,1)S(1)} %get-tuple-element.38.d_1, bf16[100,1024]{1,0:T(8,128)(2,1)S(1)} %copy-done.3, ...), custom_call_target="tpu_custom_call" | custom-call | tf_op jit(solution)/shard_map/backward/pallas_call | solution.py:271
  72.5 0.1 collective-permute-start.11
  72.6 0.5 collective-permute-start.12
  73.1 4.7 %backward.2 = (bf16[2,768,256]{2,1,0:T(8,128)(2,1)S(1)}, f32[2,16,2,8,128]{4,3,2,1,0:T(8,128)S(1)}) custom-call(s32[2]{0:T(128)S(1)} %get-tuple-element.56.who, bf16[128,2048]{1,0:T(8,128)(2,1)S(1)} %get-tuple-element.37.d_0, bf16[128,2048]{1,0:T(8,128)(2,1)S(1)} %get-tuple-element.38.d_1, bf16[100,1024]{1,0:T(8,128)(2,1)S(1)} %copy-done.3, ...), custom_call_target="tpu_custom_call" | custom-call | tf_op jit(solution)/shard_map/backward/pallas_call | solution.py:271
  77.9 0.0 collective-permute-done.12
  77.9 0.0 collective-permute-done.4.lat_other
  77.9 0.0 collective-permute-done.11.c_other
  77.9 1.8 %outer.1 = bf16[2,32,72,128]{3,2,1,0:T(8,128)(2,1)S(1)} custom-call(bf16[1024,768]{1,0:T(8,128)(2,1)S(1)} %turn.1.lat_own, bf16[1024,768]{1,0:T(8,128)(2,1)S(1)} %collective-permute-done.4.lat_other, bf16[2,768,256]{2,1,0:T(8,128)(2,1)S(1)} %get-tuple-element.44.c_own, bf16[2,768,256]{2,1,0:T(8,128)(2,1)S(1)} %collective-permute-done.11.c_other, ...), custom_call_target="tpu_custom_call" | custom-call | tf_op jit(solution)/shard_map/outer/pallas_call | solution.py:304
  79.7 22.4 %all_to_all.10 = bf16[64,72,128]{2,1,0:T(8,128)(2,1)S(1)} all-to-all(bf16[64,72,128]{2,1,0:T(8,128)(2,1)S(1)} %bitcast.20), channel_id=1, replica_groups=mesh['ylo'=2,'core'=2,'z'=4,'yhi'=2,'x'=4] {'ylo','z','yhi','x'}, dimensions={0} | all-to-all | bytes 2359296 | tf_op jit(solution)/shard_map/all_to_all | solution.py:409
  102.1 0.2 convert_reduce_fusion
  102.3 0.9 broadcast_in_dim.11
  103.2 6.3 %all-to-all-start.1 = ((f32[128,8,128]{2,1,0:T(8,128)}), f32[128,8,128]{2,1,0:T(8,128)S(1)}, u32[]{:S(2)}, u32[]{:S(2)}) async-start(f32[128,8,128]{2,1,0:T(8,128)} %broadcast_in_dim.11), calls=%async_computation.1 | async-start | bytes 1048576 | tf_op jit(solution)/shard_map/all_to_all | solution.py:414
  109.5 1.4 %collective-permute-start.13 = (f32[32,256]{1,0:T(8,128)S(1)}, f32[32,256]{1,0:T(8,128)S(1)}, u32[]{:S(2)}, u32[]{:S(2)}) collective-permute-start(f32[32,256]{1,0:T(8,128)S(1)} %pad_maximum_fusion.1), channel_id=1, source_target_pairs={{0,64},{64,0},{1,65},{65,1},{2,66},{66,2},{3,67},{67,3},{4,68},{68... | collective-permute-start | bytes 98312 | tf_op jit(solution)/shard_map/ppermute | solution.py:417
  110.9 2.6 %collective-permute-done.13 = f32[32,256]{1,0:T(8,128)S(1)} collective-permute-done((f32[32,256]{1,0:T(8,128)S(1)}, f32[32,256]{1,0:T(8,128)S(1)}, u32[]{:S(2)}, u32[]{:S(2)}) %collective-permute-start.13) | collective-permute-done | bytes 32800 | tf_op jit(solution)/shard_map/ppermute | solution.py:417
  113.6 2.4 %collective-permute-start.14 = (f32[2,32,256]{2,1,0:T(8,128)S(1)}, f32[2,32,256]{2,1,0:T(8,128)S(1)}, u32[]{:S(2)}, u32[]{:S(2)}) collective-permute-start(f32[2,32,256]{2,1,0:T(8,128)S(1)} %pad_maximum_fusion.rows_mine), channel_id=1, source_target_pairs={{0,32},{32,0},{1,33},{33,1},{2,34},{34,2},{3,35},{35,3},{4,36},{36... | collective-permute-start | bytes 196616 | tf_op jit(solution)/shard_map/ppermute | solution.py:420
  116.0 0.1 pad_add_fusion.where
  116.0 0.8 collective-permute-done.14.rows_others
  116.9 6.5 %all-to-all-done.1.table = f32[128,8,128]{2,1,0:T(8,128)S(1)} async-done(((f32[128,8,128]{2,1,0:T(8,128)}), f32[128,8,128]{2,1,0:T(8,128)S(1)}, u32[]{:S(2)}, u32[]{:S(2)}) %all-to-all-start.1) | async-done | bytes 524320 | tf_op jit(solution)/shard_map/all_to_all | solution.py:414
  123.3 1.4 %finish.1 = (f32[32,1024]{1,0:T(8,128)}, f32[100,1024]{1,0:T(8,128)}, f32[1,1024]{1,0:T(1,128)}, f32[1,1]{1,0:T(1,128)}) custom-call(s32[2]{0:T(128)S(1)} %pad_add_fusion.where, f32[128,8,128]{2,1,0:T(8,128)S(1)} %all-to-all-done.1.table, f32[2,32,256]{2,1,0:T(8,128)S(1)} %pad_maximum_fusion.rows_mine, f32[2,32,256]{2,1,0:T(8,128)S(1)} %collective-permute-done.14.rows_others), custom_call_target="tpu_custom_call" | custom-call | tf_op jit(solution)/shard_map/finish/pallas_call | solution.py:344
  (6 shorter events, 0.0 us)
Async XLA Ops:
  0.6 24.4 %copy-start.3 = (bf16[100,1024]{1,0:T(8,128)(2,1)S(1)}, bf16[100,1024]{1,0:T(8,128)(2,1)}, u32[]{:S(2)}) copy-start(bf16[100,1024]{1,0:T(8,128)(2,1)} %w_out.7) | copy-start | bytes 614404
  0.6 24.4 %copy-start.2 = (f32[100,2048]{1,0:T(8,128)S(1)}, f32[100,2048]{1,0:T(8,128)}, u32[]{:S(2)}) copy-start(f32[100,2048]{1,0:T(8,128)} %target.3) | copy-start | bytes 2457604
  1.7 23.3 %collective-permute-start = (bf16[128,1024]{1,0:T(8,128)(2,1)S(1)}, bf16[128,1024]{1,0:T(8,128)(2,1)S(1)}, u32[]{:S(2)}, u32[]{:S(2)}) collective-permute-start(bf16[128,1024]{1,0:T(8,128)(2,1)S(1)} %slice_bitcast_fusion.1.refs_1_.own), channel_id=1, source_target_pairs={{0,1},{1,2},{2,3},{3,4},{4,5},{5,6},{6,7},{7,8},{8,9},{9,10},{10,1... | collective-permute-start | bytes 786440 | tf_op jit(solution)/shard_map/ppermute | solution.py:373
  3.8 21.2 %collective-permute-start.3 = (bf16[128,1024]{1,0:T(8,128)(2,1)S(1)}, bf16[128,1024]{1,0:T(8,128)(2,1)S(1)}, u32[]{:S(2)}, u32[]{:S(2)}) collective-permute-start(bf16[128,1024]{1,0:T(8,128)(2,1)S(1)} %slice_bitcast_fusion.1.refs_1_.own), channel_id=1, source_target_pairs={{1,0},{2,1},{3,2},{4,3},{5,4},{6,5},{7,6},{8,7},{9,8},{10,9},{11,1... | collective-permute-start | bytes 786440 | tf_op jit(solution)/shard_map/ppermute | solution.py:374
  12.2 21.2 %collective-permute-start.1 = (bf16[128,1024]{1,0:T(8,128)(2,1)S(1)}, bf16[128,1024]{1,0:T(8,128)(2,1)S(1)}, u32[]{:S(2)}, u32[]{:S(2)}) collective-permute-start(bf16[128,1024]{1,0:T(8,128)(2,1)S(1)} %slice_bitcast_fusion.own.refs_4_), channel_id=1, source_target_pairs={{0,1},{1,2},{2,3},{3,4},{4,5},{5,6},{6,7},{7,8},{8,9},{9,10},{10,1... | collective-permute-start | bytes 786440 | tf_op jit(solution)/shard_map/ppermute | solution.py:373
  12.3 21.1 %collective-permute-start.2 = (bf16[128,1024]{1,0:T(8,128)(2,1)S(1)}, bf16[128,1024]{1,0:T(8,128)(2,1)S(1)}, u32[]{:S(2)}, u32[]{:S(2)}) collective-permute-start(bf16[128,1024]{1,0:T(8,128)(2,1)S(1)} %slice_bitcast_fusion.own.refs_4_), channel_id=1, source_target_pairs={{1,0},{2,1},{3,2},{4,3},{5,4},{6,5},{7,6},{8,7},{9,8},{10,9},{11,1... | collective-permute-start | bytes 786440 | tf_op jit(solution)/shard_map/ppermute | solution.py:374
  19.5 1.6 %copy-start = (bf16[1024,1024]{1,0:T(8,128)(2,1)S(1)}, bf16[1024,1024]{1,0:T(8,128)(2,1)}, u32[]{:S(2)}) copy-start(bf16[1024,1024]{1,0:T(8,128)(2,1)} %w_node.3) | copy-start | bytes 6291460
  21.1 3.9 %copy-start.1 = (bf16[1024,1024]{1,0:T(8,128)(2,1)S(1)}, bf16[1024,1024]{1,0:T(8,128)(2,1)}, u32[]{:S(2)}) copy-start(bf16[1024,1024]{1,0:T(8,128)(2,1)} %w_node.3) | copy-start | bytes 6291460
  31.6 30.1 %collective-permute-start.7 = (f32[100,2048]{1,0:T(8,128)S(1)}, f32[100,2048]{1,0:T(8,128)S(1)}, u32[]{:S(2)}, u32[]{:S(2)}) collective-permute-start(f32[100,2048]{1,0:T(8,128)S(1)} %get-tuple-element.32.refs_0_), channel_id=1, source_target_pairs={{0,32},{32,0},{1,33},{33,1},{2,34},{34,2},{3,35},{35,3},{4,36},{36... | collective-permute-start | bytes 2457608 | tf_op jit(solution)/shard_map/ppermute | solution.py:384
  40.0 21.7 %collective-permute-start.8 = (f32[100,2048]{1,0:T(8,128)S(1)}, f32[100,2048]{1,0:T(8,128)S(1)}, u32[]{:S(2)}, u32[]{:S(2)}) collective-permute-start(f32[100,2048]{1,0:T(8,128)S(1)} %get-tuple-element.33.refs_1_), channel_id=1, source_target_pairs={{0,32},{32,0},{1,33},{33,1},{2,34},{34,2},{3,35},{35,3},{4,36},{36... | collective-permute-start | bytes 2457608 | tf_op jit(solution)/shard_map/ppermute | solution.py:384
  40.1 11.0 %collective-permute-start.9 = (f16[100,2048]{1,0:T(8,128)(2,1)S(1)}, f16[100,2048]{1,0:T(8,128)(2,1)S(1)}, u32[]{:S(2)}, u32[]{:S(2)}) collective-permute-start(f16[100,2048]{1,0:T(8,128)(2,1)S(1)} %multiply_convert_fusion), channel_id=1, source_target_pairs={{0,64},{64,0},{1,65},{65,1},{2,66},{66,2},{3,67},{67,3},{4,68},{68... | collective-permute-start | bytes 1228808 | tf_op jit(solution)/shard_map/ppermute | solution.py:383
  40.6 19.6 %collective-permute-start.5 = (f16[100,2048]{1,0:T(8,128)(2,1)S(1)}, f16[100,2048]{1,0:T(8,128)(2,1)S(1)}, u32[]{:S(2)}, u32[]{:S(2)}) collective-permute-start(f16[100,2048]{1,0:T(8,128)(2,1)S(1)} %multiply_convert_fusion.1), channel_id=1, source_target_pairs={{0,64},{64,0},{1,65},{65,1},{2,66},{66,2},{3,67},{67,3},{4,68},{68... | collective-permute-start | bytes 1228808 | tf_op jit(solution)/shard_map/ppermute | solution.py:383
  42.7 19.0 %copy-start.4 = (f32[2048]{0:T(1024)S(1)}, f32[2048]{0:T(1024)}, u32[]{:S(2)}) copy-start(f32[2048]{0:T(1024)} %param.15) | copy-start | bytes 24580
  42.7 35.2 %collective-permute-start.4 = (bf16[1024,768]{1,0:T(8,128)(2,1)S(1)}, bf16[1024,768]{1,0:T(8,128)(2,1)S(1)}, u32[]{:S(2)}, u32[]{:S(2)}) collective-permute-start(bf16[1024,768]{1,0:T(8,128)(2,1)S(1)} %turn.1.lat_own), channel_id=1, source_target_pairs={{0,32},{32,0},{1,33},{33,1},{2,34},{34,2},{3,35},{35,3},{4,36},{36... | collective-permute-start | bytes 4718600 | tf_op jit(solution)/shard_map/ppermute | solution.py:390
  51.1 10.5 %collective-permute-start.10 = (f16[100,2048]{1,0:T(8,128)(2,1)S(1)}, f16[100,2048]{1,0:T(8,128)(2,1)S(1)}, u32[]{:S(2)}, u32[]{:S(2)}) collective-permute-start(f16[100,2048]{1,0:T(8,128)(2,1)S(1)} %collective-permute-done.9), channel_id=1, source_target_pairs={{0,32},{32,0},{1,33},{33,1},{2,34},{34,2},{3,35},{35,3},{4,36},{36... | collective-permute-start | bytes 1228808 | tf_op jit(solution)/shard_map/ppermute | solution.py:386
  60.2 5.5 %collective-permute-start.6 = (f16[100,2048]{1,0:T(8,128)(2,1)S(1)}, f16[100,2048]{1,0:T(8,128)(2,1)S(1)}, u32[]{:S(2)}, u32[]{:S(2)}) collective-permute-start(f16[100,2048]{1,0:T(8,128)(2,1)S(1)} %collective-permute-done.5), channel_id=1, source_target_pairs={{0,32},{32,0},{1,33},{33,1},{2,34},{34,2},{3,35},{35,3},{4,36},{36... | collective-permute-start | bytes 1228808 | tf_op jit(solution)/shard_map/ppermute | solution.py:386
  72.5 5.4 %collective-permute-start.11 = (bf16[2,768,256]{2,1,0:T(8,128)(2,1)S(1)}, bf16[2,768,256]{2,1,0:T(8,128)(2,1)S(1)}, u32[]{:S(2)}, u32[]{:S(2)}) collective-permute-start(bf16[2,768,256]{2,1,0:T(8,128)(2,1)S(1)} %get-tuple-element.45), channel_id=1, source_target_pairs={{0,32},{32,0},{1,33},{33,1},{2,34},{34,2},{3,35},{35,3},{4,36},{36... | collective-permute-start | bytes 2359304 | tf_op jit(solution)/shard_map/ppermute | solution.py:402
  72.6 5.2 %collective-permute-start.12 = (f32[2,16,2,8,128]{4,3,2,1,0:T(8,128)S(1)}, f32[2,16,2,8,128]{4,3,2,1,0:T(8,128)S(1)}, u32[]{:S(2)}, u32[]{:S(2)}) collective-permute-start(f32[2,16,2,8,128]{4,3,2,1,0:T(8,128)S(1)} %get-tuple-element.47), channel_id=1, source_target_pairs={{0,32},{32,0},{1,33},{33,1},{2,34},{34,2},{3,35},{35,3},{4,36},{36... | collective-permute-start | bytes 786440 | tf_op jit(solution)/shard_map/ppermute | solution.py:403
  103.2 20.2 %all-to-all-start.1 = ((f32[128,8,128]{2,1,0:T(8,128)}), f32[128,8,128]{2,1,0:T(8,128)S(1)}, u32[]{:S(2)}, u32[]{:S(2)}) async-start(f32[128,8,128]{2,1,0:T(8,128)} %broadcast_in_dim.11), calls=%async_computation.1 | async-start | bytes 1048576 | tf_op jit(solution)/shard_map/all_to_all | solution.py:414
  109.5 4.1 %collective-permute-start.13 = (f32[32,256]{1,0:T(8,128)S(1)}, f32[32,256]{1,0:T(8,128)S(1)}, u32[]{:S(2)}, u32[]{:S(2)}) collective-permute-start(f32[32,256]{1,0:T(8,128)S(1)} %pad_maximum_fusion.1), channel_id=1, source_target_pairs={{0,64},{64,0},{1,65},{65,1},{2,66},{66,2},{3,67},{67,3},{4,68},{68... | collective-permute-start | bytes 98312 | tf_op jit(solution)/shard_map/ppermute | solution.py:417
  113.6 3.3 %collective-permute-start.14 = (f32[2,32,256]{2,1,0:T(8,128)S(1)}, f32[2,32,256]{2,1,0:T(8,128)S(1)}, u32[]{:S(2)}, u32[]{:S(2)}) collective-permute-start(f32[2,32,256]{2,1,0:T(8,128)S(1)} %pad_maximum_fusion.rows_mine), channel_id=1, source_target_pairs={{0,32},{32,0},{1,33},{33,1},{2,34},{34,2},{3,35},{35,3},{4,36},{36... | collective-permute-start | bytes 196616 | tf_op jit(solution)/shard_map/ppermute | solution.py:420

commit v9 on v8

--- a/solution.py
+++ b/solution.py
@@ -115,11 +115,14 @@
             u = 0.5 + 0.5 * jnp.tanh(x * (C0 + (C0 * C1) * sq))
             h = x * u
             hid[rows, cols] = h.astype(bf16)
-            slope[rows, cols] = (u + h * (1.0 - u) * (2.0 * C0 + (6.0 * C0 * C1) * sq)).astype(bf16)
+            if slope.dtype == f32:
+                slope[rows, cols] = x
+            else:
+                slope[rows, cols] = (u + h * (1.0 - u) * (2.0 * C0 + (6.0 * C0 * C1) * sq)).astype(bf16)
     err[...] = dot(w_out[...], hid[...]) - target[...]
 
 
-def forward(low, own, high, w_node, at, bias, w_out, target):
+def forward(low, own, high, w_node, at, bias, w_out, target, kept):
     width = w_node.shape[1]
     points = at.shape[1]
     variables = target.shape[0]
@@ -130,13 +133,36 @@
         out_specs=[vm] * 3,
         out_shape=[
             pltpu.VMEM((width, points), bf16),
-            pltpu.VMEM((width, points), bf16),
+            pltpu.VMEM((width, points), kept),
             pltpu.VMEM((variables, points), f32),
         ],
         scratch_shapes=[pltpu.VMEM((width, at.shape[0]), bf16)],
-        compiler_params=pltpu.CompilerParams(vmem_limit_bytes=24 << 20),
+        compiler_params=pltpu.CompilerParams(vmem_limit_bytes=12 << 20),
         name="forward",
     )(parked(low), parked(own), parked(high), parked(w_node), parked(at), parked(bias), parked(w_out), parked(target))
+
+
+def slope_kernel(pre, out):
+    for g in range(pre.shape[1] // WIDE):
+        cols = slice(g * WIDE, (g + 1) * WIDE)
+        x = pre[:, cols]
+        sq = x * x
+        u = 0.5 + 0.5 * jnp.tanh(x * (C0 + (C0 * C1) * sq))
+        out[:, cols] = (u + (x * u) * (1.0 - u) * (2.0 * C0 + (6.0 * C0 * C1) * sq)).astype(bf16)
+
+
+def slopes(pre):
+    width, points = pre.shape
+    rows = pl.BlockSpec((128, points), lambda i: (i, 0))
+    return pl.pallas_call(
+        slope_kernel,
+        grid=(width // 128,),
+        in_specs=[rows],
+        out_specs=rows,
+        out_shape=pltpu.VMEM((width, points), bf16),
+        compiler_params=params(("arbitrary",), 8),
+        name="slope",
+    )(parked(pre))
 
 
 def apart(d):
@@ -238,16 +264,15 @@
     )(*map(parked, own), *others, *map(parked, partial), area, before)
 
 
-def backward_kernel(who, d_0, d_1, w_out, s_0, s_1, h_0, h_1, at, loss, contrib, heads, dpre):
+def backward_kernel(who, d_0, d_1, w_out, s_0, s_1, h_0, h_1, at, contrib, heads, dpre):
     nodes = at.shape[0] - DEEP
     variables = w_out.shape[0]
     shape = (PAD, WIDE)
     row = lax.broadcasted_iota(jnp.int32, shape, 0)
-    lane = lax.broadcasted_iota(jnp.int32, shape, 1)
     for y in range(contrib.shape[0]):
         first = pl.multiple_of((2 * y + who[0]) * WIDE, WIDE)
         rows = pl.ds(first, WIDE)
-        total = jnp.where((row == variables + 1) & (lane + first == who[1]), jnp.sum(loss[...]), 0.0)
+        total = jnp.zeros(shape, f32)
         turned = w_out[:, rows].T
         for m, (d, slope, hid) in enumerate(((d_0, s_0, h_0), (d_1, s_1, h_1))):
             for g in range(d.shape[1] // WIDE):
@@ -263,14 +288,14 @@
                 heads[y, i, j] = total[i * 8 : (i + 1) * 8, j * 128 : (j + 1) * 128]
 
 
-def backward(who, dpred, w_out, slope, hid, at, loss):
+def backward(who, dpred, w_out, slope, hid, at):
     width, points = slope[0].shape
     nodes = at.shape[0] - DEEP
     count = width // WIDE // 2
     vm = pl.BlockSpec(memory_space=pltpu.VMEM)
     return pl.pallas_call(
         backward_kernel,
-        in_specs=[pl.BlockSpec(memory_space=pltpu.SMEM)] + [vm] * 9,
+        in_specs=[pl.BlockSpec(memory_space=pltpu.SMEM)] + [vm] * 8,
         out_specs=[vm, vm],
         out_shape=[
             pltpu.VMEM((count, 2 * nodes, WIDE), bf16),
@@ -279,7 +304,7 @@
         scratch_shapes=[pltpu.VMEM((count, 2, WIDE, points), bf16)],
         compiler_params=pltpu.CompilerParams(vmem_limit_bytes=24 << 20),
         name="backward",
-    )(who, *map(parked, dpred), parked(w_out), *map(parked, slope), *map(parked, hid), parked(at), parked(loss))
+    )(who, *map(parked, dpred), parked(w_out), *map(parked, slope), *map(parked, hid), parked(at))
 
 
 def outer_kernel(lat_own, lat_other, c_own, c_other, h_own, h_other, out):
@@ -314,29 +339,30 @@
 def finish_kernel(where, table, rows_mine, rows_others, grad_node, grad_out, grad_bias, loss):
     variables, _ = grad_out.shape
     per_row = WIDE // 128
-    lower = where[1] == 0
+    lower = where[0] == 0
+    share = grad_node.shape[0]
+    total = jnp.zeros((1, 1), f32)
     for core in range(2):
         first = lower if core == 0 else jnp.logical_not(lower)
         for ylo in range(rows_mine.shape[0]):
             left = (2 * ylo + core) * WIDE
-            grad_node[:, left : left + WIDE] = jnp.where(first, rows_mine[ylo], rows_others[ylo])
+            both = jnp.where(first, rows_mine[ylo], rows_others[ylo])
+            grad_node[:, left : left + WIDE] = both[:share]
+            total = total + both[share : share + 1, :1]
         for at in range(table.shape[0]):
             ylo, place = at // 64, at % 32
             i, j = place // per_row, place % per_row
             left, top = (2 * ylo + core) * WIDE + j * 128, i * 8
             if top >= variables + 2 or at // 32 % 2 != core:
                 continue
-            piece = table[at]
+            piece = table[at].astype(f32)
             rows = min(8, variables - top)
             if rows > 0:
                 grad_out[top : top + rows, left : left + 128] = piece[:rows]
             line = variables - top
             if 0 <= line < 7:
                 grad_bias[:, left : left + 128] = piece[line : line + 1]
-                if left == 0:
-                    values = piece[line + 1 : line + 2]
-                    spot = lax.broadcasted_iota(jnp.int32, values.shape, 1)
-                    loss[...] = jnp.sum(jnp.where(spot == where[0], values, 0.0), axis=1, keepdims=True)
+    loss[...] = total
 
 
 def finish(where, table, rows_mine, rows_others, variables, width):
@@ -345,7 +371,7 @@
         finish_kernel,
         in_specs=[pl.BlockSpec(memory_space=pltpu.SMEM)] + [vm] * 3,
         out_shape=[
-            jax.ShapeDtypeStruct((rows_mine.shape[1], width), f32),
+            jax.ShapeDtypeStruct((rows_mine.shape[1] - 8, width), f32),
             jax.ShapeDtypeStruct((variables, width), f32),
             jax.ShapeDtypeStruct((1, width), f32),
             jax.ShapeDtypeStruct((1, 1), f32),
@@ -364,7 +390,6 @@
     behind = [(t, s) for s, t in ahead]
     swap = [(0, 1), (1, 0)]
     core = lax.axis_index("core")
-    where = lax.axis_index(REGION)
 
     mine = [latent[0]] + [lax.optimization_barrier(latent)[m] for m in range(1, members)]
 
@@ -372,13 +397,13 @@
     for m in range(members):
         low.append(lax.ppermute(mine[m], REGION, ahead))
         high.append(lax.ppermute(mine[m], REGION, behind))
-    at, lift = prep(edge_src.T, edge_weight.T, bias[None, :], 3 * nodes, (w_node,))
+    at, lift = prep(edge_src.T, edge_weight.T, bias[None, :], 3 * nodes, (w_node, target))
 
     hid, slope, err, near, far, beside = [], [], [], [], [], []
     for m in range(members):
-        h, s, e = forward(low[m], mine[m], high[m], w_node, at, lift, w_out, target)
+        h, s, e = forward(low[m], mine[m], high[m], w_node, at, lift, w_out, target, f32 if m else bf16)
         hid.append(h)
-        slope.append(s)
+        slope.append(slopes(s) if m else s)
         err.append(e)
         over = lax.ppermute((e * 0.125).astype(f16), "ylo", swap)
         near.append(lax.ppermute(e, "core", swap))
@@ -395,8 +420,7 @@
 
 
     def back(side):
-        who = jnp.stack([side, where]).astype(jnp.int32)
-        return backward(who, (d_0, d_1), w_out, slope, hid, at, loss)
+        return backward(side[None].astype(jnp.int32), (d_0, d_1), w_out, slope, hid, at)
 
     given, heads_given = back(1 - core)
     taken = lax.ppermute(given, "core", swap)
@@ -411,14 +435,15 @@
     )
     summed = shares.astype(f32).sum(axis=0)
     own = jnp.concatenate([summed[:share], summed[share : 2 * share]], axis=1)
+    own = jnp.concatenate([own, jnp.full((8, own.shape[1]), jnp.sum(loss), f32)])
     table = lax.all_to_all(
-        jnp.broadcast_to(summed[2 * share :], (every, 8, 128)), EVERY, split_axis=0, concat_axis=0, tiled=True
+        jnp.broadcast_to(summed[2 * share :].astype(bf16), (every, 8, 128)), EVERY, split_axis=0, concat_axis=0, tiled=True
     )
     across = lax.ppermute(own, "ylo", swap)
     upper = lax.axis_index("ylo") == 1
     rows = jnp.stack([jnp.where(upper, across, own), jnp.where(upper, own, across)])
     rows_others = lax.ppermute(rows, "core", swap)
-    who = jnp.stack([where, core]).astype(jnp.int32)
+    who = core[None].astype(jnp.int32)
     grad_node, grad_out, grad_bias, loss_here = finish(who, table, rows, rows_others, variables, width)
     grad_bias = grad_bias.reshape(width)
     loss_here = loss_here.reshape(1)

time: 125 us -> 125 us (level)
  blocking collectives: 22.4 us -> 0 us
  waiting for transfers between devices: 24.2 us -> 37.7 us
  starting transfers between devices: 35.5 us -> 39 us
  Pallas kernels: 36.4 us -> 38.4 us
  other arithmetic: 0.85 us -> 2.6 us
    all_to_all x1 -> x0, blocking collectives: 22.4 us -> none  [local(): lax.all_to_all(part.reshape(chips, 2 * share + 8, 128), CHIPS, split_axis...]
    all_to_all x1 -> x2, waiting for transfers between devices: 6.47 us -> 26.6 us  [the longest x1 18 us: local(): lax.all_to_all(part.reshape(chips, 2 * share + 8, 128), CHIPS, split_axis...]
    all_to_all x1 -> x2, starting transfers between devices: 6.29 us -> 12.3 us  [the longest x1 7.68 us: local(): lax.all_to_all(jnp.broadcast_to(summed[2 * share:].astype(bf16), (every,...]
    ppermute x2, waiting for transfers between devices: 14.2 us -> 10.2 us  [local(): over = lax.ppermute((e * 0.125).astype(f16), 'ylo', swap)]
    pallas_call x0 -> x1, Pallas kernels: none -> 4.05 us  [slopes(): pl.pallas_call(slope_kernel, grid=(width // 128,), in_specs=[rows], out_s...]
    ppermute x1, waiting for transfers between devices: 2.62 us -> 0.01 us  [local(): across = lax.ppermute(own, 'ylo', swap)]
    pallas_call x2, Pallas kernels: 13.1 us -> 11.5 us  [forward(): pl.pallas_call(forward_kernel, in_specs=[vm] * 8, out_specs=[vm] * 3, out...]
    ppermute x1, starting transfers between devices: 1.43 us -> 0.14 us  [local(): across = lax.ppermute(own, 'ylo', swap)]
  transfers between devices with their start and end apart: 16 -> 17, of which waited for: 5 -> 5; matrix products, arithmetic and copies ran while one was open for 1% -> 3% of each run, Pallas kernels for 27% -> 28%
where the time goes in v9:
time: 125 us; the launch traced here: 124 us
  starting transfers between devices  39 us (31%)
  Pallas kernels  38.4 us (31%)
  waiting for transfers between devices  37.7 us (30%)
  local copies, waits for them, and re-layouts  5.49 us (4%)
  other arithmetic  2.6 us (2%)
    all_to_all x1, waiting for transfers between devices, local(): lax.all_to_all(part.reshape(chips, 2 * share + 8, 128), CHIPS, split_axis...  18 us
    ppermute x2, starting transfers between devices, local(): high.append(lax.ppermute(mine[m], REGION, behind))  14.6 us
    pallas_call x2, Pallas kernels, forward(): pl.pallas_call(forward_kernel, in_specs=[vm] * 8, out_specs=[vm] * 3, out...  11.5 us
    ppermute x2, waiting for transfers between devices, local(): over = lax.ppermute((e * 0.125).astype(f16), 'ylo', swap)  10.2 us
    all_to_all x1, waiting for transfers between devices, local(): lax.all_to_all(jnp.broadcast_to(summed[2 * share:].astype(bf16), (every,...  8.63 us
    pallas_call x2, Pallas kernels, backward(): pl.pallas_call(backward_kernel, in_specs=[pl.BlockSpec(memory_space=pltpu...  8.53 us
    all_to_all x1, starting transfers between devices, local(): lax.all_to_all(jnp.broadcast_to(summed[2 * share:].astype(bf16), (every,...  7.68 us
    all_to_all x1, starting transfers between devices, local(): lax.all_to_all(part.reshape(chips, 2 * share + 8, 128), CHIPS, split_axis...  4.66 us
  transfers between devices with their start and end apart: 17, of which 5 were waited for; matrix products, arithmetic and copies ran while one was open for 3% of the time, Pallas kernels for 28%

profile of v9, /device:TPU:1, one launch (start us, length us, event | category | flops | bytes accessed | tf_op | source)
XLA Modules:
  0.0 124.1 jit_solution(1090038048361401608)
XLA Ops:
  0.6 0.0 copy-start.4
  0.6 1.0 slice_bitcast_fusion.1.refs_1_.own
  1.7 2.1 %collective-permute-start = (bf16[128,1024]{1,0:T(8,128)(2,1)S(1)}, bf16[128,1024]{1,0:T(8,128)(2,1)S(1)}, u32[]{:S(2)}, u32[]{:S(2)}) collective-permute-start(bf16[128,1024]{1,0:T(8,128)(2,1)S(1)} %slice_bitcast_fusion.1.refs_1_.own), channel_id=1, source_target_pairs={{0,1},{1,2},{2,3},{3,4},{4,5},{5,6},{6,7},{7,8},{8,9},{9,10},{10,1... | collective-permute-start | bytes 786440 | tf_op jit(solution)/shard_map/ppermute | solution.py:398
  3.8 7.5 %collective-permute-start.3 = (bf16[128,1024]{1,0:T(8,128)(2,1)S(1)}, bf16[128,1024]{1,0:T(8,128)(2,1)S(1)}, u32[]{:S(2)}, u32[]{:S(2)}) collective-permute-start(bf16[128,1024]{1,0:T(8,128)(2,1)S(1)} %slice_bitcast_fusion.1.refs_1_.own), channel_id=1, source_target_pairs={{1,0},{2,1},{3,2},{4,3},{5,4},{6,5},{7,6},{8,7},{9,8},{10,9},{11,1... | collective-permute-start | bytes 786440 | tf_op jit(solution)/shard_map/ppermute | solution.py:399
  11.2 1.0 slice_bitcast_fusion.own.refs_4_
  12.2 0.1 collective-permute-start.1
  12.3 7.2 %collective-permute-start.2 = (bf16[128,1024]{1,0:T(8,128)(2,1)S(1)}, bf16[128,1024]{1,0:T(8,128)(2,1)S(1)}, u32[]{:S(2)}, u32[]{:S(2)}) collective-permute-start(bf16[128,1024]{1,0:T(8,128)(2,1)S(1)} %slice_bitcast_fusion.own.refs_4_), channel_id=1, source_target_pairs={{1,0},{2,1},{3,2},{4,3},{5,4},{6,5},{7,6},{8,7},{9,8},{10,9},{11,1... | collective-permute-start | bytes 786440 | tf_op jit(solution)/shard_map/ppermute | solution.py:399
  19.4 1.6 %copy-done = bf16[1024,1024]{1,0:T(8,128)(2,1)S(1)} copy-done((bf16[1024,1024]{1,0:T(8,128)(2,1)S(1)}, bf16[1024,1024]{1,0:T(8,128)(2,1)}, u32[]{:S(2)}) %copy-start) | copy-done | bytes 2097176
  21.0 1.2 copy-done.2
  22.2 3.8 %prep.1 = (bf16[512,2048]{1,0:T(8,128)(2,1)S(1)}, bf16[128,1024]{1,0:T(8,128)(2,1)S(1)}) custom-call(s32[3,2048]{1,0:T(4,128)} %bitcast.23, f32[3,2048]{1,0:T(4,128)} %bitcast.24, f32[1,1024]{1,0:T(1,128)} %bitcast.25, bf16[1024,1024]{1,0:T(8,128)(2,1)S(1)} %copy-done, f32[100,2048]{1,0:T(8,128)S(1)} %copy-done.2), custom_call_target="tpu_custom_call" | custom-call | tf_op jit(solution)/shard_map/prep/pallas_call | solution.py:68
  26.0 0.0 collective-permute-done.refs_0_.low
  26.0 0.0 collective-permute-done.3.refs_2_.high
  26.0 0.0 copy-done.4
  26.0 0.0 copy-start.3
  26.1 6.6 %forward.3 = (bf16[1024,2048]{1,0:T(8,128)(2,1)S(1)}, bf16[1024,2048]{1,0:T(8,128)(2,1)S(1)}, f32[100,2048]{1,0:T(8,128)S(1)}) custom-call(bf16[128,1024]{1,0:T(8,128)(2,1)S(1)} %collective-permute-done.refs_0_.low, bf16[128,1024]{1,0:T(8,128)(2,1)S(1)} %slice_bitcast_fusion.1.refs_1_.own, bf16[128,1024]{1,0:T(8,128)(2,1)S(1)} %collective-permute-done.3.refs_2_.high, ...), custom_call_target="tpu_custom_call" | custom-call | tf_op jit(solution)/shard_map/forward/pallas_call | solution.py:130
  32.6 1.8 %collective-permute-start.7 = (f32[100,2048]{1,0:T(8,128)S(1)}, f32[100,2048]{1,0:T(8,128)S(1)}, u32[]{:S(2)}, u32[]{:S(2)}) collective-permute-start(f32[100,2048]{1,0:T(8,128)S(1)} %get-tuple-element.32.refs_0_), channel_id=1, source_target_pairs={{0,32},{32,0},{1,33},{33,1},{2,34},{34,2},{3,35},{35,3},{4,36},{36... | collective-permute-start | bytes 2457608 | tf_op jit(solution)/shard_map/ppermute | solution.py:409
  34.4 0.1 multiply_convert_fusion
  34.5 0.0 collective-permute-done.1.low.refs_3_
  34.5 0.0 collective-permute-done.2.high.refs_5_
  34.5 4.9 %forward.2 = (bf16[1024,2048]{1,0:T(8,128)(2,1)S(1)}, f32[1024,2048]{1,0:T(8,128)S(1)}, f32[100,2048]{1,0:T(8,128)S(1)}) custom-call(bf16[128,1024]{1,0:T(8,128)(2,1)S(1)} %collective-permute-done.1.low.refs_3_, bf16[128,1024]{1,0:T(8,128)(2,1)S(1)} %slice_bitcast_fusion.own.refs_4_, bf16[128,1024]{1,0:T(8,128)(2,1)S(1)} %collective-permute-done.2.high.refs_5_, ...), custom_call_target="tpu_custom_call" | custom-call | tf_op jit(solution)/shard_map/forward/pallas_call | solution.py:130
  39.5 0.1 collective-permute-start.8
  39.6 0.5 collective-permute-start.9
  40.0 0.1 multiply_convert_fusion.1
  40.1 1.1 collective-permute-start.5
  41.3 4.1 %slope.1.s_1 = bf16[1024,2048]{1,0:T(8,128)(2,1)S(1)} custom-call(f32[1024,2048]{1,0:T(8,128)S(1)} %get-tuple-element.40.pre), custom_call_target="tpu_custom_call" | custom-call | tf_op jit(solution)/shard_map/slope/pallas_call | solution.py:157
  45.3 0.9 turn.1.lat_own
  46.3 0.0 copy-start.5
  46.3 1.1 collective-permute-start.4
  47.3 3.3 %collective-permute-done.9 = f16[100,2048]{1,0:T(8,128)(2,1)S(1)} collective-permute-done((f16[100,2048]{1,0:T(8,128)(2,1)S(1)}, f16[100,2048]{1,0:T(8,128)(2,1)S(1)}, u32[]{:S(2)}, u32[]{:S(2)}) %collective-permute-start.9) | collective-permute-done | bytes 409632 | tf_op jit(solution)/shard_map/ppermute | solution.py:408
  50.6 2.1 %collective-permute-start.10 = (f16[100,2048]{1,0:T(8,128)(2,1)S(1)}, f16[100,2048]{1,0:T(8,128)(2,1)S(1)}, u32[]{:S(2)}, u32[]{:S(2)}) collective-permute-start(f16[100,2048]{1,0:T(8,128)(2,1)S(1)} %collective-permute-done.9), channel_id=1, source_target_pairs={{0,32},{32,0},{1,33},{33,1},{2,34},{34,2},{3,35},{35,3},{4,36},{36... | collective-permute-start | bytes 1228808 | tf_op jit(solution)/shard_map/ppermute | solution.py:411
  52.7 0.1 convert_multiply_fusion.1.refs_4_
  52.8 6.9 %collective-permute-done.5 = f16[100,2048]{1,0:T(8,128)(2,1)S(1)} collective-permute-done((f16[100,2048]{1,0:T(8,128)(2,1)S(1)}, f16[100,2048]{1,0:T(8,128)(2,1)S(1)}, u32[]{:S(2)}, u32[]{:S(2)}) %collective-permute-start.5) | collective-permute-done | bytes 409632 | tf_op jit(solution)/shard_map/ppermute | solution.py:408
  59.7 1.3 %collective-permute-start.6 = (f16[100,2048]{1,0:T(8,128)(2,1)S(1)}, f16[100,2048]{1,0:T(8,128)(2,1)S(1)}, u32[]{:S(2)}, u32[]{:S(2)}) collective-permute-start(f16[100,2048]{1,0:T(8,128)(2,1)S(1)} %collective-permute-done.5), channel_id=1, source_target_pairs={{0,32},{32,0},{1,33},{33,1},{2,34},{34,2},{3,35},{35,3},{4,36},{36... | collective-permute-start | bytes 1228808 | tf_op jit(solution)/shard_map/ppermute | solution.py:411
  61.0 0.1 convert_multiply_fusion.3.refs_2_
  61.1 0.0 collective-permute-done.10
  61.1 0.1 convert_multiply_fusion.refs_5_
  61.2 0.0 collective-permute-done.7.refs_2_
  61.2 0.0 collective-permute-done.8.refs_3_
  61.2 4.0 %crps_near.1 = (f32[100,2048]{1,0:T(8,128)S(1)}, f32[100,2048]{1,0:T(8,128)S(1)}, f32[1,128]{1,0:T(1,128)S(1)}) custom-call(f32[100,2048]{1,0:T(8,128)S(1)} %get-tuple-element.32.refs_0_, f32[100,2048]{1,0:T(8,128)S(1)} %get-tuple-element.33.refs_1_, f32[100,2048]{1,0:T(8,128)S(1)} %collective-permute-done.7.refs_2_, ...), custom_call_target="tpu_custom_call" | custom-call | tf_op jit(solution)/shard_map/crps_near/pallas_call | solution.py:238
  65.2 0.0 collective-permute-done.6
  65.2 0.1 convert_multiply_fusion.2.refs_3_
  65.3 1.9 %crps_far.1 = (bf16[128,2048]{1,0:T(8,128)(2,1)S(1)}, bf16[128,2048]{1,0:T(8,128)(2,1)S(1)}, f32[1,128]{1,0:T(1,128)S(1)}) custom-call(f32[100,2048]{1,0:T(8,128)S(1)} %get-tuple-element.32.refs_0_, f32[100,2048]{1,0:T(8,128)S(1)} %get-tuple-element.33.refs_1_, f32[100,2048]{1,0:T(8,128)S(1)} %convert_multiply_fusion.3.refs_2_, ...), custom_call_target="tpu_custom_call" | custom-call | tf_op jit(solution)/shard_map/crps_far/pallas_call | solution.py:256
  67.2 4.3 %backward.3 = (bf16[2,768,256]{2,1,0:T(8,128)(2,1)S(1)}, f32[2,16,2,8,128]{4,3,2,1,0:T(8,128)S(1)}) custom-call(s32[1]{0:T(128)} %bitcast.7.who, bf16[128,2048]{1,0:T(8,128)(2,1)S(1)} %get-tuple-element.37.d_0, bf16[128,2048]{1,0:T(8,128)(2,1)S(1)} %get-tuple-element.38.d_1, bf16[100,1024]{1,0:T(8,128)(2,1)S(1)} %copy-done.4, ...), custom_call_target="tpu_custom_call" | custom-call | tf_op jit(solution)/shard_map/backward/pallas_call | solution.py:296
  71.5 0.1 collective-permute-start.11
  71.6 0.5 collective-permute-start.12
  72.1 4.3 %backward.2 = (bf16[2,768,256]{2,1,0:T(8,128)(2,1)S(1)}, f32[2,16,2,8,128]{4,3,2,1,0:T(8,128)S(1)}) custom-call(s32[1]{0:T(128)} %bitcast.who.where, bf16[128,2048]{1,0:T(8,128)(2,1)S(1)} %get-tuple-element.37.d_0, bf16[128,2048]{1,0:T(8,128)(2,1)S(1)} %get-tuple-element.38.d_1, bf16[100,1024]{1,0:T(8,128)(2,1)S(1)} %copy-done.4, ...), custom_call_target="tpu_custom_call" | custom-call | tf_op jit(solution)/shard_map/backward/pallas_call | solution.py:296
  76.4 0.0 collective-permute-done.12
  76.4 0.0 collective-permute-done.4.lat_other
  76.4 0.0 collective-permute-done.11.c_other
  76.4 2.8 %outer.1 = bf16[2,32,72,128]{3,2,1,0:T(8,128)(2,1)} custom-call(bf16[1024,768]{1,0:T(8,128)(2,1)S(1)} %turn.1.lat_own, bf16[1024,768]{1,0:T(8,128)(2,1)S(1)} %collective-permute-done.4.lat_other, bf16[2,768,256]{2,1,0:T(8,128)(2,1)S(1)} %get-tuple-element.43.c_own, bf16[2,768,256]{2,1,0:T(8,128)(2,1)S(1)} %collective-permute-done.11.c_other, ...), custom_call_target="tpu_custom_call" | custom-call | tf_op jit(solution)/shard_map/outer/pallas_call | solution.py:329
  79.2 4.7 %all-to-all-start = ((bf16[64,72,128]{2,1,0:T(8,128)(2,1)}), bf16[64,72,128]{2,1,0:T(8,128)(2,1)S(1)}, u32[]{:S(2)}, u32[]{:S(2)}) async-start(bf16[64,72,128]{2,1,0:T(8,128)(2,1)} %bitcast.10), calls=%async_computation | async-start | bytes 2359296 | tf_op jit(solution)/shard_map/all_to_all | solution.py:433
  83.9 0.6 reduce_sum.19
  84.5 18.0 %all-to-all-done = bf16[64,72,128]{2,1,0:T(8,128)(2,1)S(1)} async-done(((bf16[64,72,128]{2,1,0:T(8,128)(2,1)}), bf16[64,72,128]{2,1,0:T(8,128)(2,1)S(1)}, u32[]{:S(2)}, u32[]{:S(2)}) %all-to-all-start) | async-done | bytes 1179680 | tf_op jit(solution)/shard_map/all_to_all | solution.py:433
  102.5 0.2 convert_reduce_fusion
  102.7 0.7 select_maximum_fusion
  103.3 0.1 collective-permute-start.13
  103.5 0.7 broadcast_in_dim.21
  104.2 7.7 %all-to-all-start.1 = ((bf16[128,8,128]{2,1,0:T(8,128)(2,1)}), bf16[128,8,128]{2,1,0:T(8,128)(2,1)S(1)}, u32[]{:S(2)}, u32[]{:S(2)}) async-start(bf16[128,8,128]{2,1,0:T(8,128)(2,1)} %broadcast_in_dim.21), calls=%async_computation.1 | async-start | bytes 524288 | tf_op jit(solution)/shard_map/all_to_all | solution.py:439
  111.9 0.0 collective-permute-done.13
  111.9 0.7 select_bitcast_fusion.1
  112.6 1.1 collective-permute-start.14
  113.7 0.9 collective-permute-done.14.rows_others
  114.7 8.6 %all-to-all-done.1.table = bf16[128,8,128]{2,1,0:T(8,128)(2,1)S(1)} async-done(((bf16[128,8,128]{2,1,0:T(8,128)(2,1)}), bf16[128,8,128]{2,1,0:T(8,128)(2,1)S(1)}, u32[]{:S(2)}, u32[]{:S(2)}) %all-to-all-start.1) | async-done | bytes 262176 | tf_op jit(solution)/shard_map/all_to_all | solution.py:439
  123.3 0.8 finish.1
  (9 shorter events, 0.0 us)
Async XLA Ops:
  0.6 25.4 %copy-start.4 = (bf16[100,1024]{1,0:T(8,128)(2,1)S(1)}, bf16[100,1024]{1,0:T(8,128)(2,1)}, u32[]{:S(2)}) copy-start(bf16[100,1024]{1,0:T(8,128)(2,1)} %w_out.7) | copy-start | bytes 614404
  1.7 24.4 %collective-permute-start = (bf16[128,1024]{1,0:T(8,128)(2,1)S(1)}, bf16[128,1024]{1,0:T(8,128)(2,1)S(1)}, u32[]{:S(2)}, u32[]{:S(2)}) collective-permute-start(bf16[128,1024]{1,0:T(8,128)(2,1)S(1)} %slice_bitcast_fusion.1.refs_1_.own), channel_id=1, source_target_pairs={{0,1},{1,2},{2,3},{3,4},{4,5},{5,6},{6,7},{7,8},{8,9},{9,10},{10,1... | collective-permute-start | bytes 786440 | tf_op jit(solution)/shard_map/ppermute | solution.py:398
  3.8 22.3 %collective-permute-start.3 = (bf16[128,1024]{1,0:T(8,128)(2,1)S(1)}, bf16[128,1024]{1,0:T(8,128)(2,1)S(1)}, u32[]{:S(2)}, u32[]{:S(2)}) collective-permute-start(bf16[128,1024]{1,0:T(8,128)(2,1)S(1)} %slice_bitcast_fusion.1.refs_1_.own), channel_id=1, source_target_pairs={{1,0},{2,1},{3,2},{4,3},{5,4},{6,5},{7,6},{8,7},{9,8},{10,9},{11,1... | collective-permute-start | bytes 786440 | tf_op jit(solution)/shard_map/ppermute | solution.py:399
  12.2 22.3 %collective-permute-start.1 = (bf16[128,1024]{1,0:T(8,128)(2,1)S(1)}, bf16[128,1024]{1,0:T(8,128)(2,1)S(1)}, u32[]{:S(2)}, u32[]{:S(2)}) collective-permute-start(bf16[128,1024]{1,0:T(8,128)(2,1)S(1)} %slice_bitcast_fusion.own.refs_4_), channel_id=1, source_target_pairs={{0,1},{1,2},{2,3},{3,4},{4,5},{5,6},{6,7},{7,8},{8,9},{9,10},{10,1... | collective-permute-start | bytes 786440 | tf_op jit(solution)/shard_map/ppermute | solution.py:398
  12.3 22.2 %collective-permute-start.2 = (bf16[128,1024]{1,0:T(8,128)(2,1)S(1)}, bf16[128,1024]{1,0:T(8,128)(2,1)S(1)}, u32[]{:S(2)}, u32[]{:S(2)}) collective-permute-start(bf16[128,1024]{1,0:T(8,128)(2,1)S(1)} %slice_bitcast_fusion.own.refs_4_), channel_id=1, source_target_pairs={{1,0},{2,1},{3,2},{4,3},{5,4},{6,5},{7,6},{8,7},{9,8},{10,9},{11,1... | collective-permute-start | bytes 786440 | tf_op jit(solution)/shard_map/ppermute | solution.py:399
  19.4 1.6 %copy-start = (bf16[1024,1024]{1,0:T(8,128)(2,1)S(1)}, bf16[1024,1024]{1,0:T(8,128)(2,1)}, u32[]{:S(2)}) copy-start(bf16[1024,1024]{1,0:T(8,128)(2,1)} %w_node.3) | copy-start | bytes 6291460
  21.0 1.2 copy-start.2
  22.2 3.9 %copy-start.1 = (bf16[1024,1024]{1,0:T(8,128)(2,1)S(1)}, bf16[1024,1024]{1,0:T(8,128)(2,1)}, u32[]{:S(2)}) copy-start(bf16[1024,1024]{1,0:T(8,128)(2,1)} %w_node.3) | copy-start | bytes 6291460
  26.0 8.5 %copy-start.3 = (f32[100,2048]{1,0:T(8,128)S(1)}, f32[100,2048]{1,0:T(8,128)}, u32[]{:S(2)}) copy-start(f32[100,2048]{1,0:T(8,128)} %target.3) | copy-start | bytes 2457604
  32.6 28.5 %collective-permute-start.7 = (f32[100,2048]{1,0:T(8,128)S(1)}, f32[100,2048]{1,0:T(8,128)S(1)}, u32[]{:S(2)}, u32[]{:S(2)}) collective-permute-start(f32[100,2048]{1,0:T(8,128)S(1)} %get-tuple-element.32.refs_0_), channel_id=1, source_target_pairs={{0,32},{32,0},{1,33},{33,1},{2,34},{34,2},{3,35},{35,3},{4,36},{36... | collective-permute-start | bytes 2457608 | tf_op jit(solution)/shard_map/ppermute | solution.py:409
  39.5 21.7 %collective-permute-start.8 = (f32[100,2048]{1,0:T(8,128)S(1)}, f32[100,2048]{1,0:T(8,128)S(1)}, u32[]{:S(2)}, u32[]{:S(2)}) collective-permute-start(f32[100,2048]{1,0:T(8,128)S(1)} %get-tuple-element.33.refs_1_), channel_id=1, source_target_pairs={{0,32},{32,0},{1,33},{33,1},{2,34},{34,2},{3,35},{35,3},{4,36},{36... | collective-permute-start | bytes 2457608 | tf_op jit(solution)/shard_map/ppermute | solution.py:409
  39.6 11.0 %collective-permute-start.9 = (f16[100,2048]{1,0:T(8,128)(2,1)S(1)}, f16[100,2048]{1,0:T(8,128)(2,1)S(1)}, u32[]{:S(2)}, u32[]{:S(2)}) collective-permute-start(f16[100,2048]{1,0:T(8,128)(2,1)S(1)} %multiply_convert_fusion), channel_id=1, source_target_pairs={{0,64},{64,0},{1,65},{65,1},{2,66},{66,2},{3,67},{67,3},{4,68},{68... | collective-permute-start | bytes 1228808 | tf_op jit(solution)/shard_map/ppermute | solution.py:408
  40.1 19.6 %collective-permute-start.5 = (f16[100,2048]{1,0:T(8,128)(2,1)S(1)}, f16[100,2048]{1,0:T(8,128)(2,1)S(1)}, u32[]{:S(2)}, u32[]{:S(2)}) collective-permute-start(f16[100,2048]{1,0:T(8,128)(2,1)S(1)} %multiply_convert_fusion.1), channel_id=1, source_target_pairs={{0,64},{64,0},{1,65},{65,1},{2,66},{66,2},{3,67},{67,3},{4,68},{68... | collective-permute-start | bytes 1228808 | tf_op jit(solution)/shard_map/ppermute | solution.py:408
  46.3 15.0 %copy-start.5 = (f32[2048]{0:T(1024)S(1)}, f32[2048]{0:T(1024)}, u32[]{:S(2)}) copy-start(f32[2048]{0:T(1024)} %param.15) | copy-start | bytes 24580
  46.3 30.1 %collective-permute-start.4 = (bf16[1024,768]{1,0:T(8,128)(2,1)S(1)}, bf16[1024,768]{1,0:T(8,128)(2,1)S(1)}, u32[]{:S(2)}, u32[]{:S(2)}) collective-permute-start(bf16[1024,768]{1,0:T(8,128)(2,1)S(1)} %turn.1.lat_own), channel_id=1, source_target_pairs={{0,32},{32,0},{1,33},{33,1},{2,34},{34,2},{3,35},{35,3},{4,36},{36... | collective-permute-start | bytes 4718600 | tf_op jit(solution)/shard_map/ppermute | solution.py:415
  50.6 10.5 %collective-permute-start.10 = (f16[100,2048]{1,0:T(8,128)(2,1)S(1)}, f16[100,2048]{1,0:T(8,128)(2,1)S(1)}, u32[]{:S(2)}, u32[]{:S(2)}) collective-permute-start(f16[100,2048]{1,0:T(8,128)(2,1)S(1)} %collective-permute-done.9), channel_id=1, source_target_pairs={{0,32},{32,0},{1,33},{33,1},{2,34},{34,2},{3,35},{35,3},{4,36},{36... | collective-permute-start | bytes 1228808 | tf_op jit(solution)/shard_map/ppermute | solution.py:411
  59.7 5.5 %collective-permute-start.6 = (f16[100,2048]{1,0:T(8,128)(2,1)S(1)}, f16[100,2048]{1,0:T(8,128)(2,1)S(1)}, u32[]{:S(2)}, u32[]{:S(2)}) collective-permute-start(f16[100,2048]{1,0:T(8,128)(2,1)S(1)} %collective-permute-done.5), channel_id=1, source_target_pairs={{0,32},{32,0},{1,33},{33,1},{2,34},{34,2},{3,35},{35,3},{4,36},{36... | collective-permute-start | bytes 1228808 | tf_op jit(solution)/shard_map/ppermute | solution.py:411
  71.5 4.9 %collective-permute-start.11 = (bf16[2,768,256]{2,1,0:T(8,128)(2,1)S(1)}, bf16[2,768,256]{2,1,0:T(8,128)(2,1)S(1)}, u32[]{:S(2)}, u32[]{:S(2)}) collective-permute-start(bf16[2,768,256]{2,1,0:T(8,128)(2,1)S(1)} %get-tuple-element.44), channel_id=1, source_target_pairs={{0,32},{32,0},{1,33},{33,1},{2,34},{34,2},{3,35},{35,3},{4,36},{36... | collective-permute-start | bytes 2359304 | tf_op jit(solution)/shard_map/ppermute | solution.py:426
  71.6 4.8 %collective-permute-start.12 = (f32[2,16,2,8,128]{4,3,2,1,0:T(8,128)S(1)}, f32[2,16,2,8,128]{4,3,2,1,0:T(8,128)S(1)}, u32[]{:S(2)}, u32[]{:S(2)}) collective-permute-start(f32[2,16,2,8,128]{4,3,2,1,0:T(8,128)S(1)} %get-tuple-element.46), channel_id=1, source_target_pairs={{0,32},{32,0},{1,33},{33,1},{2,34},{34,2},{3,35},{35,3},{4,36},{36... | collective-permute-start | bytes 786440 | tf_op jit(solution)/shard_map/ppermute | solution.py:427
  79.2 23.2 %all-to-all-start = ((bf16[64,72,128]{2,1,0:T(8,128)(2,1)}), bf16[64,72,128]{2,1,0:T(8,128)(2,1)S(1)}, u32[]{:S(2)}, u32[]{:S(2)}) async-start(bf16[64,72,128]{2,1,0:T(8,128)(2,1)} %bitcast.10), calls=%async_computation | async-start | bytes 2359296 | tf_op jit(solution)/shard_map/all_to_all | solution.py:433
  103.3 8.6 %collective-permute-start.13 = (f32[40,256]{1,0:T(8,128)S(1)}, f32[40,256]{1,0:T(8,128)S(1)}, u32[]{:S(2)}, u32[]{:S(2)}) collective-permute-start(f32[40,256]{1,0:T(8,128)S(1)} %select_maximum_fusion), channel_id=1, source_target_pairs={{0,64},{64,0},{1,65},{65,1},{2,66},{66,2},{3,67},{67,3},{4,68},{68... | collective-permute-start | bytes 122888 | tf_op jit(solution)/shard_map/ppermute | solution.py:442
  104.2 19.1 %all-to-all-start.1 = ((bf16[128,8,128]{2,1,0:T(8,128)(2,1)}), bf16[128,8,128]{2,1,0:T(8,128)(2,1)S(1)}, u32[]{:S(2)}, u32[]{:S(2)}) async-start(bf16[128,8,128]{2,1,0:T(8,128)(2,1)} %broadcast_in_dim.21), calls=%async_computation.1 | async-start | bytes 524288 | tf_op jit(solution)/shard_map/all_to_all | solution.py:439
  112.6 2.1 %collective-permute-start.14 = (f32[2,40,256]{2,1,0:T(8,128)S(1)}, f32[2,40,256]{2,1,0:T(8,128)S(1)}, u32[]{:S(2)}, u32[]{:S(2)}) collective-permute-start(f32[2,40,256]{2,1,0:T(8,128)S(1)} %pad_maximum_fusion.rows_mine), channel_id=1, source_target_pairs={{0,32},{32,0},{1,33},{33,1},{2,34},{34,2},{3,35},{35,3},{4,36},{36... | collective-permute-start | bytes 245768 | tf_op jit(solution)/shard_map/ppermute | solution.py:445
